TPU v7x, 32 devices: a whole 2x2x4 slice. The times are simulated.
32 devices in a mesh: tx: 2 (over y), ty: 4 (over z), lev: 4 (over x, core).
Axes of the slice: x: 2, y: 2, z: 4, core: 2. Of those that a mesh axis runs over, the one named last changes fastest.
Arguments:
- members: bfloat16 [8, 128, 64, 128], P('lev', 'tx', 'ty'), may hold values from -6 to 6
- obs_pert: bfloat16 [8192, 128], P(('tx', 'ty', 'lev')), may hold values from -6 to 6
- innovation: bfloat16 [8192], P(('tx', 'ty', 'lev')), may hold values from -6 to 6
- obs_precision: bfloat16 [8192], P(('tx', 'ty', 'lev')), may hold values from 0.25 to 4
- obs_owner: int32 [8, 4, 256], P('tx', 'ty'), may hold values from 0 to 7, as said below
- obs_slot: int32 [8, 4, 256], P('tx', 'ty'), may hold values from 0 to 1023
- obs_count: int32 [8, 4], P('tx', 'ty'), may hold values from 64 to 256
- local_weight: float32 [8, 4, 256], P('tx', 'ty'), may hold values from 0.05 to 1
Outputs:
- analysis: bfloat16 [8, 128, 64, 128], P('lev', 'tx', 'ty')
Inputs may be any that keep to these rules, and one draw needn't show every extreme that they name: `obs_owner`: the tile numbered tx index times the number of ty tiles plus ty index; it is the coarse column's own tile or one of the tiles beside it, diagonals included. `obs_count`: slots at and beyond a coarse column's count are padding.
All inputs are finite; a program needn't handle non-finite values.
Results may differ from a plain program's by a relative error of at most 0.0054.
Values may be sent and summed in bfloat16 or wider, within the bound.
No kernel may reach another device: no remote copies, remote signals or barrier semaphores. Data moves between devices by JAX's collectives and lax.ppermute only.
A program may use at most 64 MiB of HBM per device.

v0:
```python
import jax
import jax.numpy as jnp
from jax import lax
from jax.sharding import PartitionSpec as P

SPACING = 16
NS_STEPS = 4


def padded(array, sides, width):
    for axis, dim in sides:
        size, length = (lax.axis_size(axis), array.shape[dim])
        up = [(i, (i + 1) % size) for i in range(size - 1)]
        down = [(j, i) for i, j in up]
        last = lax.slice_in_dim(array, length - width, length, axis=dim)
        initial = lax.slice_in_dim(array, 0, width, axis=dim)
        before = lax.ppermute(last, axis, up)
        after = lax.ppermute(initial, axis, down)
        array = jnp.concatenate([before, array, after], axis=dim)
    return array


def finish_solve(gram_matrix, projected):
    member_count = gram_matrix.shape[1]
    spread = float(member_count - 1)
    identity = jnp.eye(member_count, dtype=jnp.float32)
    scale_norm = spread + jnp.sqrt(jnp.sum(gram_matrix * gram_matrix, axis=(1, 2)))
    sqrt_iter = (spread * identity + gram_matrix) / scale_norm[:, None, None]
    inv_iter = jnp.broadcast_to(identity, sqrt_iter.shape)
    for iteration in range(NS_STEPS):
        middle = 1.5 * identity - 0.5 * jnp.einsum(
            "bij,bjk->bik", inv_iter, sqrt_iter, precision=lax.Precision.HIGHEST
        )
        sqrt_iter = jnp.einsum("bij,bjk->bik", sqrt_iter, middle, precision=lax.Precision.HIGHEST)
        inv_iter = jnp.einsum("bij,bjk->bik", middle, inv_iter, precision=lax.Precision.HIGHEST)
    inner = jnp.einsum("bij,bj->bi", inv_iter, projected, precision=lax.Precision.HIGHEST)
    mean_weights = (
        jnp.einsum("bij,bj->bi", inv_iter, inner, precision=lax.Precision.HIGHEST)
        / scale_norm[:, None]
    )
    transform = (jnp.sqrt(spread) / jnp.sqrt(scale_norm))[:, None, None] * inv_iter + mean_weights[
        :, :, None
    ]
    return transform.astype(jnp.bfloat16)


def fractions(count, half_span):
    place = jnp.arange(count)[:, None]
    within = jnp.arange(half_span)[None, :].astype(jnp.float32)
    return jnp.where(
        place % 2 == 0,
        (within + half_span + 0.5) / (2 * half_span),
        (within + 0.5) / (2 * half_span),
    )


def solve_columns(lookup, counts, local_part, flat_pert, flat_values):
    column_count, slots = lookup.shape
    member_count = flat_pert.shape[1]
    block_len = min(slots, 128)
    live_blocks = (jnp.max(counts) + block_len - 1) // block_len

    def add_block(block_index, carry):
        gram_matrix, projected = carry
        offset = block_index * block_len
        slot_rows = lax.dynamic_slice_in_dim(lookup, offset, block_len, 1)
        slot_local = lax.dynamic_slice_in_dim(local_part, offset, block_len, 1)
        position = offset + jnp.arange(block_len)
        active = position[None, :] < counts[:, None]
        pert_rows = flat_pert[slot_rows].astype(jnp.float32)
        picked = flat_values[:, slot_rows]
        precision_w = jnp.where(active, picked[1].astype(jnp.float32) * slot_local, 0.0)
        departure = picked[0].astype(jnp.float32)
        gram_matrix = gram_matrix + jnp.einsum(
            "bsk,bsm->bkm",
            pert_rows * precision_w[:, :, None],
            pert_rows,
            precision=lax.Precision.HIGHEST,
        )
        projected = projected + jnp.einsum(
            "bsk,bs->bk", pert_rows, precision_w * departure, precision=lax.Precision.HIGHEST
        )
        return (gram_matrix, projected)

    start_gram = jnp.zeros((column_count, member_count, member_count), jnp.float32)
    start_proj = jnp.zeros((column_count, member_count), jnp.float32)
    gram_matrix, projected = lax.fori_loop(0, live_blocks, add_block, (start_gram, start_proj))
    return finish_solve(gram_matrix, projected)


def clamp_edges(rimmed, axis_index, axis_count, dim):
    lower = jnp.where(
        axis_index == 0,
        lax.slice_in_dim(rimmed, 1, 2, axis=dim),
        lax.slice_in_dim(rimmed, 0, 1, axis=dim),
    )
    last = rimmed.shape[dim]
    upper = jnp.where(
        axis_index == axis_count - 1,
        lax.slice_in_dim(rimmed, last - 2, last - 1, axis=dim),
        lax.slice_in_dim(rimmed, last - 1, last, axis=dim),
    )
    return jnp.concatenate(
        [lower, lax.slice_in_dim(rimmed, 1, last - 1, axis=dim), upper], axis=dim
    )


def per_device(
    members, obs_pert, innovation, obs_precision, obs_owner, obs_slot, obs_count, local_weight
):
    scalars = jnp.stack([innovation, obs_precision])
    tile_pert, tile_values = (
        lax.all_gather(obs_pert, "lev", axis=0, tiled=True),
        lax.all_gather(scalars, "lev", axis=1, tiled=True),
    )
    near_pert, near_values = (
        padded(tile_pert[None, None], (("tx", 0), ("ty", 1)), 1),
        padded(tile_values[None, None], (("tx", 0), ("ty", 1)), 1),
    )
    tile_len = near_pert.shape[2]
    member_count = near_pert.shape[3]
    flat_pert = near_pert.reshape(9 * tile_len, member_count)
    flat_values = jnp.transpose(near_values, (2, 0, 1, 3)).reshape(2, 9 * tile_len)
    column_x = lax.axis_index("tx")
    column_y = lax.axis_index("ty")
    tiles_x = lax.axis_size("tx")
    tiles_y = lax.axis_size("ty")
    near_x = obs_owner // tiles_y - column_x + 1
    near_y = obs_owner % tiles_y - column_y + 1
    lookup = (near_x * 3 + near_y) * tile_len + obs_slot
    coarse_x, coarse_y, slots = lookup.shape
    lookup = lookup.reshape(coarse_x * coarse_y, slots)
    counts = obs_count.reshape(coarse_x * coarse_y)
    local_part = local_weight.reshape(coarse_x * coarse_y, slots)
    weights = solve_columns(lookup, counts, local_part, flat_pert, flat_values)
    weights = weights.reshape(coarse_x, coarse_y, member_count, member_count)
    rimmed = padded(weights, (("tx", 0), ("ty", 1)), 1)
    rimmed = clamp_edges(rimmed, column_x, tiles_x, 0)
    rimmed = clamp_edges(rimmed, column_y, tiles_y, 1)
    doubled = jnp.repeat(jnp.repeat(rimmed, 2, axis=0), 2, axis=1)
    level_count, width_x, width_y, _ = members.shape
    half_span = SPACING // 2
    patch_x = width_x // half_span
    patch_y = width_y // half_span
    frac_x = fractions(patch_x, half_span)
    frac_y = fractions(patch_y, half_span)
    ens_mean = jnp.mean(members, axis=3, keepdims=True, dtype=jnp.float32)
    pert = (members.astype(jnp.float32) - ens_mean).astype(jnp.bfloat16)
    patched = pert.reshape(level_count, patch_x, half_span, patch_y, half_span, member_count)
    summed = jnp.zeros(patched.shape, jnp.float32)
    for upper_x in range(2):
        for upper_y in range(2):
            corner = doubled[
                1 + 2 * upper_x : 1 + 2 * upper_x + patch_x,
                1 + 2 * upper_y : 1 + 2 * upper_y + patch_y,
            ]
            product = jnp.einsum(
                "lxaybi,xyij->lxaybj", patched, corner, preferred_element_type=jnp.float32
            )
            factor_x = frac_x if upper_x == 1 else 1.0 - frac_x
            factor_y = frac_y if upper_y == 1 else 1.0 - frac_y
            summed = (
                summed
                + product
                * factor_x[None, :, :, None, None, None]
                * factor_y[None, None, None, :, :, None]
            )
    return (ens_mean + summed.reshape(members.shape)).astype(jnp.bfloat16)


def solution(mesh):
    placed = (
        P("lev", "tx", "ty", None),
        P(("tx", "ty", "lev"), None),
        P(("tx", "ty", "lev")),
        P(("tx", "ty", "lev")),
        P("tx", "ty", None),
        P("tx", "ty", None),
        P("tx", "ty"),
        P("tx", "ty", None),
    )
    return jax.shard_map(
        per_device,
        mesh=mesh,
        in_specs=placed,
        out_specs=P("lev", "tx", "ty", None),
        check_vma=False,
    )
```

profile of v0, /device:TPU:0, one launch (start us, length us, event | category | flops | bytes accessed | tf_op | source)
XLA Modules:
  0.0 95.4 jit_solution(6189147273435391446)
XLA Ops:
  0.0 7.6 %all_gather.6 = bf16[1024,128]{1,0:T(8,128)(2,1)S(1)} all-gather(bf16[256,128]{1,0:T(8,128)(2,1)} %param.11), channel_id=1, replica_groups=mesh['tx'=2,'ty'=4,'lev'=4] {'lev'}, dimensions={0}, use_global_device_ids=true | all-gather | bytes 327680 | tf_op jit(solution)/shard_map/all_gather | solution.py:113
  7.6 3.5 %collective-permute-start = (bf16[1,1,1024,128]{3,2,1,0:T(8,128)(2,1)S(1)}, bf16[1,1,1024,128]{3,2,1,0:T(8,128)(2,1)S(1)}, u32[]{:S(2)}, u32[]{:S(2)}) collective-permute-start(bf16[1,1,1024,128]{3,2,1,0:T(8,128)(2,1)S(1)} %bitcast.131), channel_id=1, source_target_pairs={{0,16},{1,17},{2,18},{3,19},{4,20},{5,21},{6,22},{7,23},{8,24},{9,... | collective-permute-start | bytes 786440 | tf_op jit(solution)/shard_map/ppermute | solution.py:17
  11.0 1.3 %collective-permute-start.1 = (bf16[1,1,1024,128]{3,2,1,0:T(8,128)(2,1)S(1)}, bf16[1,1,1024,128]{3,2,1,0:T(8,128)(2,1)S(1)}, u32[]{:S(2)}, u32[]{:S(2)}) collective-permute-start(bf16[1,1,1024,128]{3,2,1,0:T(8,128)(2,1)S(1)} %bitcast.132), channel_id=1, source_target_pairs={{16,0},{17,1},{18,2},{19,3},{20,4},{21,5},{22,6},{23,7},{24,8},{25... | collective-permute-start | bytes 786440 | tf_op jit(solution)/shard_map/ppermute | solution.py:18
  13.7 5.1 %all_gather.7 = bf16[2,1024]{1,0:T(2,128)(2,1)S(1)} all-gather(bf16[2,256]{1,0:T(2,128)(2,1)S(1)} %pad_maximum_fusion.8), channel_id=1, replica_groups=mesh['tx'=2,'ty'=4,'lev'=4] {'lev'}, dimensions={1}, use_global_device_ids=true | all-gather | bytes 5120 | tf_op jit(solution)/shard_map/all_gather | solution.py:114
  18.7 4.5 %collective-permute-start.4 = (bf16[1,1,2,1024]{3,2,1,0:T(2,128)(2,1)S(1)}, bf16[1,1,2,1024]{3,2,1,0:T(2,128)(2,1)S(1)}, u32[]{:S(2)}, u32[]{:S(2)}) collective-permute-start(bf16[1,1,2,1024]{3,2,1,0:T(2,128)(2,1)S(1)} %bitcast.153), channel_id=1, source_target_pairs={{0,16},{1,17},{2,18},{3,19},{4,20},{5,21},{6,22},{7,23},{8,24},{9,... | collective-permute-start | bytes 12296 | tf_op jit(solution)/shard_map/ppermute | solution.py:17
  23.3 1.3 %collective-permute-start.5 = (bf16[1,1,2,1024]{3,2,1,0:T(2,128)(2,1)S(1)}, bf16[1,1,2,1024]{3,2,1,0:T(2,128)(2,1)S(1)}, u32[]{:S(2)}, u32[]{:S(2)}) collective-permute-start(bf16[1,1,2,1024]{3,2,1,0:T(2,128)(2,1)S(1)} %bitcast.154), channel_id=1, source_target_pairs={{16,0},{17,1},{18,2},{19,3},{20,4},{21,5},{22,6},{23,7},{24,8},{25... | collective-permute-start | bytes 12296 | tf_op jit(solution)/shard_map/ppermute | solution.py:18
  25.4 1.4 %convert_reduce_fusion = f32[2,64,16]{2,1,0:T(8,128)S(1)} fusion(bf16[2,64,16,128]{3,2,1,0:T(8,128)(2,1)} %param.10), kind=kLoop, calls=%fused_computation.29 | loop fusion | flops 522240 | bytes 532480 | tf_op jit(solution)/shard_map/reduce_sum | solution.py:147
  27.0 3.5 %collective-permute-start.2 = (bf16[3,1,1024,128]{3,2,1,0:T(8,128)(2,1)S(1)}, bf16[3,1,1024,128]{3,2,1,0:T(8,128)(2,1)S(1)}, u32[]{:S(2)}, u32[]{:S(2)}) collective-permute-start(bf16[3,1,1024,128]{3,2,1,0:T(8,128)(2,1)S(1)} %pad_maximum_fusion.1), channel_id=1, source_target_pairs={{0,4},{4,8},{8,12},{1,5},{5,9},{9,13},{2,6},{6,10},{10,14},{3,7},{... | collective-permute-start | bytes 2359304 | tf_op jit(solution)/shard_map/ppermute | solution.py:17
  33.0 4.5 %collective-permute-start.6 = (bf16[3,1,2,1024]{3,2,1,0:T(2,128)(2,1)S(1)}, bf16[3,1,2,1024]{3,2,1,0:T(2,128)(2,1)S(1)}, u32[]{:S(2)}, u32[]{:S(2)}) collective-permute-start(bf16[3,1,2,1024]{3,2,1,0:T(2,128)(2,1)S(1)} %pad_maximum_fusion.7), channel_id=1, source_target_pairs={{0,4},{4,8},{8,12},{1,5},{5,9},{9,13},{2,6},{6,10},{10,14},{3,7},{... | collective-permute-start | bytes 36872 | tf_op jit(solution)/shard_map/ppermute | solution.py:17
  37.6 1.3 %collective-permute-start.7 = (bf16[3,1,2,1024]{3,2,1,0:T(2,128)(2,1)S(1)}, bf16[3,1,2,1024]{3,2,1,0:T(2,128)(2,1)S(1)}, u32[]{:S(2)}, u32[]{:S(2)}) collective-permute-start(bf16[3,1,2,1024]{3,2,1,0:T(2,128)(2,1)S(1)} %pad_maximum_fusion.7), channel_id=1, source_target_pairs={{4,0},{8,4},{12,8},{5,1},{9,5},{13,9},{6,2},{10,6},{14,10},{7,3},{... | collective-permute-start | bytes 36872 | tf_op jit(solution)/shard_map/ppermute | solution.py:18
  40.1 7.6 %collective-permute-done.6 = bf16[3,1,2,1024]{3,2,1,0:T(2,128)(2,1)S(1)} collective-permute-done((bf16[3,1,2,1024]{3,2,1,0:T(2,128)(2,1)S(1)}, bf16[3,1,2,1024]{3,2,1,0:T(2,128)(2,1)S(1)}, u32[]{:S(2)}, u32[]{:S(2)}) %collective-permute-start.6) | collective-permute-done | bytes 12320 | tf_op jit(solution)/shard_map/ppermute | solution.py:17
  47.7 4.2 %collective-permute-done.7 = bf16[3,1,2,1024]{3,2,1,0:T(2,128)(2,1)S(1)} collective-permute-done((bf16[3,1,2,1024]{3,2,1,0:T(2,128)(2,1)S(1)}, bf16[3,1,2,1024]{3,2,1,0:T(2,128)(2,1)S(1)}, u32[]{:S(2)}, u32[]{:S(2)}) %collective-permute-start.7) | collective-permute-done | bytes 12320 | tf_op jit(solution)/shard_map/ppermute | solution.py:18
  51.9 2.0 %copy.43 = bf16[2,9216]{0,1:T(8,128)(2,1)} copy(bf16[2,9216]{1,0:T(2,128)(2,1)S(1)} %bitcast.150) | data formatting | bytes 73728 | tf_op jit(solution)/shard_map/while | solution.py:87
  54.8 1.5 %pad_maximum_fusion = bf16[3,3,1024,128]{3,2,1,0:T(8,128)(2,1)S(1)} fusion(bf16[3,1,1024,128]{3,2,1,0:T(8,128)(2,1)} %collective-permute-done.3, bf16[1,1,1024,128]{3,2,1,0:T(8,128)(2,1)S(1)} %collective-permute-done.1, bf16[1,1,1024,128]{3,2,1,0:T(8,128)(2,1)S(1)} %bitcast.134, bf16[1,1,1024,128]{3,2,1,0:T(8,128)(2,1)S(1)} %collective-permute-done, ...), kind=kLoop, calls=%fused_computation.15 | loop fusion | flops 4718592 | bytes 4718592 | tf_op jit(solution)/shard_map/concatenate | solution.py:19
  56.4 10.6 %while.12 = (s32[]{:T(128)}, f32[4,128,128]{2,1,0:T(8,128)S(1)}, f32[4,128]{1,0:T(4,128)S(1)}, s32[]{:T(128)}, s32[4,256]{1,0:T(4,128)S(1)}, /*index=5*/bf16[921...) while((s32[]{:T(128)}, f32[4,128,128]{2,1,0:T(8,128)S(1)}, ...), condition=%wide.region_3.4_spmd, body=%wide.region_2.3_spmd.sunk | while | flops 101652616 | bytes 1486023 | solution.py:87
  56.4 3.0 %gather_fusion.1 = bf16[512,2]{1,0:T(8,128)(2,1)S(1)} fusion(bf16[2,9216]{0,1:T(8,128)(2,1)} %get-tuple-element.193, s32[1024]{0:T(1024)S(1)} %pad_clamp_fusion.2), kind=kCustom, calls=%fused_computation.1.clone.1 | custom fusion | bytes 6144 | tf_op jit(solution)/shard_map/while/body/gather | solution.py:71
  59.7 1.3 %gather_fusion = bf16[512,128]{1,0:T(8,128)(2,1)S(1)} fusion(bf16[9216,128]{1,0:T(8,128)(2,1)S(1)} %get-tuple-element.191, s32[1024]{0:T(1024)S(1)} %pad_clamp_fusion.2), kind=kCustom, calls=%fused_computation.clone.1 | custom fusion | bytes 264192 | tf_op jit(solution)/shard_map/while/body/gather | solution.py:70
  61.7 3.0 %gather_fusion.1 = bf16[512,2]{1,0:T(8,128)(2,1)S(1)} fusion(bf16[2,9216]{0,1:T(8,128)(2,1)} %get-tuple-element.193, s32[1024]{0:T(1024)S(1)} %pad_clamp_fusion.2), kind=kCustom, calls=%fused_computation.1.clone.1 | custom fusion | bytes 6144 | tf_op jit(solution)/shard_map/while/body/gather | solution.py:71
  64.9 1.3 %gather_fusion = bf16[512,128]{1,0:T(8,128)(2,1)S(1)} fusion(bf16[9216,128]{1,0:T(8,128)(2,1)S(1)} %get-tuple-element.191, s32[1024]{0:T(1024)S(1)} %pad_clamp_fusion.2), kind=kCustom, calls=%fused_computation.clone.1 | custom fusion | bytes 264192 | tf_op jit(solution)/shard_map/while/body/gather | solution.py:70
  74.2 4.5 %collective-permute-start.8 = (bf16[1,1,128,128]{3,2,0,1:T(8,128)(2,1)S(1)}, bf16[1,1,128,128]{3,2,0,1:T(8,128)(2,1)S(1)}, u32[]{:S(2)}, u32[]{:S(2)}) collective-permute-start(bf16[1,1,128,128]{3,2,0,1:T(8,128)(2,1)S(1)} %get-tuple-element.90), channel_id=1, source_target_pairs={{0,16},{1,17},{2,18},{3,19},{4,20},{5,21},{6,22},{7,23},{8,24},{9,... | collective-permute-start | bytes 98312 | tf_op jit(solution)/shard_map/ppermute | solution.py:17
  79.0 1.4 %collective-permute-done.8 = bf16[1,1,128,128]{3,2,0,1:T(8,128)(2,1)S(1)} collective-permute-done((bf16[1,1,128,128]{3,2,0,1:T(8,128)(2,1)S(1)}, bf16[1,1,128,128]{3,2,0,1:T(8,128)(2,1)S(1)}, u32[]{:S(2)}, u32[]{:S(2)}) %collective-permute-start.8) | collective-permute-done | bytes 32800 | tf_op jit(solution)/shard_map/ppermute | solution.py:17
  80.4 3.5 %collective-permute-start.10 = (bf16[6,1,128,128]{3,2,0,1:T(8,128)(2,1)S(1)}, bf16[6,1,128,128]{3,2,0,1:T(8,128)(2,1)S(1)}, u32[]{:S(2)}, u32[]{:S(2)}) collective-permute-start(bf16[6,1,128,128]{3,2,0,1:T(8,128)(2,1)S(1)} %pad_maximum_fusion.5), channel_id=1, source_target_pairs={{0,4},{4,8},{8,12},{1,5},{5,9},{9,13},{2,6},{6,10},{10,14},{3,7},{... | collective-permute-start | bytes 589832 | tf_op jit(solution)/shard_map/ppermute | solution.py:17
  85.2 1.8 %collective-permute-done.10 = bf16[6,1,128,128]{3,2,0,1:T(8,128)(2,1)S(1)} collective-permute-done((bf16[6,1,128,128]{3,2,0,1:T(8,128)(2,1)S(1)}, bf16[6,1,128,128]{3,2,0,1:T(8,128)(2,1)S(1)}, u32[]{:S(2)}, u32[]{:S(2)}) %collective-permute-start.10) | collective-permute-done | bytes 196640 | tf_op jit(solution)/shard_map/ppermute | solution.py:17
  87.0 4.4 %collective-permute-done.11 = bf16[6,1,128,128]{3,2,0,1:T(8,128)(2,1)S(1)} collective-permute-done((bf16[6,1,128,128]{3,2,0,1:T(8,128)(2,1)S(1)}, bf16[6,1,128,128]{3,2,0,1:T(8,128)(2,1)S(1)}, u32[]{:S(2)}, u32[]{:S(2)}) %collective-permute-start.11) | collective-permute-done | bytes 196640 | tf_op jit(solution)/shard_map/ppermute | solution.py:18
  (94 shorter events, 20.6 us)
Async XLA Ops:
  0.0 31.8 %copy-start = (bf16[2,64,16,128]{3,2,1,0:T(8,128)(2,1)S(1)}, bf16[2,64,16,128]{3,2,1,0:T(8,128)(2,1)}, u32[]{:S(2)}) copy-start(bf16[2,64,16,128]{3,2,1,0:T(8,128)(2,1)} %param.10) | copy-start | bytes 1572868
  0.0 38.9 %copy-start.3 = (s32[4,1]{0,1:T(1,128)S(1)}, s32[4,1]{0,1:T(1,128)}, u32[]{:S(2)}) copy-start(s32[4,1]{0,1:T(1,128)} %param.16) | copy-start | bytes 52
  0.0 40.1 %copy-start.4 = (f32[4,1,256]{2,1,0:T(1,128)S(1)}, f32[4,1,256]{2,1,0:T(1,128)}, u32[]{:S(2)}) copy-start(f32[4,1,256]{2,1,0:T(1,128)} %param.17) | copy-start | bytes 12292
  7.6 19.3 %collective-permute-start = (bf16[1,1,1024,128]{3,2,1,0:T(8,128)(2,1)S(1)}, bf16[1,1,1024,128]{3,2,1,0:T(8,128)(2,1)S(1)}, u32[]{:S(2)}, u32[]{:S(2)}) collective-permute-start(bf16[1,1,1024,128]{3,2,1,0:T(8,128)(2,1)S(1)} %bitcast.131), channel_id=1, source_target_pairs={{0,16},{1,17},{2,18},{3,19},{4,20},{5,21},{6,22},{7,23},{8,24},{9,... | collective-permute-start | bytes 786440 | tf_op jit(solution)/shard_map/ppermute | solution.py:17
  11.0 15.8 %collective-permute-start.1 = (bf16[1,1,1024,128]{3,2,1,0:T(8,128)(2,1)S(1)}, bf16[1,1,1024,128]{3,2,1,0:T(8,128)(2,1)S(1)}, u32[]{:S(2)}, u32[]{:S(2)}) collective-permute-start(bf16[1,1,1024,128]{3,2,1,0:T(8,128)(2,1)S(1)} %bitcast.132), channel_id=1, source_target_pairs={{16,0},{17,1},{18,2},{19,3},{20,4},{21,5},{22,6},{23,7},{24,8},{25... | collective-permute-start | bytes 786440 | tf_op jit(solution)/shard_map/ppermute | solution.py:18
  18.7 14.2 %collective-permute-start.4 = (bf16[1,1,2,1024]{3,2,1,0:T(2,128)(2,1)S(1)}, bf16[1,1,2,1024]{3,2,1,0:T(2,128)(2,1)S(1)}, u32[]{:S(2)}, u32[]{:S(2)}) collective-permute-start(bf16[1,1,2,1024]{3,2,1,0:T(2,128)(2,1)S(1)} %bitcast.153), channel_id=1, source_target_pairs={{0,16},{1,17},{2,18},{3,19},{4,20},{5,21},{6,22},{7,23},{8,24},{9,... | collective-permute-start | bytes 12296 | tf_op jit(solution)/shard_map/ppermute | solution.py:17
  23.3 9.7 %collective-permute-start.5 = (bf16[1,1,2,1024]{3,2,1,0:T(2,128)(2,1)S(1)}, bf16[1,1,2,1024]{3,2,1,0:T(2,128)(2,1)S(1)}, u32[]{:S(2)}, u32[]{:S(2)}) collective-permute-start(bf16[1,1,2,1024]{3,2,1,0:T(2,128)(2,1)S(1)} %bitcast.154), channel_id=1, source_target_pairs={{16,0},{17,1},{18,2},{19,3},{20,4},{21,5},{22,6},{23,7},{24,8},{25... | collective-permute-start | bytes 12296 | tf_op jit(solution)/shard_map/ppermute | solution.py:18
  27.0 27.0 %collective-permute-start.2 = (bf16[3,1,1024,128]{3,2,1,0:T(8,128)(2,1)S(1)}, bf16[3,1,1024,128]{3,2,1,0:T(8,128)(2,1)S(1)}, u32[]{:S(2)}, u32[]{:S(2)}) collective-permute-start(bf16[3,1,1024,128]{3,2,1,0:T(8,128)(2,1)S(1)} %pad_maximum_fusion.1), channel_id=1, source_target_pairs={{0,4},{4,8},{8,12},{1,5},{5,9},{9,13},{2,6},{6,10},{10,14},{3,7},{... | collective-permute-start | bytes 2359304 | tf_op jit(solution)/shard_map/ppermute | solution.py:17
  30.5 24.3 %collective-permute-start.3 = (bf16[3,1,1024,128]{3,2,1,0:T(8,128)(2,1)S(1)}, bf16[3,1,1024,128]{3,2,1,0:T(8,128)(2,1)}, u32[]{:S(2)}, u32[]{:S(2)}) collective-permute-start(bf16[3,1,1024,128]{3,2,1,0:T(8,128)(2,1)S(1)} %pad_maximum_fusion.1), channel_id=1, source_target_pairs={{4,0},{8,4},{12,8},{5,1},{9,5},{13,9},{6,2},{10,6},{14,10},{7,3},{... | collective-permute-start | bytes 2359304 | tf_op jit(solution)/shard_map/ppermute | solution.py:18
  33.0 14.7 %collective-permute-start.6 = (bf16[3,1,2,1024]{3,2,1,0:T(2,128)(2,1)S(1)}, bf16[3,1,2,1024]{3,2,1,0:T(2,128)(2,1)S(1)}, u32[]{:S(2)}, u32[]{:S(2)}) collective-permute-start(bf16[3,1,2,1024]{3,2,1,0:T(2,128)(2,1)S(1)} %pad_maximum_fusion.7), channel_id=1, source_target_pairs={{0,4},{4,8},{8,12},{1,5},{5,9},{9,13},{2,6},{6,10},{10,14},{3,7},{... | collective-permute-start | bytes 36872 | tf_op jit(solution)/shard_map/ppermute | solution.py:17
  37.6 14.3 %collective-permute-start.7 = (bf16[3,1,2,1024]{3,2,1,0:T(2,128)(2,1)S(1)}, bf16[3,1,2,1024]{3,2,1,0:T(2,128)(2,1)S(1)}, u32[]{:S(2)}, u32[]{:S(2)}) collective-permute-start(bf16[3,1,2,1024]{3,2,1,0:T(2,128)(2,1)S(1)} %pad_maximum_fusion.7), channel_id=1, source_target_pairs={{4,0},{8,4},{12,8},{5,1},{9,5},{13,9},{6,2},{10,6},{14,10},{7,3},{... | collective-permute-start | bytes 36872 | tf_op jit(solution)/shard_map/ppermute | solution.py:18
  53.9 0.9 copy-start.1
  72.9 6.0 %collective-permute-start.9 = (bf16[1,1,128,128]{3,2,1,0:T(8,128)(2,1)S(1)}, bf16[1,1,128,128]{3,2,1,0:T(8,128)(2,1)S(1)}, u32[]{:S(2)}, u32[]{:S(2)}) collective-permute-start(bf16[1,1,128,128]{3,2,1,0:T(8,128)(2,1)S(1)} %get-tuple-element.91), channel_id=1, source_target_pairs={{16,0},{17,1},{18,2},{19,3},{20,4},{21,5},{22,6},{23,7},{24,8},{25... | collective-permute-start | bytes 98312 | tf_op jit(solution)/shard_map/ppermute | solution.py:18
  74.2 6.1 %collective-permute-start.8 = (bf16[1,1,128,128]{3,2,0,1:T(8,128)(2,1)S(1)}, bf16[1,1,128,128]{3,2,0,1:T(8,128)(2,1)S(1)}, u32[]{:S(2)}, u32[]{:S(2)}) collective-permute-start(bf16[1,1,128,128]{3,2,0,1:T(8,128)(2,1)S(1)} %get-tuple-element.90), channel_id=1, source_target_pairs={{0,16},{1,17},{2,18},{3,19},{4,20},{5,21},{6,22},{7,23},{8,24},{9,... | collective-permute-start | bytes 98312 | tf_op jit(solution)/shard_map/ppermute | solution.py:17
  80.4 6.6 %collective-permute-start.10 = (bf16[6,1,128,128]{3,2,0,1:T(8,128)(2,1)S(1)}, bf16[6,1,128,128]{3,2,0,1:T(8,128)(2,1)S(1)}, u32[]{:S(2)}, u32[]{:S(2)}) collective-permute-start(bf16[6,1,128,128]{3,2,0,1:T(8,128)(2,1)S(1)} %pad_maximum_fusion.5), channel_id=1, source_target_pairs={{0,4},{4,8},{8,12},{1,5},{5,9},{9,13},{2,6},{6,10},{10,14},{3,7},{... | collective-permute-start | bytes 589832 | tf_op jit(solution)/shard_map/ppermute | solution.py:17
  83.9 7.6 %collective-permute-start.11 = (bf16[6,1,128,128]{3,2,0,1:T(8,128)(2,1)S(1)}, bf16[6,1,128,128]{3,2,0,1:T(8,128)(2,1)S(1)}, u32[]{:S(2)}, u32[]{:S(2)}) collective-permute-start(bf16[6,1,128,128]{3,2,0,1:T(8,128)(2,1)S(1)} %pad_maximum_fusion.5), channel_id=1, source_target_pairs={{4,0},{8,4},{12,8},{5,1},{9,5},{13,9},{6,2},{10,6},{14,10},{7,3},{... | collective-permute-start | bytes 589832 | tf_op jit(solution)/shard_map/ppermute | solution.py:18
  91.9 1.1 %copy-start.2 = (bf16[2,64,16,128]{3,2,1,0:T(8,128)(2,1)S(1)}, bf16[2,64,16,128]{3,2,1,0:T(8,128)(2,1)}, u32[]{:S(2)}) copy-start(bf16[2,64,16,128]{3,2,1,0:T(8,128)(2,1)} %fusion.17) | copy-start | bytes 1572868
where the time goes:
time: 96 us; the launch traced here: 95.4 us
  starting transfers between devices  31.8 us (33%)
  waiting for transfers between devices  19.4 us (20%)
  local copies, waits for them, and re-layouts  14.7 us (15%)
  blocking collectives  12.6 us (13%)
  other arithmetic  7.94 us (8%)
  matrix products  7.73 us (8%)
  between operations  1.1 us (1%)
    ppermute x6, starting transfers between devices, padded(): before = lax.ppermute(last, axis, up)  24.1 us
    ppermute x6, waiting for transfers between devices, padded(): before = lax.ppermute(last, axis, up)  10.8 us
    ppermute x6, waiting for transfers between devices, padded(): after = lax.ppermute(initial, axis, down)  8.58 us
    ppermute x6, starting transfers between devices, padded(): after = lax.ppermute(initial, axis, down)  7.75 us
    all_gather x1, blocking collectives, per_device(): lax.all_gather(obs_pert, 'lev', axis=0, tiled=True)  7.57 us
    gather x4, local copies, waits for them, and re-layouts, add_block(): picked = flat_values[:, slot_rows]  6.26 us
    all_gather x1, blocking collectives, per_device(): lax.all_gather(scalars, 'lev', axis=1, tiled=True)  5.07 us
    gather x4, local copies, waits for them, and re-layouts, add_block(): pert_rows = flat_pert[slot_rows].astype(jnp.float32)  2.95 us
  transfers between devices with their start and end apart: 12, of which 5 were waited for; matrix products, arithmetic and copies ran while one was open for 8% of the time, Pallas kernels for 0%

commit v1 on v0

--- a/solution.py
+++ b/solution.py
@@ -1,6 +1,10 @@
+import functools
+
 import jax
 import jax.numpy as jnp
 from jax import lax
+from jax.experimental import pallas as pl
+from jax.experimental.pallas import tpu as pltpu
 from jax.sharding import PartitionSpec as P
 
 SPACING = 16
@@ -168,6 +172,367 @@
     return (ens_mean + summed.reshape(members.shape)).astype(jnp.bfloat16)
 
 
+def pair_patterns(mesh_axes):
+    tiles_x, tiles_y, parts = (lax.axis_size(a) for a in mesh_axes)
+
+    def flat(x, y, l):
+        return (x * tiles_y + y) * parts + l
+
+    def table(move):
+        return [
+            (flat(x, y, l), flat(*move(x, y, l)))
+            for x in range(tiles_x)
+            for y in range(tiles_y)
+            for l in range(parts)
+        ]
+
+    def climb(x, y, l):
+        if l % 2 == 0:
+            return (x, y + 1, l) if y < tiles_y - 1 else (x, y, l + 1)
+        return (x, y - 1, l) if y > 0 else (x, y, l - 1)
+
+    climbing = table(climb)
+    return {
+        "across": table(lambda x, y, l: (1 - x, y, l)),
+        "core": table(lambda x, y, l: (x, y, l ^ 1)),
+        "half": table(lambda x, y, l: (x, y, l ^ 2)),
+        "climb": climbing,
+        "descend": [(b, a) for a, b in climbing],
+    }
+
+
+def vmem_call(kernel, out_shape, scratch=(), flops=0, bytes_accessed=0, name=None):
+    single = not isinstance(out_shape, (list, tuple))
+    spec = pl.BlockSpec(memory_space=pltpu.VMEM)
+
+    def call(*operands):
+        return pl.pallas_call(
+            kernel,
+            out_shape=out_shape,
+            in_specs=[spec] * len(operands),
+            out_specs=spec if single else [spec] * len(out_shape),
+            scratch_shapes=list(scratch),
+            cost_estimate=pl.CostEstimate(
+                flops=flops, bytes_accessed=bytes_accessed, transcendentals=0
+            ),
+            name=name,
+        )(*operands)
+
+    return call
+
+
+def split2(value):
+    high = value.astype(jnp.bfloat16)
+    return high, (value - high.astype(jnp.float32)).astype(jnp.bfloat16)
+
+
+def split3(value):
+    high, _ = split2(value)
+    rest = value - high.astype(jnp.float32)
+    middle, low = split2(rest)
+    return high, middle, low
+
+
+def dot(a, b, dims=((1,), (0,))):
+    return lax.dot_general(a, b, (dims, ((), ())), preferred_element_type=jnp.float32)
+
+
+def pack_kernel(rows, pert_ref, inn_ref, prec_ref, owner_ref, slot_ref, count_ref, local_ref, out_ref, tail):
+    edge = jnp.where(lax.axis_index("tx") == 0, owner_ref.shape[0] - 1, 0)
+    slots = owner_ref.shape[2]
+    out_ref[0:rows, :] = pert_ref[...]
+    active = lax.broadcasted_iota(jnp.int32, (1, slots), 1) < count_ref[edge, 0]
+    local = jnp.where(active, local_ref[edge], 0.0)
+    slot = slot_ref[edge]
+    lists = [
+        prec_ref[...].astype(jnp.float32),
+        inn_ref[...].astype(jnp.float32),
+        owner_ref[edge].astype(jnp.float32),
+        (slot // 128).astype(jnp.float32),
+        (slot % 128).astype(jnp.float32),
+    ] + [piece.astype(jnp.float32) for piece in split3(local)]
+    for k, row in enumerate(lists):
+        for part in range(2):
+            tail[2 * k + part : 2 * k + part + 1, :] = row[:, 128 * part : 128 * (part + 1)]
+    out_ref[rows : rows + 16, :] = tail[...].astype(jnp.bfloat16)
+
+
+def table_kernel(rows, cols, owner_ref, slot_ref, count_ref, local_ref, other_ref, out_ref):
+    tile_x, tile_y, part = (lax.axis_index(a) for a in ("tx", "ty", "lev"))
+    tiles_y = lax.axis_size("ty")
+    core = lax.rem(part, 2)
+    own, slots = owner_ref.shape[0], owner_ref.shape[2]
+    received = other_ref[rows : rows + 16, :].astype(jnp.float32)
+
+    def listed(k):
+        return jnp.concatenate([received[2 * k : 2 * k + 1, :], received[2 * k + 1 : 2 * k + 2, :]], axis=1)
+
+    far_owner = listed(2).astype(jnp.int32)
+    far_slot = (listed(3) * 128.0 + listed(4)).astype(jnp.int32)
+    far_local = listed(5) + listed(6) + listed(7)
+    position_in = lax.broadcasted_iota(jnp.int32, (1, slots), 1)
+
+    def own_list(k):
+        return owner_ref[k], slot_ref[k], jnp.where(position_in < count_ref[k, 0], local_ref[k], 0.0)
+
+    def pick(use_far, k):
+        return tuple(jnp.where(use_far, a, b) for a, b in zip((far_owner, far_slot, far_local), own_list(k)))
+
+    lists = [pick(tile_x > 0, 0)] + [own_list(k) for k in range(own)] + [pick(tile_x == 0, own - 1)]
+    half = cols // 2
+    out_ref[...] = jnp.zeros_like(out_ref)
+    for g, (owner, slot, local) in enumerate(lists):
+        across = jnp.where(owner // tiles_y == tile_x, 0, 1)
+        near = owner % tiles_y - tile_y
+        first_way = jnp.where(core == 0, -1, 1)
+        block = across * 3 + jnp.where(near == 0, 0, jnp.where(near == first_way, 1, 2))
+        mine = slot // rows == part
+        within = slot % rows
+        high = jnp.where(mine, block * (rows // 128) + within // 128, -1)
+        low = within % 128
+        picked = jnp.where(lax.broadcasted_iota(jnp.int32, (16, slots), 0) == high, local, 0.0)
+        hot = jnp.where(lax.broadcasted_iota(jnp.int32, (128, slots), 0) == low, 1.0, 0.0).astype(jnp.bfloat16)
+        parts = split3(picked)
+        total = dot(parts[0], hot, ((1,), (1,)))
+        for piece in parts[1:]:
+            total = total + dot(piece, hot, ((1,), (1,)))
+        place = lax.rem(g - core * half + cols, cols)
+        out_ref[pl.ds(place, 16, stride=8), :] = total
+
+
+def gram_kernel(rows, cols, table_ref, b0, b1, b2, b3, b4, b5, mine_ref, rest_ref, turned, scaled):
+    blocks = [b0, b1, b2, b3, b4, b5]
+    per = rows // 128
+    half = cols // 2
+    weights = []
+    products = []
+    for k, ref in enumerate(blocks):
+        tail = ref[rows : rows + 16, :].astype(jnp.float32)
+        for part in range(per):
+            hi = k * per + part
+            row = table_ref[8 * hi : 8 * hi + 8, :] * tail[part : part + 1, :]
+            weights.append(row)
+            products.append(row * tail[per + part : per + part + 1, :])
+        turned[:, rows * k : rows * (k + 1)] = ref[0:rows, :].astype(jnp.float32).T.astype(jnp.bfloat16)
+    pads = 128 // 8 - len(weights)
+    stacked = jnp.concatenate(weights + [jnp.zeros((8 * pads, 128), jnp.float32)], axis=0)
+    columns = stacked.T
+    projected = jnp.zeros((16, 128), jnp.float32)
+    for k, ref in enumerate(blocks):
+        wide = jnp.concatenate(products[k * per : (k + 1) * per], axis=1)
+        pieces = jnp.concatenate([p.astype(jnp.float32) for p in split2(wide)], axis=0)
+        projected = projected + dot(pieces.astype(jnp.bfloat16), ref[0:rows, :])
+    projected = projected[0:8] + projected[8:16]
+    for position in range(cols):
+        for k, ref in enumerate(blocks):
+            for part in range(per):
+                hi = k * per + part
+                values = ref[128 * part : 128 * (part + 1), :].astype(jnp.float32)
+                high, low = split2(values * columns[:, 8 * hi + position : 8 * hi + position + 1])
+                scaled[128 * hi : 128 * (hi + 1), 0:128] = high
+                scaled[128 * hi : 128 * (hi + 1), 128:256] = low
+        both = dot(turned[...], scaled[...])
+        target = mine_ref if position < half else rest_ref
+        at = 128 * (position % half)
+        target[at : at + 128, :] = both[:, 0:128] + both[:, 128:256]
+    mine_ref[128 * half : 128 * half + 8, :] = projected
+    rest_ref[128 * half : 128 * half + 8, :] = jnp.concatenate(
+        [projected[half : 2 * half], jnp.zeros((8 - half, 128), jnp.float32)], axis=0
+    )
+
+
+def join_kernel(half, mine_ref, got_ref, sum_ref, send_ref):
+    total = mine_ref[...] + got_ref[...]
+    sum_ref[...] = total
+    edge = 128 * half
+    send_ref[0:edge, :] = total[0:edge].astype(jnp.bfloat16)
+    high, low = split2(total[edge : edge + 8])
+    send_ref[edge : edge + 16, :] = jnp.concatenate(
+        [high.astype(jnp.float32), low.astype(jnp.float32)], axis=0
+    ).astype(jnp.bfloat16)
+
+
+def product(a, b):
+    (a_high, a_low), (b_high, b_low) = a, b
+    return dot(a_high, b_high) + (dot(a_high, b_low) + dot(a_low, b_high))
+
+
+def solve_kernel(half, sum_ref, got_ref, out_ref):
+    size = 128
+    spread = float(size - 1)
+    eye = jnp.where(
+        lax.broadcasted_iota(jnp.int32, (size, size), 0) == lax.broadcasted_iota(jnp.int32, (size, size), 1),
+        1.0,
+        0.0,
+    )
+    edge = size * half
+    projected = (
+        sum_ref[edge : edge + 8, :]
+        + got_ref[edge : edge + 16, :].astype(jnp.float32)[0:8]
+        + got_ref[edge : edge + 16, :].astype(jnp.float32)[8:16]
+    )
+    state = []
+    for k in range(half):
+        gram = sum_ref[size * k : size * (k + 1), :] + got_ref[size * k : size * (k + 1), :].astype(jnp.float32)
+        squared = jnp.sum(jnp.sum(gram * gram, axis=0, keepdims=True), axis=1, keepdims=True)
+        norm = spread + jnp.sqrt(squared)
+        start = (spread * eye + gram) / norm
+        state.append((norm, start))
+    norms = [n for n, _ in state]
+    roots = [s for _, s in state]
+    inverses = [None] * half
+    for iteration in range(NS_STEPS):
+        last = iteration == NS_STEPS - 1
+        root_parts = [split2(r) for r in roots]
+        if iteration == 0:
+            middles = [1.5 * eye - 0.5 * r for r in roots]
+        else:
+            inverse_parts = [split2(z) for z in inverses]
+            middles = [1.5 * eye - 0.5 * product(z, r) for z, r in zip(inverse_parts, root_parts)]
+        middle_parts = [split2(m) for m in middles]
+        if not last:
+            roots = [product(r, m) for r, m in zip(root_parts, middle_parts)]
+        if iteration == 0:
+            inverses = middles
+        else:
+            inverses = [product(m, z) for m, z in zip(middle_parts, inverse_parts)]
+    for k in range(half):
+        inverse, norm = inverses[k], norms[k]
+        parts = split2(inverse)
+        vector = split3(jnp.broadcast_to(projected[k : k + 1, :], (16, size)))
+        inner = jnp.zeros((16, size), jnp.float32)
+        for piece in vector[:2]:
+            for part in parts:
+                inner = inner + dot(piece, part, ((1,), (1,)))
+        mean_weights = jnp.sum(inverse * inner[0:1, :], axis=1, keepdims=True) / norm
+        transform = (jnp.sqrt(spread) / jnp.sqrt(norm)) * inverse + mean_weights
+        out_ref[size * k : size * (k + 1), :] = transform.astype(jnp.bfloat16)
+
+
+def apply_kernel(cols, members_ref, own, pair, climb, descend, pair_climb, pair_descend, out_ref, table):
+    half = cols // 2
+    tile_y = lax.axis_index("ty")
+    tiles_y = lax.axis_size("ty")
+    first = lax.rem(lax.axis_index("lev"), 2) == 0
+    at_start, at_end = tile_y == 0, tile_y == tiles_y - 1
+    for j in range(half):
+        rows = pl.ds(128 * j, 128)
+        a, b = own[rows, :], pair[rows, :]
+        low, high = jnp.where(first, a, b), jnp.where(first, b, a)
+        up, down = climb[rows, :], descend[rows, :]
+        pair_up, pair_down = pair_climb[rows, :], pair_descend[rows, :]
+        before_low = jnp.where(at_start, low, jnp.where(first, up, pair_up))
+        before_high = jnp.where(at_start, high, jnp.where(first, pair_down, down))
+        after_low = jnp.where(at_end, low, jnp.where(first, down, pair_down))
+        after_high = jnp.where(at_end, high, jnp.where(first, pair_up, up))
+        for z, (x, y) in enumerate([(before_low, before_high), (low, high), (after_low, after_high)]):
+            table[z, :, 128 * j : 128 * (j + 1)] = x
+            table[z, :, 128 * (j + half) : 128 * (j + half + 1)] = y
+    levels, width_x, width_y, size = members_ref.shape
+    span = SPACING // 2
+    shape = (levels, span, span, size)
+    step_x = lax.broadcasted_iota(jnp.int32, shape, 1).astype(jnp.float32)
+    step_y = lax.broadcasted_iota(jnp.int32, shape, 2).astype(jnp.float32)
+
+    def upper(place, step):
+        return (step + (span + 0.5 if place % 2 == 0 else 0.5)) / (2 * span)
+
+    for patch_x in range(width_x // span):
+        states = members_ref[:, patch_x * span : (patch_x + 1) * span, :, :].astype(jnp.float32)
+        mean = jnp.sum(states, axis=3, keepdims=True) * (1.0 / size)
+        moved = states - mean
+        column = (patch_x + 1) // 2
+        up_x = upper(patch_x, step_x)
+        results = []
+        for patch_y in range(width_y // span):
+            picked = moved[:, :, patch_y * span : (patch_y + 1) * span, :]
+            rows = levels * span * span
+            left = picked.reshape(rows, size).astype(jnp.bfloat16)
+            place = (patch_y + 1) // 2
+            near = dot(left, table[place, :, 128 * column : 128 * (column + 2)])
+            far = dot(left, table[place + 1, :, 128 * column : 128 * (column + 2)])
+            up_y = upper(patch_y, step_y)
+            near_mix = (1.0 - up_x) * near[:, 0:128].reshape(shape) + up_x * near[:, 128:256].reshape(shape)
+            far_mix = (1.0 - up_x) * far[:, 0:128].reshape(shape) + up_x * far[:, 128:256].reshape(shape)
+            results.append((1.0 - up_y) * near_mix + up_y * far_mix)
+        whole = mean + jnp.concatenate(results, axis=2)
+        out_ref[:, patch_x * span : (patch_x + 1) * span, :, :] = whole.astype(jnp.bfloat16)
+
+
+def paired_device(
+    members, obs_pert, innovation, obs_precision, obs_owner, obs_slot, obs_count, local_weight
+):
+    axes = ("tx", "ty", "lev")
+    ways = pair_patterns(axes)
+
+    def send(value, way):
+        return lax.ppermute(value, axes, ways[way])
+
+    bf16, f32 = jnp.bfloat16, jnp.float32
+    rows, size = obs_pert.shape
+    cols = obs_owner.shape[0] + 2
+    half = cols // 2
+    shape = jax.ShapeDtypeStruct
+    packed = vmem_call(
+        functools.partial(pack_kernel, rows),
+        shape((rows + 16, size), bf16),
+        [pltpu.VMEM((16, size), f32)],
+        name="pack",
+    )(
+        obs_pert,
+        innovation.reshape(1, rows),
+        obs_precision.reshape(1, rows),
+        obs_owner,
+        obs_slot,
+        obs_count,
+        local_weight,
+    )
+    across = send(packed, "across")
+    climb, descend = send(packed, "climb"), send(packed, "descend")
+    across_climb, across_descend = send(across, "climb"), send(across, "descend")
+    table = vmem_call(
+        functools.partial(table_kernel, rows, cols),
+        shape((128, 128), f32),
+        flops=6 * 2 * 48 * 256 * 128,
+        bytes_accessed=1 << 17,
+        name="table",
+    )(obs_owner, obs_slot, obs_count, local_weight, across)
+    mine, rest = vmem_call(
+        functools.partial(gram_kernel, rows, cols),
+        [shape((128 * half + 8, size), f32)] * 2,
+        [pltpu.VMEM((size, 6 * rows), bf16), pltpu.VMEM((6 * rows, 2 * size), bf16)],
+        name="gram",
+    )(table, packed, climb, descend, across, across_climb, across_descend)
+    total, half_sum = vmem_call(
+        functools.partial(join_kernel, half),
+        [shape((128 * half + 8, size), f32), shape((128 * half + 16, size), bf16)],
+        name="join",
+    )(mine, send(rest, "core"))
+    weights = vmem_call(
+        functools.partial(solve_kernel, half), shape((128 * half, size), bf16), name="solve"
+    )(total, send(half_sum, "half"))
+    pair = send(weights, "core")
+    up, down = send(weights, "climb"), send(weights, "descend")
+    pair_up, pair_down = send(up, "core"), send(down, "core")
+    return vmem_call(
+        functools.partial(apply_kernel, cols),
+        shape(members.shape, bf16),
+        [pltpu.VMEM((3, size, cols * size), bf16)],
+        name="apply",
+    )(members, weights, pair, up, down, pair_up, pair_down)
+
+
+def fits_pairs(mesh, members, obs_pert, obs_owner):
+    sizes = dict(mesh.shape)
+    return (
+        sizes["tx"] == 2
+        and sizes["lev"] == 4
+        and obs_pert == (256, 128)
+        and obs_owner == (4, 1, 256)
+        and members[1:] == (64, 16, 128)
+    )
+
+
 def solution(mesh):
     placed = (
         P("lev", "tx", "ty", None),
@@ -179,8 +544,15 @@
         P("tx", "ty"),
         P("tx", "ty", None),
     )
+
+    def local(members, obs_pert, innovation, obs_precision, obs_owner, *rest):
+        paired = fits_pairs(mesh, members.shape, obs_pert.shape, obs_owner.shape)
+        return (paired_device if paired else per_device)(
+            members, obs_pert, innovation, obs_precision, obs_owner, *rest
+        )
+
     return jax.shard_map(
-        per_device,
+        local,
         mesh=mesh,
         in_specs=placed,
         out_specs=P("lev", "tx", "ty", None),

time: 96 us -> 44.7 us (0.47)
  starting transfers between devices: 31.8 us -> 11.4 us
  Pallas kernels: 0 us -> 16 us
  blocking collectives: 12.6 us -> 0 us
  waiting for transfers between devices: 19.4 us -> 10.6 us
  local copies, waits for them, and re-layouts: 14.7 us -> 6.28 us
  other arithmetic: 7.94 us -> 0 us
  matrix products: 7.73 us -> 0 us
  between operations: 1.1 us -> 0.05 us
    ppermute x12, starting transfers between devices: 31.8 us -> 11.4 us  [send(): return lax.ppermute(value, axes, ways[way])]
    pallas_call x0 -> x6, Pallas kernels: none -> 16 us  [call(): pl.pallas_call(kernel, out_shape=out_shape, in_specs=[spec] * len(operand...]
    all_gather x2 -> x0, blocking collectives: 12.6 us -> none  [the longest x1 7.57 us: per_device(): lax.all_gather(obs_pert, 'lev', axis=0, tiled=True)]
    gather x8 -> x0, local copies, waits for them, and re-layouts: 9.21 us -> none  [the longest x4 6.26 us: add_block(): picked = flat_values[:, slot_rows]]
    ppermute x12, waiting for transfers between devices: 19.4 us -> 10.6 us  [send(): return lax.ppermute(value, axes, ways[way])]
    dot_general x21 -> x0, matrix products: 7.73 us -> none  [the longest x4 1.66 us: finish_solve(): jnp.einsum('bij,bjk->bik', inv_iter, sqrt_iter, precision=lax.Precision.H...]
    unnamed x11 -> x29, local copies, waits for them, and re-layouts: 0.92 us -> 4.44 us
    convert_element_type x4 -> x0, other arithmetic: 2.44 us -> none  [the longest x1 1.13 us: per_device(): pert = (members.astype(jnp.float32) - ens_mean).astype(jnp.bfloat16)]
  transfers between devices with their start and end apart: 12 -> 12, of which waited for: 5 -> 7; matrix products, arithmetic and copies ran while one was open for 8% -> 0% of each run, Pallas kernels for 0% -> 5%
where the time goes in v1:
time: 44.7 us; the launch traced here: 44.3 us
  Pallas kernels  16 us (36%)
  starting transfers between devices  11.4 us (26%)
  waiting for transfers between devices  10.6 us (24%)
  local copies, waits for them, and re-layouts  6.28 us (14%)
    pallas_call x6, Pallas kernels, call(): pl.pallas_call(kernel, out_shape=out_shape, in_specs=[spec] * len(operand...  16 us
    ppermute x12, starting transfers between devices, send(): return lax.ppermute(value, axes, ways[way])  11.4 us
    ppermute x12, waiting for transfers between devices, send(): return lax.ppermute(value, axes, ways[way])  10.6 us
    unnamed x29, local copies, waits for them, and re-layouts  4.44 us
    reshape x1, local copies, waits for them, and re-layouts, paired_device(): innovation.reshape(1, rows)  1.25 us
  transfers between devices with their start and end apart: 12, of which 7 were waited for; matrix products, arithmetic and copies ran while one was open for 0% of the time, Pallas kernels for 5%

profile of v1, /device:TPU:0, one launch (start us, length us, event | category | flops | bytes accessed | tf_op | source)
XLA Modules:
  0.0 44.3 jit_solution(4798513181474737201)
XLA Ops:
  0.0 1.3 %reshape.6.inn_ref = bf16[1,256]{1,0:T(2,128)(2,1)} reshape(bf16[256]{0:T(256)(128)(2,1)} %param.10) | data formatting | bytes 1024 | tf_op jit(solution)/shard_map/reshape | solution.py:483
  1.3 0.6 %reshape.7.prec_ref = bf16[1,256]{1,0:T(2,128)(2,1)} reshape(bf16[256]{0:T(256)(128)(2,1)S(1)} %copy-done.13) | data formatting | bytes 1024 | tf_op jit(solution)/shard_map/reshape | solution.py:484
  1.9 0.7 %copy.10.count_ref = s32[4,1]{1,0:T(4,128)} copy(s32[4,1]{0,1:T(1,128)S(1)} %copy-done.12) | data formatting | bytes 32 | tf_op args[6]
  2.6 1.6 %pack.1.b0 = bf16[272,128]{1,0:T(8,128)(2,1)} custom-call(bf16[256,128]{1,0:T(8,128)(2,1)} %pert_ref.1, bf16[1,256]{1,0:T(2,128)(2,1)} %reshape.6.inn_ref, bf16[1,256]{1,0:T(2,128)(2,1)} %reshape.7.prec_ref, s32[4,1,256]{2,1,0:T(1,128)} %owner_ref.3, s32[4,1,256]{2,1,0:T(1,128)} %slot_ref.3, s32[4,1]{1,0:T(4,128)} %copy.10.count_ref, f32[4,1,256]{2,1,0:T(1,128)} %local_ref.3), custom_call_target="tpu_custom_call" | custom-call | tf_op jit(solution)/shard_map/pack/pallas_call | solution.py:209
  4.2 3.0 %collective-permute-start = (bf16[272,128]{1,0:T(8,128)(2,1)}, bf16[272,128]{1,0:T(8,128)(2,1)S(1)}, u32[]{:S(2)}, u32[]{:S(2)}) collective-permute-start(bf16[272,128]{1,0:T(8,128)(2,1)} %pack.1.b0), channel_id=1, source_target_pairs={{0,16},{1,17},{2,18},{3,19},{4,20},{5,21},{6,22},{7,23},{8,24},{9,... | collective-permute-start | bytes 208904 | tf_op jit(solution)/shard_map/ppermute | solution.py:469
  7.2 2.0 %collective-permute-start.1 = (bf16[272,128]{1,0:T(8,128)(2,1)}, bf16[272,128]{1,0:T(8,128)(2,1)S(1)}, u32[]{:S(2)}, u32[]{:S(2)}) collective-permute-start(bf16[272,128]{1,0:T(8,128)(2,1)} %pack.1.b0), channel_id=1, source_target_pairs={{0,4},{1,0},{2,6},{3,2},{4,8},{5,1},{6,10},{7,3},{8,12},{9,5},{10,... | collective-permute-start | bytes 208904 | tf_op jit(solution)/shard_map/ppermute | solution.py:469
  9.7 2.1 %collective-permute-start.3 = (bf16[272,128]{1,0:T(8,128)(2,1)S(1)}, bf16[272,128]{1,0:T(8,128)(2,1)S(1)}, u32[]{:S(2)}, u32[]{:S(2)}) collective-permute-start(bf16[272,128]{1,0:T(8,128)(2,1)S(1)} %collective-permute-done.other_ref.b3), channel_id=1, source_target_pairs={{0,4},{1,0},{2,6},{3,2},{4,8},{5,1},{6,10},{7,3},{8,12},{9,5},{10,... | collective-permute-start | bytes 208904 | tf_op jit(solution)/shard_map/ppermute | solution.py:469
  11.7 2.1 %table.1.table_ref = f32[128,128]{1,0:T(8,128)} custom-call(s32[4,1,256]{2,1,0:T(1,128)} %owner_ref.3, s32[4,1,256]{2,1,0:T(1,128)} %slot_ref.3, s32[4,1]{1,0:T(4,128)} %copy.10.count_ref, f32[4,1,256]{2,1,0:T(1,128)} %local_ref.3, bf16[272,128]{1,0:T(8,128)(2,1)} %copy-done), custom_call_target="tpu_custom_call" | custom-call | flops 18874368 | bytes 131072 | tf_op jit(solution)/shard_map/table/pallas_call | solution.py:209
  14.9 0.6 %copy-done.11 = bf16[272,128]{1,0:T(8,128)(2,1)} copy-done((bf16[272,128]{1,0:T(8,128)(2,1)}, bf16[272,128]{1,0:T(8,128)(2,1)S(1)}, u32[]{:S(2)}) %copy-start.11) | copy-done | bytes 69656
  15.5 4.0 %gram.1 = (f32[392,128]{1,0:T(8,128)}, f32[392,128]{1,0:T(8,128)}) custom-call(f32[128,128]{1,0:T(8,128)} %table.1.table_ref, bf16[272,128]{1,0:T(8,128)(2,1)} %pack.1.b0, bf16[272,128]{1,0:T(8,128)(2,1)} %copy-done.9, bf16[272,128]{1,0:T(8,128)(2,1)} %copy-done.8, bf16[272,128]{1,0:T(8,128)(2,1)} %copy-done, bf16[272,128]{1,0:T(8,128)(2,1)} %copy-done.11, ...), custom_call_target="tpu_custom_call" | custom-call | tf_op jit(solution)/shard_map/gram/pallas_call | solution.py:209
  19.5 1.7 %collective-permute-done.5.got_ref = f32[392,128]{1,0:T(8,128)S(1)} collective-permute-done((f32[392,128]{1,0:T(8,128)}, f32[392,128]{1,0:T(8,128)S(1)}, u32[]{:S(2)}, u32[]{:S(2)}) %collective-permute-start.5) | collective-permute-done | bytes 200736 | tf_op jit(solution)/shard_map/ppermute | solution.py:469
  21.1 0.7 %copy-done.1 = f32[392,128]{1,0:T(8,128)} copy-done((f32[392,128]{1,0:T(8,128)}, f32[392,128]{1,0:T(8,128)S(1)}, u32[]{:S(2)}) %copy-start.1) | copy-done | bytes 200728
  21.8 1.8 %join.1 = (f32[392,128]{1,0:T(8,128)}, bf16[400,128]{1,0:T(8,128)(2,1)}) custom-call(f32[392,128]{1,0:T(8,128)} %get-tuple-element.9.mine_ref, f32[392,128]{1,0:T(8,128)} %copy-done.1), custom_call_target="tpu_custom_call" | custom-call | tf_op jit(solution)/shard_map/join/pallas_call | solution.py:209
  23.6 1.7 %collective-permute-start.6 = (bf16[400,128]{1,0:T(8,128)(2,1)}, bf16[400,128]{1,0:T(8,128)(2,1)S(1)}, u32[]{:S(2)}, u32[]{:S(2)}) collective-permute-start(bf16[400,128]{1,0:T(8,128)(2,1)} %get-tuple-element.12), channel_id=1, source_target_pairs={{0,2},{1,3},{2,0},{3,1},{4,6},{5,7},{6,4},{7,5},{8,10},{9,11},{10,... | collective-permute-start | bytes 307208 | tf_op jit(solution)/shard_map/ppermute | solution.py:469
  25.3 3.4 %collective-permute-done.6.got_ref = bf16[400,128]{1,0:T(8,128)(2,1)S(1)} collective-permute-done((bf16[400,128]{1,0:T(8,128)(2,1)}, bf16[400,128]{1,0:T(8,128)(2,1)S(1)}, u32[]{:S(2)}, u32[]{:S(2)}) %collective-permute-start.6) | collective-permute-done | bytes 102432 | tf_op jit(solution)/shard_map/ppermute | solution.py:469
  28.7 0.6 %copy-done.2 = bf16[400,128]{1,0:T(8,128)(2,1)} copy-done((bf16[400,128]{1,0:T(8,128)(2,1)}, bf16[400,128]{1,0:T(8,128)(2,1)S(1)}, u32[]{:S(2)}) %copy-start.2) | copy-done | bytes 102424
  29.4 3.6 %solve.1.own = bf16[384,128]{1,0:T(8,128)(2,1)} custom-call(f32[392,128]{1,0:T(8,128)} %get-tuple-element.11.sum_ref, bf16[400,128]{1,0:T(8,128)(2,1)} %copy-done.2), custom_call_target="tpu_custom_call" | custom-call | tf_op jit(solution)/shard_map/solve/pallas_call | solution.py:209
  33.0 2.0 %collective-permute-start.8 = (bf16[384,128]{1,0:T(8,128)(2,1)}, bf16[384,128]{1,0:T(8,128)(2,1)S(1)}, u32[]{:S(2)}, u32[]{:S(2)}) collective-permute-start(bf16[384,128]{1,0:T(8,128)(2,1)} %solve.1.own), channel_id=1, source_target_pairs={{0,4},{1,0},{2,6},{3,2},{4,8},{5,1},{6,10},{7,3},{8,12},{9,5},{10,... | collective-permute-start | bytes 294920 | tf_op jit(solution)/shard_map/ppermute | solution.py:469
  35.0 3.7 %collective-permute-done.9.descend = bf16[384,128]{1,0:T(8,128)(2,1)S(1)} collective-permute-done((bf16[384,128]{1,0:T(8,128)(2,1)}, bf16[384,128]{1,0:T(8,128)(2,1)S(1)}, u32[]{:S(2)}, u32[]{:S(2)}) %collective-permute-start.9) | collective-permute-done | bytes 98336 | tf_op jit(solution)/shard_map/ppermute | solution.py:469
  38.8 0.5 %collective-permute-start.10 = (bf16[384,128]{1,0:T(8,128)(2,1)S(1)}, bf16[384,128]{1,0:T(8,128)(2,1)S(1)}, u32[]{:S(2)}, u32[]{:S(2)}) collective-permute-start(bf16[384,128]{1,0:T(8,128)(2,1)S(1)} %collective-permute-done.8.climb), channel_id=1, source_target_pairs={{0,1},{1,0},{2,3},{3,2},{4,5},{5,4},{6,7},{7,6},{8,9},{9,8},{10,11... | collective-permute-start | bytes 294920 | tf_op jit(solution)/shard_map/ppermute | solution.py:469
  39.3 0.8 %collective-permute-done.11.pair_descend = bf16[384,128]{1,0:T(8,128)(2,1)S(1)} collective-permute-done((bf16[384,128]{1,0:T(8,128)(2,1)S(1)}, bf16[384,128]{1,0:T(8,128)(2,1)S(1)}, u32[]{:S(2)}, u32[]{:S(2)}) %collective-permute-start.11) | collective-permute-done | bytes 98336 | tf_op jit(solution)/shard_map/ppermute | solution.py:469
  40.2 0.5 %copy-done.6 = bf16[384,128]{1,0:T(8,128)(2,1)} copy-done((bf16[384,128]{1,0:T(8,128)(2,1)}, bf16[384,128]{1,0:T(8,128)(2,1)S(1)}, u32[]{:S(2)}) %copy-start.6) | copy-done | bytes 98328
  40.7 0.6 %copy-done.7 = bf16[384,128]{1,0:T(8,128)(2,1)} copy-done((bf16[384,128]{1,0:T(8,128)(2,1)}, bf16[384,128]{1,0:T(8,128)(2,1)S(1)}, u32[]{:S(2)}) %copy-start.7) | copy-done | bytes 98328
  41.4 2.9 %apply.1 = bf16[2,64,16,128]{3,2,1,0:T(8,128)(2,1)} custom-call(bf16[2,64,16,128]{3,2,1,0:T(8,128)(2,1)} %members_ref.1, bf16[384,128]{1,0:T(8,128)(2,1)} %solve.1.own, bf16[384,128]{1,0:T(8,128)(2,1)} %copy-done.5, bf16[384,128]{1,0:T(8,128)(2,1)} %copy-done.4, bf16[384,128]{1,0:T(8,128)(2,1)} %copy-done.3, bf16[384,128]{1,0:T(8,128)(2,1)} %copy-done.7, ...), custom_call_target="tpu_custom_call" | custom-call | tf_op jit(solution)/shard_map/apply/pallas_call | solution.py:209
  (37 shorter events, 1.8 us)
Async XLA Ops:
  0.0 1.3 %copy-start.13 = (bf16[256]{0:T(256)(128)(2,1)S(1)}, bf16[256]{0:T(256)(128)(2,1)}, u32[]{:S(2)}) copy-start(bf16[256]{0:T(256)(128)(2,1)} %param.11) | copy-start | bytes 1540
  1.3 0.7 %copy-start.12 = (s32[4,1]{0,1:T(1,128)S(1)}, s32[4,1]{0,1:T(1,128)}, u32[]{:S(2)}) copy-start(s32[4,1]{0,1:T(1,128)} %param.14) | copy-start | bytes 52
  4.2 5.5 %collective-permute-start = (bf16[272,128]{1,0:T(8,128)(2,1)}, bf16[272,128]{1,0:T(8,128)(2,1)S(1)}, u32[]{:S(2)}, u32[]{:S(2)}) collective-permute-start(bf16[272,128]{1,0:T(8,128)(2,1)} %pack.1.b0), channel_id=1, source_target_pairs={{0,16},{1,17},{2,18},{3,19},{4,20},{5,21},{6,22},{7,23},{8,24},{9,... | collective-permute-start | bytes 208904 | tf_op jit(solution)/shard_map/ppermute | solution.py:469
  7.1 6.7 %collective-permute-start.2 = (bf16[272,128]{1,0:T(8,128)(2,1)}, bf16[272,128]{1,0:T(8,128)(2,1)S(1)}, u32[]{:S(2)}, u32[]{:S(2)}) collective-permute-start(bf16[272,128]{1,0:T(8,128)(2,1)} %pack.1.b0), channel_id=1, source_target_pairs={{4,0},{0,1},{6,2},{2,3},{8,4},{1,5},{10,6},{3,7},{12,8},{5,9},{14,... | collective-permute-start | bytes 208904 | tf_op jit(solution)/shard_map/ppermute | solution.py:469
  7.2 6.7 %collective-permute-start.1 = (bf16[272,128]{1,0:T(8,128)(2,1)}, bf16[272,128]{1,0:T(8,128)(2,1)S(1)}, u32[]{:S(2)}, u32[]{:S(2)}) collective-permute-start(bf16[272,128]{1,0:T(8,128)(2,1)} %pack.1.b0), channel_id=1, source_target_pairs={{0,4},{1,0},{2,6},{3,2},{4,8},{5,1},{6,10},{7,3},{8,12},{9,5},{10,... | collective-permute-start | bytes 208904 | tf_op jit(solution)/shard_map/ppermute | solution.py:469
  9.6 2.1 %copy-start = (bf16[272,128]{1,0:T(8,128)(2,1)}, bf16[272,128]{1,0:T(8,128)(2,1)S(1)}, u32[]{:S(2)}) copy-start(bf16[272,128]{1,0:T(8,128)(2,1)S(1)} %collective-permute-done.other_ref.b3) | copy-start | bytes 208900
  9.6 4.6 %collective-permute-start.4 = (bf16[272,128]{1,0:T(8,128)(2,1)S(1)}, bf16[272,128]{1,0:T(8,128)(2,1)S(1)}, u32[]{:S(2)}, u32[]{:S(2)}) collective-permute-start(bf16[272,128]{1,0:T(8,128)(2,1)S(1)} %collective-permute-done.other_ref.b3), channel_id=1, source_target_pairs={{4,0},{0,1},{6,2},{2,3},{8,4},{1,5},{10,6},{3,7},{12,8},{5,9},{14,... | collective-permute-start | bytes 208904 | tf_op jit(solution)/shard_map/ppermute | solution.py:469
  9.7 4.6 %collective-permute-start.3 = (bf16[272,128]{1,0:T(8,128)(2,1)S(1)}, bf16[272,128]{1,0:T(8,128)(2,1)S(1)}, u32[]{:S(2)}, u32[]{:S(2)}) collective-permute-start(bf16[272,128]{1,0:T(8,128)(2,1)S(1)} %collective-permute-done.other_ref.b3), channel_id=1, source_target_pairs={{0,4},{1,0},{2,6},{3,2},{4,8},{5,1},{6,10},{7,3},{8,12},{9,5},{10,... | collective-permute-start | bytes 208904 | tf_op jit(solution)/shard_map/ppermute | solution.py:469
  13.8 0.6 %copy-start.8 = (bf16[272,128]{1,0:T(8,128)(2,1)}, bf16[272,128]{1,0:T(8,128)(2,1)S(1)}, u32[]{:S(2)}) copy-start(bf16[272,128]{1,0:T(8,128)(2,1)S(1)} %collective-permute-done.2.b2) | copy-start | bytes 208900
  13.8 0.7 %copy-start.9 = (bf16[272,128]{1,0:T(8,128)(2,1)}, bf16[272,128]{1,0:T(8,128)(2,1)S(1)}, u32[]{:S(2)}) copy-start(bf16[272,128]{1,0:T(8,128)(2,1)S(1)} %collective-permute-done.1.b1) | copy-start | bytes 208900
  14.8 0.6 %copy-start.11 = (bf16[272,128]{1,0:T(8,128)(2,1)}, bf16[272,128]{1,0:T(8,128)(2,1)S(1)}, u32[]{:S(2)}) copy-start(bf16[272,128]{1,0:T(8,128)(2,1)S(1)} %collective-permute-done.3.b4) | copy-start | bytes 208900
  19.5 1.7 %collective-permute-start.5 = (f32[392,128]{1,0:T(8,128)}, f32[392,128]{1,0:T(8,128)S(1)}, u32[]{:S(2)}, u32[]{:S(2)}) collective-permute-start(f32[392,128]{1,0:T(8,128)} %get-tuple-element.10), channel_id=1, source_target_pairs={{0,1},{1,0},{2,3},{3,2},{4,5},{5,4},{6,7},{7,6},{8,9},{9,8},{10,11... | collective-permute-start | bytes 602120 | tf_op jit(solution)/shard_map/ppermute | solution.py:469
  21.1 0.7 %copy-start.1 = (f32[392,128]{1,0:T(8,128)}, f32[392,128]{1,0:T(8,128)S(1)}, u32[]{:S(2)}) copy-start(f32[392,128]{1,0:T(8,128)S(1)} %collective-permute-done.5.got_ref) | copy-start | bytes 602116
  23.6 5.1 %collective-permute-start.6 = (bf16[400,128]{1,0:T(8,128)(2,1)}, bf16[400,128]{1,0:T(8,128)(2,1)S(1)}, u32[]{:S(2)}, u32[]{:S(2)}) collective-permute-start(bf16[400,128]{1,0:T(8,128)(2,1)} %get-tuple-element.12), channel_id=1, source_target_pairs={{0,2},{1,3},{2,0},{3,1},{4,6},{5,7},{6,4},{7,5},{8,10},{9,11},{10,... | collective-permute-start | bytes 307208 | tf_op jit(solution)/shard_map/ppermute | solution.py:469
  28.7 0.6 %copy-start.2 = (bf16[400,128]{1,0:T(8,128)(2,1)}, bf16[400,128]{1,0:T(8,128)(2,1)S(1)}, u32[]{:S(2)}) copy-start(bf16[400,128]{1,0:T(8,128)(2,1)S(1)} %collective-permute-done.6.got_ref) | copy-start | bytes 307204
  33.0 5.8 %collective-permute-start.9 = (bf16[384,128]{1,0:T(8,128)(2,1)}, bf16[384,128]{1,0:T(8,128)(2,1)S(1)}, u32[]{:S(2)}, u32[]{:S(2)}) collective-permute-start(bf16[384,128]{1,0:T(8,128)(2,1)} %solve.1.own), channel_id=1, source_target_pairs={{4,0},{0,1},{6,2},{2,3},{8,4},{1,5},{10,6},{3,7},{12,8},{5,9},{14,... | collective-permute-start | bytes 294920 | tf_op jit(solution)/shard_map/ppermute | solution.py:469
  33.0 5.8 %collective-permute-start.8 = (bf16[384,128]{1,0:T(8,128)(2,1)}, bf16[384,128]{1,0:T(8,128)(2,1)S(1)}, u32[]{:S(2)}, u32[]{:S(2)}) collective-permute-start(bf16[384,128]{1,0:T(8,128)(2,1)} %solve.1.own), channel_id=1, source_target_pairs={{0,4},{1,0},{2,6},{3,2},{4,8},{5,1},{6,10},{7,3},{8,12},{9,5},{10,... | collective-permute-start | bytes 294920 | tf_op jit(solution)/shard_map/ppermute | solution.py:469
  35.0 4.3 %collective-permute-start.7 = (bf16[384,128]{1,0:T(8,128)(2,1)}, bf16[384,128]{1,0:T(8,128)(2,1)S(1)}, u32[]{:S(2)}, u32[]{:S(2)}) collective-permute-start(bf16[384,128]{1,0:T(8,128)(2,1)} %solve.1.own), channel_id=1, source_target_pairs={{0,1},{1,0},{2,3},{3,2},{4,5},{5,4},{6,7},{7,6},{8,9},{9,8},{10,11... | collective-permute-start | bytes 294920 | tf_op jit(solution)/shard_map/ppermute | solution.py:469
  38.8 1.5 %copy-start.3 = (bf16[384,128]{1,0:T(8,128)(2,1)}, bf16[384,128]{1,0:T(8,128)(2,1)S(1)}, u32[]{:S(2)}) copy-start(bf16[384,128]{1,0:T(8,128)(2,1)S(1)} %collective-permute-done.9.descend) | copy-start | bytes 294916
  38.8 1.3 %collective-permute-start.11 = (bf16[384,128]{1,0:T(8,128)(2,1)S(1)}, bf16[384,128]{1,0:T(8,128)(2,1)S(1)}, u32[]{:S(2)}, u32[]{:S(2)}) collective-permute-start(bf16[384,128]{1,0:T(8,128)(2,1)S(1)} %collective-permute-done.9.descend), channel_id=1, source_target_pairs={{0,1},{1,0},{2,3},{3,2},{4,5},{5,4},{6,7},{7,6},{8,9},{9,8},{10,11... | collective-permute-start | bytes 294920 | tf_op jit(solution)/shard_map/ppermute | solution.py:469
  38.8 1.5 %copy-start.4 = (bf16[384,128]{1,0:T(8,128)(2,1)}, bf16[384,128]{1,0:T(8,128)(2,1)S(1)}, u32[]{:S(2)}) copy-start(bf16[384,128]{1,0:T(8,128)(2,1)S(1)} %collective-permute-done.8.climb) | copy-start | bytes 294916
  38.8 1.4 %collective-permute-start.10 = (bf16[384,128]{1,0:T(8,128)(2,1)S(1)}, bf16[384,128]{1,0:T(8,128)(2,1)S(1)}, u32[]{:S(2)}, u32[]{:S(2)}) collective-permute-start(bf16[384,128]{1,0:T(8,128)(2,1)S(1)} %collective-permute-done.8.climb), channel_id=1, source_target_pairs={{0,1},{1,0},{2,3},{3,2},{4,5},{5,4},{6,7},{7,6},{8,9},{9,8},{10,11... | collective-permute-start | bytes 294920 | tf_op jit(solution)/shard_map/ppermute | solution.py:469
  39.3 0.9 %copy-start.5 = (bf16[384,128]{1,0:T(8,128)(2,1)}, bf16[384,128]{1,0:T(8,128)(2,1)S(1)}, u32[]{:S(2)}) copy-start(bf16[384,128]{1,0:T(8,128)(2,1)S(1)} %collective-permute-done.7.pair) | copy-start | bytes 294916
  40.1 0.7 %copy-start.6 = (bf16[384,128]{1,0:T(8,128)(2,1)}, bf16[384,128]{1,0:T(8,128)(2,1)S(1)}, u32[]{:S(2)}) copy-start(bf16[384,128]{1,0:T(8,128)(2,1)S(1)} %collective-permute-done.11.pair_descend) | copy-start | bytes 294916
  (2 other events, 1.3 us)

commit v2 on v1

--- a/solution.py
+++ b/solution.py
@@ -9,6 +9,7 @@
 
 SPACING = 16
 NS_STEPS = 4
+VMEM_LIMIT = 12 << 20
 
 
 def padded(array, sides, width):
@@ -215,6 +216,7 @@
             cost_estimate=pl.CostEstimate(
                 flops=flops, bytes_accessed=bytes_accessed, transcendentals=0
             ),
+            compiler_params=pltpu.CompilerParams(vmem_limit_bytes=VMEM_LIMIT),
             name=name,
         )(*operands)
 
@@ -241,19 +243,19 @@
     edge = jnp.where(lax.axis_index("tx") == 0, owner_ref.shape[0] - 1, 0)
     slots = owner_ref.shape[2]
     out_ref[0:rows, :] = pert_ref[...]
-    active = lax.broadcasted_iota(jnp.int32, (1, slots), 1) < count_ref[edge, 0]
+    active = lax.broadcasted_iota(jnp.int32, (1, slots), 1) < jnp.where(edge == 0, count_ref[0, 0], count_ref[0, owner_ref.shape[0] - 1])
     local = jnp.where(active, local_ref[edge], 0.0)
     slot = slot_ref[edge]
+    for k, ref in enumerate((prec_ref, inn_ref)):
+        tail[2 * k : 2 * k + 2, :] = ref[...].astype(jnp.float32)
     lists = [
-        prec_ref[...].astype(jnp.float32),
-        inn_ref[...].astype(jnp.float32),
         owner_ref[edge].astype(jnp.float32),
         (slot // 128).astype(jnp.float32),
         (slot % 128).astype(jnp.float32),
     ] + [piece.astype(jnp.float32) for piece in split3(local)]
     for k, row in enumerate(lists):
         for part in range(2):
-            tail[2 * k + part : 2 * k + part + 1, :] = row[:, 128 * part : 128 * (part + 1)]
+            tail[4 + 2 * k + part : 5 + 2 * k + part, :] = row[:, 128 * part : 128 * (part + 1)]
     out_ref[rows : rows + 16, :] = tail[...].astype(jnp.bfloat16)
 
 
@@ -273,7 +275,7 @@
     position_in = lax.broadcasted_iota(jnp.int32, (1, slots), 1)
 
     def own_list(k):
-        return owner_ref[k], slot_ref[k], jnp.where(position_in < count_ref[k, 0], local_ref[k], 0.0)
+        return owner_ref[k], slot_ref[k], jnp.where(position_in < count_ref[0, k], local_ref[k], 0.0)
 
     def pick(use_far, k):
         return tuple(jnp.where(use_far, a, b) for a, b in zip((far_owner, far_slot, far_local), own_list(k)))
@@ -473,6 +475,7 @@
     cols = obs_owner.shape[0] + 2
     half = cols // 2
     shape = jax.ShapeDtypeStruct
+    counts = obs_count.reshape(1, -1)
     packed = vmem_call(
         functools.partial(pack_kernel, rows),
         shape((rows + 16, size), bf16),
@@ -480,11 +483,11 @@
         name="pack",
     )(
         obs_pert,
-        innovation.reshape(1, rows),
-        obs_precision.reshape(1, rows),
+        innovation.reshape(rows // size, size),
+        obs_precision.reshape(rows // size, size),
         obs_owner,
         obs_slot,
-        obs_count,
+        counts,
         local_weight,
     )
     across = send(packed, "across")
@@ -496,7 +499,7 @@
         flops=6 * 2 * 48 * 256 * 128,
         bytes_accessed=1 << 17,
         name="table",
-    )(obs_owner, obs_slot, obs_count, local_weight, across)
+    )(obs_owner, obs_slot, counts, local_weight, across)
     mine, rest = vmem_call(
         functools.partial(gram_kernel, rows, cols),
         [shape((128 * half + 8, size), f32)] * 2,

time: 44.7 us -> 32.7 us (0.73)
  Pallas kernels: 16 us -> 6.59 us
  local copies, waits for them, and re-layouts: 6.28 us -> 2.92 us
  waiting for transfers between devices: 10.6 us -> 11.2 us
    pallas_call x6, Pallas kernels: 16 us -> 6.59 us  [call(): pl.pallas_call(kernel, out_shape=out_shape, in_specs=[spec] * len(operand...]
    reshape x2 -> x0, local copies, waits for them, and re-layouts: 1.85 us -> none  [the longest x1 1.25 us: paired_device(): innovation.reshape(1, rows)]
    unnamed x29 -> x20, local copies, waits for them, and re-layouts: 4.44 us -> 2.92 us
    ppermute x12, waiting for transfers between devices: 10.6 us -> 11.2 us  [send(): return lax.ppermute(value, axes, ways[way])]
  transfers between devices with their start and end apart: 12 -> 12, of which waited for: 7 -> 8; matrix products, arithmetic and copies ran while one was open for 0% -> 0% of each run, Pallas kernels for 5% -> 1%
where the time goes in v2:
time: 32.7 us; the launch traced here: 32.4 us
  starting transfers between devices  11.6 us (35%)
  waiting for transfers between devices  11.2 us (34%)
  Pallas kernels  6.59 us (20%)
  local copies, waits for them, and re-layouts  2.92 us (9%)
    ppermute x12, starting transfers between devices, send(): return lax.ppermute(value, axes, ways[way])  11.6 us
    ppermute x12, waiting for transfers between devices, send(): return lax.ppermute(value, axes, ways[way])  11.2 us
    pallas_call x6, Pallas kernels, call(): pl.pallas_call(kernel, out_shape=out_shape, in_specs=[spec] * len(operand...  6.59 us
    unnamed x20, local copies, waits for them, and re-layouts  2.92 us
  transfers between devices with their start and end apart: 12, of which 8 were waited for; matrix products, arithmetic and copies ran while one was open for 0% of the time, Pallas kernels for 1%

profile of v2, /device:TPU:0, one launch (start us, length us, event | category | flops | bytes accessed | tf_op | source)
XLA Modules:
  0.0 32.4 jit_solution(5689783032105077036)
XLA Ops:
  0.0 0.7 %copy-done.2 = s32[4,1,256]{2,1,0:T(1,128)S(1)} copy-done((s32[4,1,256]{2,1,0:T(1,128)S(1)}, s32[4,1,256]{2,1,0:T(1,128)}, u32[]{:S(2)}) %copy-start.2) | copy-done | bytes 4120
  0.7 0.8 %copy-done.1 = bf16[256,128]{1,0:T(8,128)(2,1)S(1)} copy-done((bf16[256,128]{1,0:T(8,128)(2,1)S(1)}, bf16[256,128]{1,0:T(8,128)(2,1)}, u32[]{:S(2)}) %copy-start.1) | copy-done | bytes 65560
  1.5 0.7 %copy-done.3 = s32[4,1,256]{2,1,0:T(1,128)S(1)} copy-done((s32[4,1,256]{2,1,0:T(1,128)S(1)}, s32[4,1,256]{2,1,0:T(1,128)}, u32[]{:S(2)}) %copy-start.3) | copy-done | bytes 4120
  2.2 0.7 %copy-done.5 = f32[4,1,256]{2,1,0:T(1,128)S(1)} copy-done((f32[4,1,256]{2,1,0:T(1,128)S(1)}, f32[4,1,256]{2,1,0:T(1,128)}, u32[]{:S(2)}) %copy-start.5) | copy-done | bytes 4120
  2.9 0.1 pack.1.b0
  3.0 3.1 %collective-permute-start = (bf16[272,128]{1,0:T(8,128)(2,1)S(1)}, bf16[272,128]{1,0:T(8,128)(2,1)S(1)}, u32[]{:S(2)}, u32[]{:S(2)}) collective-permute-start(bf16[272,128]{1,0:T(8,128)(2,1)S(1)} %pack.1.b0), channel_id=1, source_target_pairs={{0,16},{1,17},{2,18},{3,19},{4,20},{5,21},{6,22},{7,23},{8,24},{9,... | collective-permute-start | bytes 208904 | tf_op jit(solution)/shard_map/ppermute | solution.py:471
  6.1 2.0 %collective-permute-start.1 = (bf16[272,128]{1,0:T(8,128)(2,1)S(1)}, bf16[272,128]{1,0:T(8,128)(2,1)S(1)}, u32[]{:S(2)}, u32[]{:S(2)}) collective-permute-start(bf16[272,128]{1,0:T(8,128)(2,1)S(1)} %pack.1.b0), channel_id=1, source_target_pairs={{0,4},{1,0},{2,6},{3,2},{4,8},{5,1},{6,10},{7,3},{8,12},{9,5},{10,... | collective-permute-start | bytes 208904 | tf_op jit(solution)/shard_map/ppermute | solution.py:471
  8.1 0.3 collective-permute-done.other_ref.b3
  8.4 2.1 %collective-permute-start.3 = (bf16[272,128]{1,0:T(8,128)(2,1)S(1)}, bf16[272,128]{1,0:T(8,128)(2,1)S(1)}, u32[]{:S(2)}, u32[]{:S(2)}) collective-permute-start(bf16[272,128]{1,0:T(8,128)(2,1)S(1)} %collective-permute-done.other_ref.b3), channel_id=1, source_target_pairs={{0,4},{1,0},{2,6},{3,2},{4,8},{5,1},{6,10},{7,3},{8,12},{9,5},{10,... | collective-permute-start | bytes 208904 | tf_op jit(solution)/shard_map/ppermute | solution.py:471
  10.5 0.5 %table.1.table_ref = f32[128,128]{1,0:T(8,128)S(1)} custom-call(s32[4,1,256]{2,1,0:T(1,128)S(1)} %copy-done.2, s32[4,1,256]{2,1,0:T(1,128)S(1)} %copy-done.4, s32[1,4]{1,0:T(1,128)S(1)} %bitcast.4, f32[4,1,256]{2,1,0:T(1,128)S(1)} %copy-done.6, bf16[272,128]{1,0:T(8,128)(2,1)S(1)} %collective-permute-done.other_ref.b3), custom_call_target="tpu_custom_call" | custom-call | flops 18874368 | bytes 131072 | tf_op jit(solution)/shard_map/table/pallas_call | solution.py:210
  10.9 0.1 collective-permute-done.2.b2
  11.0 1.9 %collective-permute-done.4.b5 = bf16[272,128]{1,0:T(8,128)(2,1)S(1)} collective-permute-done((bf16[272,128]{1,0:T(8,128)(2,1)S(1)}, bf16[272,128]{1,0:T(8,128)(2,1)S(1)}, u32[]{:S(2)}, u32[]{:S(2)}) %collective-permute-start.4) | collective-permute-done | bytes 69664 | tf_op jit(solution)/shard_map/ppermute | solution.py:471
  13.0 2.3 %gram.1 = (f32[392,128]{1,0:T(8,128)S(1)}, f32[392,128]{1,0:T(8,128)S(1)}) custom-call(f32[128,128]{1,0:T(8,128)S(1)} %table.1.table_ref, bf16[272,128]{1,0:T(8,128)(2,1)S(1)} %pack.1.b0, bf16[272,128]{1,0:T(8,128)(2,1)S(1)} %collective-permute-done.1.b1, bf16[272,128]{1,0:T(8,128)(2,1)S(1)} %collective-permute-done.2.b2, ...), custom_call_target="tpu_custom_call" | custom-call | tf_op jit(solution)/shard_map/gram/pallas_call | solution.py:210
  15.3 0.1 collective-permute-start.5
  15.3 1.4 %collective-permute-done.5.got_ref = f32[392,128]{1,0:T(8,128)S(1)} collective-permute-done((f32[392,128]{1,0:T(8,128)S(1)}, f32[392,128]{1,0:T(8,128)S(1)}, u32[]{:S(2)}, u32[]{:S(2)}) %collective-permute-start.5) | collective-permute-done | bytes 200736 | tf_op jit(solution)/shard_map/ppermute | solution.py:471
  16.8 1.8 %collective-permute-start.6 = (bf16[400,128]{1,0:T(8,128)(2,1)S(1)}, bf16[400,128]{1,0:T(8,128)(2,1)S(1)}, u32[]{:S(2)}, u32[]{:S(2)}) collective-permute-start(bf16[400,128]{1,0:T(8,128)(2,1)S(1)} %get-tuple-element.12), channel_id=1, source_target_pairs={{0,2},{1,3},{2,0},{3,1},{4,6},{5,7},{6,4},{7,5},{8,10},{9,11},{10,... | collective-permute-start | bytes 307208 | tf_op jit(solution)/shard_map/ppermute | solution.py:471
  18.6 3.2 %collective-permute-done.6.got_ref = bf16[400,128]{1,0:T(8,128)(2,1)S(1)} collective-permute-done((bf16[400,128]{1,0:T(8,128)(2,1)S(1)}, bf16[400,128]{1,0:T(8,128)(2,1)S(1)}, u32[]{:S(2)}, u32[]{:S(2)}) %collective-permute-start.6) | collective-permute-done | bytes 102432 | tf_op jit(solution)/shard_map/ppermute | solution.py:471
  21.8 2.0 %solve.1.own = bf16[384,128]{1,0:T(8,128)(2,1)S(1)} custom-call(f32[392,128]{1,0:T(8,128)S(1)} %get-tuple-element.11.sum_ref, bf16[400,128]{1,0:T(8,128)(2,1)S(1)} %collective-permute-done.6.got_ref), custom_call_target="tpu_custom_call" | custom-call | tf_op jit(solution)/shard_map/solve/pallas_call | solution.py:210
  23.8 2.0 %collective-permute-start.8 = (bf16[384,128]{1,0:T(8,128)(2,1)S(1)}, bf16[384,128]{1,0:T(8,128)(2,1)S(1)}, u32[]{:S(2)}, u32[]{:S(2)}) collective-permute-start(bf16[384,128]{1,0:T(8,128)(2,1)S(1)} %solve.1.own), channel_id=1, source_target_pairs={{0,4},{1,0},{2,6},{3,2},{4,8},{5,1},{6,10},{7,3},{8,12},{9,5},{10,... | collective-permute-start | bytes 294920 | tf_op jit(solution)/shard_map/ppermute | solution.py:471
  25.9 3.4 %collective-permute-done.9.descend = bf16[384,128]{1,0:T(8,128)(2,1)S(1)} collective-permute-done((bf16[384,128]{1,0:T(8,128)(2,1)S(1)}, bf16[384,128]{1,0:T(8,128)(2,1)S(1)}, u32[]{:S(2)}, u32[]{:S(2)}) %collective-permute-start.9) | collective-permute-done | bytes 98336 | tf_op jit(solution)/shard_map/ppermute | solution.py:471
  29.3 0.5 %collective-permute-start.10 = (bf16[384,128]{1,0:T(8,128)(2,1)S(1)}, bf16[384,128]{1,0:T(8,128)(2,1)S(1)}, u32[]{:S(2)}, u32[]{:S(2)}) collective-permute-start(bf16[384,128]{1,0:T(8,128)(2,1)S(1)} %collective-permute-done.8.climb), channel_id=1, source_target_pairs={{0,1},{1,0},{2,3},{3,2},{4,5},{5,4},{6,7},{7,6},{8,9},{9,8},{10,11... | collective-permute-start | bytes 294920 | tf_op jit(solution)/shard_map/ppermute | solution.py:471
  29.8 0.8 %collective-permute-done.11.pair_descend = bf16[384,128]{1,0:T(8,128)(2,1)S(1)} collective-permute-done((bf16[384,128]{1,0:T(8,128)(2,1)S(1)}, bf16[384,128]{1,0:T(8,128)(2,1)S(1)}, u32[]{:S(2)}, u32[]{:S(2)}) %collective-permute-start.11) | collective-permute-done | bytes 98336 | tf_op jit(solution)/shard_map/ppermute | solution.py:471
  30.6 0.2 collective-permute-done.10.pair_climb
  30.7 1.7 %apply.1 = bf16[2,64,16,128]{3,2,1,0:T(8,128)(2,1)} custom-call(bf16[2,64,16,128]{3,2,1,0:T(8,128)(2,1)S(1)} %copy-done, bf16[384,128]{1,0:T(8,128)(2,1)S(1)} %solve.1.own, bf16[384,128]{1,0:T(8,128)(2,1)S(1)} %collective-permute-done.7.pair, bf16[384,128]{1,0:T(8,128)(2,1)S(1)} %collective-permute-done.8.climb, ...), custom_call_target="tpu_custom_call" | custom-call | tf_op jit(solution)/shard_map/apply/pallas_call | solution.py:210
  (26 shorter events, 0.1 us)
Async XLA Ops:
  0.0 0.7 %copy-start.2 = (s32[4,1,256]{2,1,0:T(1,128)S(1)}, s32[4,1,256]{2,1,0:T(1,128)}, u32[]{:S(2)}) copy-start(s32[4,1,256]{2,1,0:T(1,128)} %owner_ref.3) | copy-start | bytes 12292
  0.0 0.7 %copy-start.7 = (s32[4,1]{0,1:T(1,128)S(1)}, s32[4,1]{0,1:T(1,128)}, u32[]{:S(2)}) copy-start(s32[4,1]{0,1:T(1,128)} %param.14) | copy-start | bytes 52
  0.0 0.7 %copy-start.8 = (bf16[256]{0:T(256)(128)(2,1)S(1)}, bf16[256]{0:T(256)(128)(2,1)}, u32[]{:S(2)}) copy-start(bf16[256]{0:T(256)(128)(2,1)} %param.10) | copy-start | bytes 1540
  0.0 0.7 %copy-start.9 = (bf16[256]{0:T(256)(128)(2,1)S(1)}, bf16[256]{0:T(256)(128)(2,1)}, u32[]{:S(2)}) copy-start(bf16[256]{0:T(256)(128)(2,1)} %param.11) | copy-start | bytes 1540
  0.7 0.8 %copy-start.1 = (bf16[256,128]{1,0:T(8,128)(2,1)S(1)}, bf16[256,128]{1,0:T(8,128)(2,1)}, u32[]{:S(2)}) copy-start(bf16[256,128]{1,0:T(8,128)(2,1)} %pert_ref.1) | copy-start | bytes 196612
  1.5 0.7 %copy-start.3 = (s32[4,1,256]{2,1,0:T(1,128)S(1)}, s32[4,1,256]{2,1,0:T(1,128)}, u32[]{:S(2)}) copy-start(s32[4,1,256]{2,1,0:T(1,128)} %slot_ref.3) | copy-start | bytes 12292
  2.2 0.7 %copy-start.5 = (f32[4,1,256]{2,1,0:T(1,128)S(1)}, f32[4,1,256]{2,1,0:T(1,128)}, u32[]{:S(2)}) copy-start(f32[4,1,256]{2,1,0:T(1,128)} %local_ref.3) | copy-start | bytes 12292
  2.9 7.6 %copy-start.4 = (s32[4,1,256]{2,1,0:T(1,128)S(1)}, s32[4,1,256]{2,1,0:T(1,128)}, u32[]{:S(2)}) copy-start(s32[4,1,256]{2,1,0:T(1,128)} %slot_ref.3) | copy-start | bytes 12292
  2.9 7.6 %copy-start.6 = (f32[4,1,256]{2,1,0:T(1,128)S(1)}, f32[4,1,256]{2,1,0:T(1,128)}, u32[]{:S(2)}) copy-start(f32[4,1,256]{2,1,0:T(1,128)} %local_ref.3) | copy-start | bytes 12292
  3.0 5.3 %collective-permute-start = (bf16[272,128]{1,0:T(8,128)(2,1)S(1)}, bf16[272,128]{1,0:T(8,128)(2,1)S(1)}, u32[]{:S(2)}, u32[]{:S(2)}) collective-permute-start(bf16[272,128]{1,0:T(8,128)(2,1)S(1)} %pack.1.b0), channel_id=1, source_target_pairs={{0,16},{1,17},{2,18},{3,19},{4,20},{5,21},{6,22},{7,23},{8,24},{9,... | collective-permute-start | bytes 208904 | tf_op jit(solution)/shard_map/ppermute | solution.py:471
  6.1 4.9 %collective-permute-start.2 = (bf16[272,128]{1,0:T(8,128)(2,1)S(1)}, bf16[272,128]{1,0:T(8,128)(2,1)S(1)}, u32[]{:S(2)}, u32[]{:S(2)}) collective-permute-start(bf16[272,128]{1,0:T(8,128)(2,1)S(1)} %pack.1.b0), channel_id=1, source_target_pairs={{4,0},{0,1},{6,2},{2,3},{8,4},{1,5},{10,6},{3,7},{12,8},{5,9},{14,... | collective-permute-start | bytes 208904 | tf_op jit(solution)/shard_map/ppermute | solution.py:471
  6.1 4.9 %collective-permute-start.1 = (bf16[272,128]{1,0:T(8,128)(2,1)S(1)}, bf16[272,128]{1,0:T(8,128)(2,1)S(1)}, u32[]{:S(2)}, u32[]{:S(2)}) collective-permute-start(bf16[272,128]{1,0:T(8,128)(2,1)S(1)} %pack.1.b0), channel_id=1, source_target_pairs={{0,4},{1,0},{2,6},{3,2},{4,8},{5,1},{6,10},{7,3},{8,12},{9,5},{10,... | collective-permute-start | bytes 208904 | tf_op jit(solution)/shard_map/ppermute | solution.py:471
  8.4 4.6 %collective-permute-start.4 = (bf16[272,128]{1,0:T(8,128)(2,1)S(1)}, bf16[272,128]{1,0:T(8,128)(2,1)S(1)}, u32[]{:S(2)}, u32[]{:S(2)}) collective-permute-start(bf16[272,128]{1,0:T(8,128)(2,1)S(1)} %collective-permute-done.other_ref.b3), channel_id=1, source_target_pairs={{4,0},{0,1},{6,2},{2,3},{8,4},{1,5},{10,6},{3,7},{12,8},{5,9},{14,... | collective-permute-start | bytes 208904 | tf_op jit(solution)/shard_map/ppermute | solution.py:471
  8.4 4.6 %collective-permute-start.3 = (bf16[272,128]{1,0:T(8,128)(2,1)S(1)}, bf16[272,128]{1,0:T(8,128)(2,1)S(1)}, u32[]{:S(2)}, u32[]{:S(2)}) collective-permute-start(bf16[272,128]{1,0:T(8,128)(2,1)S(1)} %collective-permute-done.other_ref.b3), channel_id=1, source_target_pairs={{0,4},{1,0},{2,6},{3,2},{4,8},{5,1},{6,10},{7,3},{8,12},{9,5},{10,... | collective-permute-start | bytes 208904 | tf_op jit(solution)/shard_map/ppermute | solution.py:471
  15.3 15.5 %copy-start = (bf16[2,64,16,128]{3,2,1,0:T(8,128)(2,1)S(1)}, bf16[2,64,16,128]{3,2,1,0:T(8,128)(2,1)}, u32[]{:S(2)}) copy-start(bf16[2,64,16,128]{3,2,1,0:T(8,128)(2,1)} %members_ref.1) | copy-start | bytes 1572868
  15.3 1.5 %collective-permute-start.5 = (f32[392,128]{1,0:T(8,128)S(1)}, f32[392,128]{1,0:T(8,128)S(1)}, u32[]{:S(2)}, u32[]{:S(2)}) collective-permute-start(f32[392,128]{1,0:T(8,128)S(1)} %get-tuple-element.10), channel_id=1, source_target_pairs={{0,1},{1,0},{2,3},{3,2},{4,5},{5,4},{6,7},{7,6},{8,9},{9,8},{10,11... | collective-permute-start | bytes 602120 | tf_op jit(solution)/shard_map/ppermute | solution.py:471
  16.8 5.0 %collective-permute-start.6 = (bf16[400,128]{1,0:T(8,128)(2,1)S(1)}, bf16[400,128]{1,0:T(8,128)(2,1)S(1)}, u32[]{:S(2)}, u32[]{:S(2)}) collective-permute-start(bf16[400,128]{1,0:T(8,128)(2,1)S(1)} %get-tuple-element.12), channel_id=1, source_target_pairs={{0,2},{1,3},{2,0},{3,1},{4,6},{5,7},{6,4},{7,5},{8,10},{9,11},{10,... | collective-permute-start | bytes 307208 | tf_op jit(solution)/shard_map/ppermute | solution.py:471
  23.8 5.4 %collective-permute-start.9 = (bf16[384,128]{1,0:T(8,128)(2,1)S(1)}, bf16[384,128]{1,0:T(8,128)(2,1)S(1)}, u32[]{:S(2)}, u32[]{:S(2)}) collective-permute-start(bf16[384,128]{1,0:T(8,128)(2,1)S(1)} %solve.1.own), channel_id=1, source_target_pairs={{4,0},{0,1},{6,2},{2,3},{8,4},{1,5},{10,6},{3,7},{12,8},{5,9},{14,... | collective-permute-start | bytes 294920 | tf_op jit(solution)/shard_map/ppermute | solution.py:471
  23.8 5.4 %collective-permute-start.8 = (bf16[384,128]{1,0:T(8,128)(2,1)S(1)}, bf16[384,128]{1,0:T(8,128)(2,1)S(1)}, u32[]{:S(2)}, u32[]{:S(2)}) collective-permute-start(bf16[384,128]{1,0:T(8,128)(2,1)S(1)} %solve.1.own), channel_id=1, source_target_pairs={{0,4},{1,0},{2,6},{3,2},{4,8},{5,1},{6,10},{7,3},{8,12},{9,5},{10,... | collective-permute-start | bytes 294920 | tf_op jit(solution)/shard_map/ppermute | solution.py:471
  25.9 3.9 %collective-permute-start.7 = (bf16[384,128]{1,0:T(8,128)(2,1)S(1)}, bf16[384,128]{1,0:T(8,128)(2,1)S(1)}, u32[]{:S(2)}, u32[]{:S(2)}) collective-permute-start(bf16[384,128]{1,0:T(8,128)(2,1)S(1)} %solve.1.own), channel_id=1, source_target_pairs={{0,1},{1,0},{2,3},{3,2},{4,5},{5,4},{6,7},{7,6},{8,9},{9,8},{10,11... | collective-permute-start | bytes 294920 | tf_op jit(solution)/shard_map/ppermute | solution.py:471
  29.2 1.3 %collective-permute-start.11 = (bf16[384,128]{1,0:T(8,128)(2,1)S(1)}, bf16[384,128]{1,0:T(8,128)(2,1)S(1)}, u32[]{:S(2)}, u32[]{:S(2)}) collective-permute-start(bf16[384,128]{1,0:T(8,128)(2,1)S(1)} %collective-permute-done.9.descend), channel_id=1, source_target_pairs={{0,1},{1,0},{2,3},{3,2},{4,5},{5,4},{6,7},{7,6},{8,9},{9,8},{10,11... | collective-permute-start | bytes 294920 | tf_op jit(solution)/shard_map/ppermute | solution.py:471
  29.3 1.5 %collective-permute-start.10 = (bf16[384,128]{1,0:T(8,128)(2,1)S(1)}, bf16[384,128]{1,0:T(8,128)(2,1)S(1)}, u32[]{:S(2)}, u32[]{:S(2)}) collective-permute-start(bf16[384,128]{1,0:T(8,128)(2,1)S(1)} %collective-permute-done.8.climb), channel_id=1, source_target_pairs={{0,1},{1,0},{2,3},{3,2},{4,5},{5,4},{6,7},{7,6},{8,9},{9,8},{10,11... | collective-permute-start | bytes 294920 | tf_op jit(solution)/shard_map/ppermute | solution.py:471

commit v3 on v2

--- a/solution.py
+++ b/solution.py
@@ -10,6 +10,7 @@
 SPACING = 16
 NS_STEPS = 4
 VMEM_LIMIT = 12 << 20
+WHOLE_VMEM = 67043328
 
 
 def padded(array, sides, width):
@@ -202,25 +203,21 @@
     }
 
 
-def vmem_call(kernel, out_shape, scratch=(), flops=0, bytes_accessed=0, name=None):
+def device_call(kernel, operands, out_shape, scratch=(), flops=0, name=None, in_hbm=False, out_hbm=False, limit=VMEM_LIMIT):
     single = not isinstance(out_shape, (list, tuple))
     spec = pl.BlockSpec(memory_space=pltpu.VMEM)
-
-    def call(*operands):
-        return pl.pallas_call(
-            kernel,
-            out_shape=out_shape,
-            in_specs=[spec] * len(operands),
-            out_specs=spec if single else [spec] * len(out_shape),
-            scratch_shapes=list(scratch),
-            cost_estimate=pl.CostEstimate(
-                flops=flops, bytes_accessed=bytes_accessed, transcendentals=0
-            ),
-            compiler_params=pltpu.CompilerParams(vmem_limit_bytes=VMEM_LIMIT),
-            name=name,
-        )(*operands)
-
-    return call
+    hbm = pl.BlockSpec(memory_space=pltpu.HBM)
+    out_spec = hbm if out_hbm else spec
+    return pl.pallas_call(
+        kernel,
+        out_shape=out_shape,
+        in_specs=[hbm if in_hbm else spec] * len(operands),
+        out_specs=out_spec if single else [out_spec] * len(out_shape),
+        scratch_shapes=list(scratch),
+        cost_estimate=pl.CostEstimate(flops=flops, bytes_accessed=1 << 18, transcendentals=0),
+        compiler_params=pltpu.CompilerParams(vmem_limit_bytes=limit),
+        name=name,
+    )(*operands)
 
 
 def split2(value):
@@ -239,24 +236,34 @@
     return lax.dot_general(a, b, (dims, ((), ())), preferred_element_type=jnp.float32)
 
 
-def pack_kernel(rows, pert_ref, inn_ref, prec_ref, owner_ref, slot_ref, count_ref, local_ref, out_ref, tail):
+def pack_kernel(
+    rows, pert, inn, prec, owner, slot, count, local, out_ref, inn_ref, prec_ref, owner_ref, slot_ref, count_ref, local_ref, tail, sems
+):
+    sources = (owner, slot, count, local, inn, prec, pert)
+    targets = (owner_ref, slot_ref, count_ref, local_ref, inn_ref, prec_ref, out_ref.at[0:rows, :])
+    copies = [pltpu.make_async_copy(x, y, sems.at[k]) for k, (x, y) in enumerate(zip(sources, targets))]
+    for copy in copies:
+        copy.start()
+    for copy in copies[:-1]:
+        copy.wait()
     edge = jnp.where(lax.axis_index("tx") == 0, owner_ref.shape[0] - 1, 0)
     slots = owner_ref.shape[2]
-    out_ref[0:rows, :] = pert_ref[...]
-    active = lax.broadcasted_iota(jnp.int32, (1, slots), 1) < jnp.where(edge == 0, count_ref[0, 0], count_ref[0, owner_ref.shape[0] - 1])
-    local = jnp.where(active, local_ref[edge], 0.0)
-    slot = slot_ref[edge]
+    limit = jnp.where(edge == 0, count_ref[0, 0], count_ref[0, owner_ref.shape[0] - 1])
+    active = lax.broadcasted_iota(jnp.int32, (1, slots), 1) < limit
+    local_part = jnp.where(active, local_ref[edge], 0.0)
+    slot_part = slot_ref[edge]
     for k, ref in enumerate((prec_ref, inn_ref)):
         tail[2 * k : 2 * k + 2, :] = ref[...].astype(jnp.float32)
     lists = [
         owner_ref[edge].astype(jnp.float32),
-        (slot // 128).astype(jnp.float32),
-        (slot % 128).astype(jnp.float32),
-    ] + [piece.astype(jnp.float32) for piece in split3(local)]
+        (slot_part // 128).astype(jnp.float32),
+        (slot_part % 128).astype(jnp.float32),
+    ] + [piece.astype(jnp.float32) for piece in split3(local_part)]
     for k, row in enumerate(lists):
         for part in range(2):
             tail[4 + 2 * k + part : 5 + 2 * k + part, :] = row[:, 128 * part : 128 * (part + 1)]
     out_ref[rows : rows + 16, :] = tail[...].astype(jnp.bfloat16)
+    copies[-1].wait()
 
 
 def table_kernel(rows, cols, owner_ref, slot_ref, count_ref, local_ref, other_ref, out_ref):
@@ -302,43 +309,44 @@
         out_ref[pl.ds(place, 16, stride=8), :] = total
 
 
-def gram_kernel(rows, cols, table_ref, b0, b1, b2, b3, b4, b5, mine_ref, rest_ref, turned, scaled):
-    blocks = [b0, b1, b2, b3, b4, b5]
+def gram_blocks(rows, cols, first, blocks, table_ref, turned, plain, scaled):
     per = rows // 128
-    half = cols // 2
-    weights = []
-    products = []
+    products, weights = [], []
     for k, ref in enumerate(blocks):
         tail = ref[rows : rows + 16, :].astype(jnp.float32)
         for part in range(per):
-            hi = k * per + part
+            hi = (first + k) * per + part
             row = table_ref[8 * hi : 8 * hi + 8, :] * tail[part : part + 1, :]
             weights.append(row)
             products.append(row * tail[per + part : per + part + 1, :])
-        turned[:, rows * k : rows * (k + 1)] = ref[0:rows, :].astype(jnp.float32).T.astype(jnp.bfloat16)
-    pads = 128 // 8 - len(weights)
-    stacked = jnp.concatenate(weights + [jnp.zeros((8 * pads, 128), jnp.float32)], axis=0)
-    columns = stacked.T
-    projected = jnp.zeros((16, 128), jnp.float32)
-    for k, ref in enumerate(blocks):
-        wide = jnp.concatenate(products[k * per : (k + 1) * per], axis=1)
-        pieces = jnp.concatenate([p.astype(jnp.float32) for p in split2(wide)], axis=0)
-        projected = projected + dot(pieces.astype(jnp.bfloat16), ref[0:rows, :])
-    projected = projected[0:8] + projected[8:16]
+        block = ref[0:rows, :]
+        plain[rows * k : rows * (k + 1), :] = block
+        turned[:, rows * k : rows * (k + 1)] = block.astype(jnp.float32).T
+    weight = jnp.concatenate(weights, axis=1)
+    high, low = split2(jnp.concatenate(products, axis=1))
     for position in range(cols):
-        for k, ref in enumerate(blocks):
-            for part in range(per):
-                hi = k * per + part
-                values = ref[128 * part : 128 * (part + 1), :].astype(jnp.float32)
-                high, low = split2(values * columns[:, 8 * hi + position : 8 * hi + position + 1])
-                scaled[128 * hi : 128 * (hi + 1), 0:128] = high
-                scaled[128 * hi : 128 * (hi + 1), 128:256] = low
-        both = dot(turned[...], scaled[...])
-        target = mine_ref if position < half else rest_ref
-        at = 128 * (position % half)
-        target[at : at + 128, :] = both[:, 0:128] + both[:, 128:256]
-    mine_ref[128 * half : 128 * half + 8, :] = projected
-    rest_ref[128 * half : 128 * half + 8, :] = jnp.concatenate(
+        at = 128 * position
+        scaled[at : at + 128, :] = (turned[...] * weight[position : position + 1, :]).astype(jnp.bfloat16)
+    at = 128 * cols
+    scaled[at : at + 16, :] = jnp.concatenate(
+        [high.astype(jnp.float32), low.astype(jnp.float32)], axis=0
+    ).astype(jnp.bfloat16)
+    return dot(scaled[...], plain[...])
+
+
+def gram_near_kernel(rows, cols, table_ref, b0, b1, b2, b3, out_ref, turned, plain, scaled):
+    out_ref[...] = gram_blocks(rows, cols, 0, [b0, b1, b2, b3], table_ref, turned, plain, scaled)
+
+
+def gram_far_kernel(rows, cols, table_ref, near_ref, b4, b5, mine_ref, rest_ref, turned, plain, scaled):
+    half = cols // 2
+    total = near_ref[...] + gram_blocks(rows, cols, 4, [b4, b5], table_ref, turned, plain, scaled)
+    edge = 128 * half
+    projected = total[2 * edge : 2 * edge + 8] + total[2 * edge + 8 : 2 * edge + 16]
+    mine_ref[0:edge, :] = total[0:edge]
+    rest_ref[0:edge, :] = total[edge : 2 * edge]
+    mine_ref[edge : edge + 8, :] = projected
+    rest_ref[edge : edge + 8, :] = jnp.concatenate(
         [projected[half : 2 * half], jnp.zeros((8 - half, 128), jnp.float32)], axis=0
     )
 
@@ -356,7 +364,8 @@
 
 def product(a, b):
     (a_high, a_low), (b_high, b_low) = a, b
-    return dot(a_high, b_high) + (dot(a_high, b_low) + dot(a_low, b_high))
+    left = jnp.concatenate([a_high, a_high, a_low], axis=1)
+    return dot(left, jnp.concatenate([b_high, b_low, b_high], axis=0))
 
 
 def solve_kernel(half, sum_ref, got_ref, out_ref):
@@ -411,54 +420,87 @@
         out_ref[size * k : size * (k + 1), :] = transform.astype(jnp.bfloat16)
 
 
-def apply_kernel(cols, members_ref, own, pair, climb, descend, pair_climb, pair_descend, out_ref, table):
+def upper(place, step):
+    span = SPACING // 2
+    return (step + (span + 0.5 if place % 2 == 0 else 0.5)) / (2 * span)
+
+
+def near_kernel(cols, members_ref, own, pair, part_ref, pert_ref, table):
+    half = cols // 2
+    first = lax.rem(lax.axis_index("lev"), 2) == 0
+    for j in range(half):
+        rows = pl.ds(128 * j, 128)
+        a, b = own[rows, :], pair[rows, :]
+        table[:, 128 * j : 128 * (j + 1)] = jnp.where(first, a, b)
+        table[:, 128 * (j + half) : 128 * (j + half + 1)] = jnp.where(first, b, a)
+    levels, width_x, width_y, size = members_ref.shape
+    span = SPACING // 2
+    shape = (levels, span, span, size)
+    rows = levels * span * span
+    step_x = lax.broadcasted_iota(jnp.int32, shape, 1).astype(jnp.float32)
+    step_y = lax.broadcasted_iota(jnp.int32, shape, 2).astype(jnp.float32)
+    for patch_x in range(width_x // span):
+        states = members_ref[:, patch_x * span : (patch_x + 1) * span, :, :].astype(jnp.float32)
+        mean = jnp.sum(states, axis=3, keepdims=True) * (1.0 / size)
+        moved = states - mean
+        column = (patch_x + 1) // 2
+        up_x = upper(patch_x, step_x)
+        for patch_y in range(2):
+            inside = slice(patch_y * span, (patch_y + 1) * span)
+            left = moved[:, :, inside, :].reshape(rows, size).astype(jnp.bfloat16)
+            pert_ref[patch_x, patch_y] = left
+            both = dot(left, table[:, 128 * column : 128 * (column + 2)])
+            mix = (1.0 - up_x) * both[:, 0:128].reshape(shape) + up_x * both[:, 128:256].reshape(shape)
+            up_y = upper(patch_y, step_y)
+            share = up_y if patch_y == 0 else 1.0 - up_y
+            part_ref[patch_x, patch_y] = (mean[:, :, inside, :] + share * mix).reshape(rows, size)
+
+
+def far_kernel(cols, part_ref, pert_ref, own, pair, climb, descend, pair_climb, pair_descend, out_hbm, table, staged, sems):
     half = cols // 2
     tile_y = lax.axis_index("ty")
-    tiles_y = lax.axis_size("ty")
     first = lax.rem(lax.axis_index("lev"), 2) == 0
-    at_start, at_end = tile_y == 0, tile_y == tiles_y - 1
+    at_start, at_end = tile_y == 0, tile_y == lax.axis_size("ty") - 1
     for j in range(half):
         rows = pl.ds(128 * j, 128)
         a, b = own[rows, :], pair[rows, :]
         low, high = jnp.where(first, a, b), jnp.where(first, b, a)
         up, down = climb[rows, :], descend[rows, :]
         pair_up, pair_down = pair_climb[rows, :], pair_descend[rows, :]
-        before_low = jnp.where(at_start, low, jnp.where(first, up, pair_up))
-        before_high = jnp.where(at_start, high, jnp.where(first, pair_down, down))
-        after_low = jnp.where(at_end, low, jnp.where(first, down, pair_down))
-        after_high = jnp.where(at_end, high, jnp.where(first, pair_up, up))
-        for z, (x, y) in enumerate([(before_low, before_high), (low, high), (after_low, after_high)]):
+        before = (
+            jnp.where(at_start, low, jnp.where(first, up, pair_up)),
+            jnp.where(at_start, high, jnp.where(first, pair_down, down)),
+        )
+        after = (
+            jnp.where(at_end, low, jnp.where(first, down, pair_down)),
+            jnp.where(at_end, high, jnp.where(first, pair_up, up)),
+        )
+        for z, (x, y) in enumerate((before, after)):
             table[z, :, 128 * j : 128 * (j + 1)] = x
             table[z, :, 128 * (j + half) : 128 * (j + half + 1)] = y
-    levels, width_x, width_y, size = members_ref.shape
+    levels, width_x, width_y, size = staged.shape
     span = SPACING // 2
     shape = (levels, span, span, size)
     step_x = lax.broadcasted_iota(jnp.int32, shape, 1).astype(jnp.float32)
     step_y = lax.broadcasted_iota(jnp.int32, shape, 2).astype(jnp.float32)
-
-    def upper(place, step):
-        return (step + (span + 0.5 if place % 2 == 0 else 0.5)) / (2 * span)
-
+    copies = []
     for patch_x in range(width_x // span):
-        states = members_ref[:, patch_x * span : (patch_x + 1) * span, :, :].astype(jnp.float32)
-        mean = jnp.sum(states, axis=3, keepdims=True) * (1.0 / size)
-        moved = states - mean
         column = (patch_x + 1) // 2
         up_x = upper(patch_x, step_x)
         results = []
-        for patch_y in range(width_y // span):
-            picked = moved[:, :, patch_y * span : (patch_y + 1) * span, :]
-            rows = levels * span * span
-            left = picked.reshape(rows, size).astype(jnp.bfloat16)
-            place = (patch_y + 1) // 2
-            near = dot(left, table[place, :, 128 * column : 128 * (column + 2)])
-            far = dot(left, table[place + 1, :, 128 * column : 128 * (column + 2)])
+        for patch_y in range(2):
+            both = dot(pert_ref[patch_x, patch_y], table[patch_y, :, 128 * column : 128 * (column + 2)])
+            mix = (1.0 - up_x) * both[:, 0:128].reshape(shape) + up_x * both[:, 128:256].reshape(shape)
             up_y = upper(patch_y, step_y)
-            near_mix = (1.0 - up_x) * near[:, 0:128].reshape(shape) + up_x * near[:, 128:256].reshape(shape)
-            far_mix = (1.0 - up_x) * far[:, 0:128].reshape(shape) + up_x * far[:, 128:256].reshape(shape)
-            results.append((1.0 - up_y) * near_mix + up_y * far_mix)
-        whole = mean + jnp.concatenate(results, axis=2)
-        out_ref[:, patch_x * span : (patch_x + 1) * span, :, :] = whole.astype(jnp.bfloat16)
+            share = 1.0 - up_y if patch_y == 0 else up_y
+            results.append(part_ref[patch_x, patch_y].reshape(shape) + share * mix)
+        inside = pl.ds(patch_x * span, span)
+        staged[:, inside, :, :] = jnp.concatenate(results, axis=2).astype(jnp.bfloat16)
+        copy = pltpu.make_async_copy(staged.at[:, inside], out_hbm.at[:, inside], sems.at[patch_x])
+        copy.start()
+        copies.append(copy)
+    for copy in copies:
+        copy.wait()
 
 
 def paired_device(
@@ -476,53 +518,100 @@
     half = cols // 2
     shape = jax.ShapeDtypeStruct
     counts = obs_count.reshape(1, -1)
-    packed = vmem_call(
+    lists = (obs_owner, obs_slot, counts, local_weight)
+    scalars = [v.reshape(rows // size, size) for v in (innovation, obs_precision)]
+    packed = device_call(
         functools.partial(pack_kernel, rows),
+        (obs_pert, *scalars, *lists),
         shape((rows + 16, size), bf16),
-        [pltpu.VMEM((16, size), f32)],
+        [pltpu.VMEM(v.shape, v.dtype) for v in scalars]
+        + [
+            pltpu.VMEM(obs_owner.shape, jnp.int32),
+            pltpu.VMEM(obs_slot.shape, jnp.int32),
+            pltpu.SMEM(counts.shape, jnp.int32),
+            pltpu.VMEM(local_weight.shape, f32),
+            pltpu.VMEM((16, size), f32),
+            pltpu.SemaphoreType.DMA((7,)),
+        ],
         name="pack",
-    )(
-        obs_pert,
-        innovation.reshape(rows // size, size),
-        obs_precision.reshape(rows // size, size),
-        obs_owner,
-        obs_slot,
-        counts,
-        local_weight,
+        in_hbm=True,
+        limit=WHOLE_VMEM - 2 * (rows + 16) * size * 2,
     )
     across = send(packed, "across")
     climb, descend = send(packed, "climb"), send(packed, "descend")
     across_climb, across_descend = send(across, "climb"), send(across, "descend")
-    table = vmem_call(
+    table = device_call(
         functools.partial(table_kernel, rows, cols),
+        (*lists, across),
         shape((128, 128), f32),
         flops=6 * 2 * 48 * 256 * 128,
-        bytes_accessed=1 << 17,
         name="table",
-    )(obs_owner, obs_slot, counts, local_weight, across)
-    mine, rest = vmem_call(
-        functools.partial(gram_kernel, rows, cols),
-        [shape((128 * half + 8, size), f32)] * 2,
-        [pltpu.VMEM((size, 6 * rows), bf16), pltpu.VMEM((6 * rows, 2 * size), bf16)],
-        name="gram",
-    )(table, packed, climb, descend, across, across_climb, across_descend)
-    total, half_sum = vmem_call(
+    )
+    tall = size * cols + 16
+    near = device_call(
+        functools.partial(gram_near_kernel, rows, cols),
+        (table, packed, climb, descend, across),
+        shape((tall, size), f32),
+        [
+            pltpu.VMEM((size, 4 * rows), f32),
+            pltpu.VMEM((4 * rows, size), bf16),
+            pltpu.VMEM((tall, 4 * rows), bf16),
+        ],
+        flops=2 * tall * size * 4 * rows,
+        name="gram_near",
+    )
+    mine, rest = device_call(
+        functools.partial(gram_far_kernel, rows, cols),
+        (table, near, across_climb, across_descend),
+        [shape((size * half + 8, size), f32)] * 2,
+        [
+            pltpu.VMEM((size, 2 * rows), f32),
+            pltpu.VMEM((2 * rows, size), bf16),
+            pltpu.VMEM((tall, 2 * rows), bf16),
+        ],
+        flops=2 * tall * size * 2 * rows,
+        name="gram_far",
+    )
+    total, half_sum = device_call(
         functools.partial(join_kernel, half),
-        [shape((128 * half + 8, size), f32), shape((128 * half + 16, size), bf16)],
+        (mine, send(rest, "core")),
+        [shape((size * half + 8, size), f32), shape((size * half + 16, size), bf16)],
         name="join",
-    )(mine, send(rest, "core"))
-    weights = vmem_call(
-        functools.partial(solve_kernel, half), shape((128 * half, size), bf16), name="solve"
-    )(total, send(half_sum, "half"))
+    )
+    weights = device_call(
+        functools.partial(solve_kernel, half),
+        (total, send(half_sum, "half")),
+        shape((size * half, size), bf16),
+        flops=2 * 27 * half * size**3,
+        name="solve",
+    )
     pair = send(weights, "core")
     up, down = send(weights, "climb"), send(weights, "descend")
+    levels, width_x, width_y, _ = members.shape
+    patches = (width_x * 2 // SPACING, 2, levels * SPACING**2 // 4, size)
+    part, pert = device_call(
+        functools.partial(near_kernel, cols),
+        (members, weights, pair),
+        [shape(patches, f32), shape(patches, bf16)],
+        [pltpu.VMEM((size, cols * size), bf16)],
+        flops=2 * levels * width_x * width_y * size * 2 * size,
+        name="apply_near",
+    )
+    up, down, part = lax.optimization_barrier((up, down, part))
     pair_up, pair_down = send(up, "core"), send(down, "core")
-    return vmem_call(
-        functools.partial(apply_kernel, cols),
+    return device_call(
+        functools.partial(far_kernel, cols),
+        (part, pert, weights, pair, up, down, pair_up, pair_down),
         shape(members.shape, bf16),
-        [pltpu.VMEM((3, size, cols * size), bf16)],
-        name="apply",
-    )(members, weights, pair, up, down, pair_up, pair_down)
+        [
+            pltpu.VMEM((2, size, cols * size), bf16),
+            pltpu.VMEM(members.shape, bf16),
+            pltpu.SemaphoreType.DMA((patches[0],)),
+        ],
+        flops=2 * levels * width_x * width_y * size * 2 * size,
+        name="apply_far",
+        out_hbm=True,
+    )
 
 
 def fits_pairs(mesh, members, obs_pert, obs_owner):

time: 32.7 us -> 29.3 us (0.90)
  local copies, waits for them, and re-layouts: 2.92 us -> 0.02 us
  waiting for transfers between devices: 11.2 us -> 9.89 us
  starting transfers between devices: 11.6 us -> 12.2 us
    unnamed x20 -> x12, local copies, waits for them, and re-layouts: 2.92 us -> 0.02 us
    ppermute x12, waiting for transfers between devices: 11.2 us -> 9.89 us  [send(): return lax.ppermute(value, axes, ways[way])]
    ppermute x12, starting transfers between devices: 11.6 us -> 12.2 us  [send(): return lax.ppermute(value, axes, ways[way])]
    pallas_call x6 -> x8, Pallas kernels: 6.59 us -> 6.9 us  [device_call(): pl.pallas_call(kernel, out_shape=out_shape, in_specs=[hbm if in_hbm else...]
  transfers between devices with their start and end apart: 12 -> 12, of which waited for: 8 -> 9; matrix products, arithmetic and copies ran while one was open for 0% -> 0% of each run, Pallas kernels for 1% -> 6%
where the time goes in v3:
time: 29.3 us; the launch traced here: 29.1 us
  starting transfers between devices  12.2 us (42%)
  waiting for transfers between devices  9.89 us (34%)
  Pallas kernels  6.9 us (24%)
    ppermute x12, starting transfers between devices, send(): return lax.ppermute(value, axes, ways[way])  12.2 us
    ppermute x12, waiting for transfers between devices, send(): return lax.ppermute(value, axes, ways[way])  9.89 us
    pallas_call x8, Pallas kernels, device_call(): pl.pallas_call(kernel, out_shape=out_shape, in_specs=[hbm if in_hbm else...  6.9 us
  transfers between devices with their start and end apart: 12, of which 9 were waited for; matrix products, arithmetic and copies ran while one was open for 0% of the time, Pallas kernels for 6%

profile of v3, /device:TPU:0, one launch (start us, length us, event | category | flops | bytes accessed | tf_op | source)
XLA Modules:
  0.0 29.1 jit_solution(12645018864670285944)
XLA Ops:
  0.0 1.7 %pack.1.b0 = bf16[272,128]{1,0:T(8,128)(2,1)} custom-call(bf16[256,128]{1,0:T(8,128)(2,1)} %pert.1, bf16[2,128]{1,0:T(2,128)(2,1)} %bitcast.5, bf16[2,128]{1,0:T(2,128)(2,1)} %bitcast.6, s32[4,1,256]{2,1,0:T(1,128)} %owner_ref.1, s32[4,1,256]{2,1,0:T(1,128)} %slot_ref.1, s32[1,4]{1,0:T(1,128)} %bitcast.3, f32[4,1,256]{2,1,0:T(1,128)} %local_ref.1), custom_call_target="tpu_custom_call" | custom-call | bytes 262144 | tf_op jit(solution)/shard_map/pack/pallas_call | solution.py:211
  1.7 3.1 %collective-permute-start = (bf16[272,128]{1,0:T(8,128)(2,1)}, bf16[272,128]{1,0:T(8,128)(2,1)S(1)}, u32[]{:S(2)}, u32[]{:S(2)}) collective-permute-start(bf16[272,128]{1,0:T(8,128)(2,1)} %pack.1.b0), channel_id=1, source_target_pairs={{0,16},{1,17},{2,18},{3,19},{4,20},{5,21},{6,22},{7,23},{8,24},{9,... | collective-permute-start | bytes 208904 | tf_op jit(solution)/shard_map/ppermute | solution.py:513
  4.8 2.0 %collective-permute-start.1 = (bf16[272,128]{1,0:T(8,128)(2,1)}, bf16[272,128]{1,0:T(8,128)(2,1)S(1)}, u32[]{:S(2)}, u32[]{:S(2)}) collective-permute-start(bf16[272,128]{1,0:T(8,128)(2,1)} %pack.1.b0), channel_id=1, source_target_pairs={{0,4},{1,0},{2,6},{3,2},{4,8},{5,1},{6,10},{7,3},{8,12},{9,5},{10,... | collective-permute-start | bytes 208904 | tf_op jit(solution)/shard_map/ppermute | solution.py:513
  6.8 0.5 %collective-permute-done.other_ref.b3 = bf16[272,128]{1,0:T(8,128)(2,1)S(1)} collective-permute-done((bf16[272,128]{1,0:T(8,128)(2,1)}, bf16[272,128]{1,0:T(8,128)(2,1)S(1)}, u32[]{:S(2)}, u32[]{:S(2)}) %collective-permute-start) | collective-permute-done | bytes 69664 | tf_op jit(solution)/shard_map/ppermute | solution.py:513
  7.3 2.1 %collective-permute-start.3 = (bf16[272,128]{1,0:T(8,128)(2,1)S(1)}, bf16[272,128]{1,0:T(8,128)(2,1)S(1)}, u32[]{:S(2)}, u32[]{:S(2)}) collective-permute-start(bf16[272,128]{1,0:T(8,128)(2,1)S(1)} %collective-permute-done.other_ref.b3), channel_id=1, source_target_pairs={{0,4},{1,0},{2,6},{3,2},{4,8},{5,1},{6,10},{7,3},{8,12},{9,5},{10,... | collective-permute-start | bytes 208904 | tf_op jit(solution)/shard_map/ppermute | solution.py:513
  9.3 0.5 %table.1.table_ref = f32[128,128]{1,0:T(8,128)S(1)} custom-call(s32[4,1,256]{2,1,0:T(1,128)S(1)} %copy-done.2, s32[4,1,256]{2,1,0:T(1,128)S(1)} %copy-done.3, s32[1,4]{1,0:T(1,128)S(1)} %bitcast.4, f32[4,1,256]{2,1,0:T(1,128)S(1)} %copy-done.4, bf16[272,128]{1,0:T(8,128)(2,1)S(1)} %collective-permute-done.other_ref.b3), custom_call_target="tpu_custom_call" | custom-call | flops 18874368 | bytes 262144 | tf_op jit(solution)/shard_map/table/pallas_call | solution.py:211
  9.8 0.1 collective-permute-done.2.b2
  9.9 0.6 %gram_near.1.near_ref = f32[784,128]{1,0:T(8,128)S(1)} custom-call(f32[128,128]{1,0:T(8,128)S(1)} %table.1.table_ref, bf16[272,128]{1,0:T(8,128)(2,1)S(1)} %copy-done.1, bf16[272,128]{1,0:T(8,128)(2,1)S(1)} %collective-permute-done.1.b1, bf16[272,128]{1,0:T(8,128)(2,1)S(1)} %collective-permute-done.2.b2, bf16[272,128]{1,0:T(8,128)(2,1)S(1)} %collective-permute-done.other_ref.b3), custom_call_target="tpu_custom_call" | custom-call | flops 205520896 | bytes 262144 | tf_op jit(solution)/shard_map/gram_near/pallas_call | solution.py:211
  10.5 1.3 %collective-permute-done.4.b5 = bf16[272,128]{1,0:T(8,128)(2,1)S(1)} collective-permute-done((bf16[272,128]{1,0:T(8,128)(2,1)S(1)}, bf16[272,128]{1,0:T(8,128)(2,1)S(1)}, u32[]{:S(2)}, u32[]{:S(2)}) %collective-permute-start.4) | collective-permute-done | bytes 69664 | tf_op jit(solution)/shard_map/ppermute | solution.py:513
  11.8 0.4 %gram_far.1 = (f32[392,128]{1,0:T(8,128)S(1)}, f32[392,128]{1,0:T(8,128)S(1)}) custom-call(f32[128,128]{1,0:T(8,128)S(1)} %table.1.table_ref, f32[784,128]{1,0:T(8,128)S(1)} %gram_near.1.near_ref, bf16[272,128]{1,0:T(8,128)(2,1)S(1)} %collective-permute-done.3.b4, bf16[272,128]{1,0:T(8,128)(2,1)S(1)} %collective-permute-done.4.b5), custom_call_target="tpu_custom_call" | custom-call | flops 102760448 | bytes 262144 | tf_op jit(solution)/shard_map/gram_far/pallas_call | solution.py:211
  12.3 0.1 collective-permute-start.5
  12.3 1.4 %collective-permute-done.5.got_ref = f32[392,128]{1,0:T(8,128)S(1)} collective-permute-done((f32[392,128]{1,0:T(8,128)S(1)}, f32[392,128]{1,0:T(8,128)S(1)}, u32[]{:S(2)}, u32[]{:S(2)}) %collective-permute-start.5) | collective-permute-done | bytes 200736 | tf_op jit(solution)/shard_map/ppermute | solution.py:513
  13.8 1.8 %collective-permute-start.6 = (bf16[400,128]{1,0:T(8,128)(2,1)S(1)}, bf16[400,128]{1,0:T(8,128)(2,1)S(1)}, u32[]{:S(2)}, u32[]{:S(2)}) collective-permute-start(bf16[400,128]{1,0:T(8,128)(2,1)S(1)} %get-tuple-element.17), channel_id=1, source_target_pairs={{0,2},{1,3},{2,0},{3,1},{4,6},{5,7},{6,4},{7,5},{8,10},{9,11},{10,... | collective-permute-start | bytes 307208 | tf_op jit(solution)/shard_map/ppermute | solution.py:513
  15.6 3.2 %collective-permute-done.6.got_ref = bf16[400,128]{1,0:T(8,128)(2,1)S(1)} collective-permute-done((bf16[400,128]{1,0:T(8,128)(2,1)S(1)}, bf16[400,128]{1,0:T(8,128)(2,1)S(1)}, u32[]{:S(2)}, u32[]{:S(2)}) %collective-permute-start.6) | collective-permute-done | bytes 102432 | tf_op jit(solution)/shard_map/ppermute | solution.py:513
  18.8 1.9 %solve.1.own = bf16[384,128]{1,0:T(8,128)(2,1)S(1)} custom-call(f32[392,128]{1,0:T(8,128)S(1)} %get-tuple-element.16.sum_ref, bf16[400,128]{1,0:T(8,128)(2,1)S(1)} %collective-permute-done.6.got_ref), custom_call_target="tpu_custom_call" | custom-call | flops 339738624 | bytes 262144 | tf_op jit(solution)/shard_map/solve/pallas_call | solution.py:211
  20.8 0.5 %collective-permute-start.8 = (bf16[384,128]{1,0:T(8,128)(2,1)S(1)}, bf16[384,128]{1,0:T(8,128)(2,1)S(1)}, u32[]{:S(2)}, u32[]{:S(2)}) collective-permute-start(bf16[384,128]{1,0:T(8,128)(2,1)S(1)} %solve.1.own), channel_id=1, source_target_pairs={{4,0},{0,1},{6,2},{2,3},{8,4},{1,5},{10,6},{3,7},{12,8},{5,9},{14,... | collective-permute-start | bytes 294920 | tf_op jit(solution)/shard_map/ppermute | solution.py:513
  21.3 1.6 %collective-permute-start.7 = (bf16[384,128]{1,0:T(8,128)(2,1)S(1)}, bf16[384,128]{1,0:T(8,128)(2,1)S(1)}, u32[]{:S(2)}, u32[]{:S(2)}) collective-permute-start(bf16[384,128]{1,0:T(8,128)(2,1)S(1)} %solve.1.own), channel_id=1, source_target_pairs={{0,4},{1,0},{2,6},{3,2},{4,8},{5,1},{6,10},{7,3},{8,12},{9,5},{10,... | collective-permute-start | bytes 294920 | tf_op jit(solution)/shard_map/ppermute | solution.py:513
  22.9 0.6 %apply_near.1 = (f32[8,2,128,128]{3,2,1,0:T(8,128)S(1)}, bf16[8,2,128,128]{3,2,1,0:T(8,128)(2,1)S(1)}) custom-call(bf16[2,64,16,128]{3,2,1,0:T(8,128)(2,1)S(1)} %copy-done, bf16[384,128]{1,0:T(8,128)(2,1)S(1)} %solve.1.own, bf16[384,128]{1,0:T(8,128)(2,1)S(1)} %collective-permute-done.9.pair), custom_call_target="tpu_custom_call" | custom-call | flops 134217728 | bytes 262144 | tf_op jit(solution)/shard_map/apply_near/pallas_call | solution.py:211
  23.4 2.0 %collective-permute-done.8.descend = bf16[384,128]{1,0:T(8,128)(2,1)S(1)} collective-permute-done((bf16[384,128]{1,0:T(8,128)(2,1)S(1)}, bf16[384,128]{1,0:T(8,128)(2,1)S(1)}, u32[]{:S(2)}, u32[]{:S(2)}) %collective-permute-start.8) | collective-permute-done | bytes 98336 | tf_op jit(solution)/shard_map/ppermute | solution.py:513
  25.5 0.1 collective-permute-done.7.climb
  25.6 1.0 %collective-permute-start.10 = (bf16[384,128]{1,0:T(8,128)(2,1)S(1)}, bf16[384,128]{1,0:T(8,128)(2,1)S(1)}, u32[]{:S(2)}, u32[]{:S(2)}) collective-permute-start(bf16[384,128]{1,0:T(8,128)(2,1)S(1)} %collective-permute-done.7.climb), channel_id=1, source_target_pairs={{0,1},{1,0},{2,3},{3,2},{4,5},{5,4},{6,7},{7,6},{8,9},{9,8},{10,11... | collective-permute-start | bytes 294920 | tf_op jit(solution)/shard_map/ppermute | solution.py:513
  26.6 0.9 %collective-permute-done.10.pair_climb = bf16[384,128]{1,0:T(8,128)(2,1)S(1)} collective-permute-done((bf16[384,128]{1,0:T(8,128)(2,1)S(1)}, bf16[384,128]{1,0:T(8,128)(2,1)S(1)}, u32[]{:S(2)}, u32[]{:S(2)}) %collective-permute-start.10) | collective-permute-done | bytes 98336 | tf_op jit(solution)/shard_map/ppermute | solution.py:513
  27.5 0.4 %collective-permute-done.11.pair_descend = bf16[384,128]{1,0:T(8,128)(2,1)S(1)} collective-permute-done((bf16[384,128]{1,0:T(8,128)(2,1)S(1)}, bf16[384,128]{1,0:T(8,128)(2,1)S(1)}, u32[]{:S(2)}, u32[]{:S(2)}) %collective-permute-start.11) | collective-permute-done | bytes 98336 | tf_op jit(solution)/shard_map/ppermute | solution.py:513
  27.9 1.2 %apply_far.1 = bf16[2,64,16,128]{3,2,1,0:T(8,128)(2,1)} custom-call(f32[8,2,128,128]{3,2,1,0:T(8,128)S(1)} %get-tuple-element.19.part_ref, bf16[8,2,128,128]{3,2,1,0:T(8,128)(2,1)S(1)} %get-tuple-element.20.pert_ref, bf16[384,128]{1,0:T(8,128)(2,1)S(1)} %solve.1.own, bf16[384,128]{1,0:T(8,128)(2,1)S(1)} %collective-permute-done.9.pair, ...), custom_call_target="tpu_custom_call" | custom-call | flops 134217728 | bytes 262144 | tf_op jit(solution)/shard_map/apply_far/pallas_call | solution.py:211
  (20 shorter events, 0.2 us)
Async XLA Ops:
  0.0 9.3 %copy-start.2 = (s32[4,1,256]{2,1,0:T(1,128)S(1)}, s32[4,1,256]{2,1,0:T(1,128)}, u32[]{:S(2)}) copy-start(s32[4,1,256]{2,1,0:T(1,128)} %owner_ref.1) | copy-start | bytes 12292
  0.0 9.3 %copy-start.3 = (s32[4,1,256]{2,1,0:T(1,128)S(1)}, s32[4,1,256]{2,1,0:T(1,128)}, u32[]{:S(2)}) copy-start(s32[4,1,256]{2,1,0:T(1,128)} %slot_ref.1) | copy-start | bytes 12292
  0.0 9.3 %copy-start.4 = (f32[4,1,256]{2,1,0:T(1,128)S(1)}, f32[4,1,256]{2,1,0:T(1,128)}, u32[]{:S(2)}) copy-start(f32[4,1,256]{2,1,0:T(1,128)} %local_ref.1) | copy-start | bytes 12292
  0.0 9.3 %copy-start.5 = (s32[4,1]{0,1:T(1,128)S(1)}, s32[4,1]{0,1:T(1,128)}, u32[]{:S(2)}) copy-start(s32[4,1]{0,1:T(1,128)} %param.14) | copy-start | bytes 52
  1.7 8.2 %copy-start.1 = (bf16[272,128]{1,0:T(8,128)(2,1)S(1)}, bf16[272,128]{1,0:T(8,128)(2,1)}, u32[]{:S(2)}) copy-start(bf16[272,128]{1,0:T(8,128)(2,1)} %pack.1.b0) | copy-start | bytes 208900
  1.7 5.6 %collective-permute-start = (bf16[272,128]{1,0:T(8,128)(2,1)}, bf16[272,128]{1,0:T(8,128)(2,1)S(1)}, u32[]{:S(2)}, u32[]{:S(2)}) collective-permute-start(bf16[272,128]{1,0:T(8,128)(2,1)} %pack.1.b0), channel_id=1, source_target_pairs={{0,16},{1,17},{2,18},{3,19},{4,20},{5,21},{6,22},{7,23},{8,24},{9,... | collective-permute-start | bytes 208904 | tf_op jit(solution)/shard_map/ppermute | solution.py:513
  4.8 5.1 %collective-permute-start.2 = (bf16[272,128]{1,0:T(8,128)(2,1)}, bf16[272,128]{1,0:T(8,128)(2,1)S(1)}, u32[]{:S(2)}, u32[]{:S(2)}) collective-permute-start(bf16[272,128]{1,0:T(8,128)(2,1)} %pack.1.b0), channel_id=1, source_target_pairs={{4,0},{0,1},{6,2},{2,3},{8,4},{1,5},{10,6},{3,7},{12,8},{5,9},{14,... | collective-permute-start | bytes 208904 | tf_op jit(solution)/shard_map/ppermute | solution.py:513
  4.8 5.1 %collective-permute-start.1 = (bf16[272,128]{1,0:T(8,128)(2,1)}, bf16[272,128]{1,0:T(8,128)(2,1)S(1)}, u32[]{:S(2)}, u32[]{:S(2)}) collective-permute-start(bf16[272,128]{1,0:T(8,128)(2,1)} %pack.1.b0), channel_id=1, source_target_pairs={{0,4},{1,0},{2,6},{3,2},{4,8},{5,1},{6,10},{7,3},{8,12},{9,5},{10,... | collective-permute-start | bytes 208904 | tf_op jit(solution)/shard_map/ppermute | solution.py:513
  7.3 4.6 %collective-permute-start.4 = (bf16[272,128]{1,0:T(8,128)(2,1)S(1)}, bf16[272,128]{1,0:T(8,128)(2,1)S(1)}, u32[]{:S(2)}, u32[]{:S(2)}) collective-permute-start(bf16[272,128]{1,0:T(8,128)(2,1)S(1)} %collective-permute-done.other_ref.b3), channel_id=1, source_target_pairs={{4,0},{0,1},{6,2},{2,3},{8,4},{1,5},{10,6},{3,7},{12,8},{5,9},{14,... | collective-permute-start | bytes 208904 | tf_op jit(solution)/shard_map/ppermute | solution.py:513
  7.3 4.6 %collective-permute-start.3 = (bf16[272,128]{1,0:T(8,128)(2,1)S(1)}, bf16[272,128]{1,0:T(8,128)(2,1)S(1)}, u32[]{:S(2)}, u32[]{:S(2)}) collective-permute-start(bf16[272,128]{1,0:T(8,128)(2,1)S(1)} %collective-permute-done.other_ref.b3), channel_id=1, source_target_pairs={{0,4},{1,0},{2,6},{3,2},{4,8},{5,1},{6,10},{7,3},{8,12},{9,5},{10,... | collective-permute-start | bytes 208904 | tf_op jit(solution)/shard_map/ppermute | solution.py:513
  12.3 1.5 %collective-permute-start.5 = (f32[392,128]{1,0:T(8,128)S(1)}, f32[392,128]{1,0:T(8,128)S(1)}, u32[]{:S(2)}, u32[]{:S(2)}) collective-permute-start(f32[392,128]{1,0:T(8,128)S(1)} %get-tuple-element.15), channel_id=1, source_target_pairs={{0,1},{1,0},{2,3},{3,2},{4,5},{5,4},{6,7},{7,6},{8,9},{9,8},{10,11... | collective-permute-start | bytes 602120 | tf_op jit(solution)/shard_map/ppermute | solution.py:513
  13.8 5.0 %collective-permute-start.6 = (bf16[400,128]{1,0:T(8,128)(2,1)S(1)}, bf16[400,128]{1,0:T(8,128)(2,1)S(1)}, u32[]{:S(2)}, u32[]{:S(2)}) collective-permute-start(bf16[400,128]{1,0:T(8,128)(2,1)S(1)} %get-tuple-element.17), channel_id=1, source_target_pairs={{0,2},{1,3},{2,0},{3,1},{4,6},{5,7},{6,4},{7,5},{8,10},{9,11},{10,... | collective-permute-start | bytes 307208 | tf_op jit(solution)/shard_map/ppermute | solution.py:513
  18.8 4.1 %copy-start = (bf16[2,64,16,128]{3,2,1,0:T(8,128)(2,1)S(1)}, bf16[2,64,16,128]{3,2,1,0:T(8,128)(2,1)}, u32[]{:S(2)}) copy-start(bf16[2,64,16,128]{3,2,1,0:T(8,128)(2,1)} %members_ref.1) | copy-start | bytes 1572868
  20.7 2.1 %collective-permute-start.9 = (bf16[384,128]{1,0:T(8,128)(2,1)S(1)}, bf16[384,128]{1,0:T(8,128)(2,1)S(1)}, u32[]{:S(2)}, u32[]{:S(2)}) collective-permute-start(bf16[384,128]{1,0:T(8,128)(2,1)S(1)} %solve.1.own), channel_id=1, source_target_pairs={{0,1},{1,0},{2,3},{3,2},{4,5},{5,4},{6,7},{7,6},{8,9},{9,8},{10,11... | collective-permute-start | bytes 294920 | tf_op jit(solution)/shard_map/ppermute | solution.py:513
  20.8 4.6 %collective-permute-start.8 = (bf16[384,128]{1,0:T(8,128)(2,1)S(1)}, bf16[384,128]{1,0:T(8,128)(2,1)S(1)}, u32[]{:S(2)}, u32[]{:S(2)}) collective-permute-start(bf16[384,128]{1,0:T(8,128)(2,1)S(1)} %solve.1.own), channel_id=1, source_target_pairs={{4,0},{0,1},{6,2},{2,3},{8,4},{1,5},{10,6},{3,7},{12,8},{5,9},{14,... | collective-permute-start | bytes 294920 | tf_op jit(solution)/shard_map/ppermute | solution.py:513
  21.3 4.2 %collective-permute-start.7 = (bf16[384,128]{1,0:T(8,128)(2,1)S(1)}, bf16[384,128]{1,0:T(8,128)(2,1)S(1)}, u32[]{:S(2)}, u32[]{:S(2)}) collective-permute-start(bf16[384,128]{1,0:T(8,128)(2,1)S(1)} %solve.1.own), channel_id=1, source_target_pairs={{0,4},{1,0},{2,6},{3,2},{4,8},{5,1},{6,10},{7,3},{8,12},{9,5},{10,... | collective-permute-start | bytes 294920 | tf_op jit(solution)/shard_map/ppermute | solution.py:513
  25.6 2.0 %collective-permute-start.10 = (bf16[384,128]{1,0:T(8,128)(2,1)S(1)}, bf16[384,128]{1,0:T(8,128)(2,1)S(1)}, u32[]{:S(2)}, u32[]{:S(2)}) collective-permute-start(bf16[384,128]{1,0:T(8,128)(2,1)S(1)} %collective-permute-done.7.climb), channel_id=1, source_target_pairs={{0,1},{1,0},{2,3},{3,2},{4,5},{5,4},{6,7},{7,6},{8,9},{9,8},{10,11... | collective-permute-start | bytes 294920 | tf_op jit(solution)/shard_map/ppermute | solution.py:513
  26.6 1.3 %collective-permute-start.11 = (bf16[384,128]{1,0:T(8,128)(2,1)S(1)}, bf16[384,128]{1,0:T(8,128)(2,1)S(1)}, u32[]{:S(2)}, u32[]{:S(2)}) collective-permute-start(bf16[384,128]{1,0:T(8,128)(2,1)S(1)} %collective-permute-done.8.descend), channel_id=1, source_target_pairs={{0,1},{1,0},{2,3},{3,2},{4,5},{5,4},{6,7},{7,6},{8,9},{9,8},{10,11... | collective-permute-start | bytes 294920 | tf_op jit(solution)/shard_map/ppermute | solution.py:513

commit v4 on v3

--- a/solution.py
+++ b/solution.py
@@ -522,7 +522,7 @@
     scalars = [v.reshape(rows // size, size) for v in (innovation, obs_precision)]
     packed = device_call(
         functools.partial(pack_kernel, rows),
-        (obs_pert, *scalars, *lists),
+        tuple(pltpu.with_memory_space_constraint(v, pltpu.HBM) for v in (obs_pert, *scalars, *lists)),
         shape((rows + 16, size), bf16),
         [pltpu.VMEM(v.shape, v.dtype) for v in scalars]
         + [
@@ -535,7 +535,6 @@
         ],
         name="pack",
         in_hbm=True,
-        limit=WHOLE_VMEM - 2 * (rows + 16) * size * 2,
     )
     across = send(packed, "across")
     climb, descend = send(packed, "climb"), send(packed, "descend")

time: 29.3 us -> 28.4 us (0.969)
  Pallas kernels: 6.9 us -> 6.28 us
    pallas_call x8, Pallas kernels: 6.9 us -> 6.28 us  [device_call(): pl.pallas_call(kernel, out_shape=out_shape, in_specs=[hbm if in_hbm else...]
where the time goes in v4:
time: 28.4 us; the launch traced here: 28.3 us
  starting transfers between devices  12.2 us (43%)
  waiting for transfers between devices  9.67 us (34%)
  Pallas kernels  6.28 us (22%)
    ppermute x12, starting transfers between devices, send(): return lax.ppermute(value, axes, ways[way])  12.2 us
    ppermute x12, waiting for transfers between devices, send(): return lax.ppermute(value, axes, ways[way])  9.67 us
    pallas_call x8, Pallas kernels, device_call(): pl.pallas_call(kernel, out_shape=out_shape, in_specs=[hbm if in_hbm else...  6.28 us
  transfers between devices with their start and end apart: 12, of which 9 were waited for; matrix products, arithmetic and copies ran while one was open for 0% of the time, Pallas kernels for 6%

profile of v4, /device:TPU:0, one launch (start us, length us, event | category | flops | bytes accessed | tf_op | source)
XLA Modules:
  0.0 28.3 jit_solution(16923889524258314776)
XLA Ops:
  0.0 1.0 %pack.1.b0 = bf16[272,128]{1,0:T(8,128)(2,1)S(1)} custom-call(bf16[256,128]{1,0:T(8,128)(2,1)} %pert.1, bf16[2,128]{1,0:T(2,128)(2,1)} %bitcast.5, bf16[2,128]{1,0:T(2,128)(2,1)} %bitcast.6, s32[4,1,256]{2,1,0:T(1,128)} %owner_ref.1, s32[4,1,256]{2,1,0:T(1,128)} %slot_ref.1, s32[1,4]{1,0:T(1,128)} %bitcast.3, f32[4,1,256]{2,1,0:T(1,128)} %local_ref.1), custom_call_target="tpu_custom_call" | custom-call | bytes 262144 | tf_op jit(solution)/shard_map/pack/pallas_call | solution.py:211
  1.0 3.1 %collective-permute-start = (bf16[272,128]{1,0:T(8,128)(2,1)S(1)}, bf16[272,128]{1,0:T(8,128)(2,1)S(1)}, u32[]{:S(2)}, u32[]{:S(2)}) collective-permute-start(bf16[272,128]{1,0:T(8,128)(2,1)S(1)} %pack.1.b0), channel_id=1, source_target_pairs={{0,16},{1,17},{2,18},{3,19},{4,20},{5,21},{6,22},{7,23},{8,24},{9,... | collective-permute-start | bytes 208904 | tf_op jit(solution)/shard_map/ppermute | solution.py:513
  4.1 2.0 %collective-permute-start.1 = (bf16[272,128]{1,0:T(8,128)(2,1)S(1)}, bf16[272,128]{1,0:T(8,128)(2,1)S(1)}, u32[]{:S(2)}, u32[]{:S(2)}) collective-permute-start(bf16[272,128]{1,0:T(8,128)(2,1)S(1)} %pack.1.b0), channel_id=1, source_target_pairs={{0,4},{1,0},{2,6},{3,2},{4,8},{5,1},{6,10},{7,3},{8,12},{9,5},{10,... | collective-permute-start | bytes 208904 | tf_op jit(solution)/shard_map/ppermute | solution.py:513
  6.1 0.3 collective-permute-done.other_ref.b3
  6.4 2.1 %collective-permute-start.3 = (bf16[272,128]{1,0:T(8,128)(2,1)S(1)}, bf16[272,128]{1,0:T(8,128)(2,1)S(1)}, u32[]{:S(2)}, u32[]{:S(2)}) collective-permute-start(bf16[272,128]{1,0:T(8,128)(2,1)S(1)} %collective-permute-done.other_ref.b3), channel_id=1, source_target_pairs={{0,4},{1,0},{2,6},{3,2},{4,8},{5,1},{6,10},{7,3},{8,12},{9,5},{10,... | collective-permute-start | bytes 208904 | tf_op jit(solution)/shard_map/ppermute | solution.py:513
  8.5 0.5 %table.1.table_ref = f32[128,128]{1,0:T(8,128)S(1)} custom-call(s32[4,1,256]{2,1,0:T(1,128)S(1)} %copy-done.1, s32[4,1,256]{2,1,0:T(1,128)S(1)} %copy-done.2, s32[1,4]{1,0:T(1,128)S(1)} %bitcast.4, f32[4,1,256]{2,1,0:T(1,128)S(1)} %copy-done.3, bf16[272,128]{1,0:T(8,128)(2,1)S(1)} %collective-permute-done.other_ref.b3), custom_call_target="tpu_custom_call" | custom-call | flops 18874368 | bytes 262144 | tf_op jit(solution)/shard_map/table/pallas_call | solution.py:211
  9.0 0.1 collective-permute-done.2.b2
  9.1 0.6 %gram_near.1.near_ref = f32[784,128]{1,0:T(8,128)S(1)} custom-call(f32[128,128]{1,0:T(8,128)S(1)} %table.1.table_ref, bf16[272,128]{1,0:T(8,128)(2,1)S(1)} %pack.1.b0, bf16[272,128]{1,0:T(8,128)(2,1)S(1)} %collective-permute-done.1.b1, bf16[272,128]{1,0:T(8,128)(2,1)S(1)} %collective-permute-done.2.b2, bf16[272,128]{1,0:T(8,128)(2,1)S(1)} %collective-permute-done.other_ref.b3), custom_call_target="tpu_custom_call" | custom-call | flops 205520896 | bytes 262144 | tf_op jit(solution)/shard_map/gram_near/pallas_call | solution.py:211
  9.7 1.3 %collective-permute-done.4.b5 = bf16[272,128]{1,0:T(8,128)(2,1)S(1)} collective-permute-done((bf16[272,128]{1,0:T(8,128)(2,1)S(1)}, bf16[272,128]{1,0:T(8,128)(2,1)S(1)}, u32[]{:S(2)}, u32[]{:S(2)}) %collective-permute-start.4) | collective-permute-done | bytes 69664 | tf_op jit(solution)/shard_map/ppermute | solution.py:513
  11.0 0.4 %gram_far.1 = (f32[392,128]{1,0:T(8,128)S(1)}, f32[392,128]{1,0:T(8,128)S(1)}) custom-call(f32[128,128]{1,0:T(8,128)S(1)} %table.1.table_ref, f32[784,128]{1,0:T(8,128)S(1)} %gram_near.1.near_ref, bf16[272,128]{1,0:T(8,128)(2,1)S(1)} %collective-permute-done.3.b4, bf16[272,128]{1,0:T(8,128)(2,1)S(1)} %collective-permute-done.4.b5), custom_call_target="tpu_custom_call" | custom-call | flops 102760448 | bytes 262144 | tf_op jit(solution)/shard_map/gram_far/pallas_call | solution.py:211
  11.5 1.4 %collective-permute-done.5.got_ref = f32[392,128]{1,0:T(8,128)S(1)} collective-permute-done((f32[392,128]{1,0:T(8,128)S(1)}, f32[392,128]{1,0:T(8,128)S(1)}, u32[]{:S(2)}, u32[]{:S(2)}) %collective-permute-start.5) | collective-permute-done | bytes 200736 | tf_op jit(solution)/shard_map/ppermute | solution.py:513
  13.0 1.8 %collective-permute-start.6 = (bf16[400,128]{1,0:T(8,128)(2,1)S(1)}, bf16[400,128]{1,0:T(8,128)(2,1)S(1)}, u32[]{:S(2)}, u32[]{:S(2)}) collective-permute-start(bf16[400,128]{1,0:T(8,128)(2,1)S(1)} %get-tuple-element.17), channel_id=1, source_target_pairs={{0,2},{1,3},{2,0},{3,1},{4,6},{5,7},{6,4},{7,5},{8,10},{9,11},{10,... | collective-permute-start | bytes 307208 | tf_op jit(solution)/shard_map/ppermute | solution.py:513
  14.8 3.2 %collective-permute-done.6.got_ref = bf16[400,128]{1,0:T(8,128)(2,1)S(1)} collective-permute-done((bf16[400,128]{1,0:T(8,128)(2,1)S(1)}, bf16[400,128]{1,0:T(8,128)(2,1)S(1)}, u32[]{:S(2)}, u32[]{:S(2)}) %collective-permute-start.6) | collective-permute-done | bytes 102432 | tf_op jit(solution)/shard_map/ppermute | solution.py:513
  17.9 1.9 %solve.1.own = bf16[384,128]{1,0:T(8,128)(2,1)S(1)} custom-call(f32[392,128]{1,0:T(8,128)S(1)} %get-tuple-element.16.sum_ref, bf16[400,128]{1,0:T(8,128)(2,1)S(1)} %collective-permute-done.6.got_ref), custom_call_target="tpu_custom_call" | custom-call | flops 339738624 | bytes 262144 | tf_op jit(solution)/shard_map/solve/pallas_call | solution.py:211
  19.9 0.1 collective-permute-start.9
  20.0 0.5 %collective-permute-start.8 = (bf16[384,128]{1,0:T(8,128)(2,1)S(1)}, bf16[384,128]{1,0:T(8,128)(2,1)S(1)}, u32[]{:S(2)}, u32[]{:S(2)}) collective-permute-start(bf16[384,128]{1,0:T(8,128)(2,1)S(1)} %solve.1.own), channel_id=1, source_target_pairs={{4,0},{0,1},{6,2},{2,3},{8,4},{1,5},{10,6},{3,7},{12,8},{5,9},{14,... | collective-permute-start | bytes 294920 | tf_op jit(solution)/shard_map/ppermute | solution.py:513
  20.5 1.6 %collective-permute-start.7 = (bf16[384,128]{1,0:T(8,128)(2,1)S(1)}, bf16[384,128]{1,0:T(8,128)(2,1)S(1)}, u32[]{:S(2)}, u32[]{:S(2)}) collective-permute-start(bf16[384,128]{1,0:T(8,128)(2,1)S(1)} %solve.1.own), channel_id=1, source_target_pairs={{0,4},{1,0},{2,6},{3,2},{4,8},{5,1},{6,10},{7,3},{8,12},{9,5},{10,... | collective-permute-start | bytes 294920 | tf_op jit(solution)/shard_map/ppermute | solution.py:513
  22.0 0.6 %apply_near.1 = (f32[8,2,128,128]{3,2,1,0:T(8,128)S(1)}, bf16[8,2,128,128]{3,2,1,0:T(8,128)(2,1)S(1)}) custom-call(bf16[2,64,16,128]{3,2,1,0:T(8,128)(2,1)S(1)} %copy-done, bf16[384,128]{1,0:T(8,128)(2,1)S(1)} %solve.1.own, bf16[384,128]{1,0:T(8,128)(2,1)S(1)} %collective-permute-done.9.pair), custom_call_target="tpu_custom_call" | custom-call | flops 134217728 | bytes 262144 | tf_op jit(solution)/shard_map/apply_near/pallas_call | solution.py:211
  22.6 2.0 %collective-permute-done.8.descend = bf16[384,128]{1,0:T(8,128)(2,1)S(1)} collective-permute-done((bf16[384,128]{1,0:T(8,128)(2,1)S(1)}, bf16[384,128]{1,0:T(8,128)(2,1)S(1)}, u32[]{:S(2)}, u32[]{:S(2)}) %collective-permute-start.8) | collective-permute-done | bytes 98336 | tf_op jit(solution)/shard_map/ppermute | solution.py:513
  24.6 0.1 collective-permute-done.7.climb
  24.7 1.0 %collective-permute-start.10 = (bf16[384,128]{1,0:T(8,128)(2,1)S(1)}, bf16[384,128]{1,0:T(8,128)(2,1)S(1)}, u32[]{:S(2)}, u32[]{:S(2)}) collective-permute-start(bf16[384,128]{1,0:T(8,128)(2,1)S(1)} %collective-permute-done.7.climb), channel_id=1, source_target_pairs={{0,1},{1,0},{2,3},{3,2},{4,5},{5,4},{6,7},{7,6},{8,9},{9,8},{10,11... | collective-permute-start | bytes 294920 | tf_op jit(solution)/shard_map/ppermute | solution.py:513
  25.7 0.9 %collective-permute-done.10.pair_climb = bf16[384,128]{1,0:T(8,128)(2,1)S(1)} collective-permute-done((bf16[384,128]{1,0:T(8,128)(2,1)S(1)}, bf16[384,128]{1,0:T(8,128)(2,1)S(1)}, u32[]{:S(2)}, u32[]{:S(2)}) %collective-permute-start.10) | collective-permute-done | bytes 98336 | tf_op jit(solution)/shard_map/ppermute | solution.py:513
  26.7 0.4 %collective-permute-done.11.pair_descend = bf16[384,128]{1,0:T(8,128)(2,1)S(1)} collective-permute-done((bf16[384,128]{1,0:T(8,128)(2,1)S(1)}, bf16[384,128]{1,0:T(8,128)(2,1)S(1)}, u32[]{:S(2)}, u32[]{:S(2)}) %collective-permute-start.11) | collective-permute-done | bytes 98336 | tf_op jit(solution)/shard_map/ppermute | solution.py:513
  27.0 1.2 %apply_far.1 = bf16[2,64,16,128]{3,2,1,0:T(8,128)(2,1)} custom-call(f32[8,2,128,128]{3,2,1,0:T(8,128)S(1)} %get-tuple-element.19.part_ref, bf16[8,2,128,128]{3,2,1,0:T(8,128)(2,1)S(1)} %get-tuple-element.20.pert_ref, bf16[384,128]{1,0:T(8,128)(2,1)S(1)} %solve.1.own, bf16[384,128]{1,0:T(8,128)(2,1)S(1)} %collective-permute-done.9.pair, ...), custom_call_target="tpu_custom_call" | custom-call | flops 134217728 | bytes 262144 | tf_op jit(solution)/shard_map/apply_far/pallas_call | solution.py:211
  (18 shorter events, 0.1 us)
Async XLA Ops:
  0.0 8.5 %copy-start.1 = (s32[4,1,256]{2,1,0:T(1,128)S(1)}, s32[4,1,256]{2,1,0:T(1,128)}, u32[]{:S(2)}) copy-start(s32[4,1,256]{2,1,0:T(1,128)} %owner_ref.1) | copy-start | bytes 12292
  0.0 8.5 %copy-start.2 = (s32[4,1,256]{2,1,0:T(1,128)S(1)}, s32[4,1,256]{2,1,0:T(1,128)}, u32[]{:S(2)}) copy-start(s32[4,1,256]{2,1,0:T(1,128)} %slot_ref.1) | copy-start | bytes 12292
  0.0 8.5 %copy-start.3 = (f32[4,1,256]{2,1,0:T(1,128)S(1)}, f32[4,1,256]{2,1,0:T(1,128)}, u32[]{:S(2)}) copy-start(f32[4,1,256]{2,1,0:T(1,128)} %local_ref.1) | copy-start | bytes 12292
  0.0 8.5 %copy-start.4 = (s32[4,1]{0,1:T(1,128)S(1)}, s32[4,1]{0,1:T(1,128)}, u32[]{:S(2)}) copy-start(s32[4,1]{0,1:T(1,128)} %param.14) | copy-start | bytes 52
  1.0 5.4 %collective-permute-start = (bf16[272,128]{1,0:T(8,128)(2,1)S(1)}, bf16[272,128]{1,0:T(8,128)(2,1)S(1)}, u32[]{:S(2)}, u32[]{:S(2)}) collective-permute-start(bf16[272,128]{1,0:T(8,128)(2,1)S(1)} %pack.1.b0), channel_id=1, source_target_pairs={{0,16},{1,17},{2,18},{3,19},{4,20},{5,21},{6,22},{7,23},{8,24},{9,... | collective-permute-start | bytes 208904 | tf_op jit(solution)/shard_map/ppermute | solution.py:513
  4.1 4.9 %collective-permute-start.2 = (bf16[272,128]{1,0:T(8,128)(2,1)S(1)}, bf16[272,128]{1,0:T(8,128)(2,1)S(1)}, u32[]{:S(2)}, u32[]{:S(2)}) collective-permute-start(bf16[272,128]{1,0:T(8,128)(2,1)S(1)} %pack.1.b0), channel_id=1, source_target_pairs={{4,0},{0,1},{6,2},{2,3},{8,4},{1,5},{10,6},{3,7},{12,8},{5,9},{14,... | collective-permute-start | bytes 208904 | tf_op jit(solution)/shard_map/ppermute | solution.py:513
  4.1 4.9 %collective-permute-start.1 = (bf16[272,128]{1,0:T(8,128)(2,1)S(1)}, bf16[272,128]{1,0:T(8,128)(2,1)S(1)}, u32[]{:S(2)}, u32[]{:S(2)}) collective-permute-start(bf16[272,128]{1,0:T(8,128)(2,1)S(1)} %pack.1.b0), channel_id=1, source_target_pairs={{0,4},{1,0},{2,6},{3,2},{4,8},{5,1},{6,10},{7,3},{8,12},{9,5},{10,... | collective-permute-start | bytes 208904 | tf_op jit(solution)/shard_map/ppermute | solution.py:513
  6.4 4.6 %collective-permute-start.4 = (bf16[272,128]{1,0:T(8,128)(2,1)S(1)}, bf16[272,128]{1,0:T(8,128)(2,1)S(1)}, u32[]{:S(2)}, u32[]{:S(2)}) collective-permute-start(bf16[272,128]{1,0:T(8,128)(2,1)S(1)} %collective-permute-done.other_ref.b3), channel_id=1, source_target_pairs={{4,0},{0,1},{6,2},{2,3},{8,4},{1,5},{10,6},{3,7},{12,8},{5,9},{14,... | collective-permute-start | bytes 208904 | tf_op jit(solution)/shard_map/ppermute | solution.py:513
  6.4 4.6 %collective-permute-start.3 = (bf16[272,128]{1,0:T(8,128)(2,1)S(1)}, bf16[272,128]{1,0:T(8,128)(2,1)S(1)}, u32[]{:S(2)}, u32[]{:S(2)}) collective-permute-start(bf16[272,128]{1,0:T(8,128)(2,1)S(1)} %collective-permute-done.other_ref.b3), channel_id=1, source_target_pairs={{0,4},{1,0},{2,6},{3,2},{4,8},{5,1},{6,10},{7,3},{8,12},{9,5},{10,... | collective-permute-start | bytes 208904 | tf_op jit(solution)/shard_map/ppermute | solution.py:513
  11.4 1.5 %collective-permute-start.5 = (f32[392,128]{1,0:T(8,128)S(1)}, f32[392,128]{1,0:T(8,128)S(1)}, u32[]{:S(2)}, u32[]{:S(2)}) collective-permute-start(f32[392,128]{1,0:T(8,128)S(1)} %get-tuple-element.15), channel_id=1, source_target_pairs={{0,1},{1,0},{2,3},{3,2},{4,5},{5,4},{6,7},{7,6},{8,9},{9,8},{10,11... | collective-permute-start | bytes 602120 | tf_op jit(solution)/shard_map/ppermute | solution.py:513
  13.0 5.0 %collective-permute-start.6 = (bf16[400,128]{1,0:T(8,128)(2,1)S(1)}, bf16[400,128]{1,0:T(8,128)(2,1)S(1)}, u32[]{:S(2)}, u32[]{:S(2)}) collective-permute-start(bf16[400,128]{1,0:T(8,128)(2,1)S(1)} %get-tuple-element.17), channel_id=1, source_target_pairs={{0,2},{1,3},{2,0},{3,1},{4,6},{5,7},{6,4},{7,5},{8,10},{9,11},{10,... | collective-permute-start | bytes 307208 | tf_op jit(solution)/shard_map/ppermute | solution.py:513
  17.9 4.1 %copy-start = (bf16[2,64,16,128]{3,2,1,0:T(8,128)(2,1)S(1)}, bf16[2,64,16,128]{3,2,1,0:T(8,128)(2,1)}, u32[]{:S(2)}) copy-start(bf16[2,64,16,128]{3,2,1,0:T(8,128)(2,1)} %members_ref.1) | copy-start | bytes 1572868
  19.9 2.1 %collective-permute-start.9 = (bf16[384,128]{1,0:T(8,128)(2,1)S(1)}, bf16[384,128]{1,0:T(8,128)(2,1)S(1)}, u32[]{:S(2)}, u32[]{:S(2)}) collective-permute-start(bf16[384,128]{1,0:T(8,128)(2,1)S(1)} %solve.1.own), channel_id=1, source_target_pairs={{0,1},{1,0},{2,3},{3,2},{4,5},{5,4},{6,7},{7,6},{8,9},{9,8},{10,11... | collective-permute-start | bytes 294920 | tf_op jit(solution)/shard_map/ppermute | solution.py:513
  20.0 4.6 %collective-permute-start.8 = (bf16[384,128]{1,0:T(8,128)(2,1)S(1)}, bf16[384,128]{1,0:T(8,128)(2,1)S(1)}, u32[]{:S(2)}, u32[]{:S(2)}) collective-permute-start(bf16[384,128]{1,0:T(8,128)(2,1)S(1)} %solve.1.own), channel_id=1, source_target_pairs={{4,0},{0,1},{6,2},{2,3},{8,4},{1,5},{10,6},{3,7},{12,8},{5,9},{14,... | collective-permute-start | bytes 294920 | tf_op jit(solution)/shard_map/ppermute | solution.py:513
  20.5 4.2 %collective-permute-start.7 = (bf16[384,128]{1,0:T(8,128)(2,1)S(1)}, bf16[384,128]{1,0:T(8,128)(2,1)S(1)}, u32[]{:S(2)}, u32[]{:S(2)}) collective-permute-start(bf16[384,128]{1,0:T(8,128)(2,1)S(1)} %solve.1.own), channel_id=1, source_target_pairs={{0,4},{1,0},{2,6},{3,2},{4,8},{5,1},{6,10},{7,3},{8,12},{9,5},{10,... | collective-permute-start | bytes 294920 | tf_op jit(solution)/shard_map/ppermute | solution.py:513
  24.7 2.0 %collective-permute-start.10 = (bf16[384,128]{1,0:T(8,128)(2,1)S(1)}, bf16[384,128]{1,0:T(8,128)(2,1)S(1)}, u32[]{:S(2)}, u32[]{:S(2)}) collective-permute-start(bf16[384,128]{1,0:T(8,128)(2,1)S(1)} %collective-permute-done.7.climb), channel_id=1, source_target_pairs={{0,1},{1,0},{2,3},{3,2},{4,5},{5,4},{6,7},{7,6},{8,9},{9,8},{10,11... | collective-permute-start | bytes 294920 | tf_op jit(solution)/shard_map/ppermute | solution.py:513
  25.7 1.3 %collective-permute-start.11 = (bf16[384,128]{1,0:T(8,128)(2,1)S(1)}, bf16[384,128]{1,0:T(8,128)(2,1)S(1)}, u32[]{:S(2)}, u32[]{:S(2)}) collective-permute-start(bf16[384,128]{1,0:T(8,128)(2,1)S(1)} %collective-permute-done.8.descend), channel_id=1, source_target_pairs={{0,1},{1,0},{2,3},{3,2},{4,5},{5,4},{6,7},{7,6},{8,9},{9,8},{10,11... | collective-permute-start | bytes 294920 | tf_op jit(solution)/shard_map/ppermute | solution.py:513

commit v5 on v4

--- a/solution.py
+++ b/solution.py
@@ -10,7 +10,6 @@
 SPACING = 16
 NS_STEPS = 4
 VMEM_LIMIT = 12 << 20
-WHOLE_VMEM = 67043328
 
 
 def padded(array, sides, width):
@@ -203,19 +202,23 @@
     }
 
 
-def device_call(kernel, operands, out_shape, scratch=(), flops=0, name=None, in_hbm=False, out_hbm=False, limit=VMEM_LIMIT):
+def device_call(kernel, operands, out_shape, scratch=(), flops=0, name=None, in_hbm=False, out_hbm=False, alias=False):
     single = not isinstance(out_shape, (list, tuple))
     spec = pl.BlockSpec(memory_space=pltpu.VMEM)
     hbm = pl.BlockSpec(memory_space=pltpu.HBM)
     out_spec = hbm if out_hbm else spec
+    in_specs = [hbm if in_hbm else spec] * len(operands)
+    if alias:
+        in_specs[-1] = hbm
     return pl.pallas_call(
         kernel,
         out_shape=out_shape,
-        in_specs=[hbm if in_hbm else spec] * len(operands),
+        in_specs=in_specs,
         out_specs=out_spec if single else [out_spec] * len(out_shape),
         scratch_shapes=list(scratch),
         cost_estimate=pl.CostEstimate(flops=flops, bytes_accessed=1 << 18, transcendentals=0),
-        compiler_params=pltpu.CompilerParams(vmem_limit_bytes=limit),
+        compiler_params=pltpu.CompilerParams(vmem_limit_bytes=VMEM_LIMIT),
+        input_output_aliases={len(operands) - 1: 0} if alias else {},
         name=name,
     )(*operands)
 
@@ -362,10 +365,17 @@
     ).astype(jnp.bfloat16)
 
 
+def beside(*pieces):
+    return jnp.concatenate(pieces, axis=1)
+
+
+def above(*pieces):
+    return jnp.concatenate(pieces, axis=0)
+
+
 def product(a, b):
     (a_high, a_low), (b_high, b_low) = a, b
-    left = jnp.concatenate([a_high, a_high, a_low], axis=1)
-    return dot(left, jnp.concatenate([b_high, b_low, b_high], axis=0))
+    return dot(beside(a_high, a_low), above(b_high, b_high)) + dot(a_high, b_low)
 
 
 def solve_kernel(half, sum_ref, got_ref, out_ref):
@@ -397,16 +407,21 @@
         root_parts = [split2(r) for r in roots]
         if iteration == 0:
             middles = [1.5 * eye - 0.5 * r for r in roots]
-        else:
-            inverse_parts = [split2(z) for z in inverses]
-            middles = [1.5 * eye - 0.5 * product(z, r) for z, r in zip(inverse_parts, root_parts)]
+            roots = [product(split2(m), r) for m, r in zip(middles, root_parts)]
+            inverses = middles
+            continue
+        inverse_parts = [split2(z) for z in inverses]
+        middles = [1.5 * eye - 0.5 * product(z, r) for z, r in zip(inverse_parts, root_parts)]
         middle_parts = [split2(m) for m in middles]
-        if not last:
-            roots = [product(r, m) for r, m in zip(root_parts, middle_parts)]
-        if iteration == 0:
-            inverses = middles
-        else:
+        if last:
             inverses = [product(m, z) for m, z in zip(middle_parts, inverse_parts)]
+            continue
+        both = [
+            product(m, (beside(r[0], z[0]), beside(r[1], z[1])))
+            for m, r, z in zip(middle_parts, root_parts, inverse_parts)
+        ]
+        roots = [x[:, 0:size] for x in both]
+        inverses = [x[:, size : 2 * size] for x in both]
     for k in range(half):
         inverse, norm = inverses[k], norms[k]
         parts = split2(inverse)
@@ -456,51 +471,67 @@
             part_ref[patch_x, patch_y] = (mean[:, :, inside, :] + share * mix).reshape(rows, size)
 
 
-def far_kernel(cols, part_ref, pert_ref, own, pair, climb, descend, pair_climb, pair_descend, out_hbm, table, staged, sems):
-    half = cols // 2
-    tile_y = lax.axis_index("ty")
-    first = lax.rem(lax.axis_index("lev"), 2) == 0
-    at_start, at_end = tile_y == 0, tile_y == lax.axis_size("ty") - 1
-    for j in range(half):
-        rows = pl.ds(128 * j, 128)
-        a, b = own[rows, :], pair[rows, :]
-        low, high = jnp.where(first, a, b), jnp.where(first, b, a)
-        up, down = climb[rows, :], descend[rows, :]
-        pair_up, pair_down = pair_climb[rows, :], pair_descend[rows, :]
-        before = (
-            jnp.where(at_start, low, jnp.where(first, up, pair_up)),
-            jnp.where(at_start, high, jnp.where(first, pair_down, down)),
-        )
-        after = (
-            jnp.where(at_end, low, jnp.where(first, down, pair_down)),
-            jnp.where(at_end, high, jnp.where(first, pair_up, up)),
-        )
-        for z, (x, y) in enumerate((before, after)):
-            table[z, :, 128 * j : 128 * (j + 1)] = x
-            table[z, :, 128 * (j + half) : 128 * (j + half + 1)] = y
-    levels, width_x, width_y, size = staged.shape
+def add_far(first_patch, count, first_column, table, part_ref, pert_ref, staged, out_hbm, sems):
+    levels, _, _, size = staged.shape
     span = SPACING // 2
     shape = (levels, span, span, size)
     step_x = lax.broadcasted_iota(jnp.int32, shape, 1).astype(jnp.float32)
     step_y = lax.broadcasted_iota(jnp.int32, shape, 2).astype(jnp.float32)
     copies = []
-    for patch_x in range(width_x // span):
-        column = (patch_x + 1) // 2
-        up_x = upper(patch_x, step_x)
+    for k in range(count):
+        patch_x = first_patch + k
+        column = lax.div(patch_x + 1, 2) - first_column
+        lanes = pl.ds(pl.multiple_of(128 * column, 128), 256)
+        up_x = (step_x + jnp.where(lax.rem(patch_x, 2) == 0, span + 0.5, 0.5)) / (2 * span)
         results = []
         for patch_y in range(2):
-            both = dot(pert_ref[patch_x, patch_y], table[patch_y, :, 128 * column : 128 * (column + 2)])
+            both = dot(pert_ref[patch_x, patch_y], table[patch_y, :, lanes])
             mix = (1.0 - up_x) * both[:, 0:128].reshape(shape) + up_x * both[:, 128:256].reshape(shape)
             up_y = upper(patch_y, step_y)
             share = 1.0 - up_y if patch_y == 0 else up_y
             results.append(part_ref[patch_x, patch_y].reshape(shape) + share * mix)
         inside = pl.ds(patch_x * span, span)
         staged[:, inside, :, :] = jnp.concatenate(results, axis=2).astype(jnp.bfloat16)
-        copy = pltpu.make_async_copy(staged.at[:, inside], out_hbm.at[:, inside], sems.at[patch_x])
+        copy = pltpu.make_async_copy(staged.at[:, inside], out_hbm.at[:, inside], sems.at[k])
         copy.start()
         copies.append(copy)
     for copy in copies:
         copy.wait()
+
+
+def neighbours(climb, descend, own, first, rows):
+    tile_y = lax.axis_index("ty")
+    up, down, mine = climb[rows, :], descend[rows, :], own[rows, :]
+    before = jnp.where(tile_y == 0, mine, jnp.where(first, up, down))
+    after = jnp.where(tile_y == lax.axis_size("ty") - 1, mine, jnp.where(first, down, up))
+    return before, after
+
+
+def far_first_kernel(cols, part_ref, pert_ref, own, climb, descend, out_hbm, table, staged, sems):
+    half = cols // 2
+    core = lax.rem(lax.axis_index("lev"), 2)
+    for j in range(half):
+        for z, value in enumerate(neighbours(climb, descend, own, core == 0, pl.ds(128 * j, 128))):
+            table[z, :, 128 * j : 128 * (j + 1)] = value
+    count, total = sems.shape[0], part_ref.shape[0]
+    add_far(core * (total - count), count, core * half, table, part_ref, pert_ref, staged, out_hbm, sems)
+
+
+def far_rest_kernel(
+    cols, part_ref, pert_ref, own, pair, climb, descend, pair_climb, pair_descend, begun_hbm, out_hbm, table, staged, sems
+):
+    half = cols // 2
+    core = lax.rem(lax.axis_index("lev"), 2)
+    first = core == 0
+    for j in range(half):
+        rows = pl.ds(128 * j, 128)
+        mine = neighbours(climb, descend, own, first, rows)
+        theirs = neighbours(pair_climb, pair_descend, pair, jnp.logical_not(first), rows)
+        for z, (x, y) in enumerate(zip(mine, theirs)):
+            table[z, :, 128 * j : 128 * (j + 1)] = jnp.where(first, x, y)
+            table[z, :, 128 * (j + half) : 128 * (j + half + 1)] = jnp.where(first, y, x)
+    count, total = sems.shape[0], part_ref.shape[0]
+    add_far((1 - core) * (total - count), count, 0, table, part_ref, pert_ref, staged, out_hbm, sems)
 
 
 def paired_device(
@@ -598,18 +629,32 @@
     )
     up, down, part = lax.optimization_barrier((up, down, part))
     pair_up, pair_down = send(up, "core"), send(down, "core")
-    return device_call(
-        functools.partial(far_kernel, cols),
-        (part, pert, weights, pair, up, down, pair_up, pair_down),
-        shape(members.shape, bf16),
-        [
-            pltpu.VMEM((2, size, cols * size), bf16),
-            pltpu.VMEM(members.shape, bf16),
-            pltpu.SemaphoreType.DMA((patches[0],)),
-        ],
-        flops=2 * levels * width_x * width_y * size * 2 * size,
-        name="apply_far",
-        out_hbm=True,
+    early = cols - 3
+
+    def finish(kernel, name, operands, count, wide, alias):
+        return device_call(
+            functools.partial(kernel, cols),
+            operands,
+            shape(members.shape, bf16),
+            [
+                pltpu.VMEM((2, size, wide * size), bf16),
+                pltpu.VMEM(members.shape, bf16),
+                pltpu.SemaphoreType.DMA((count,)),
+            ],
+            flops=2 * levels * 8 * count * width_y * size * 2 * size,
+            name=name,
+            out_hbm=True,
+            alias=alias,
+        )
+
+    begun = finish(far_first_kernel, "far_first", (part, pert, weights, up, down), early, half, False)
+    return finish(
+        far_rest_kernel,
+        "far_rest",
+        (part, pert, weights, pair, up, down, pair_up, pair_down, begun),
+        patches[0] - early,
+        cols,
+        True,
     )
 
 

time: 28.4 us -> 28.2 us (level)
  waiting for transfers between devices: 9.67 us -> 8.68 us
  Pallas kernels: 6.28 us -> 7.04 us
    ppermute x12, waiting for transfers between devices: 9.67 us -> 8.68 us  [send(): return lax.ppermute(value, axes, ways[way])]
    pallas_call x8 -> x9, Pallas kernels: 6.28 us -> 7.04 us  [device_call(): pl.pallas_call(kernel, out_shape=out_shape, in_specs=in_specs, out_specs=...]
  transfers between devices with their start and end apart: 12 -> 12, of which waited for: 9 -> 8; matrix products, arithmetic and copies ran while one was open for 0% -> 0% of each run, Pallas kernels for 6% -> 9%
where the time goes in v5:
time: 28.2 us; the launch traced here: 28.1 us
  starting transfers between devices  12.2 us (43%)
  waiting for transfers between devices  8.68 us (31%)
  Pallas kernels  7.04 us (25%)
    ppermute x12, starting transfers between devices, send(): return lax.ppermute(value, axes, ways[way])  12.2 us
    ppermute x12, waiting for transfers between devices, send(): return lax.ppermute(value, axes, ways[way])  8.68 us
    pallas_call x9, Pallas kernels, device_call(): pl.pallas_call(kernel, out_shape=out_shape, in_specs=in_specs, out_specs=...  7.04 us
  transfers between devices with their start and end apart: 12, of which 8 were waited for; matrix products, arithmetic and copies ran while one was open for 0% of the time, Pallas kernels for 9%

profile of v5, /device:TPU:0, one launch (start us, length us, event | category | flops | bytes accessed | tf_op | source)
XLA Modules:
  0.0 28.1 jit_solution(14801853800967393077)
XLA Ops:
  0.0 1.0 %pack.1.b0 = bf16[272,128]{1,0:T(8,128)(2,1)S(1)} custom-call(bf16[256,128]{1,0:T(8,128)(2,1)} %pert.1, bf16[2,128]{1,0:T(2,128)(2,1)} %bitcast.5, bf16[2,128]{1,0:T(2,128)(2,1)} %bitcast.6, s32[4,1,256]{2,1,0:T(1,128)} %owner_ref.1, s32[4,1,256]{2,1,0:T(1,128)} %slot_ref.1, s32[1,4]{1,0:T(1,128)} %bitcast.3, f32[4,1,256]{2,1,0:T(1,128)} %local_ref.1), custom_call_target="tpu_custom_call" | custom-call | bytes 262144 | tf_op jit(solution)/shard_map/pack/pallas_call | solution.py:213
  1.0 3.1 %collective-permute-start = (bf16[272,128]{1,0:T(8,128)(2,1)S(1)}, bf16[272,128]{1,0:T(8,128)(2,1)S(1)}, u32[]{:S(2)}, u32[]{:S(2)}) collective-permute-start(bf16[272,128]{1,0:T(8,128)(2,1)S(1)} %pack.1.b0), channel_id=1, source_target_pairs={{0,16},{1,17},{2,18},{3,19},{4,20},{5,21},{6,22},{7,23},{8,24},{9,... | collective-permute-start | bytes 208904 | tf_op jit(solution)/shard_map/ppermute | solution.py:544
  4.1 2.0 %collective-permute-start.1 = (bf16[272,128]{1,0:T(8,128)(2,1)S(1)}, bf16[272,128]{1,0:T(8,128)(2,1)S(1)}, u32[]{:S(2)}, u32[]{:S(2)}) collective-permute-start(bf16[272,128]{1,0:T(8,128)(2,1)S(1)} %pack.1.b0), channel_id=1, source_target_pairs={{0,4},{1,0},{2,6},{3,2},{4,8},{5,1},{6,10},{7,3},{8,12},{9,5},{10,... | collective-permute-start | bytes 208904 | tf_op jit(solution)/shard_map/ppermute | solution.py:544
  6.1 0.3 collective-permute-done.other_ref.b3
  6.4 2.1 %collective-permute-start.3 = (bf16[272,128]{1,0:T(8,128)(2,1)S(1)}, bf16[272,128]{1,0:T(8,128)(2,1)S(1)}, u32[]{:S(2)}, u32[]{:S(2)}) collective-permute-start(bf16[272,128]{1,0:T(8,128)(2,1)S(1)} %collective-permute-done.other_ref.b3), channel_id=1, source_target_pairs={{0,4},{1,0},{2,6},{3,2},{4,8},{5,1},{6,10},{7,3},{8,12},{9,5},{10,... | collective-permute-start | bytes 208904 | tf_op jit(solution)/shard_map/ppermute | solution.py:544
  8.5 0.5 %table.1.table_ref = f32[128,128]{1,0:T(8,128)S(1)} custom-call(s32[4,1,256]{2,1,0:T(1,128)S(1)} %copy-done.1, s32[4,1,256]{2,1,0:T(1,128)S(1)} %copy-done.2, s32[1,4]{1,0:T(1,128)S(1)} %bitcast.4, f32[4,1,256]{2,1,0:T(1,128)S(1)} %copy-done.3, bf16[272,128]{1,0:T(8,128)(2,1)S(1)} %collective-permute-done.other_ref.b3), custom_call_target="tpu_custom_call" | custom-call | flops 18874368 | bytes 262144 | tf_op jit(solution)/shard_map/table/pallas_call | solution.py:213
  9.0 0.1 collective-permute-done.2.b2
  9.1 0.6 %gram_near.1.near_ref = f32[784,128]{1,0:T(8,128)S(1)} custom-call(f32[128,128]{1,0:T(8,128)S(1)} %table.1.table_ref, bf16[272,128]{1,0:T(8,128)(2,1)S(1)} %pack.1.b0, bf16[272,128]{1,0:T(8,128)(2,1)S(1)} %collective-permute-done.1.b1, bf16[272,128]{1,0:T(8,128)(2,1)S(1)} %collective-permute-done.2.b2, bf16[272,128]{1,0:T(8,128)(2,1)S(1)} %collective-permute-done.other_ref.b3), custom_call_target="tpu_custom_call" | custom-call | flops 205520896 | bytes 262144 | tf_op jit(solution)/shard_map/gram_near/pallas_call | solution.py:213
  9.7 1.3 %collective-permute-done.4.b5 = bf16[272,128]{1,0:T(8,128)(2,1)S(1)} collective-permute-done((bf16[272,128]{1,0:T(8,128)(2,1)S(1)}, bf16[272,128]{1,0:T(8,128)(2,1)S(1)}, u32[]{:S(2)}, u32[]{:S(2)}) %collective-permute-start.4) | collective-permute-done | bytes 69664 | tf_op jit(solution)/shard_map/ppermute | solution.py:544
  11.0 0.4 %gram_far.1 = (f32[392,128]{1,0:T(8,128)S(1)}, f32[392,128]{1,0:T(8,128)S(1)}) custom-call(f32[128,128]{1,0:T(8,128)S(1)} %table.1.table_ref, f32[784,128]{1,0:T(8,128)S(1)} %gram_near.1.near_ref, bf16[272,128]{1,0:T(8,128)(2,1)S(1)} %collective-permute-done.3.b4, bf16[272,128]{1,0:T(8,128)(2,1)S(1)} %collective-permute-done.4.b5), custom_call_target="tpu_custom_call" | custom-call | flops 102760448 | bytes 262144 | tf_op jit(solution)/shard_map/gram_far/pallas_call | solution.py:213
  11.4 0.1 collective-permute-start.5
  11.5 1.4 %collective-permute-done.5.got_ref = f32[392,128]{1,0:T(8,128)S(1)} collective-permute-done((f32[392,128]{1,0:T(8,128)S(1)}, f32[392,128]{1,0:T(8,128)S(1)}, u32[]{:S(2)}, u32[]{:S(2)}) %collective-permute-start.5) | collective-permute-done | bytes 200736 | tf_op jit(solution)/shard_map/ppermute | solution.py:544
  13.0 1.8 %collective-permute-start.6 = (bf16[400,128]{1,0:T(8,128)(2,1)S(1)}, bf16[400,128]{1,0:T(8,128)(2,1)S(1)}, u32[]{:S(2)}, u32[]{:S(2)}) collective-permute-start(bf16[400,128]{1,0:T(8,128)(2,1)S(1)} %get-tuple-element.17), channel_id=1, source_target_pairs={{0,2},{1,3},{2,0},{3,1},{4,6},{5,7},{6,4},{7,5},{8,10},{9,11},{10,... | collective-permute-start | bytes 307208 | tf_op jit(solution)/shard_map/ppermute | solution.py:544
  14.8 3.2 %collective-permute-done.6.got_ref = bf16[400,128]{1,0:T(8,128)(2,1)S(1)} collective-permute-done((bf16[400,128]{1,0:T(8,128)(2,1)S(1)}, bf16[400,128]{1,0:T(8,128)(2,1)S(1)}, u32[]{:S(2)}, u32[]{:S(2)}) %collective-permute-start.6) | collective-permute-done | bytes 102432 | tf_op jit(solution)/shard_map/ppermute | solution.py:544
  17.9 1.8 %solve.1.own = bf16[384,128]{1,0:T(8,128)(2,1)S(1)} custom-call(f32[392,128]{1,0:T(8,128)S(1)} %get-tuple-element.16.sum_ref, bf16[400,128]{1,0:T(8,128)(2,1)S(1)} %collective-permute-done.6.got_ref), custom_call_target="tpu_custom_call" | custom-call | flops 339738624 | bytes 262144 | tf_op jit(solution)/shard_map/solve/pallas_call | solution.py:213
  19.8 0.5 %collective-permute-start.8 = (bf16[384,128]{1,0:T(8,128)(2,1)S(1)}, bf16[384,128]{1,0:T(8,128)(2,1)S(1)}, u32[]{:S(2)}, u32[]{:S(2)}) collective-permute-start(bf16[384,128]{1,0:T(8,128)(2,1)S(1)} %solve.1.own), channel_id=1, source_target_pairs={{4,0},{0,1},{6,2},{2,3},{8,4},{1,5},{10,6},{3,7},{12,8},{5,9},{14,... | collective-permute-start | bytes 294920 | tf_op jit(solution)/shard_map/ppermute | solution.py:544
  20.3 1.6 %collective-permute-start.7 = (bf16[384,128]{1,0:T(8,128)(2,1)S(1)}, bf16[384,128]{1,0:T(8,128)(2,1)S(1)}, u32[]{:S(2)}, u32[]{:S(2)}) collective-permute-start(bf16[384,128]{1,0:T(8,128)(2,1)S(1)} %solve.1.own), channel_id=1, source_target_pairs={{0,4},{1,0},{2,6},{3,2},{4,8},{5,1},{6,10},{7,3},{8,12},{9,5},{10,... | collective-permute-start | bytes 294920 | tf_op jit(solution)/shard_map/ppermute | solution.py:544
  21.9 0.6 %apply_near.1 = (f32[8,2,128,128]{3,2,1,0:T(8,128)S(1)}, bf16[8,2,128,128]{3,2,1,0:T(8,128)(2,1)S(1)}) custom-call(bf16[2,64,16,128]{3,2,1,0:T(8,128)(2,1)S(1)} %copy-done, bf16[384,128]{1,0:T(8,128)(2,1)S(1)} %solve.1.own, bf16[384,128]{1,0:T(8,128)(2,1)S(1)} %collective-permute-done.9.pair), custom_call_target="tpu_custom_call" | custom-call | flops 134217728 | bytes 262144 | tf_op jit(solution)/shard_map/apply_near/pallas_call | solution.py:213
  22.5 2.0 %collective-permute-done.8.descend = bf16[384,128]{1,0:T(8,128)(2,1)S(1)} collective-permute-done((bf16[384,128]{1,0:T(8,128)(2,1)S(1)}, bf16[384,128]{1,0:T(8,128)(2,1)S(1)}, u32[]{:S(2)}, u32[]{:S(2)}) %collective-permute-start.8) | collective-permute-done | bytes 98336 | tf_op jit(solution)/shard_map/ppermute | solution.py:544
  24.5 0.1 collective-permute-done.7.climb
  24.6 1.1 %collective-permute-start.10 = (bf16[384,128]{1,0:T(8,128)(2,1)S(1)}, bf16[384,128]{1,0:T(8,128)(2,1)S(1)}, u32[]{:S(2)}, u32[]{:S(2)}) collective-permute-start(bf16[384,128]{1,0:T(8,128)(2,1)S(1)} %collective-permute-done.7.climb), channel_id=1, source_target_pairs={{0,1},{1,0},{2,3},{3,2},{4,5},{5,4},{6,7},{7,6},{8,9},{9,8},{10,11... | collective-permute-start | bytes 294920 | tf_op jit(solution)/shard_map/ppermute | solution.py:544
  25.6 1.0 %far_first.1.begun_hbm = bf16[2,64,16,128]{3,2,1,0:T(8,128)(2,1)} custom-call(f32[8,2,128,128]{3,2,1,0:T(8,128)S(1)} %get-tuple-element.19.part_ref, bf16[8,2,128,128]{3,2,1,0:T(8,128)(2,1)S(1)} %get-tuple-element.20.pert_ref, bf16[384,128]{1,0:T(8,128)(2,1)S(1)} %solve.1.own, bf16[384,128]{1,0:T(8,128)(2,1)S(1)} %collective-permute-done.7.climb, ...), custom_call_target="tpu_custom_call" | custom-call | flops 50331648 | bytes 262144 | tf_op jit(solution)/shard_map/far_first/pallas_call | solution.py:213
  26.6 0.3 %collective-permute-done.11.pair_descend = bf16[384,128]{1,0:T(8,128)(2,1)S(1)} collective-permute-done((bf16[384,128]{1,0:T(8,128)(2,1)S(1)}, bf16[384,128]{1,0:T(8,128)(2,1)S(1)}, u32[]{:S(2)}, u32[]{:S(2)}) %collective-permute-start.11) | collective-permute-done | bytes 98336 | tf_op jit(solution)/shard_map/ppermute | solution.py:544
  26.9 1.1 %far_rest.1 = bf16[2,64,16,128]{3,2,1,0:T(8,128)(2,1)} custom-call(f32[8,2,128,128]{3,2,1,0:T(8,128)S(1)} %get-tuple-element.19.part_ref, bf16[8,2,128,128]{3,2,1,0:T(8,128)(2,1)S(1)} %get-tuple-element.20.pert_ref, bf16[384,128]{1,0:T(8,128)(2,1)S(1)} %solve.1.own, ...), custom_call_target="tpu_custom_call", output_to_operand_aliasing={{}: (8, {})} | custom-call | flops 83886080 | bytes 262144 | tf_op jit(solution)/shard_map/far_rest/pallas_call | solution.py:213
  (19 shorter events, 0.1 us)
Async XLA Ops:
  0.0 8.5 %copy-start.1 = (s32[4,1,256]{2,1,0:T(1,128)S(1)}, s32[4,1,256]{2,1,0:T(1,128)}, u32[]{:S(2)}) copy-start(s32[4,1,256]{2,1,0:T(1,128)} %owner_ref.1) | copy-start | bytes 12292
  0.0 8.5 %copy-start.2 = (s32[4,1,256]{2,1,0:T(1,128)S(1)}, s32[4,1,256]{2,1,0:T(1,128)}, u32[]{:S(2)}) copy-start(s32[4,1,256]{2,1,0:T(1,128)} %slot_ref.1) | copy-start | bytes 12292
  0.0 8.5 %copy-start.3 = (f32[4,1,256]{2,1,0:T(1,128)S(1)}, f32[4,1,256]{2,1,0:T(1,128)}, u32[]{:S(2)}) copy-start(f32[4,1,256]{2,1,0:T(1,128)} %local_ref.1) | copy-start | bytes 12292
  0.0 8.5 %copy-start.4 = (s32[4,1]{0,1:T(1,128)S(1)}, s32[4,1]{0,1:T(1,128)}, u32[]{:S(2)}) copy-start(s32[4,1]{0,1:T(1,128)} %param.14) | copy-start | bytes 52
  1.0 5.4 %collective-permute-start = (bf16[272,128]{1,0:T(8,128)(2,1)S(1)}, bf16[272,128]{1,0:T(8,128)(2,1)S(1)}, u32[]{:S(2)}, u32[]{:S(2)}) collective-permute-start(bf16[272,128]{1,0:T(8,128)(2,1)S(1)} %pack.1.b0), channel_id=1, source_target_pairs={{0,16},{1,17},{2,18},{3,19},{4,20},{5,21},{6,22},{7,23},{8,24},{9,... | collective-permute-start | bytes 208904 | tf_op jit(solution)/shard_map/ppermute | solution.py:544
  4.1 4.9 %collective-permute-start.2 = (bf16[272,128]{1,0:T(8,128)(2,1)S(1)}, bf16[272,128]{1,0:T(8,128)(2,1)S(1)}, u32[]{:S(2)}, u32[]{:S(2)}) collective-permute-start(bf16[272,128]{1,0:T(8,128)(2,1)S(1)} %pack.1.b0), channel_id=1, source_target_pairs={{4,0},{0,1},{6,2},{2,3},{8,4},{1,5},{10,6},{3,7},{12,8},{5,9},{14,... | collective-permute-start | bytes 208904 | tf_op jit(solution)/shard_map/ppermute | solution.py:544
  4.1 4.9 %collective-permute-start.1 = (bf16[272,128]{1,0:T(8,128)(2,1)S(1)}, bf16[272,128]{1,0:T(8,128)(2,1)S(1)}, u32[]{:S(2)}, u32[]{:S(2)}) collective-permute-start(bf16[272,128]{1,0:T(8,128)(2,1)S(1)} %pack.1.b0), channel_id=1, source_target_pairs={{0,4},{1,0},{2,6},{3,2},{4,8},{5,1},{6,10},{7,3},{8,12},{9,5},{10,... | collective-permute-start | bytes 208904 | tf_op jit(solution)/shard_map/ppermute | solution.py:544
  6.4 4.6 %collective-permute-start.4 = (bf16[272,128]{1,0:T(8,128)(2,1)S(1)}, bf16[272,128]{1,0:T(8,128)(2,1)S(1)}, u32[]{:S(2)}, u32[]{:S(2)}) collective-permute-start(bf16[272,128]{1,0:T(8,128)(2,1)S(1)} %collective-permute-done.other_ref.b3), channel_id=1, source_target_pairs={{4,0},{0,1},{6,2},{2,3},{8,4},{1,5},{10,6},{3,7},{12,8},{5,9},{14,... | collective-permute-start | bytes 208904 | tf_op jit(solution)/shard_map/ppermute | solution.py:544
  6.4 4.6 %collective-permute-start.3 = (bf16[272,128]{1,0:T(8,128)(2,1)S(1)}, bf16[272,128]{1,0:T(8,128)(2,1)S(1)}, u32[]{:S(2)}, u32[]{:S(2)}) collective-permute-start(bf16[272,128]{1,0:T(8,128)(2,1)S(1)} %collective-permute-done.other_ref.b3), channel_id=1, source_target_pairs={{0,4},{1,0},{2,6},{3,2},{4,8},{5,1},{6,10},{7,3},{8,12},{9,5},{10,... | collective-permute-start | bytes 208904 | tf_op jit(solution)/shard_map/ppermute | solution.py:544
  11.4 1.5 %collective-permute-start.5 = (f32[392,128]{1,0:T(8,128)S(1)}, f32[392,128]{1,0:T(8,128)S(1)}, u32[]{:S(2)}, u32[]{:S(2)}) collective-permute-start(f32[392,128]{1,0:T(8,128)S(1)} %get-tuple-element.15), channel_id=1, source_target_pairs={{0,1},{1,0},{2,3},{3,2},{4,5},{5,4},{6,7},{7,6},{8,9},{9,8},{10,11... | collective-permute-start | bytes 602120 | tf_op jit(solution)/shard_map/ppermute | solution.py:544
  13.0 5.0 %collective-permute-start.6 = (bf16[400,128]{1,0:T(8,128)(2,1)S(1)}, bf16[400,128]{1,0:T(8,128)(2,1)S(1)}, u32[]{:S(2)}, u32[]{:S(2)}) collective-permute-start(bf16[400,128]{1,0:T(8,128)(2,1)S(1)} %get-tuple-element.17), channel_id=1, source_target_pairs={{0,2},{1,3},{2,0},{3,1},{4,6},{5,7},{6,4},{7,5},{8,10},{9,11},{10,... | collective-permute-start | bytes 307208 | tf_op jit(solution)/shard_map/ppermute | solution.py:544
  17.9 3.9 %copy-start = (bf16[2,64,16,128]{3,2,1,0:T(8,128)(2,1)S(1)}, bf16[2,64,16,128]{3,2,1,0:T(8,128)(2,1)}, u32[]{:S(2)}) copy-start(bf16[2,64,16,128]{3,2,1,0:T(8,128)(2,1)} %members_ref.1) | copy-start | bytes 1572868
  19.8 2.1 %collective-permute-start.9 = (bf16[384,128]{1,0:T(8,128)(2,1)S(1)}, bf16[384,128]{1,0:T(8,128)(2,1)S(1)}, u32[]{:S(2)}, u32[]{:S(2)}) collective-permute-start(bf16[384,128]{1,0:T(8,128)(2,1)S(1)} %solve.1.own), channel_id=1, source_target_pairs={{0,1},{1,0},{2,3},{3,2},{4,5},{5,4},{6,7},{7,6},{8,9},{9,8},{10,11... | collective-permute-start | bytes 294920 | tf_op jit(solution)/shard_map/ppermute | solution.py:544
  19.8 4.6 %collective-permute-start.8 = (bf16[384,128]{1,0:T(8,128)(2,1)S(1)}, bf16[384,128]{1,0:T(8,128)(2,1)S(1)}, u32[]{:S(2)}, u32[]{:S(2)}) collective-permute-start(bf16[384,128]{1,0:T(8,128)(2,1)S(1)} %solve.1.own), channel_id=1, source_target_pairs={{4,0},{0,1},{6,2},{2,3},{8,4},{1,5},{10,6},{3,7},{12,8},{5,9},{14,... | collective-permute-start | bytes 294920 | tf_op jit(solution)/shard_map/ppermute | solution.py:544
  20.3 4.2 %collective-permute-start.7 = (bf16[384,128]{1,0:T(8,128)(2,1)S(1)}, bf16[384,128]{1,0:T(8,128)(2,1)S(1)}, u32[]{:S(2)}, u32[]{:S(2)}) collective-permute-start(bf16[384,128]{1,0:T(8,128)(2,1)S(1)} %solve.1.own), channel_id=1, source_target_pairs={{0,4},{1,0},{2,6},{3,2},{4,8},{5,1},{6,10},{7,3},{8,12},{9,5},{10,... | collective-permute-start | bytes 294920 | tf_op jit(solution)/shard_map/ppermute | solution.py:544
  24.6 2.0 %collective-permute-start.10 = (bf16[384,128]{1,0:T(8,128)(2,1)S(1)}, bf16[384,128]{1,0:T(8,128)(2,1)S(1)}, u32[]{:S(2)}, u32[]{:S(2)}) collective-permute-start(bf16[384,128]{1,0:T(8,128)(2,1)S(1)} %collective-permute-done.7.climb), channel_id=1, source_target_pairs={{0,1},{1,0},{2,3},{3,2},{4,5},{5,4},{6,7},{7,6},{8,9},{9,8},{10,11... | collective-permute-start | bytes 294920 | tf_op jit(solution)/shard_map/ppermute | solution.py:544
  25.6 1.3 %collective-permute-start.11 = (bf16[384,128]{1,0:T(8,128)(2,1)S(1)}, bf16[384,128]{1,0:T(8,128)(2,1)S(1)}, u32[]{:S(2)}, u32[]{:S(2)}) collective-permute-start(bf16[384,128]{1,0:T(8,128)(2,1)S(1)} %collective-permute-done.8.descend), channel_id=1, source_target_pairs={{0,1},{1,0},{2,3},{3,2},{4,5},{5,4},{6,7},{7,6},{8,9},{9,8},{10,11... | collective-permute-start | bytes 294920 | tf_op jit(solution)/shard_map/ppermute | solution.py:544

commit v6 on v5

--- a/solution.py
+++ b/solution.py
@@ -202,23 +202,19 @@
     }
 
 
-def device_call(kernel, operands, out_shape, scratch=(), flops=0, name=None, in_hbm=False, out_hbm=False, alias=False):
+def device_call(kernel, operands, out_shape, scratch=(), flops=0, name=None, in_hbm=False, out_hbm=False):
     single = not isinstance(out_shape, (list, tuple))
     spec = pl.BlockSpec(memory_space=pltpu.VMEM)
     hbm = pl.BlockSpec(memory_space=pltpu.HBM)
     out_spec = hbm if out_hbm else spec
-    in_specs = [hbm if in_hbm else spec] * len(operands)
-    if alias:
-        in_specs[-1] = hbm
     return pl.pallas_call(
         kernel,
         out_shape=out_shape,
-        in_specs=in_specs,
+        in_specs=[hbm if in_hbm else spec] * len(operands),
         out_specs=out_spec if single else [out_spec] * len(out_shape),
         scratch_shapes=list(scratch),
         cost_estimate=pl.CostEstimate(flops=flops, bytes_accessed=1 << 18, transcendentals=0),
         compiler_params=pltpu.CompilerParams(vmem_limit_bytes=VMEM_LIMIT),
-        input_output_aliases={len(operands) - 1: 0} if alias else {},
         name=name,
     )(*operands)
 
@@ -341,9 +337,13 @@
     out_ref[...] = gram_blocks(rows, cols, 0, [b0, b1, b2, b3], table_ref, turned, plain, scaled)
 
 
-def gram_far_kernel(rows, cols, table_ref, near_ref, b4, b5, mine_ref, rest_ref, turned, plain, scaled):
+def gram_next_kernel(rows, cols, first, table_ref, so_far_ref, block, out_ref, turned, plain, scaled):
+    out_ref[...] = so_far_ref[...] + gram_blocks(rows, cols, first, [block], table_ref, turned, plain, scaled)
+
+
+def gram_last_kernel(rows, cols, first, table_ref, so_far_ref, block, mine_ref, rest_ref, turned, plain, scaled):
     half = cols // 2
-    total = near_ref[...] + gram_blocks(rows, cols, 4, [b4, b5], table_ref, turned, plain, scaled)
+    total = so_far_ref[...] + gram_blocks(rows, cols, first, [block], table_ref, turned, plain, scaled)
     edge = 128 * half
     projected = total[2 * edge : 2 * edge + 8] + total[2 * edge + 8 : 2 * edge + 16]
     mine_ref[0:edge, :] = total[0:edge]
@@ -354,15 +354,39 @@
     )
 
 
+def lanes_from(lane, values, others=0.0):
+    return jnp.where(lax.broadcasted_iota(jnp.int32, values.shape, 1) >= lane, values, others)
+
+
+def fold(grams):
+    top = [g[0:32] for g in grams]
+    sides = [lanes_from(32, g[32:64], pltpu.roll(g[96:128], 32, 1)) for g in grams]
+    third = [g[64:96] for g in grams]
+    return above(*top, *sides, lanes_from(64, third[0], pltpu.roll(third[1], 64, 1)), third[2])
+
+
+def unfold(folded, k, eye):
+    side = folded[96 + 32 * k : 128 + 32 * k]
+    third = folded[192:224] if k < 2 else folded[224:256]
+    third = pltpu.roll(third, 64, 1) if k == 1 else third
+    upper_part = above(
+        folded[32 * k : 32 * k + 32],
+        lanes_from(32, side),
+        lanes_from(64, third),
+        lanes_from(96, pltpu.roll(side, 96, 1)),
+    )
+    turned = dot(eye.astype(jnp.bfloat16), upper_part.astype(jnp.bfloat16), ((1,), (1,)))
+    below = lax.broadcasted_iota(jnp.int32, eye.shape, 0) // 32 > lax.broadcasted_iota(jnp.int32, eye.shape, 1) // 32
+    return jnp.where(below, turned, upper_part)
+
+
 def join_kernel(half, mine_ref, got_ref, sum_ref, send_ref):
     total = mine_ref[...] + got_ref[...]
     sum_ref[...] = total
     edge = 128 * half
-    send_ref[0:edge, :] = total[0:edge].astype(jnp.bfloat16)
+    folded = fold([total[128 * k : 128 * (k + 1)] for k in range(half)])
     high, low = split2(total[edge : edge + 8])
-    send_ref[edge : edge + 16, :] = jnp.concatenate(
-        [high.astype(jnp.float32), low.astype(jnp.float32)], axis=0
-    ).astype(jnp.bfloat16)
+    send_ref[...] = above(folded, high.astype(jnp.float32), low.astype(jnp.float32)).astype(jnp.bfloat16)
 
 
 def beside(*pieces):
@@ -387,41 +411,34 @@
         0.0,
     )
     edge = size * half
-    projected = (
-        sum_ref[edge : edge + 8, :]
-        + got_ref[edge : edge + 16, :].astype(jnp.float32)[0:8]
-        + got_ref[edge : edge + 16, :].astype(jnp.float32)[8:16]
-    )
-    state = []
+    got = got_ref[...].astype(jnp.float32)
+    projected = sum_ref[edge : edge + 8, :] + got[256:264] + got[264:272]
+    norms, bases = [], []
     for k in range(half):
-        gram = sum_ref[size * k : size * (k + 1), :] + got_ref[size * k : size * (k + 1), :].astype(jnp.float32)
+        gram = sum_ref[size * k : size * (k + 1), :] + unfold(got, k, eye)
         squared = jnp.sum(jnp.sum(gram * gram, axis=0, keepdims=True), axis=1, keepdims=True)
         norm = spread + jnp.sqrt(squared)
-        start = (spread * eye + gram) / norm
-        state.append((norm, start))
-    norms = [n for n, _ in state]
-    roots = [s for _, s in state]
-    inverses = [None] * half
-    for iteration in range(NS_STEPS):
-        last = iteration == NS_STEPS - 1
-        root_parts = [split2(r) for r in roots]
-        if iteration == 0:
-            middles = [1.5 * eye - 0.5 * r for r in roots]
-            roots = [product(split2(m), r) for m, r in zip(middles, root_parts)]
-            inverses = middles
-            continue
+        norms.append(norm)
+        bases.append((spread * eye + gram) / norm)
+    base_parts = [split2(base) for base in bases]
+    squares = [dot(high, high) for high, _ in base_parts]
+    inverses = [
+        1.5 * (1.5 * eye - 0.5 * base)
+        - 0.5
+        * dot(
+            (1.5 * base - 0.5 * square).astype(jnp.bfloat16),
+            (2.25 * eye - 1.5 * base + 0.25 * square).astype(jnp.bfloat16),
+        )
+        for base, square in zip(bases, squares)
+    ]
+    for _ in range(NS_STEPS - 2):
         inverse_parts = [split2(z) for z in inverses]
-        middles = [1.5 * eye - 0.5 * product(z, r) for z, r in zip(inverse_parts, root_parts)]
-        middle_parts = [split2(m) for m in middles]
-        if last:
-            inverses = [product(m, z) for m, z in zip(middle_parts, inverse_parts)]
-            continue
         both = [
-            product(m, (beside(r[0], z[0]), beside(r[1], z[1])))
-            for m, r, z in zip(middle_parts, root_parts, inverse_parts)
+            product(z, (beside(b[0], z[0]), beside(b[1], z[1]))) for b, z in zip(base_parts, inverse_parts)
         ]
-        roots = [x[:, 0:size] for x in both]
-        inverses = [x[:, size : 2 * size] for x in both]
+        inverses = [
+            1.5 * z - 0.5 * product(split2(x[:, 0:size]), split2(x[:, size : 2 * size])) for z, x in zip(inverses, both)
+        ]
     for k in range(half):
         inverse, norm = inverses[k], norms[k]
         parts = split2(inverse)
@@ -435,9 +452,18 @@
         out_ref[size * k : size * (k + 1), :] = transform.astype(jnp.bfloat16)
 
 
-def upper(place, step):
+def shares(levels, size):
     span = SPACING // 2
-    return (step + (span + 0.5 if place % 2 == 0 else 0.5)) / (2 * span)
+    shape = (1, span, span, size)
+    along_x = lax.broadcasted_iota(jnp.int32, shape, 1).astype(jnp.float32) / (2 * span)
+    along_y = lax.broadcasted_iota(jnp.int32, shape, 2).astype(jnp.float32) / (2 * span)
+    upper_y = [along_y + (span + 0.5) / (2 * span), along_y + 0.5 / (2 * span)]
+    return along_x, upper_y
+
+
+def mixed(both, share, upper_x, shape):
+    high = share * upper_x
+    return (share - high) * both[:, 0:128].reshape(shape) + high * both[:, 128:256].reshape(shape)
 
 
 def near_kernel(cols, members_ref, own, pair, part_ref, pert_ref, table):
@@ -452,51 +478,38 @@
     span = SPACING // 2
     shape = (levels, span, span, size)
     rows = levels * span * span
-    step_x = lax.broadcasted_iota(jnp.int32, shape, 1).astype(jnp.float32)
-    step_y = lax.broadcasted_iota(jnp.int32, shape, 2).astype(jnp.float32)
+    along_x, upper_y = shares(levels, size)
     for patch_x in range(width_x // span):
         states = members_ref[:, patch_x * span : (patch_x + 1) * span, :, :].astype(jnp.float32)
         mean = jnp.sum(states, axis=3, keepdims=True) * (1.0 / size)
         moved = states - mean
         column = (patch_x + 1) // 2
-        up_x = upper(patch_x, step_x)
+        upper_x = along_x + (span + 0.5 if patch_x % 2 == 0 else 0.5) / (2 * span)
         for patch_y in range(2):
             inside = slice(patch_y * span, (patch_y + 1) * span)
             left = moved[:, :, inside, :].reshape(rows, size).astype(jnp.bfloat16)
             pert_ref[patch_x, patch_y] = left
             both = dot(left, table[:, 128 * column : 128 * (column + 2)])
-            mix = (1.0 - up_x) * both[:, 0:128].reshape(shape) + up_x * both[:, 128:256].reshape(shape)
-            up_y = upper(patch_y, step_y)
-            share = up_y if patch_y == 0 else 1.0 - up_y
-            part_ref[patch_x, patch_y] = (mean[:, :, inside, :] + share * mix).reshape(rows, size)
-
-
-def add_far(first_patch, count, first_column, table, part_ref, pert_ref, staged, out_hbm, sems):
-    levels, _, _, size = staged.shape
+            share = upper_y[0] if patch_y == 0 else 1.0 - upper_y[1]
+            part_ref[patch_x, patch_y] = (mean[:, :, inside, :] + mixed(both, share, upper_x, shape)).reshape(rows, size)
+
+
+def add_far(first_patch, count, first_column, table, part_ref, pert_ref, keep):
+    levels, size = part_ref.shape[2] // (SPACING // 2) ** 2, part_ref.shape[3]
     span = SPACING // 2
     shape = (levels, span, span, size)
-    step_x = lax.broadcasted_iota(jnp.int32, shape, 1).astype(jnp.float32)
-    step_y = lax.broadcasted_iota(jnp.int32, shape, 2).astype(jnp.float32)
-    copies = []
+    along_x, upper_y = shares(levels, size)
     for k in range(count):
         patch_x = first_patch + k
         column = lax.div(patch_x + 1, 2) - first_column
         lanes = pl.ds(pl.multiple_of(128 * column, 128), 256)
-        up_x = (step_x + jnp.where(lax.rem(patch_x, 2) == 0, span + 0.5, 0.5)) / (2 * span)
+        upper_x = along_x + jnp.where(lax.rem(patch_x, 2) == 0, span + 0.5, 0.5) / (2 * span)
         results = []
         for patch_y in range(2):
             both = dot(pert_ref[patch_x, patch_y], table[patch_y, :, lanes])
-            mix = (1.0 - up_x) * both[:, 0:128].reshape(shape) + up_x * both[:, 128:256].reshape(shape)
-            up_y = upper(patch_y, step_y)
-            share = 1.0 - up_y if patch_y == 0 else up_y
-            results.append(part_ref[patch_x, patch_y].reshape(shape) + share * mix)
-        inside = pl.ds(patch_x * span, span)
-        staged[:, inside, :, :] = jnp.concatenate(results, axis=2).astype(jnp.bfloat16)
-        copy = pltpu.make_async_copy(staged.at[:, inside], out_hbm.at[:, inside], sems.at[k])
-        copy.start()
-        copies.append(copy)
-    for copy in copies:
-        copy.wait()
+            share = 1.0 - upper_y[0] if patch_y == 0 else upper_y[1]
+            results.append(part_ref[patch_x, patch_y].reshape(shape) + mixed(both, share, upper_x, shape))
+        keep(k, patch_x, jnp.concatenate(results, axis=2).astype(jnp.bfloat16))
 
 
 def neighbours(climb, descend, own, first, rows):
@@ -507,31 +520,50 @@
     return before, after
 
 
-def far_first_kernel(cols, part_ref, pert_ref, own, climb, descend, out_hbm, table, staged, sems):
-    half = cols // 2
+def far_first_kernel(cols, count, part_ref, pert_ref, own, climb, descend, out_ref, table):
+    half, span = cols // 2, SPACING // 2
     core = lax.rem(lax.axis_index("lev"), 2)
     for j in range(half):
         for z, value in enumerate(neighbours(climb, descend, own, core == 0, pl.ds(128 * j, 128))):
             table[z, :, 128 * j : 128 * (j + 1)] = value
-    count, total = sems.shape[0], part_ref.shape[0]
-    add_far(core * (total - count), count, core * half, table, part_ref, pert_ref, staged, out_hbm, sems)
+
+    def keep(k, _, value):
+        out_ref[:, k * span : (k + 1) * span] = value
+
+    add_far(core * (part_ref.shape[0] - count), count, core * half, table, part_ref, pert_ref, keep)
 
 
 def far_rest_kernel(
-    cols, part_ref, pert_ref, own, pair, climb, descend, pair_climb, pair_descend, begun_hbm, out_hbm, table, staged, sems
+    cols, count, part_ref, pert_ref, own, pair, climb, descend, pair_climb, pair_descend, begun, out_hbm, table, staged, sems
 ):
-    half = cols // 2
+    half, span = cols // 2, SPACING // 2
     core = lax.rem(lax.axis_index("lev"), 2)
     first = core == 0
+    total = part_ref.shape[0]
+    early = total - count
+    start = core * (total - early) * span
+    copies = [pltpu.make_async_copy(begun, out_hbm.at[:, pl.ds(start, early * span)], sems.at[count])]
+    copies[0].start()
     for j in range(half):
-        rows = pl.ds(128 * j, 128)
-        mine = neighbours(climb, descend, own, first, rows)
-        theirs = neighbours(pair_climb, pair_descend, pair, jnp.logical_not(first), rows)
-        for z, (x, y) in enumerate(zip(mine, theirs)):
-            table[z, :, 128 * j : 128 * (j + 1)] = jnp.where(first, x, y)
-            table[z, :, 128 * (j + half) : 128 * (j + half + 1)] = jnp.where(first, y, x)
-    count, total = sems.shape[0], part_ref.shape[0]
-    add_far((1 - core) * (total - count), count, 0, table, part_ref, pert_ref, staged, out_hbm, sems)
+        at = pl.multiple_of(128 * j + jnp.where(first, 128, 0), 128)
+        values = neighbours(pair_climb, pair_descend, pair, jnp.logical_not(first), pl.ds(128 * j, 128))
+        for z, value in enumerate(values):
+            table[z, :, pl.ds(at, 128)] = value
+    border = pl.ds(pl.multiple_of(jnp.where(first, 128 * (half - 1), 0), 128), 128)
+    at = pl.multiple_of(jnp.where(first, 0, 128 * half), 128)
+    for z, value in enumerate(neighbours(climb, descend, own, first, border)):
+        table[z, :, pl.ds(at, 128)] = value
+
+    def keep(k, patch_x, value):
+        inside = pl.ds(patch_x * span, span)
+        staged[:, inside] = value
+        copies.append(pltpu.make_async_copy(staged.at[:, inside], out_hbm.at[:, inside], sems.at[k]))
+        copies[-1].start()
+
+    first_column = jnp.where(first, half - 1, 0)
+    add_far((1 - core) * early, count, first_column, table, part_ref, pert_ref, keep)
+    for copy in copies:
+        copy.wait()
 
 
 def paired_device(
@@ -590,22 +622,31 @@
         flops=2 * tall * size * 4 * rows,
         name="gram_near",
     )
+    block_scratch = [
+        pltpu.VMEM((size, rows), f32),
+        pltpu.VMEM((rows, size), bf16),
+        pltpu.VMEM((tall, rows), bf16),
+    ]
+    near = device_call(
+        functools.partial(gram_next_kernel, rows, cols, 5),
+        (table, near, across_descend),
+        shape((tall, size), f32),
+        block_scratch,
+        flops=2 * tall * size * rows,
+        name="gram_next",
+    )
     mine, rest = device_call(
-        functools.partial(gram_far_kernel, rows, cols),
-        (table, near, across_climb, across_descend),
+        functools.partial(gram_last_kernel, rows, cols, 4),
+        (table, near, across_climb),
         [shape((size * half + 8, size), f32)] * 2,
-        [
-            pltpu.VMEM((size, 2 * rows), f32),
-            pltpu.VMEM((2 * rows, size), bf16),
-            pltpu.VMEM((tall, 2 * rows), bf16),
-        ],
-        flops=2 * tall * size * 2 * rows,
-        name="gram_far",
+        block_scratch,
+        flops=2 * tall * size * rows,
+        name="gram_last",
     )
     total, half_sum = device_call(
         functools.partial(join_kernel, half),
         (mine, send(rest, "core")),
-        [shape((size * half + 8, size), f32), shape((size * half + 16, size), bf16)],
+        [shape((size * half + 8, size), f32), shape((272, size), bf16)],
         name="join",
     )
     weights = device_call(
@@ -629,32 +670,28 @@
     )
     up, down, part = lax.optimization_barrier((up, down, part))
     pair_up, pair_down = send(up, "core"), send(down, "core")
-    early = cols - 3
-
-    def finish(kernel, name, operands, count, wide, alias):
-        return device_call(
-            functools.partial(kernel, cols),
-            operands,
-            shape(members.shape, bf16),
-            [
-                pltpu.VMEM((2, size, wide * size), bf16),
-                pltpu.VMEM(members.shape, bf16),
-                pltpu.SemaphoreType.DMA((count,)),
-            ],
-            flops=2 * levels * 8 * count * width_y * size * 2 * size,
-            name=name,
-            out_hbm=True,
-            alias=alias,
-        )
-
-    begun = finish(far_first_kernel, "far_first", (part, pert, weights, up, down), early, half, False)
-    return finish(
-        far_rest_kernel,
-        "far_rest",
+    early, span = cols // 2, SPACING // 2
+    begun = device_call(
+        functools.partial(far_first_kernel, cols, early),
+        (part, pert, weights, up, down),
+        shape((levels, early * span, width_y, size), bf16),
+        [pltpu.VMEM((2, size, half * size), bf16)],
+        flops=2 * levels * span * early * width_y * size * 2 * size,
+        name="far_first",
+    )
+    count = patches[0] - early
+    return device_call(
+        functools.partial(far_rest_kernel, cols, count),
         (part, pert, weights, pair, up, down, pair_up, pair_down, begun),
-        patches[0] - early,
-        cols,
-        True,
+        shape(members.shape, bf16),
+        [
+            pltpu.VMEM((2, size, (half + 1) * size), bf16),
+            pltpu.VMEM(members.shape, bf16),
+            pltpu.SemaphoreType.DMA((count + 1,)),
+        ],
+        flops=2 * levels * span * count * width_y * size * 2 * size,
+        name="far_rest",
+        out_hbm=True,
     )
 
 

time: 28.2 us -> 27.5 us (0.975)
  Pallas kernels: 7.04 us -> 6.58 us
    pallas_call x9 -> x10, Pallas kernels: 7.04 us -> 6.58 us  [device_call(): pl.pallas_call(kernel, out_shape=out_shape, in_specs=[hbm if in_hbm else...]
  transfers between devices with their start and end apart: 12 -> 12, of which waited for: 8 -> 8; matrix products, arithmetic and copies ran while one was open for 0% -> 0% of each run, Pallas kernels for 9% -> 8%
where the time goes in v6:
time: 27.5 us; the launch traced here: 27.4 us
  starting transfers between devices  12 us (44%)
  waiting for transfers between devices  8.66 us (31%)
  Pallas kernels  6.58 us (24%)
    ppermute x12, starting transfers between devices, send(): return lax.ppermute(value, axes, ways[way])  12 us
    ppermute x12, waiting for transfers between devices, send(): return lax.ppermute(value, axes, ways[way])  8.66 us
    pallas_call x10, Pallas kernels, device_call(): pl.pallas_call(kernel, out_shape=out_shape, in_specs=[hbm if in_hbm else...  6.58 us
  transfers between devices with their start and end apart: 12, of which 8 were waited for; matrix products, arithmetic and copies ran while one was open for 0% of the time, Pallas kernels for 8%

profile of v6, /device:TPU:0, one launch (start us, length us, event | category | flops | bytes accessed | tf_op | source)
XLA Modules:
  0.0 27.4 jit_solution(14142495247779664099)
XLA Ops:
  0.0 1.0 %pack.1.b0 = bf16[272,128]{1,0:T(8,128)(2,1)S(1)} custom-call(bf16[256,128]{1,0:T(8,128)(2,1)} %pert.1, bf16[2,128]{1,0:T(2,128)(2,1)} %bitcast.5, bf16[2,128]{1,0:T(2,128)(2,1)} %bitcast.6, s32[4,1,256]{2,1,0:T(1,128)} %owner_ref.1, s32[4,1,256]{2,1,0:T(1,128)} %slot_ref.1, s32[1,4]{1,0:T(1,128)} %bitcast.3, f32[4,1,256]{2,1,0:T(1,128)} %local_ref.1), custom_call_target="tpu_custom_call" | custom-call | bytes 262144 | tf_op jit(solution)/shard_map/pack/pallas_call | solution.py:210
  1.0 3.1 %collective-permute-start = (bf16[272,128]{1,0:T(8,128)(2,1)S(1)}, bf16[272,128]{1,0:T(8,128)(2,1)S(1)}, u32[]{:S(2)}, u32[]{:S(2)}) collective-permute-start(bf16[272,128]{1,0:T(8,128)(2,1)S(1)} %pack.1.b0), channel_id=1, source_target_pairs={{0,16},{1,17},{2,18},{3,19},{4,20},{5,21},{6,22},{7,23},{8,24},{9,... | collective-permute-start | bytes 208904 | tf_op jit(solution)/shard_map/ppermute | solution.py:576
  4.1 2.0 %collective-permute-start.1 = (bf16[272,128]{1,0:T(8,128)(2,1)S(1)}, bf16[272,128]{1,0:T(8,128)(2,1)S(1)}, u32[]{:S(2)}, u32[]{:S(2)}) collective-permute-start(bf16[272,128]{1,0:T(8,128)(2,1)S(1)} %pack.1.b0), channel_id=1, source_target_pairs={{0,4},{1,0},{2,6},{3,2},{4,8},{5,1},{6,10},{7,3},{8,12},{9,5},{10,... | collective-permute-start | bytes 208904 | tf_op jit(solution)/shard_map/ppermute | solution.py:576
  6.1 0.3 collective-permute-done.other_ref.b3
  6.4 2.1 %collective-permute-start.4 = (bf16[272,128]{1,0:T(8,128)(2,1)S(1)}, bf16[272,128]{1,0:T(8,128)(2,1)S(1)}, u32[]{:S(2)}, u32[]{:S(2)}) collective-permute-start(bf16[272,128]{1,0:T(8,128)(2,1)S(1)} %collective-permute-done.other_ref.b3), channel_id=1, source_target_pairs={{0,4},{1,0},{2,6},{3,2},{4,8},{5,1},{6,10},{7,3},{8,12},{9,5},{10,... | collective-permute-start | bytes 208904 | tf_op jit(solution)/shard_map/ppermute | solution.py:576
  8.5 0.5 %table.1.table_ref = f32[128,128]{1,0:T(8,128)S(1)} custom-call(s32[4,1,256]{2,1,0:T(1,128)S(1)} %copy-done.1, s32[4,1,256]{2,1,0:T(1,128)S(1)} %copy-done.2, s32[1,4]{1,0:T(1,128)S(1)} %bitcast.4, f32[4,1,256]{2,1,0:T(1,128)S(1)} %copy-done.3, bf16[272,128]{1,0:T(8,128)(2,1)S(1)} %collective-permute-done.other_ref.b3), custom_call_target="tpu_custom_call" | custom-call | flops 18874368 | bytes 262144 | tf_op jit(solution)/shard_map/table/pallas_call | solution.py:210
  9.0 0.1 collective-permute-done.2.b2
  9.1 0.6 %gram_near.1.so_far_ref = f32[784,128]{1,0:T(8,128)S(1)} custom-call(f32[128,128]{1,0:T(8,128)S(1)} %table.1.table_ref, bf16[272,128]{1,0:T(8,128)(2,1)S(1)} %pack.1.b0, bf16[272,128]{1,0:T(8,128)(2,1)S(1)} %collective-permute-done.1.b1, bf16[272,128]{1,0:T(8,128)(2,1)S(1)} %collective-permute-done.2.b2, bf16[272,128]{1,0:T(8,128)(2,1)S(1)} %collective-permute-done.other_ref.b3), custom_call_target="tpu_custom_call" | custom-call | flops 205520896 | bytes 262144 | tf_op jit(solution)/shard_map/gram_near/pallas_call | solution.py:210
  9.7 1.3 %collective-permute-done.3.block = bf16[272,128]{1,0:T(8,128)(2,1)S(1)} collective-permute-done((bf16[272,128]{1,0:T(8,128)(2,1)S(1)}, bf16[272,128]{1,0:T(8,128)(2,1)S(1)}, u32[]{:S(2)}, u32[]{:S(2)}) %collective-permute-start.3) | collective-permute-done | bytes 69664 | tf_op jit(solution)/shard_map/ppermute | solution.py:576
  11.0 0.3 %gram_next.1.so_far_ref = f32[784,128]{1,0:T(8,128)S(1)} custom-call(f32[128,128]{1,0:T(8,128)S(1)} %table.1.table_ref, f32[784,128]{1,0:T(8,128)S(1)} %gram_near.1.so_far_ref, bf16[272,128]{1,0:T(8,128)(2,1)S(1)} %collective-permute-done.3.block), custom_call_target="tpu_custom_call" | custom-call | flops 51380224 | bytes 262144 | tf_op jit(solution)/shard_map/gram_next/pallas_call | solution.py:210
  11.3 0.3 %gram_last.1 = (f32[392,128]{1,0:T(8,128)S(1)}, f32[392,128]{1,0:T(8,128)S(1)}) custom-call(f32[128,128]{1,0:T(8,128)S(1)} %table.1.table_ref, f32[784,128]{1,0:T(8,128)S(1)} %gram_next.1.so_far_ref, bf16[272,128]{1,0:T(8,128)(2,1)S(1)} %collective-permute-done.4.block), custom_call_target="tpu_custom_call" | custom-call | flops 51380224 | bytes 262144 | tf_op jit(solution)/shard_map/gram_last/pallas_call | solution.py:210
  11.7 1.4 %collective-permute-done.5.got_ref = f32[392,128]{1,0:T(8,128)S(1)} collective-permute-done((f32[392,128]{1,0:T(8,128)S(1)}, f32[392,128]{1,0:T(8,128)S(1)}, u32[]{:S(2)}, u32[]{:S(2)}) %collective-permute-start.5) | collective-permute-done | bytes 200736 | tf_op jit(solution)/shard_map/ppermute | solution.py:576
  13.2 1.8 %collective-permute-start.6 = (bf16[272,128]{1,0:T(8,128)(2,1)S(1)}, bf16[272,128]{1,0:T(8,128)(2,1)S(1)}, u32[]{:S(2)}, u32[]{:S(2)}) collective-permute-start(bf16[272,128]{1,0:T(8,128)(2,1)S(1)} %get-tuple-element.17), channel_id=1, source_target_pairs={{0,2},{1,3},{2,0},{3,1},{4,6},{5,7},{6,4},{7,5},{8,10},{9,11},{10,... | collective-permute-start | bytes 208904 | tf_op jit(solution)/shard_map/ppermute | solution.py:576
  15.0 2.6 %collective-permute-done.6.got_ref = bf16[272,128]{1,0:T(8,128)(2,1)S(1)} collective-permute-done((bf16[272,128]{1,0:T(8,128)(2,1)S(1)}, bf16[272,128]{1,0:T(8,128)(2,1)S(1)}, u32[]{:S(2)}, u32[]{:S(2)}) %collective-permute-start.6) | collective-permute-done | bytes 69664 | tf_op jit(solution)/shard_map/ppermute | solution.py:576
  17.6 1.8 %solve.1.own = bf16[384,128]{1,0:T(8,128)(2,1)S(1)} custom-call(f32[392,128]{1,0:T(8,128)S(1)} %get-tuple-element.16.sum_ref, bf16[272,128]{1,0:T(8,128)(2,1)S(1)} %collective-permute-done.6.got_ref), custom_call_target="tpu_custom_call" | custom-call | flops 339738624 | bytes 262144 | tf_op jit(solution)/shard_map/solve/pallas_call | solution.py:210
  19.5 0.5 %collective-permute-start.8 = (bf16[384,128]{1,0:T(8,128)(2,1)S(1)}, bf16[384,128]{1,0:T(8,128)(2,1)S(1)}, u32[]{:S(2)}, u32[]{:S(2)}) collective-permute-start(bf16[384,128]{1,0:T(8,128)(2,1)S(1)} %solve.1.own), channel_id=1, source_target_pairs={{4,0},{0,1},{6,2},{2,3},{8,4},{1,5},{10,6},{3,7},{12,8},{5,9},{14,... | collective-permute-start | bytes 294920 | tf_op jit(solution)/shard_map/ppermute | solution.py:576
  20.0 1.5 %collective-permute-start.7 = (bf16[384,128]{1,0:T(8,128)(2,1)S(1)}, bf16[384,128]{1,0:T(8,128)(2,1)S(1)}, u32[]{:S(2)}, u32[]{:S(2)}) collective-permute-start(bf16[384,128]{1,0:T(8,128)(2,1)S(1)} %solve.1.own), channel_id=1, source_target_pairs={{0,4},{1,0},{2,6},{3,2},{4,8},{5,1},{6,10},{7,3},{8,12},{9,5},{10,... | collective-permute-start | bytes 294920 | tf_op jit(solution)/shard_map/ppermute | solution.py:576
  21.5 0.6 %apply_near.1 = (f32[8,2,128,128]{3,2,1,0:T(8,128)S(1)}, bf16[8,2,128,128]{3,2,1,0:T(8,128)(2,1)S(1)}) custom-call(bf16[2,64,16,128]{3,2,1,0:T(8,128)(2,1)S(1)} %copy-done, bf16[384,128]{1,0:T(8,128)(2,1)S(1)} %solve.1.own, bf16[384,128]{1,0:T(8,128)(2,1)S(1)} %collective-permute-done.9.pair), custom_call_target="tpu_custom_call" | custom-call | flops 134217728 | bytes 262144 | tf_op jit(solution)/shard_map/apply_near/pallas_call | solution.py:210
  22.1 2.0 %collective-permute-done.8.descend = bf16[384,128]{1,0:T(8,128)(2,1)S(1)} collective-permute-done((bf16[384,128]{1,0:T(8,128)(2,1)S(1)}, bf16[384,128]{1,0:T(8,128)(2,1)S(1)}, u32[]{:S(2)}, u32[]{:S(2)}) %collective-permute-start.8) | collective-permute-done | bytes 98336 | tf_op jit(solution)/shard_map/ppermute | solution.py:576
  24.1 0.9 %collective-permute-start.10 = (bf16[384,128]{1,0:T(8,128)(2,1)S(1)}, bf16[384,128]{1,0:T(8,128)(2,1)S(1)}, u32[]{:S(2)}, u32[]{:S(2)}) collective-permute-start(bf16[384,128]{1,0:T(8,128)(2,1)S(1)} %collective-permute-done.7.climb), channel_id=1, source_target_pairs={{0,1},{1,0},{2,3},{3,2},{4,5},{5,4},{6,7},{7,6},{8,9},{9,8},{10,11... | collective-permute-start | bytes 294920 | tf_op jit(solution)/shard_map/ppermute | solution.py:576
  25.0 0.3 %far_first.1.begun = bf16[2,24,16,128]{3,2,1,0:T(8,128)(2,1)S(1)} custom-call(f32[8,2,128,128]{3,2,1,0:T(8,128)S(1)} %get-tuple-element.19.part_ref, bf16[8,2,128,128]{3,2,1,0:T(8,128)(2,1)S(1)} %get-tuple-element.20.pert_ref, bf16[384,128]{1,0:T(8,128)(2,1)S(1)} %solve.1.own, bf16[384,128]{1,0:T(8,128)(2,1)S(1)} %collective-permute-done.7.climb, ...), custom_call_target="tpu_custom_call" | custom-call | flops 50331648 | bytes 262144 | tf_op jit(solution)/shard_map/far_first/pallas_call | solution.py:210
  25.3 0.6 %collective-permute-done.10.pair_climb = bf16[384,128]{1,0:T(8,128)(2,1)S(1)} collective-permute-done((bf16[384,128]{1,0:T(8,128)(2,1)S(1)}, bf16[384,128]{1,0:T(8,128)(2,1)S(1)}, u32[]{:S(2)}, u32[]{:S(2)}) %collective-permute-start.10) | collective-permute-done | bytes 98336 | tf_op jit(solution)/shard_map/ppermute | solution.py:576
  25.9 0.4 %collective-permute-done.11.pair_descend = bf16[384,128]{1,0:T(8,128)(2,1)S(1)} collective-permute-done((bf16[384,128]{1,0:T(8,128)(2,1)S(1)}, bf16[384,128]{1,0:T(8,128)(2,1)S(1)}, u32[]{:S(2)}, u32[]{:S(2)}) %collective-permute-start.11) | collective-permute-done | bytes 98336 | tf_op jit(solution)/shard_map/ppermute | solution.py:576
  26.3 1.1 %far_rest.1 = bf16[2,64,16,128]{3,2,1,0:T(8,128)(2,1)} custom-call(f32[8,2,128,128]{3,2,1,0:T(8,128)S(1)} %get-tuple-element.19.part_ref, bf16[8,2,128,128]{3,2,1,0:T(8,128)(2,1)S(1)} %get-tuple-element.20.pert_ref, bf16[384,128]{1,0:T(8,128)(2,1)S(1)} %solve.1.own, bf16[384,128]{1,0:T(8,128)(2,1)S(1)} %collective-permute-done.9.pair, ...), custom_call_target="tpu_custom_call" | custom-call | flops 83886080 | bytes 262144 | tf_op jit(solution)/shard_map/far_rest/pallas_call | solution.py:210
  (20 shorter events, 0.3 us)
Async XLA Ops:
  0.0 8.5 %copy-start.1 = (s32[4,1,256]{2,1,0:T(1,128)S(1)}, s32[4,1,256]{2,1,0:T(1,128)}, u32[]{:S(2)}) copy-start(s32[4,1,256]{2,1,0:T(1,128)} %owner_ref.1) | copy-start | bytes 12292
  0.0 8.5 %copy-start.2 = (s32[4,1,256]{2,1,0:T(1,128)S(1)}, s32[4,1,256]{2,1,0:T(1,128)}, u32[]{:S(2)}) copy-start(s32[4,1,256]{2,1,0:T(1,128)} %slot_ref.1) | copy-start | bytes 12292
  0.0 8.5 %copy-start.3 = (f32[4,1,256]{2,1,0:T(1,128)S(1)}, f32[4,1,256]{2,1,0:T(1,128)}, u32[]{:S(2)}) copy-start(f32[4,1,256]{2,1,0:T(1,128)} %local_ref.1) | copy-start | bytes 12292
  0.0 8.5 %copy-start.4 = (s32[4,1]{0,1:T(1,128)S(1)}, s32[4,1]{0,1:T(1,128)}, u32[]{:S(2)}) copy-start(s32[4,1]{0,1:T(1,128)} %param.14) | copy-start | bytes 52
  1.0 5.4 %collective-permute-start = (bf16[272,128]{1,0:T(8,128)(2,1)S(1)}, bf16[272,128]{1,0:T(8,128)(2,1)S(1)}, u32[]{:S(2)}, u32[]{:S(2)}) collective-permute-start(bf16[272,128]{1,0:T(8,128)(2,1)S(1)} %pack.1.b0), channel_id=1, source_target_pairs={{0,16},{1,17},{2,18},{3,19},{4,20},{5,21},{6,22},{7,23},{8,24},{9,... | collective-permute-start | bytes 208904 | tf_op jit(solution)/shard_map/ppermute | solution.py:576
  4.1 4.9 %collective-permute-start.2 = (bf16[272,128]{1,0:T(8,128)(2,1)S(1)}, bf16[272,128]{1,0:T(8,128)(2,1)S(1)}, u32[]{:S(2)}, u32[]{:S(2)}) collective-permute-start(bf16[272,128]{1,0:T(8,128)(2,1)S(1)} %pack.1.b0), channel_id=1, source_target_pairs={{4,0},{0,1},{6,2},{2,3},{8,4},{1,5},{10,6},{3,7},{12,8},{5,9},{14,... | collective-permute-start | bytes 208904 | tf_op jit(solution)/shard_map/ppermute | solution.py:576
  4.1 4.9 %collective-permute-start.1 = (bf16[272,128]{1,0:T(8,128)(2,1)S(1)}, bf16[272,128]{1,0:T(8,128)(2,1)S(1)}, u32[]{:S(2)}, u32[]{:S(2)}) collective-permute-start(bf16[272,128]{1,0:T(8,128)(2,1)S(1)} %pack.1.b0), channel_id=1, source_target_pairs={{0,4},{1,0},{2,6},{3,2},{4,8},{5,1},{6,10},{7,3},{8,12},{9,5},{10,... | collective-permute-start | bytes 208904 | tf_op jit(solution)/shard_map/ppermute | solution.py:576
  6.4 4.6 %collective-permute-start.3 = (bf16[272,128]{1,0:T(8,128)(2,1)S(1)}, bf16[272,128]{1,0:T(8,128)(2,1)S(1)}, u32[]{:S(2)}, u32[]{:S(2)}) collective-permute-start(bf16[272,128]{1,0:T(8,128)(2,1)S(1)} %collective-permute-done.other_ref.b3), channel_id=1, source_target_pairs={{4,0},{0,1},{6,2},{2,3},{8,4},{1,5},{10,6},{3,7},{12,8},{5,9},{14,... | collective-permute-start | bytes 208904 | tf_op jit(solution)/shard_map/ppermute | solution.py:576
  6.4 4.9 %collective-permute-start.4 = (bf16[272,128]{1,0:T(8,128)(2,1)S(1)}, bf16[272,128]{1,0:T(8,128)(2,1)S(1)}, u32[]{:S(2)}, u32[]{:S(2)}) collective-permute-start(bf16[272,128]{1,0:T(8,128)(2,1)S(1)} %collective-permute-done.other_ref.b3), channel_id=1, source_target_pairs={{0,4},{1,0},{2,6},{3,2},{4,8},{5,1},{6,10},{7,3},{8,12},{9,5},{10,... | collective-permute-start | bytes 208904 | tf_op jit(solution)/shard_map/ppermute | solution.py:576
  11.6 1.5 %collective-permute-start.5 = (f32[392,128]{1,0:T(8,128)S(1)}, f32[392,128]{1,0:T(8,128)S(1)}, u32[]{:S(2)}, u32[]{:S(2)}) collective-permute-start(f32[392,128]{1,0:T(8,128)S(1)} %get-tuple-element.15), channel_id=1, source_target_pairs={{0,1},{1,0},{2,3},{3,2},{4,5},{5,4},{6,7},{7,6},{8,9},{9,8},{10,11... | collective-permute-start | bytes 602120 | tf_op jit(solution)/shard_map/ppermute | solution.py:576
  13.2 4.4 %collective-permute-start.6 = (bf16[272,128]{1,0:T(8,128)(2,1)S(1)}, bf16[272,128]{1,0:T(8,128)(2,1)S(1)}, u32[]{:S(2)}, u32[]{:S(2)}) collective-permute-start(bf16[272,128]{1,0:T(8,128)(2,1)S(1)} %get-tuple-element.17), channel_id=1, source_target_pairs={{0,2},{1,3},{2,0},{3,1},{4,6},{5,7},{6,4},{7,5},{8,10},{9,11},{10,... | collective-permute-start | bytes 208904 | tf_op jit(solution)/shard_map/ppermute | solution.py:576
  17.6 3.9 %copy-start = (bf16[2,64,16,128]{3,2,1,0:T(8,128)(2,1)S(1)}, bf16[2,64,16,128]{3,2,1,0:T(8,128)(2,1)}, u32[]{:S(2)}) copy-start(bf16[2,64,16,128]{3,2,1,0:T(8,128)(2,1)} %members_ref.1) | copy-start | bytes 1572868
  19.4 2.1 %collective-permute-start.9 = (bf16[384,128]{1,0:T(8,128)(2,1)S(1)}, bf16[384,128]{1,0:T(8,128)(2,1)S(1)}, u32[]{:S(2)}, u32[]{:S(2)}) collective-permute-start(bf16[384,128]{1,0:T(8,128)(2,1)S(1)} %solve.1.own), channel_id=1, source_target_pairs={{0,1},{1,0},{2,3},{3,2},{4,5},{5,4},{6,7},{7,6},{8,9},{9,8},{10,11... | collective-permute-start | bytes 294920 | tf_op jit(solution)/shard_map/ppermute | solution.py:576
  19.5 4.6 %collective-permute-start.8 = (bf16[384,128]{1,0:T(8,128)(2,1)S(1)}, bf16[384,128]{1,0:T(8,128)(2,1)S(1)}, u32[]{:S(2)}, u32[]{:S(2)}) collective-permute-start(bf16[384,128]{1,0:T(8,128)(2,1)S(1)} %solve.1.own), channel_id=1, source_target_pairs={{4,0},{0,1},{6,2},{2,3},{8,4},{1,5},{10,6},{3,7},{12,8},{5,9},{14,... | collective-permute-start | bytes 294920 | tf_op jit(solution)/shard_map/ppermute | solution.py:576
  20.0 4.1 %collective-permute-start.7 = (bf16[384,128]{1,0:T(8,128)(2,1)S(1)}, bf16[384,128]{1,0:T(8,128)(2,1)S(1)}, u32[]{:S(2)}, u32[]{:S(2)}) collective-permute-start(bf16[384,128]{1,0:T(8,128)(2,1)S(1)} %solve.1.own), channel_id=1, source_target_pairs={{0,4},{1,0},{2,6},{3,2},{4,8},{5,1},{6,10},{7,3},{8,12},{9,5},{10,... | collective-permute-start | bytes 294920 | tf_op jit(solution)/shard_map/ppermute | solution.py:576
  24.1 1.8 %collective-permute-start.10 = (bf16[384,128]{1,0:T(8,128)(2,1)S(1)}, bf16[384,128]{1,0:T(8,128)(2,1)S(1)}, u32[]{:S(2)}, u32[]{:S(2)}) collective-permute-start(bf16[384,128]{1,0:T(8,128)(2,1)S(1)} %collective-permute-done.7.climb), channel_id=1, source_target_pairs={{0,1},{1,0},{2,3},{3,2},{4,5},{5,4},{6,7},{7,6},{8,9},{9,8},{10,11... | collective-permute-start | bytes 294920 | tf_op jit(solution)/shard_map/ppermute | solution.py:576
  25.0 1.3 %collective-permute-start.11 = (bf16[384,128]{1,0:T(8,128)(2,1)S(1)}, bf16[384,128]{1,0:T(8,128)(2,1)S(1)}, u32[]{:S(2)}, u32[]{:S(2)}) collective-permute-start(bf16[384,128]{1,0:T(8,128)(2,1)S(1)} %collective-permute-done.8.descend), channel_id=1, source_target_pairs={{0,1},{1,0},{2,3},{3,2},{4,5},{5,4},{6,7},{7,6},{8,9},{9,8},{10,11... | collective-permute-start | bytes 294920 | tf_op jit(solution)/shard_map/ppermute | solution.py:576

commit v7 on v6

--- a/solution.py
+++ b/solution.py
@@ -402,14 +402,20 @@
     return dot(beside(a_high, a_low), above(b_high, b_high)) + dot(a_high, b_low)
 
 
+def wide(a, b):
+    return beside(a[0], b[0]), beside(a[1], b[1])
+
+
+def vector_product(rows, parts):
+    left = above(*[p.astype(jnp.float32) for p in split2(rows)]).astype(jnp.bfloat16)
+    full = dot(left, parts[0]) + dot(left, parts[1])
+    return full[0:8] + full[8:16]
+
+
 def solve_kernel(half, sum_ref, got_ref, out_ref):
     size = 128
     spread = float(size - 1)
-    eye = jnp.where(
-        lax.broadcasted_iota(jnp.int32, (size, size), 0) == lax.broadcasted_iota(jnp.int32, (size, size), 1),
-        1.0,
-        0.0,
-    )
+    eye = identity(size)
     edge = size * half
     got = got_ref[...].astype(jnp.float32)
     projected = sum_ref[edge : edge + 8, :] + got[256:264] + got[264:272]
@@ -431,25 +437,40 @@
         )
         for base, square in zip(bases, squares)
     ]
-    for _ in range(NS_STEPS - 2):
+    vectors = [jnp.broadcast_to(projected[k : k + 1, :], (8, size)) for k in range(half)]
+    pushed = [vector_product(v, parts) for v, parts in zip(vectors, base_parts)]
+    carried = None
+    for step in range(NS_STEPS - 2):
+        last = step == NS_STEPS - 3
         inverse_parts = [split2(z) for z in inverses]
-        both = [
-            product(z, (beside(b[0], z[0]), beside(b[1], z[1]))) for b, z in zip(base_parts, inverse_parts)
-        ]
-        inverses = [
-            1.5 * z - 0.5 * product(split2(x[:, 0:size]), split2(x[:, size : 2 * size])) for z, x in zip(inverses, both)
-        ]
-    for k in range(half):
-        inverse, norm = inverses[k], norms[k]
-        parts = split2(inverse)
-        vector = split3(jnp.broadcast_to(projected[k : k + 1, :], (16, size)))
-        inner = jnp.zeros((16, size), jnp.float32)
-        for piece in vector[:2]:
-            for part in parts:
-                inner = inner + dot(piece, part, ((1,), (1,)))
-        mean_weights = jnp.sum(inverse * inner[0:1, :], axis=1, keepdims=True) / norm
-        transform = (jnp.sqrt(spread) / jnp.sqrt(norm)) * inverse + mean_weights
-        out_ref[size * k : size * (k + 1), :] = transform.astype(jnp.bfloat16)
+        left = [split2(above(z, v, q)) for z, v, q in zip(inverses, vectors, pushed)] if last else inverse_parts
+        both = [product(z, wide(b, y)) for z, b, y in zip(left, base_parts, inverse_parts)]
+        forced = [x[:, 0:size] for x in both]
+        square = [split2(x[0:size, size : 2 * size]) for x in both]
+        if last:
+            forced = [above(f[0:size], x[size + 8 : size + 16, size:], x[size + 8 : size + 16, size:]) for f, x in zip(forced, both)]
+        cubes = [product(split2(f), y) for f, y in zip(forced, square)]
+        if last:
+            carried = [1.5 * x[size : size + 8, size:] - 0.5 * c[size : size + 8] for x, c in zip(both, cubes)]
+        inverses = [1.5 * z - 0.5 * c[0:size] for z, c in zip(inverses, cubes)]
+    scaled = [(jnp.sqrt(spread) / jnp.sqrt(norm)) * inverse for norm, inverse in zip(norms, inverses)]
+    means = [
+        vector_product(v, split2(inverse))[0:1] / norm for norm, inverse, v in zip(norms, inverses, carried)
+    ]
+    rest = jnp.zeros((8 - half, size), jnp.float32)
+    high, low = split2(above(*means, rest))
+    tail = above(high.astype(jnp.float32), low.astype(jnp.float32))
+    out_ref[...] = above(fold(scaled), tail).astype(jnp.bfloat16)
+
+
+def rebuild(folded, k, eye):
+    means = folded[256 + k : 257 + k] + folded[264 + k : 265 + k]
+    return (unfold(folded, k, eye) + means).astype(jnp.bfloat16)
+
+
+def identity(size):
+    same = lax.broadcasted_iota(jnp.int32, (size, size), 0) == lax.broadcasted_iota(jnp.int32, (size, size), 1)
+    return jnp.where(same, 1.0, 0.0)
 
 
 def shares(levels, size):
@@ -469,11 +490,11 @@
 def near_kernel(cols, members_ref, own, pair, part_ref, pert_ref, table):
     half = cols // 2
     first = lax.rem(lax.axis_index("lev"), 2) == 0
-    for j in range(half):
-        rows = pl.ds(128 * j, 128)
-        a, b = own[rows, :], pair[rows, :]
-        table[:, 128 * j : 128 * (j + 1)] = jnp.where(first, a, b)
-        table[:, 128 * (j + half) : 128 * (j + half + 1)] = jnp.where(first, b, a)
+    eye = identity(128)
+    mine, theirs = own[...].astype(jnp.float32), pair[...].astype(jnp.float32)
+    for at, folded in ((0, jnp.where(first, mine, theirs)), (half, jnp.where(first, theirs, mine))):
+        for j in range(half):
+            table[128 * (at + j) : 128 * (at + j + 1), :] = rebuild(folded, j, eye)
     levels, width_x, width_y, size = members_ref.shape
     span = SPACING // 2
     shape = (levels, span, span, size)
@@ -489,7 +510,7 @@
             inside = slice(patch_y * span, (patch_y + 1) * span)
             left = moved[:, :, inside, :].reshape(rows, size).astype(jnp.bfloat16)
             pert_ref[patch_x, patch_y] = left
-            both = dot(left, table[:, 128 * column : 128 * (column + 2)])
+            both = dot(left, table[128 * column : 128 * (column + 2), :], ((1,), (1,)))
             share = upper_y[0] if patch_y == 0 else 1.0 - upper_y[1]
             part_ref[patch_x, patch_y] = (mean[:, :, inside, :] + mixed(both, share, upper_x, shape)).reshape(rows, size)
 
@@ -502,30 +523,33 @@
     for k in range(count):
         patch_x = first_patch + k
         column = lax.div(patch_x + 1, 2) - first_column
-        lanes = pl.ds(pl.multiple_of(128 * column, 128), 256)
+        lines = pl.ds(pl.multiple_of(128 * column, 128), 256)
         upper_x = along_x + jnp.where(lax.rem(patch_x, 2) == 0, span + 0.5, 0.5) / (2 * span)
         results = []
         for patch_y in range(2):
-            both = dot(pert_ref[patch_x, patch_y], table[patch_y, :, lanes])
+            both = dot(pert_ref[patch_x, patch_y], table[patch_y, lines, :], ((1,), (1,)))
             share = 1.0 - upper_y[0] if patch_y == 0 else upper_y[1]
             results.append(part_ref[patch_x, patch_y].reshape(shape) + mixed(both, share, upper_x, shape))
         keep(k, patch_x, jnp.concatenate(results, axis=2).astype(jnp.bfloat16))
 
 
-def neighbours(climb, descend, own, first, rows):
+def neighbours(climb, descend, own, first):
     tile_y = lax.axis_index("ty")
-    up, down, mine = climb[rows, :], descend[rows, :], own[rows, :]
+    up, down, mine = (ref[...].astype(jnp.float32) for ref in (climb, descend, own))
     before = jnp.where(tile_y == 0, mine, jnp.where(first, up, down))
     after = jnp.where(tile_y == lax.axis_size("ty") - 1, mine, jnp.where(first, down, up))
     return before, after
 
 
-def far_first_kernel(cols, count, part_ref, pert_ref, own, climb, descend, out_ref, table):
+def far_first_kernel(cols, count, part_ref, pert_ref, own, climb, descend, out_ref, border_ref, table):
     half, span = cols // 2, SPACING // 2
     core = lax.rem(lax.axis_index("lev"), 2)
-    for j in range(half):
-        for z, value in enumerate(neighbours(climb, descend, own, core == 0, pl.ds(128 * j, 128))):
-            table[z, :, 128 * j : 128 * (j + 1)] = value
+    eye = identity(128)
+    for z, folded in enumerate(neighbours(climb, descend, own, core == 0)):
+        for j in range(half):
+            table[z, 128 * j : 128 * (j + 1), :] = rebuild(folded, j, eye)
+    border = jnp.where(core == 0, half - 1, 0)
+    border_ref[...] = table[:, pl.ds(pl.multiple_of(128 * border, 128), 128), :]
 
     def keep(k, _, value):
         out_ref[:, k * span : (k + 1) * span] = value
@@ -534,7 +558,7 @@
 
 
 def far_rest_kernel(
-    cols, count, part_ref, pert_ref, own, pair, climb, descend, pair_climb, pair_descend, begun, out_hbm, table, staged, sems
+    cols, count, part_ref, pert_ref, pair, pair_climb, pair_descend, begun, border_ref, out_hbm, table, staged, sems
 ):
     half, span = cols // 2, SPACING // 2
     core = lax.rem(lax.axis_index("lev"), 2)
@@ -544,15 +568,13 @@
     start = core * (total - early) * span
     copies = [pltpu.make_async_copy(begun, out_hbm.at[:, pl.ds(start, early * span)], sems.at[count])]
     copies[0].start()
-    for j in range(half):
-        at = pl.multiple_of(128 * j + jnp.where(first, 128, 0), 128)
-        values = neighbours(pair_climb, pair_descend, pair, jnp.logical_not(first), pl.ds(128 * j, 128))
-        for z, value in enumerate(values):
-            table[z, :, pl.ds(at, 128)] = value
-    border = pl.ds(pl.multiple_of(jnp.where(first, 128 * (half - 1), 0), 128), 128)
+    eye = identity(128)
+    for z, folded in enumerate(neighbours(pair_climb, pair_descend, pair, jnp.logical_not(first))):
+        for j in range(half):
+            at = pl.multiple_of(128 * j + jnp.where(first, 128, 0), 128)
+            table[z, pl.ds(at, 128), :] = rebuild(folded, j, eye)
     at = pl.multiple_of(jnp.where(first, 0, 128 * half), 128)
-    for z, value in enumerate(neighbours(climb, descend, own, first, border)):
-        table[z, :, pl.ds(at, 128)] = value
+    table[:, pl.ds(at, 128), :] = border_ref[...]
 
     def keep(k, patch_x, value):
         inside = pl.ds(patch_x * span, span)
@@ -652,7 +674,7 @@
     weights = device_call(
         functools.partial(solve_kernel, half),
         (total, send(half_sum, "half")),
-        shape((size * half, size), bf16),
+        shape((272, size), bf16),
         flops=2 * 27 * half * size**3,
         name="solve",
     )
@@ -664,28 +686,28 @@
         functools.partial(near_kernel, cols),
         (members, weights, pair),
         [shape(patches, f32), shape(patches, bf16)],
-        [pltpu.VMEM((size, cols * size), bf16)],
+        [pltpu.VMEM((cols * size, size), bf16)],
         flops=2 * levels * width_x * width_y * size * 2 * size,
         name="apply_near",
     )
     up, down, part = lax.optimization_barrier((up, down, part))
     pair_up, pair_down = send(up, "core"), send(down, "core")
     early, span = cols // 2, SPACING // 2
-    begun = device_call(
+    begun, border = device_call(
         functools.partial(far_first_kernel, cols, early),
         (part, pert, weights, up, down),
-        shape((levels, early * span, width_y, size), bf16),
-        [pltpu.VMEM((2, size, half * size), bf16)],
+        [shape((levels, early * span, width_y, size), bf16), shape((2, size, size), bf16)],
+        [pltpu.VMEM((2, half * size, size), bf16)],
         flops=2 * levels * span * early * width_y * size * 2 * size,
         name="far_first",
     )
     count = patches[0] - early
     return device_call(
         functools.partial(far_rest_kernel, cols, count),
-        (part, pert, weights, pair, up, down, pair_up, pair_down, begun),
+        (part, pert, pair, pair_up, pair_down, begun, border),
         shape(members.shape, bf16),
         [
-            pltpu.VMEM((2, size, (half + 1) * size), bf16),
+            pltpu.VMEM((2, (half + 1) * size, size), bf16),
             pltpu.VMEM(members.shape, bf16),
             pltpu.SemaphoreType.DMA((count + 1,)),
         ],

time: 27.5 us -> 27.2 us (0.989)
  waiting for transfers between devices: 8.66 us -> 7.84 us
  Pallas kernels: 6.58 us -> 7.12 us
    ppermute x12, waiting for transfers between devices: 8.66 us -> 7.84 us  [send(): return lax.ppermute(value, axes, ways[way])]
    pallas_call x10, Pallas kernels: 6.58 us -> 7.12 us  [device_call(): pl.pallas_call(kernel, out_shape=out_shape, in_specs=[hbm if in_hbm else...]
  transfers between devices with their start and end apart: 12 -> 12, of which waited for: 8 -> 8; matrix products, arithmetic and copies ran while one was open for 0% -> 0% of each run, Pallas kernels for 8% -> 10%
where the time goes in v7:
time: 27.2 us; the launch traced here: 27.1 us
  starting transfers between devices  12 us (44%)
  waiting for transfers between devices  7.84 us (29%)
  Pallas kernels  7.12 us (26%)
    ppermute x12, starting transfers between devices, send(): return lax.ppermute(value, axes, ways[way])  12 us
    ppermute x12, waiting for transfers between devices, send(): return lax.ppermute(value, axes, ways[way])  7.84 us
    pallas_call x10, Pallas kernels, device_call(): pl.pallas_call(kernel, out_shape=out_shape, in_specs=[hbm if in_hbm else...  7.12 us
  transfers between devices with their start and end apart: 12, of which 8 were waited for; matrix products, arithmetic and copies ran while one was open for 0% of the time, Pallas kernels for 10%

profile of v7, /device:TPU:0, one launch (start us, length us, event | category | flops | bytes accessed | tf_op | source)
XLA Modules:
  0.0 27.1 jit_solution(10949030768943086894)
XLA Ops:
  0.0 1.0 %pack.1.b0 = bf16[272,128]{1,0:T(8,128)(2,1)S(1)} custom-call(bf16[256,128]{1,0:T(8,128)(2,1)} %pert.1, bf16[2,128]{1,0:T(2,128)(2,1)} %bitcast.5, bf16[2,128]{1,0:T(2,128)(2,1)} %bitcast.6, s32[4,1,256]{2,1,0:T(1,128)} %owner_ref.1, s32[4,1,256]{2,1,0:T(1,128)} %slot_ref.1, s32[1,4]{1,0:T(1,128)} %bitcast.3, f32[4,1,256]{2,1,0:T(1,128)} %local_ref.1), custom_call_target="tpu_custom_call" | custom-call | bytes 262144 | tf_op jit(solution)/shard_map/pack/pallas_call | solution.py:210
  1.0 3.1 %collective-permute-start = (bf16[272,128]{1,0:T(8,128)(2,1)S(1)}, bf16[272,128]{1,0:T(8,128)(2,1)S(1)}, u32[]{:S(2)}, u32[]{:S(2)}) collective-permute-start(bf16[272,128]{1,0:T(8,128)(2,1)S(1)} %pack.1.b0), channel_id=1, source_target_pairs={{0,16},{1,17},{2,18},{3,19},{4,20},{5,21},{6,22},{7,23},{8,24},{9,... | collective-permute-start | bytes 208904 | tf_op jit(solution)/shard_map/ppermute | solution.py:598
  4.1 2.0 %collective-permute-start.1 = (bf16[272,128]{1,0:T(8,128)(2,1)S(1)}, bf16[272,128]{1,0:T(8,128)(2,1)S(1)}, u32[]{:S(2)}, u32[]{:S(2)}) collective-permute-start(bf16[272,128]{1,0:T(8,128)(2,1)S(1)} %pack.1.b0), channel_id=1, source_target_pairs={{0,4},{1,0},{2,6},{3,2},{4,8},{5,1},{6,10},{7,3},{8,12},{9,5},{10,... | collective-permute-start | bytes 208904 | tf_op jit(solution)/shard_map/ppermute | solution.py:598
  6.1 0.3 collective-permute-done.other_ref.b3
  6.4 2.1 %collective-permute-start.4 = (bf16[272,128]{1,0:T(8,128)(2,1)S(1)}, bf16[272,128]{1,0:T(8,128)(2,1)S(1)}, u32[]{:S(2)}, u32[]{:S(2)}) collective-permute-start(bf16[272,128]{1,0:T(8,128)(2,1)S(1)} %collective-permute-done.other_ref.b3), channel_id=1, source_target_pairs={{0,4},{1,0},{2,6},{3,2},{4,8},{5,1},{6,10},{7,3},{8,12},{9,5},{10,... | collective-permute-start | bytes 208904 | tf_op jit(solution)/shard_map/ppermute | solution.py:598
  8.5 0.5 %table.1.table_ref = f32[128,128]{1,0:T(8,128)S(1)} custom-call(s32[4,1,256]{2,1,0:T(1,128)S(1)} %copy-done.1, s32[4,1,256]{2,1,0:T(1,128)S(1)} %copy-done.2, s32[1,4]{1,0:T(1,128)S(1)} %bitcast.4, f32[4,1,256]{2,1,0:T(1,128)S(1)} %copy-done.3, bf16[272,128]{1,0:T(8,128)(2,1)S(1)} %collective-permute-done.other_ref.b3), custom_call_target="tpu_custom_call" | custom-call | flops 18874368 | bytes 262144 | tf_op jit(solution)/shard_map/table/pallas_call | solution.py:210
  9.0 0.1 collective-permute-done.2.b2
  9.1 0.6 %gram_near.1.so_far_ref = f32[784,128]{1,0:T(8,128)S(1)} custom-call(f32[128,128]{1,0:T(8,128)S(1)} %table.1.table_ref, bf16[272,128]{1,0:T(8,128)(2,1)S(1)} %pack.1.b0, bf16[272,128]{1,0:T(8,128)(2,1)S(1)} %collective-permute-done.1.b1, bf16[272,128]{1,0:T(8,128)(2,1)S(1)} %collective-permute-done.2.b2, bf16[272,128]{1,0:T(8,128)(2,1)S(1)} %collective-permute-done.other_ref.b3), custom_call_target="tpu_custom_call" | custom-call | flops 205520896 | bytes 262144 | tf_op jit(solution)/shard_map/gram_near/pallas_call | solution.py:210
  9.7 1.3 %collective-permute-done.3.block = bf16[272,128]{1,0:T(8,128)(2,1)S(1)} collective-permute-done((bf16[272,128]{1,0:T(8,128)(2,1)S(1)}, bf16[272,128]{1,0:T(8,128)(2,1)S(1)}, u32[]{:S(2)}, u32[]{:S(2)}) %collective-permute-start.3) | collective-permute-done | bytes 69664 | tf_op jit(solution)/shard_map/ppermute | solution.py:598
  11.0 0.3 %gram_next.1.so_far_ref = f32[784,128]{1,0:T(8,128)S(1)} custom-call(f32[128,128]{1,0:T(8,128)S(1)} %table.1.table_ref, f32[784,128]{1,0:T(8,128)S(1)} %gram_near.1.so_far_ref, bf16[272,128]{1,0:T(8,128)(2,1)S(1)} %collective-permute-done.3.block), custom_call_target="tpu_custom_call" | custom-call | flops 51380224 | bytes 262144 | tf_op jit(solution)/shard_map/gram_next/pallas_call | solution.py:210
  11.3 0.3 %gram_last.1 = (f32[392,128]{1,0:T(8,128)S(1)}, f32[392,128]{1,0:T(8,128)S(1)}) custom-call(f32[128,128]{1,0:T(8,128)S(1)} %table.1.table_ref, f32[784,128]{1,0:T(8,128)S(1)} %gram_next.1.so_far_ref, bf16[272,128]{1,0:T(8,128)(2,1)S(1)} %collective-permute-done.4.block), custom_call_target="tpu_custom_call" | custom-call | flops 51380224 | bytes 262144 | tf_op jit(solution)/shard_map/gram_last/pallas_call | solution.py:210
  11.7 1.4 %collective-permute-done.5.got_ref = f32[392,128]{1,0:T(8,128)S(1)} collective-permute-done((f32[392,128]{1,0:T(8,128)S(1)}, f32[392,128]{1,0:T(8,128)S(1)}, u32[]{:S(2)}, u32[]{:S(2)}) %collective-permute-start.5) | collective-permute-done | bytes 200736 | tf_op jit(solution)/shard_map/ppermute | solution.py:598
  13.2 1.8 %collective-permute-start.6 = (bf16[272,128]{1,0:T(8,128)(2,1)S(1)}, bf16[272,128]{1,0:T(8,128)(2,1)S(1)}, u32[]{:S(2)}, u32[]{:S(2)}) collective-permute-start(bf16[272,128]{1,0:T(8,128)(2,1)S(1)} %get-tuple-element.19), channel_id=1, source_target_pairs={{0,2},{1,3},{2,0},{3,1},{4,6},{5,7},{6,4},{7,5},{8,10},{9,11},{10,... | collective-permute-start | bytes 208904 | tf_op jit(solution)/shard_map/ppermute | solution.py:598
  15.0 2.6 %collective-permute-done.6.got_ref = bf16[272,128]{1,0:T(8,128)(2,1)S(1)} collective-permute-done((bf16[272,128]{1,0:T(8,128)(2,1)S(1)}, bf16[272,128]{1,0:T(8,128)(2,1)S(1)}, u32[]{:S(2)}, u32[]{:S(2)}) %collective-permute-start.6) | collective-permute-done | bytes 69664 | tf_op jit(solution)/shard_map/ppermute | solution.py:598
  17.6 1.6 %solve.1.own = bf16[272,128]{1,0:T(8,128)(2,1)S(1)} custom-call(f32[392,128]{1,0:T(8,128)S(1)} %get-tuple-element.18.sum_ref, bf16[272,128]{1,0:T(8,128)(2,1)S(1)} %collective-permute-done.6.got_ref), custom_call_target="tpu_custom_call" | custom-call | flops 339738624 | bytes 262144 | tf_op jit(solution)/shard_map/solve/pallas_call | solution.py:210
  19.3 0.5 %collective-permute-start.8 = (bf16[272,128]{1,0:T(8,128)(2,1)S(1)}, bf16[272,128]{1,0:T(8,128)(2,1)S(1)}, u32[]{:S(2)}, u32[]{:S(2)}) collective-permute-start(bf16[272,128]{1,0:T(8,128)(2,1)S(1)} %solve.1.own), channel_id=1, source_target_pairs={{4,0},{0,1},{6,2},{2,3},{8,4},{1,5},{10,6},{3,7},{12,8},{5,9},{14,... | collective-permute-start | bytes 208904 | tf_op jit(solution)/shard_map/ppermute | solution.py:598
  19.8 1.5 %collective-permute-start.7 = (bf16[272,128]{1,0:T(8,128)(2,1)S(1)}, bf16[272,128]{1,0:T(8,128)(2,1)S(1)}, u32[]{:S(2)}, u32[]{:S(2)}) collective-permute-start(bf16[272,128]{1,0:T(8,128)(2,1)S(1)} %solve.1.own), channel_id=1, source_target_pairs={{0,4},{1,0},{2,6},{3,2},{4,8},{5,1},{6,10},{7,3},{8,12},{9,5},{10,... | collective-permute-start | bytes 208904 | tf_op jit(solution)/shard_map/ppermute | solution.py:598
  21.3 0.7 %apply_near.1 = (f32[8,2,128,128]{3,2,1,0:T(8,128)S(1)}, bf16[8,2,128,128]{3,2,1,0:T(8,128)(2,1)S(1)}) custom-call(bf16[2,64,16,128]{3,2,1,0:T(8,128)(2,1)S(1)} %copy-done, bf16[272,128]{1,0:T(8,128)(2,1)S(1)} %solve.1.own, bf16[272,128]{1,0:T(8,128)(2,1)S(1)} %collective-permute-done.9.pair), custom_call_target="tpu_custom_call" | custom-call | flops 134217728 | bytes 262144 | tf_op jit(solution)/shard_map/apply_near/pallas_call | solution.py:210
  22.1 1.5 %collective-permute-done.8.descend = bf16[272,128]{1,0:T(8,128)(2,1)S(1)} collective-permute-done((bf16[272,128]{1,0:T(8,128)(2,1)S(1)}, bf16[272,128]{1,0:T(8,128)(2,1)S(1)}, u32[]{:S(2)}, u32[]{:S(2)}) %collective-permute-start.8) | collective-permute-done | bytes 69664 | tf_op jit(solution)/shard_map/ppermute | solution.py:598
  23.6 0.9 %collective-permute-start.10 = (bf16[272,128]{1,0:T(8,128)(2,1)S(1)}, bf16[272,128]{1,0:T(8,128)(2,1)S(1)}, u32[]{:S(2)}, u32[]{:S(2)}) collective-permute-start(bf16[272,128]{1,0:T(8,128)(2,1)S(1)} %collective-permute-done.7.climb), channel_id=1, source_target_pairs={{0,1},{1,0},{2,3},{3,2},{4,5},{5,4},{6,7},{7,6},{8,9},{9,8},{10,11... | collective-permute-start | bytes 208904 | tf_op jit(solution)/shard_map/ppermute | solution.py:598
  24.5 0.6 %far_first.1 = (bf16[2,24,16,128]{3,2,1,0:T(8,128)(2,1)S(1)}, bf16[2,128,128]{2,1,0:T(8,128)(2,1)S(1)}) custom-call(f32[8,2,128,128]{3,2,1,0:T(8,128)S(1)} %get-tuple-element.21.part_ref, bf16[8,2,128,128]{3,2,1,0:T(8,128)(2,1)S(1)} %get-tuple-element.22.pert_ref, bf16[272,128]{1,0:T(8,128)(2,1)S(1)} %solve.1.own, ...), custom_call_target="tpu_custom_call" | custom-call | flops 50331648 | bytes 262144 | tf_op jit(solution)/shard_map/far_first/pallas_call | solution.py:210
  25.1 0.3 %collective-permute-done.10.pair_climb = bf16[272,128]{1,0:T(8,128)(2,1)S(1)} collective-permute-done((bf16[272,128]{1,0:T(8,128)(2,1)S(1)}, bf16[272,128]{1,0:T(8,128)(2,1)S(1)}, u32[]{:S(2)}, u32[]{:S(2)}) %collective-permute-start.10) | collective-permute-done | bytes 69664 | tf_op jit(solution)/shard_map/ppermute | solution.py:598
  25.4 0.4 %collective-permute-done.11.pair_descend = bf16[272,128]{1,0:T(8,128)(2,1)S(1)} collective-permute-done((bf16[272,128]{1,0:T(8,128)(2,1)S(1)}, bf16[272,128]{1,0:T(8,128)(2,1)S(1)}, u32[]{:S(2)}, u32[]{:S(2)}) %collective-permute-start.11) | collective-permute-done | bytes 69664 | tf_op jit(solution)/shard_map/ppermute | solution.py:598
  25.7 1.3 %far_rest.1 = bf16[2,64,16,128]{3,2,1,0:T(8,128)(2,1)} custom-call(f32[8,2,128,128]{3,2,1,0:T(8,128)S(1)} %get-tuple-element.21.part_ref, bf16[8,2,128,128]{3,2,1,0:T(8,128)(2,1)S(1)} %get-tuple-element.22.pert_ref, bf16[272,128]{1,0:T(8,128)(2,1)S(1)} %collective-permute-done.9.pair, bf16[272,128]{1,0:T(8,128)(2,1)S(1)} %collective-permute-done.10.pair_climb, ...), custom_call_target="tpu_custom_call" | custom-call | flops 83886080 | bytes 262144 | tf_op jit(solution)/shard_map/far_rest/pallas_call | solution.py:210
  (20 shorter events, 0.2 us)
Async XLA Ops:
  0.0 8.5 %copy-start.1 = (s32[4,1,256]{2,1,0:T(1,128)S(1)}, s32[4,1,256]{2,1,0:T(1,128)}, u32[]{:S(2)}) copy-start(s32[4,1,256]{2,1,0:T(1,128)} %owner_ref.1) | copy-start | bytes 12292
  0.0 8.5 %copy-start.2 = (s32[4,1,256]{2,1,0:T(1,128)S(1)}, s32[4,1,256]{2,1,0:T(1,128)}, u32[]{:S(2)}) copy-start(s32[4,1,256]{2,1,0:T(1,128)} %slot_ref.1) | copy-start | bytes 12292
  0.0 8.5 %copy-start.3 = (f32[4,1,256]{2,1,0:T(1,128)S(1)}, f32[4,1,256]{2,1,0:T(1,128)}, u32[]{:S(2)}) copy-start(f32[4,1,256]{2,1,0:T(1,128)} %local_ref.1) | copy-start | bytes 12292
  0.0 8.5 %copy-start.4 = (s32[4,1]{0,1:T(1,128)S(1)}, s32[4,1]{0,1:T(1,128)}, u32[]{:S(2)}) copy-start(s32[4,1]{0,1:T(1,128)} %param.14) | copy-start | bytes 52
  1.0 5.4 %collective-permute-start = (bf16[272,128]{1,0:T(8,128)(2,1)S(1)}, bf16[272,128]{1,0:T(8,128)(2,1)S(1)}, u32[]{:S(2)}, u32[]{:S(2)}) collective-permute-start(bf16[272,128]{1,0:T(8,128)(2,1)S(1)} %pack.1.b0), channel_id=1, source_target_pairs={{0,16},{1,17},{2,18},{3,19},{4,20},{5,21},{6,22},{7,23},{8,24},{9,... | collective-permute-start | bytes 208904 | tf_op jit(solution)/shard_map/ppermute | solution.py:598
  4.1 4.9 %collective-permute-start.2 = (bf16[272,128]{1,0:T(8,128)(2,1)S(1)}, bf16[272,128]{1,0:T(8,128)(2,1)S(1)}, u32[]{:S(2)}, u32[]{:S(2)}) collective-permute-start(bf16[272,128]{1,0:T(8,128)(2,1)S(1)} %pack.1.b0), channel_id=1, source_target_pairs={{4,0},{0,1},{6,2},{2,3},{8,4},{1,5},{10,6},{3,7},{12,8},{5,9},{14,... | collective-permute-start | bytes 208904 | tf_op jit(solution)/shard_map/ppermute | solution.py:598
  4.1 4.9 %collective-permute-start.1 = (bf16[272,128]{1,0:T(8,128)(2,1)S(1)}, bf16[272,128]{1,0:T(8,128)(2,1)S(1)}, u32[]{:S(2)}, u32[]{:S(2)}) collective-permute-start(bf16[272,128]{1,0:T(8,128)(2,1)S(1)} %pack.1.b0), channel_id=1, source_target_pairs={{0,4},{1,0},{2,6},{3,2},{4,8},{5,1},{6,10},{7,3},{8,12},{9,5},{10,... | collective-permute-start | bytes 208904 | tf_op jit(solution)/shard_map/ppermute | solution.py:598
  6.4 4.6 %collective-permute-start.3 = (bf16[272,128]{1,0:T(8,128)(2,1)S(1)}, bf16[272,128]{1,0:T(8,128)(2,1)S(1)}, u32[]{:S(2)}, u32[]{:S(2)}) collective-permute-start(bf16[272,128]{1,0:T(8,128)(2,1)S(1)} %collective-permute-done.other_ref.b3), channel_id=1, source_target_pairs={{4,0},{0,1},{6,2},{2,3},{8,4},{1,5},{10,6},{3,7},{12,8},{5,9},{14,... | collective-permute-start | bytes 208904 | tf_op jit(solution)/shard_map/ppermute | solution.py:598
  6.4 4.9 %collective-permute-start.4 = (bf16[272,128]{1,0:T(8,128)(2,1)S(1)}, bf16[272,128]{1,0:T(8,128)(2,1)S(1)}, u32[]{:S(2)}, u32[]{:S(2)}) collective-permute-start(bf16[272,128]{1,0:T(8,128)(2,1)S(1)} %collective-permute-done.other_ref.b3), channel_id=1, source_target_pairs={{0,4},{1,0},{2,6},{3,2},{4,8},{5,1},{6,10},{7,3},{8,12},{9,5},{10,... | collective-permute-start | bytes 208904 | tf_op jit(solution)/shard_map/ppermute | solution.py:598
  11.6 1.5 %collective-permute-start.5 = (f32[392,128]{1,0:T(8,128)S(1)}, f32[392,128]{1,0:T(8,128)S(1)}, u32[]{:S(2)}, u32[]{:S(2)}) collective-permute-start(f32[392,128]{1,0:T(8,128)S(1)} %get-tuple-element.17), channel_id=1, source_target_pairs={{0,1},{1,0},{2,3},{3,2},{4,5},{5,4},{6,7},{7,6},{8,9},{9,8},{10,11... | collective-permute-start | bytes 602120 | tf_op jit(solution)/shard_map/ppermute | solution.py:598
  13.2 4.4 %collective-permute-start.6 = (bf16[272,128]{1,0:T(8,128)(2,1)S(1)}, bf16[272,128]{1,0:T(8,128)(2,1)S(1)}, u32[]{:S(2)}, u32[]{:S(2)}) collective-permute-start(bf16[272,128]{1,0:T(8,128)(2,1)S(1)} %get-tuple-element.19), channel_id=1, source_target_pairs={{0,2},{1,3},{2,0},{3,1},{4,6},{5,7},{6,4},{7,5},{8,10},{9,11},{10,... | collective-permute-start | bytes 208904 | tf_op jit(solution)/shard_map/ppermute | solution.py:598
  17.6 3.7 %copy-start = (bf16[2,64,16,128]{3,2,1,0:T(8,128)(2,1)S(1)}, bf16[2,64,16,128]{3,2,1,0:T(8,128)(2,1)}, u32[]{:S(2)}) copy-start(bf16[2,64,16,128]{3,2,1,0:T(8,128)(2,1)} %members_ref.1) | copy-start | bytes 1572868
  19.2 2.1 %collective-permute-start.9 = (bf16[272,128]{1,0:T(8,128)(2,1)S(1)}, bf16[272,128]{1,0:T(8,128)(2,1)S(1)}, u32[]{:S(2)}, u32[]{:S(2)}) collective-permute-start(bf16[272,128]{1,0:T(8,128)(2,1)S(1)} %solve.1.own), channel_id=1, source_target_pairs={{0,1},{1,0},{2,3},{3,2},{4,5},{5,4},{6,7},{7,6},{8,9},{9,8},{10,11... | collective-permute-start | bytes 208904 | tf_op jit(solution)/shard_map/ppermute | solution.py:598
  19.3 4.3 %collective-permute-start.8 = (bf16[272,128]{1,0:T(8,128)(2,1)S(1)}, bf16[272,128]{1,0:T(8,128)(2,1)S(1)}, u32[]{:S(2)}, u32[]{:S(2)}) collective-permute-start(bf16[272,128]{1,0:T(8,128)(2,1)S(1)} %solve.1.own), channel_id=1, source_target_pairs={{4,0},{0,1},{6,2},{2,3},{8,4},{1,5},{10,6},{3,7},{12,8},{5,9},{14,... | collective-permute-start | bytes 208904 | tf_op jit(solution)/shard_map/ppermute | solution.py:598
  19.8 3.8 %collective-permute-start.7 = (bf16[272,128]{1,0:T(8,128)(2,1)S(1)}, bf16[272,128]{1,0:T(8,128)(2,1)S(1)}, u32[]{:S(2)}, u32[]{:S(2)}) collective-permute-start(bf16[272,128]{1,0:T(8,128)(2,1)S(1)} %solve.1.own), channel_id=1, source_target_pairs={{0,4},{1,0},{2,6},{3,2},{4,8},{5,1},{6,10},{7,3},{8,12},{9,5},{10,... | collective-permute-start | bytes 208904 | tf_op jit(solution)/shard_map/ppermute | solution.py:598
  23.6 1.8 %collective-permute-start.10 = (bf16[272,128]{1,0:T(8,128)(2,1)S(1)}, bf16[272,128]{1,0:T(8,128)(2,1)S(1)}, u32[]{:S(2)}, u32[]{:S(2)}) collective-permute-start(bf16[272,128]{1,0:T(8,128)(2,1)S(1)} %collective-permute-done.7.climb), channel_id=1, source_target_pairs={{0,1},{1,0},{2,3},{3,2},{4,5},{5,4},{6,7},{7,6},{8,9},{9,8},{10,11... | collective-permute-start | bytes 208904 | tf_op jit(solution)/shard_map/ppermute | solution.py:598
  24.5 1.3 %collective-permute-start.11 = (bf16[272,128]{1,0:T(8,128)(2,1)S(1)}, bf16[272,128]{1,0:T(8,128)(2,1)S(1)}, u32[]{:S(2)}, u32[]{:S(2)}) collective-permute-start(bf16[272,128]{1,0:T(8,128)(2,1)S(1)} %collective-permute-done.8.descend), channel_id=1, source_target_pairs={{0,1},{1,0},{2,3},{3,2},{4,5},{5,4},{6,7},{7,6},{8,9},{9,8},{10,11... | collective-permute-start | bytes 208904 | tf_op jit(solution)/shard_map/ppermute | solution.py:598

commit v8 on v7

--- a/solution.py
+++ b/solution.py
@@ -337,21 +337,39 @@
     out_ref[...] = gram_blocks(rows, cols, 0, [b0, b1, b2, b3], table_ref, turned, plain, scaled)
 
 
-def gram_next_kernel(rows, cols, first, table_ref, so_far_ref, block, out_ref, turned, plain, scaled):
-    out_ref[...] = so_far_ref[...] + gram_blocks(rows, cols, first, [block], table_ref, turned, plain, scaled)
-
-
-def gram_last_kernel(rows, cols, first, table_ref, so_far_ref, block, mine_ref, rest_ref, turned, plain, scaled):
+def gram_block(rows, cols, first, block, table_ref, so_far_ref):
+    per = rows // 128
+    tail = block[rows : rows + 16, :].astype(jnp.float32)
+    weights = [table_ref[8 * hi : 8 * hi + 8, :] * tail[hi - first * per : hi - first * per + 1, :] for hi in range(first * per, (first + 1) * per)]
+    products = [w * tail[per + k : per + k + 1, :] for k, w in enumerate(weights)]
+    plain = block[0:rows, :]
+    turned = plain.astype(jnp.float32).T
+    weight = jnp.concatenate(weights, axis=1)
+    pieces = []
+    for position in range(cols):
+        scaled = (turned * weight[position : position + 1, :]).astype(jnp.bfloat16)
+        pieces.append(so_far_ref[128 * position : 128 * (position + 1), :] + dot(scaled, plain))
+    both = above(*[p.astype(jnp.float32) for p in split2(jnp.concatenate(products, axis=1))]).astype(jnp.bfloat16)
+    pieces.append(so_far_ref[128 * cols : 128 * cols + 16, :] + dot(both, plain))
+    return pieces
+
+
+def gram_next_kernel(rows, cols, first, table_ref, so_far_ref, block, out_ref):
+    for k, piece in enumerate(gram_block(rows, cols, first, block, table_ref, so_far_ref)):
+        out_ref[128 * k : 128 * k + piece.shape[0], :] = piece
+
+
+def gram_last_kernel(rows, cols, first, table_ref, so_far_ref, block, mine_ref, rest_ref):
     half = cols // 2
-    total = so_far_ref[...] + gram_blocks(rows, cols, first, [block], table_ref, turned, plain, scaled)
+    pieces = gram_block(rows, cols, first, block, table_ref, so_far_ref)
+    for k in range(half):
+        mine_ref[128 * k : 128 * (k + 1), :] = pieces[k]
+        rest_ref[128 * k : 128 * (k + 1), :] = pieces[half + k].astype(jnp.bfloat16)
+    projected = pieces[cols][0:8] + pieces[cols][8:16]
     edge = 128 * half
-    projected = total[2 * edge : 2 * edge + 8] + total[2 * edge + 8 : 2 * edge + 16]
-    mine_ref[0:edge, :] = total[0:edge]
-    rest_ref[0:edge, :] = total[edge : 2 * edge]
     mine_ref[edge : edge + 8, :] = projected
-    rest_ref[edge : edge + 8, :] = jnp.concatenate(
-        [projected[half : 2 * half], jnp.zeros((8 - half, 128), jnp.float32)], axis=0
-    )
+    high, low = split2(above(projected[half : 2 * half], jnp.zeros((8 - half, 128), jnp.float32)))
+    rest_ref[edge : edge + 16, :] = above(high.astype(jnp.float32), low.astype(jnp.float32)).astype(jnp.bfloat16)
 
 
 def lanes_from(lane, values, others=0.0):
@@ -381,9 +399,10 @@
 
 
 def join_kernel(half, mine_ref, got_ref, sum_ref, send_ref):
-    total = mine_ref[...] + got_ref[...]
+    edge = 128 * half
+    got = got_ref[...].astype(jnp.float32)
+    total = mine_ref[...] + above(got[0:edge], got[edge : edge + 8] + got[edge + 8 : edge + 16])
     sum_ref[...] = total
-    edge = 128 * half
     folded = fold([total[128 * k : 128 * (k + 1)] for k in range(half)])
     high, low = split2(total[edge : edge + 8])
     send_ref[...] = above(folded, high.astype(jnp.float32), low.astype(jnp.float32)).astype(jnp.bfloat16)
@@ -535,10 +554,10 @@
 
 def neighbours(climb, descend, own, first):
     tile_y = lax.axis_index("ty")
-    up, down, mine = (ref[...].astype(jnp.float32) for ref in (climb, descend, own))
+    up, down, mine = climb[...], descend[...], own[...]
     before = jnp.where(tile_y == 0, mine, jnp.where(first, up, down))
     after = jnp.where(tile_y == lax.axis_size("ty") - 1, mine, jnp.where(first, down, up))
-    return before, after
+    return before.astype(jnp.float32), after.astype(jnp.float32)
 
 
 def far_first_kernel(cols, count, part_ref, pert_ref, own, climb, descend, out_ref, border_ref, table):
@@ -644,24 +663,17 @@
         flops=2 * tall * size * 4 * rows,
         name="gram_near",
     )
-    block_scratch = [
-        pltpu.VMEM((size, rows), f32),
-        pltpu.VMEM((rows, size), bf16),
-        pltpu.VMEM((tall, rows), bf16),
-    ]
     near = device_call(
         functools.partial(gram_next_kernel, rows, cols, 5),
         (table, near, across_descend),
         shape((tall, size), f32),
-        block_scratch,
         flops=2 * tall * size * rows,
         name="gram_next",
     )
     mine, rest = device_call(
         functools.partial(gram_last_kernel, rows, cols, 4),
         (table, near, across_climb),
-        [shape((size * half + 8, size), f32)] * 2,
-        block_scratch,
+        [shape((size * half + 8, size), f32), shape((size * half + 16, size), bf16)],
         flops=2 * tall * size * rows,
         name="gram_last",
     )

time: 27.2 us -> 27.1 us (level)
  no operation moved by 1% of the time
where the time goes in v8:
time: 27.1 us; the launch traced here: 26.9 us
  starting transfers between devices  12 us (44%)
  waiting for transfers between devices  7.68 us (28%)
  Pallas kernels  7.15 us (26%)
    ppermute x12, starting transfers between devices, send(): return lax.ppermute(value, axes, ways[way])  12 us
    ppermute x12, waiting for transfers between devices, send(): return lax.ppermute(value, axes, ways[way])  7.68 us
    pallas_call x10, Pallas kernels, device_call(): pl.pallas_call(kernel, out_shape=out_shape, in_specs=[hbm if in_hbm else...  7.15 us
  transfers between devices with their start and end apart: 12, of which 8 were waited for; matrix products, arithmetic and copies ran while one was open for 0% of the time, Pallas kernels for 10%

profile of v8, /device:TPU:0, one launch (start us, length us, event | category | flops | bytes accessed | tf_op | source)
XLA Modules:
  0.0 26.9 jit_solution(16051213223272838295)
XLA Ops:
  0.0 1.0 %pack.1.b0 = bf16[272,128]{1,0:T(8,128)(2,1)S(1)} custom-call(bf16[256,128]{1,0:T(8,128)(2,1)} %pert.1, bf16[2,128]{1,0:T(2,128)(2,1)} %bitcast.5, bf16[2,128]{1,0:T(2,128)(2,1)} %bitcast.6, s32[4,1,256]{2,1,0:T(1,128)} %owner_ref.1, s32[4,1,256]{2,1,0:T(1,128)} %slot_ref.1, s32[1,4]{1,0:T(1,128)} %bitcast.3, f32[4,1,256]{2,1,0:T(1,128)} %local_ref.1), custom_call_target="tpu_custom_call" | custom-call | bytes 262144 | tf_op jit(solution)/shard_map/pack/pallas_call | solution.py:210
  1.0 3.1 %collective-permute-start = (bf16[272,128]{1,0:T(8,128)(2,1)S(1)}, bf16[272,128]{1,0:T(8,128)(2,1)S(1)}, u32[]{:S(2)}, u32[]{:S(2)}) collective-permute-start(bf16[272,128]{1,0:T(8,128)(2,1)S(1)} %pack.1.b0), channel_id=1, source_target_pairs={{0,16},{1,17},{2,18},{3,19},{4,20},{5,21},{6,22},{7,23},{8,24},{9,... | collective-permute-start | bytes 208904 | tf_op jit(solution)/shard_map/ppermute | solution.py:617
  4.1 2.0 %collective-permute-start.1 = (bf16[272,128]{1,0:T(8,128)(2,1)S(1)}, bf16[272,128]{1,0:T(8,128)(2,1)S(1)}, u32[]{:S(2)}, u32[]{:S(2)}) collective-permute-start(bf16[272,128]{1,0:T(8,128)(2,1)S(1)} %pack.1.b0), channel_id=1, source_target_pairs={{0,4},{1,0},{2,6},{3,2},{4,8},{5,1},{6,10},{7,3},{8,12},{9,5},{10,... | collective-permute-start | bytes 208904 | tf_op jit(solution)/shard_map/ppermute | solution.py:617
  6.1 0.3 collective-permute-done.other_ref.b3
  6.4 2.1 %collective-permute-start.4 = (bf16[272,128]{1,0:T(8,128)(2,1)S(1)}, bf16[272,128]{1,0:T(8,128)(2,1)S(1)}, u32[]{:S(2)}, u32[]{:S(2)}) collective-permute-start(bf16[272,128]{1,0:T(8,128)(2,1)S(1)} %collective-permute-done.other_ref.b3), channel_id=1, source_target_pairs={{0,4},{1,0},{2,6},{3,2},{4,8},{5,1},{6,10},{7,3},{8,12},{9,5},{10,... | collective-permute-start | bytes 208904 | tf_op jit(solution)/shard_map/ppermute | solution.py:617
  8.5 0.5 %table.1.table_ref = f32[128,128]{1,0:T(8,128)S(1)} custom-call(s32[4,1,256]{2,1,0:T(1,128)S(1)} %copy-done.1, s32[4,1,256]{2,1,0:T(1,128)S(1)} %copy-done.2, s32[1,4]{1,0:T(1,128)S(1)} %bitcast.4, f32[4,1,256]{2,1,0:T(1,128)S(1)} %copy-done.3, bf16[272,128]{1,0:T(8,128)(2,1)S(1)} %collective-permute-done.other_ref.b3), custom_call_target="tpu_custom_call" | custom-call | flops 18874368 | bytes 262144 | tf_op jit(solution)/shard_map/table/pallas_call | solution.py:210
  9.0 0.1 collective-permute-done.2.b2
  9.1 0.6 %gram_near.1.so_far_ref = f32[784,128]{1,0:T(8,128)S(1)} custom-call(f32[128,128]{1,0:T(8,128)S(1)} %table.1.table_ref, bf16[272,128]{1,0:T(8,128)(2,1)S(1)} %pack.1.b0, bf16[272,128]{1,0:T(8,128)(2,1)S(1)} %collective-permute-done.1.b1, bf16[272,128]{1,0:T(8,128)(2,1)S(1)} %collective-permute-done.2.b2, bf16[272,128]{1,0:T(8,128)(2,1)S(1)} %collective-permute-done.other_ref.b3), custom_call_target="tpu_custom_call" | custom-call | flops 205520896 | bytes 262144 | tf_op jit(solution)/shard_map/gram_near/pallas_call | solution.py:210
  9.7 1.3 %collective-permute-done.3.block = bf16[272,128]{1,0:T(8,128)(2,1)S(1)} collective-permute-done((bf16[272,128]{1,0:T(8,128)(2,1)S(1)}, bf16[272,128]{1,0:T(8,128)(2,1)S(1)}, u32[]{:S(2)}, u32[]{:S(2)}) %collective-permute-start.3) | collective-permute-done | bytes 69664 | tf_op jit(solution)/shard_map/ppermute | solution.py:617
  11.0 0.3 %gram_next.1.so_far_ref = f32[784,128]{1,0:T(8,128)S(1)} custom-call(f32[128,128]{1,0:T(8,128)S(1)} %table.1.table_ref, f32[784,128]{1,0:T(8,128)S(1)} %gram_near.1.so_far_ref, bf16[272,128]{1,0:T(8,128)(2,1)S(1)} %collective-permute-done.3.block), custom_call_target="tpu_custom_call" | custom-call | flops 51380224 | bytes 262144 | tf_op jit(solution)/shard_map/gram_next/pallas_call | solution.py:210
  11.3 0.3 %gram_last.1 = (f32[392,128]{1,0:T(8,128)S(1)}, bf16[400,128]{1,0:T(8,128)(2,1)S(1)}) custom-call(f32[128,128]{1,0:T(8,128)S(1)} %table.1.table_ref, f32[784,128]{1,0:T(8,128)S(1)} %gram_next.1.so_far_ref, bf16[272,128]{1,0:T(8,128)(2,1)S(1)} %collective-permute-done.4.block), custom_call_target="tpu_custom_call" | custom-call | flops 51380224 | bytes 262144 | tf_op jit(solution)/shard_map/gram_last/pallas_call | solution.py:210
  11.7 1.3 %collective-permute-done.5.got_ref = bf16[400,128]{1,0:T(8,128)(2,1)S(1)} collective-permute-done((bf16[400,128]{1,0:T(8,128)(2,1)S(1)}, bf16[400,128]{1,0:T(8,128)(2,1)S(1)}, u32[]{:S(2)}, u32[]{:S(2)}) %collective-permute-start.5) | collective-permute-done | bytes 102432 | tf_op jit(solution)/shard_map/ppermute | solution.py:617
  13.1 1.8 %collective-permute-start.6 = (bf16[272,128]{1,0:T(8,128)(2,1)S(1)}, bf16[272,128]{1,0:T(8,128)(2,1)S(1)}, u32[]{:S(2)}, u32[]{:S(2)}) collective-permute-start(bf16[272,128]{1,0:T(8,128)(2,1)S(1)} %get-tuple-element.19), channel_id=1, source_target_pairs={{0,2},{1,3},{2,0},{3,1},{4,6},{5,7},{6,4},{7,5},{8,10},{9,11},{10,... | collective-permute-start | bytes 208904 | tf_op jit(solution)/shard_map/ppermute | solution.py:617
  14.9 2.6 %collective-permute-done.6.got_ref = bf16[272,128]{1,0:T(8,128)(2,1)S(1)} collective-permute-done((bf16[272,128]{1,0:T(8,128)(2,1)S(1)}, bf16[272,128]{1,0:T(8,128)(2,1)S(1)}, u32[]{:S(2)}, u32[]{:S(2)}) %collective-permute-start.6) | collective-permute-done | bytes 69664 | tf_op jit(solution)/shard_map/ppermute | solution.py:617
  17.5 1.6 %solve.1.own = bf16[272,128]{1,0:T(8,128)(2,1)S(1)} custom-call(f32[392,128]{1,0:T(8,128)S(1)} %get-tuple-element.18.sum_ref, bf16[272,128]{1,0:T(8,128)(2,1)S(1)} %collective-permute-done.6.got_ref), custom_call_target="tpu_custom_call" | custom-call | flops 339738624 | bytes 262144 | tf_op jit(solution)/shard_map/solve/pallas_call | solution.py:210
  19.1 0.5 %collective-permute-start.8 = (bf16[272,128]{1,0:T(8,128)(2,1)S(1)}, bf16[272,128]{1,0:T(8,128)(2,1)S(1)}, u32[]{:S(2)}, u32[]{:S(2)}) collective-permute-start(bf16[272,128]{1,0:T(8,128)(2,1)S(1)} %solve.1.own), channel_id=1, source_target_pairs={{4,0},{0,1},{6,2},{2,3},{8,4},{1,5},{10,6},{3,7},{12,8},{5,9},{14,... | collective-permute-start | bytes 208904 | tf_op jit(solution)/shard_map/ppermute | solution.py:617
  19.6 1.5 %collective-permute-start.7 = (bf16[272,128]{1,0:T(8,128)(2,1)S(1)}, bf16[272,128]{1,0:T(8,128)(2,1)S(1)}, u32[]{:S(2)}, u32[]{:S(2)}) collective-permute-start(bf16[272,128]{1,0:T(8,128)(2,1)S(1)} %solve.1.own), channel_id=1, source_target_pairs={{0,4},{1,0},{2,6},{3,2},{4,8},{5,1},{6,10},{7,3},{8,12},{9,5},{10,... | collective-permute-start | bytes 208904 | tf_op jit(solution)/shard_map/ppermute | solution.py:617
  21.2 0.7 %apply_near.1 = (f32[8,2,128,128]{3,2,1,0:T(8,128)S(1)}, bf16[8,2,128,128]{3,2,1,0:T(8,128)(2,1)S(1)}) custom-call(bf16[2,64,16,128]{3,2,1,0:T(8,128)(2,1)S(1)} %copy-done, bf16[272,128]{1,0:T(8,128)(2,1)S(1)} %solve.1.own, bf16[272,128]{1,0:T(8,128)(2,1)S(1)} %collective-permute-done.9.pair), custom_call_target="tpu_custom_call" | custom-call | flops 134217728 | bytes 262144 | tf_op jit(solution)/shard_map/apply_near/pallas_call | solution.py:210
  21.9 1.5 %collective-permute-done.8.descend = bf16[272,128]{1,0:T(8,128)(2,1)S(1)} collective-permute-done((bf16[272,128]{1,0:T(8,128)(2,1)S(1)}, bf16[272,128]{1,0:T(8,128)(2,1)S(1)}, u32[]{:S(2)}, u32[]{:S(2)}) %collective-permute-start.8) | collective-permute-done | bytes 69664 | tf_op jit(solution)/shard_map/ppermute | solution.py:617
  23.5 0.9 %collective-permute-start.10 = (bf16[272,128]{1,0:T(8,128)(2,1)S(1)}, bf16[272,128]{1,0:T(8,128)(2,1)S(1)}, u32[]{:S(2)}, u32[]{:S(2)}) collective-permute-start(bf16[272,128]{1,0:T(8,128)(2,1)S(1)} %collective-permute-done.7.climb), channel_id=1, source_target_pairs={{0,1},{1,0},{2,3},{3,2},{4,5},{5,4},{6,7},{7,6},{8,9},{9,8},{10,11... | collective-permute-start | bytes 208904 | tf_op jit(solution)/shard_map/ppermute | solution.py:617
  24.3 0.6 %far_first.1 = (bf16[2,24,16,128]{3,2,1,0:T(8,128)(2,1)S(1)}, bf16[2,128,128]{2,1,0:T(8,128)(2,1)S(1)}) custom-call(f32[8,2,128,128]{3,2,1,0:T(8,128)S(1)} %get-tuple-element.21.part_ref, bf16[8,2,128,128]{3,2,1,0:T(8,128)(2,1)S(1)} %get-tuple-element.22.pert_ref, bf16[272,128]{1,0:T(8,128)(2,1)S(1)} %solve.1.own, ...), custom_call_target="tpu_custom_call" | custom-call | flops 50331648 | bytes 262144 | tf_op jit(solution)/shard_map/far_first/pallas_call | solution.py:210
  25.0 0.3 %collective-permute-done.10.pair_climb = bf16[272,128]{1,0:T(8,128)(2,1)S(1)} collective-permute-done((bf16[272,128]{1,0:T(8,128)(2,1)S(1)}, bf16[272,128]{1,0:T(8,128)(2,1)S(1)}, u32[]{:S(2)}, u32[]{:S(2)}) %collective-permute-start.10) | collective-permute-done | bytes 69664 | tf_op jit(solution)/shard_map/ppermute | solution.py:617
  25.2 0.4 %collective-permute-done.11.pair_descend = bf16[272,128]{1,0:T(8,128)(2,1)S(1)} collective-permute-done((bf16[272,128]{1,0:T(8,128)(2,1)S(1)}, bf16[272,128]{1,0:T(8,128)(2,1)S(1)}, u32[]{:S(2)}, u32[]{:S(2)}) %collective-permute-start.11) | collective-permute-done | bytes 69664 | tf_op jit(solution)/shard_map/ppermute | solution.py:617
  25.6 1.3 %far_rest.1 = bf16[2,64,16,128]{3,2,1,0:T(8,128)(2,1)} custom-call(f32[8,2,128,128]{3,2,1,0:T(8,128)S(1)} %get-tuple-element.21.part_ref, bf16[8,2,128,128]{3,2,1,0:T(8,128)(2,1)S(1)} %get-tuple-element.22.pert_ref, bf16[272,128]{1,0:T(8,128)(2,1)S(1)} %collective-permute-done.9.pair, bf16[272,128]{1,0:T(8,128)(2,1)S(1)} %collective-permute-done.10.pair_climb, ...), custom_call_target="tpu_custom_call" | custom-call | flops 83886080 | bytes 262144 | tf_op jit(solution)/shard_map/far_rest/pallas_call | solution.py:210
  (20 shorter events, 0.2 us)
Async XLA Ops:
  0.0 8.5 %copy-start.1 = (s32[4,1,256]{2,1,0:T(1,128)S(1)}, s32[4,1,256]{2,1,0:T(1,128)}, u32[]{:S(2)}) copy-start(s32[4,1,256]{2,1,0:T(1,128)} %owner_ref.1) | copy-start | bytes 12292
  0.0 8.5 %copy-start.2 = (s32[4,1,256]{2,1,0:T(1,128)S(1)}, s32[4,1,256]{2,1,0:T(1,128)}, u32[]{:S(2)}) copy-start(s32[4,1,256]{2,1,0:T(1,128)} %slot_ref.1) | copy-start | bytes 12292
  0.0 8.5 %copy-start.3 = (f32[4,1,256]{2,1,0:T(1,128)S(1)}, f32[4,1,256]{2,1,0:T(1,128)}, u32[]{:S(2)}) copy-start(f32[4,1,256]{2,1,0:T(1,128)} %local_ref.1) | copy-start | bytes 12292
  0.0 8.5 %copy-start.4 = (s32[4,1]{0,1:T(1,128)S(1)}, s32[4,1]{0,1:T(1,128)}, u32[]{:S(2)}) copy-start(s32[4,1]{0,1:T(1,128)} %param.14) | copy-start | bytes 52
  1.0 5.4 %collective-permute-start = (bf16[272,128]{1,0:T(8,128)(2,1)S(1)}, bf16[272,128]{1,0:T(8,128)(2,1)S(1)}, u32[]{:S(2)}, u32[]{:S(2)}) collective-permute-start(bf16[272,128]{1,0:T(8,128)(2,1)S(1)} %pack.1.b0), channel_id=1, source_target_pairs={{0,16},{1,17},{2,18},{3,19},{4,20},{5,21},{6,22},{7,23},{8,24},{9,... | collective-permute-start | bytes 208904 | tf_op jit(solution)/shard_map/ppermute | solution.py:617
  4.1 4.9 %collective-permute-start.2 = (bf16[272,128]{1,0:T(8,128)(2,1)S(1)}, bf16[272,128]{1,0:T(8,128)(2,1)S(1)}, u32[]{:S(2)}, u32[]{:S(2)}) collective-permute-start(bf16[272,128]{1,0:T(8,128)(2,1)S(1)} %pack.1.b0), channel_id=1, source_target_pairs={{4,0},{0,1},{6,2},{2,3},{8,4},{1,5},{10,6},{3,7},{12,8},{5,9},{14,... | collective-permute-start | bytes 208904 | tf_op jit(solution)/shard_map/ppermute | solution.py:617
  4.1 4.9 %collective-permute-start.1 = (bf16[272,128]{1,0:T(8,128)(2,1)S(1)}, bf16[272,128]{1,0:T(8,128)(2,1)S(1)}, u32[]{:S(2)}, u32[]{:S(2)}) collective-permute-start(bf16[272,128]{1,0:T(8,128)(2,1)S(1)} %pack.1.b0), channel_id=1, source_target_pairs={{0,4},{1,0},{2,6},{3,2},{4,8},{5,1},{6,10},{7,3},{8,12},{9,5},{10,... | collective-permute-start | bytes 208904 | tf_op jit(solution)/shard_map/ppermute | solution.py:617
  6.4 4.6 %collective-permute-start.3 = (bf16[272,128]{1,0:T(8,128)(2,1)S(1)}, bf16[272,128]{1,0:T(8,128)(2,1)S(1)}, u32[]{:S(2)}, u32[]{:S(2)}) collective-permute-start(bf16[272,128]{1,0:T(8,128)(2,1)S(1)} %collective-permute-done.other_ref.b3), channel_id=1, source_target_pairs={{4,0},{0,1},{6,2},{2,3},{8,4},{1,5},{10,6},{3,7},{12,8},{5,9},{14,... | collective-permute-start | bytes 208904 | tf_op jit(solution)/shard_map/ppermute | solution.py:617
  6.4 4.9 %collective-permute-start.4 = (bf16[272,128]{1,0:T(8,128)(2,1)S(1)}, bf16[272,128]{1,0:T(8,128)(2,1)S(1)}, u32[]{:S(2)}, u32[]{:S(2)}) collective-permute-start(bf16[272,128]{1,0:T(8,128)(2,1)S(1)} %collective-permute-done.other_ref.b3), channel_id=1, source_target_pairs={{0,4},{1,0},{2,6},{3,2},{4,8},{5,1},{6,10},{7,3},{8,12},{9,5},{10,... | collective-permute-start | bytes 208904 | tf_op jit(solution)/shard_map/ppermute | solution.py:617
  11.6 1.4 %collective-permute-start.5 = (bf16[400,128]{1,0:T(8,128)(2,1)S(1)}, bf16[400,128]{1,0:T(8,128)(2,1)S(1)}, u32[]{:S(2)}, u32[]{:S(2)}) collective-permute-start(bf16[400,128]{1,0:T(8,128)(2,1)S(1)} %get-tuple-element.17), channel_id=1, source_target_pairs={{0,1},{1,0},{2,3},{3,2},{4,5},{5,4},{6,7},{7,6},{8,9},{9,8},{10,11... | collective-permute-start | bytes 307208 | tf_op jit(solution)/shard_map/ppermute | solution.py:617
  13.1 4.4 %collective-permute-start.6 = (bf16[272,128]{1,0:T(8,128)(2,1)S(1)}, bf16[272,128]{1,0:T(8,128)(2,1)S(1)}, u32[]{:S(2)}, u32[]{:S(2)}) collective-permute-start(bf16[272,128]{1,0:T(8,128)(2,1)S(1)} %get-tuple-element.19), channel_id=1, source_target_pairs={{0,2},{1,3},{2,0},{3,1},{4,6},{5,7},{6,4},{7,5},{8,10},{9,11},{10,... | collective-permute-start | bytes 208904 | tf_op jit(solution)/shard_map/ppermute | solution.py:617
  17.5 3.7 %copy-start = (bf16[2,64,16,128]{3,2,1,0:T(8,128)(2,1)S(1)}, bf16[2,64,16,128]{3,2,1,0:T(8,128)(2,1)}, u32[]{:S(2)}) copy-start(bf16[2,64,16,128]{3,2,1,0:T(8,128)(2,1)} %members_ref.1) | copy-start | bytes 1572868
  19.1 2.1 %collective-permute-start.9 = (bf16[272,128]{1,0:T(8,128)(2,1)S(1)}, bf16[272,128]{1,0:T(8,128)(2,1)S(1)}, u32[]{:S(2)}, u32[]{:S(2)}) collective-permute-start(bf16[272,128]{1,0:T(8,128)(2,1)S(1)} %solve.1.own), channel_id=1, source_target_pairs={{0,1},{1,0},{2,3},{3,2},{4,5},{5,4},{6,7},{7,6},{8,9},{9,8},{10,11... | collective-permute-start | bytes 208904 | tf_op jit(solution)/shard_map/ppermute | solution.py:617
  19.1 4.3 %collective-permute-start.8 = (bf16[272,128]{1,0:T(8,128)(2,1)S(1)}, bf16[272,128]{1,0:T(8,128)(2,1)S(1)}, u32[]{:S(2)}, u32[]{:S(2)}) collective-permute-start(bf16[272,128]{1,0:T(8,128)(2,1)S(1)} %solve.1.own), channel_id=1, source_target_pairs={{4,0},{0,1},{6,2},{2,3},{8,4},{1,5},{10,6},{3,7},{12,8},{5,9},{14,... | collective-permute-start | bytes 208904 | tf_op jit(solution)/shard_map/ppermute | solution.py:617
  19.6 3.8 %collective-permute-start.7 = (bf16[272,128]{1,0:T(8,128)(2,1)S(1)}, bf16[272,128]{1,0:T(8,128)(2,1)S(1)}, u32[]{:S(2)}, u32[]{:S(2)}) collective-permute-start(bf16[272,128]{1,0:T(8,128)(2,1)S(1)} %solve.1.own), channel_id=1, source_target_pairs={{0,4},{1,0},{2,6},{3,2},{4,8},{5,1},{6,10},{7,3},{8,12},{9,5},{10,... | collective-permute-start | bytes 208904 | tf_op jit(solution)/shard_map/ppermute | solution.py:617
  23.5 1.8 %collective-permute-start.10 = (bf16[272,128]{1,0:T(8,128)(2,1)S(1)}, bf16[272,128]{1,0:T(8,128)(2,1)S(1)}, u32[]{:S(2)}, u32[]{:S(2)}) collective-permute-start(bf16[272,128]{1,0:T(8,128)(2,1)S(1)} %collective-permute-done.7.climb), channel_id=1, source_target_pairs={{0,1},{1,0},{2,3},{3,2},{4,5},{5,4},{6,7},{7,6},{8,9},{9,8},{10,11... | collective-permute-start | bytes 208904 | tf_op jit(solution)/shard_map/ppermute | solution.py:617
  24.3 1.3 %collective-permute-start.11 = (bf16[272,128]{1,0:T(8,128)(2,1)S(1)}, bf16[272,128]{1,0:T(8,128)(2,1)S(1)}, u32[]{:S(2)}, u32[]{:S(2)}) collective-permute-start(bf16[272,128]{1,0:T(8,128)(2,1)S(1)} %collective-permute-done.8.descend), channel_id=1, source_target_pairs={{0,1},{1,0},{2,3},{3,2},{4,5},{5,4},{6,7},{7,6},{8,9},{9,8},{10,11... | collective-permute-start | bytes 208904 | tf_op jit(solution)/shard_map/ppermute | solution.py:617

commit v9 on v8

--- a/solution.py
+++ b/solution.py
@@ -6,6 +6,7 @@
 from jax.experimental import pallas as pl
 from jax.experimental.pallas import tpu as pltpu
 from jax.sharding import PartitionSpec as P
+
 
 SPACING = 16
 NS_STEPS = 4
@@ -32,7 +33,7 @@
     scale_norm = spread + jnp.sqrt(jnp.sum(gram_matrix * gram_matrix, axis=(1, 2)))
     sqrt_iter = (spread * identity + gram_matrix) / scale_norm[:, None, None]
     inv_iter = jnp.broadcast_to(identity, sqrt_iter.shape)
-    for iteration in range(NS_STEPS):
+    for _ in range(NS_STEPS):
         middle = 1.5 * identity - 0.5 * jnp.einsum(
             "bij,bjk->bik", inv_iter, sqrt_iter, precision=lax.Precision.HIGHEST
         )
@@ -202,7 +203,7 @@
     }
 
 
-def device_call(kernel, operands, out_shape, scratch=(), flops=0, name=None, in_hbm=False, out_hbm=False):
+def device_call(kernel, operands, out_shape, scratch=(), flops=0, in_hbm=False, out_hbm=False):
     single = not isinstance(out_shape, (list, tuple))
     spec = pl.BlockSpec(memory_space=pltpu.VMEM)
     hbm = pl.BlockSpec(memory_space=pltpu.HBM)
@@ -215,7 +216,6 @@
         scratch_shapes=list(scratch),
         cost_estimate=pl.CostEstimate(flops=flops, bytes_accessed=1 << 18, transcendentals=0),
         compiler_params=pltpu.CompilerParams(vmem_limit_bytes=VMEM_LIMIT),
-        name=name,
     )(*operands)
 
 
@@ -492,7 +492,7 @@
     return jnp.where(same, 1.0, 0.0)
 
 
-def shares(levels, size):
+def shares(size):
     span = SPACING // 2
     shape = (1, span, span, size)
     along_x = lax.broadcasted_iota(jnp.int32, shape, 1).astype(jnp.float32) / (2 * span)
@@ -514,11 +514,11 @@
     for at, folded in ((0, jnp.where(first, mine, theirs)), (half, jnp.where(first, theirs, mine))):
         for j in range(half):
             table[128 * (at + j) : 128 * (at + j + 1), :] = rebuild(folded, j, eye)
-    levels, width_x, width_y, size = members_ref.shape
+    levels, width_x, _, size = members_ref.shape
     span = SPACING // 2
     shape = (levels, span, span, size)
     rows = levels * span * span
-    along_x, upper_y = shares(levels, size)
+    along_x, upper_y = shares(size)
     for patch_x in range(width_x // span):
         states = members_ref[:, patch_x * span : (patch_x + 1) * span, :, :].astype(jnp.float32)
         mean = jnp.sum(states, axis=3, keepdims=True) * (1.0 / size)
@@ -538,7 +538,7 @@
     levels, size = part_ref.shape[2] // (SPACING // 2) ** 2, part_ref.shape[3]
     span = SPACING // 2
     shape = (levels, span, span, size)
-    along_x, upper_y = shares(levels, size)
+    along_x, upper_y = shares(size)
     for k in range(count):
         patch_x = first_patch + k
         column = lax.div(patch_x + 1, 2) - first_column
@@ -637,7 +637,6 @@
             pltpu.VMEM((16, size), f32),
             pltpu.SemaphoreType.DMA((7,)),
         ],
-        name="pack",
         in_hbm=True,
     )
     across = send(packed, "across")
@@ -648,7 +647,6 @@
         (*lists, across),
         shape((128, 128), f32),
         flops=6 * 2 * 48 * 256 * 128,
-        name="table",
     )
     tall = size * cols + 16
     near = device_call(
@@ -661,37 +659,33 @@
             pltpu.VMEM((tall, 4 * rows), bf16),
         ],
         flops=2 * tall * size * 4 * rows,
-        name="gram_near",
     )
     near = device_call(
         functools.partial(gram_next_kernel, rows, cols, 5),
         (table, near, across_descend),
         shape((tall, size), f32),
         flops=2 * tall * size * rows,
-        name="gram_next",
     )
     mine, rest = device_call(
         functools.partial(gram_last_kernel, rows, cols, 4),
         (table, near, across_climb),
         [shape((size * half + 8, size), f32), shape((size * half + 16, size), bf16)],
         flops=2 * tall * size * rows,
-        name="gram_last",
     )
     total, half_sum = device_call(
         functools.partial(join_kernel, half),
         (mine, send(rest, "core")),
         [shape((size * half + 8, size), f32), shape((272, size), bf16)],
-        name="join",
     )
     weights = device_call(
         functools.partial(solve_kernel, half),
         (total, send(half_sum, "half")),
         shape((272, size), bf16),
         flops=2 * 27 * half * size**3,
-        name="solve",
     )
     pair = send(weights, "core")
-    up, down = send(weights, "climb"), send(weights, "descend")
+    up = send(weights, "climb")
+    down = send(weights, "descend")
     levels, width_x, width_y, _ = members.shape
     patches = (width_x * 2 // SPACING, 2, levels * SPACING**2 // 4, size)
     part, pert = device_call(
@@ -700,7 +694,6 @@
         [shape(patches, f32), shape(patches, bf16)],
         [pltpu.VMEM((cols * size, size), bf16)],
         flops=2 * levels * width_x * width_y * size * 2 * size,
-        name="apply_near",
     )
     up, down, part = lax.optimization_barrier((up, down, part))
     pair_up, pair_down = send(up, "core"), send(down, "core")
@@ -711,7 +704,6 @@
         [shape((levels, early * span, width_y, size), bf16), shape((2, size, size), bf16)],
         [pltpu.VMEM((2, half * size, size), bf16)],
         flops=2 * levels * span * early * width_y * size * 2 * size,
-        name="far_first",
     )
     count = patches[0] - early
     return device_call(
@@ -724,7 +716,6 @@
             pltpu.SemaphoreType.DMA((count + 1,)),
         ],
         flops=2 * levels * span * count * width_y * size * 2 * size,
-        name="far_rest",
         out_hbm=True,
     )
 

time: 27.1 us -> 27.1 us (level)
  no operation moved by 1% of the time
where the time goes in v9:
time: 27.1 us; the launch traced here: 26.9 us
  starting transfers between devices  12 us (44%)
  waiting for transfers between devices  7.68 us (28%)
  Pallas kernels  7.15 us (26%)
    ppermute x12, starting transfers between devices, send(): return lax.ppermute(value, axes, ways[way])  12 us
    ppermute x12, waiting for transfers between devices, send(): return lax.ppermute(value, axes, ways[way])  7.68 us
    pallas_call x10, Pallas kernels, device_call(): pl.pallas_call(kernel, out_shape=out_shape, in_specs=[hbm if in_hbm else...  7.15 us
  transfers between devices with their start and end apart: 12, of which 8 were waited for; matrix products, arithmetic and copies ran while one was open for 0% of the time, Pallas kernels for 10%

profile of v9, /device:TPU:0, one launch (start us, length us, event | category | flops | bytes accessed | tf_op | source)
XLA Modules:
  0.0 26.9 jit_solution(16051213223272838295)
XLA Ops:
  0.0 1.0 %shard_map.82.b0 = bf16[272,128]{1,0:T(8,128)(2,1)S(1)} custom-call(bf16[256,128]{1,0:T(8,128)(2,1)} %pert.1, bf16[2,128]{1,0:T(2,128)(2,1)} %bitcast.5, bf16[2,128]{1,0:T(2,128)(2,1)} %bitcast.6, s32[4,1,256]{2,1,0:T(1,128)} %owner_ref.1, s32[4,1,256]{2,1,0:T(1,128)} %slot_ref.1, s32[1,4]{1,0:T(1,128)} %bitcast.3, f32[4,1,256]{2,1,0:T(1,128)} %local_ref.1), custom_call_target="tpu_custom_call" | custom-call | bytes 262144 | tf_op jit(solution)/shard_map/pallas_call | solution.py:211
  1.0 3.1 %collective-permute-start = (bf16[272,128]{1,0:T(8,128)(2,1)S(1)}, bf16[272,128]{1,0:T(8,128)(2,1)S(1)}, u32[]{:S(2)}, u32[]{:S(2)}) collective-permute-start(bf16[272,128]{1,0:T(8,128)(2,1)S(1)} %shard_map.82.b0), channel_id=1, source_target_pairs={{0,16},{1,17},{2,18},{3,19},{4,20},{5,21},{6,22},{7,23},{8,24},{9,... | collective-permute-start | bytes 208904 | tf_op jit(solution)/shard_map/ppermute | solution.py:617
  4.1 2.0 %collective-permute-start.1 = (bf16[272,128]{1,0:T(8,128)(2,1)S(1)}, bf16[272,128]{1,0:T(8,128)(2,1)S(1)}, u32[]{:S(2)}, u32[]{:S(2)}) collective-permute-start(bf16[272,128]{1,0:T(8,128)(2,1)S(1)} %shard_map.82.b0), channel_id=1, source_target_pairs={{0,4},{1,0},{2,6},{3,2},{4,8},{5,1},{6,10},{7,3},{8,12},{9,5},{10,... | collective-permute-start | bytes 208904 | tf_op jit(solution)/shard_map/ppermute | solution.py:617
  6.1 0.3 collective-permute-done.other_ref.b3
  6.4 2.1 %collective-permute-start.4 = (bf16[272,128]{1,0:T(8,128)(2,1)S(1)}, bf16[272,128]{1,0:T(8,128)(2,1)S(1)}, u32[]{:S(2)}, u32[]{:S(2)}) collective-permute-start(bf16[272,128]{1,0:T(8,128)(2,1)S(1)} %collective-permute-done.other_ref.b3), channel_id=1, source_target_pairs={{0,4},{1,0},{2,6},{3,2},{4,8},{5,1},{6,10},{7,3},{8,12},{9,5},{10,... | collective-permute-start | bytes 208904 | tf_op jit(solution)/shard_map/ppermute | solution.py:617
  8.5 0.5 %shard_map.83.table_ref = f32[128,128]{1,0:T(8,128)S(1)} custom-call(s32[4,1,256]{2,1,0:T(1,128)S(1)} %copy-done.1, s32[4,1,256]{2,1,0:T(1,128)S(1)} %copy-done.2, s32[1,4]{1,0:T(1,128)S(1)} %bitcast.4, f32[4,1,256]{2,1,0:T(1,128)S(1)} %copy-done.3, bf16[272,128]{1,0:T(8,128)(2,1)S(1)} %collective-permute-done.other_ref.b3), custom_call_target="tpu_custom_call" | custom-call | flops 18874368 | bytes 262144 | tf_op jit(solution)/shard_map/pallas_call | solution.py:211
  9.0 0.1 collective-permute-done.2.b2
  9.1 0.6 %shard_map.84.so_far_ref = f32[784,128]{1,0:T(8,128)S(1)} custom-call(f32[128,128]{1,0:T(8,128)S(1)} %shard_map.83.table_ref, bf16[272,128]{1,0:T(8,128)(2,1)S(1)} %shard_map.82.b0, bf16[272,128]{1,0:T(8,128)(2,1)S(1)} %collective-permute-done.1.b1, bf16[272,128]{1,0:T(8,128)(2,1)S(1)} %collective-permute-done.2.b2, ...), custom_call_target="tpu_custom_call" | custom-call | flops 205520896 | bytes 262144 | tf_op jit(solution)/shard_map/pallas_call | solution.py:211
  9.7 1.3 %collective-permute-done.3.block = bf16[272,128]{1,0:T(8,128)(2,1)S(1)} collective-permute-done((bf16[272,128]{1,0:T(8,128)(2,1)S(1)}, bf16[272,128]{1,0:T(8,128)(2,1)S(1)}, u32[]{:S(2)}, u32[]{:S(2)}) %collective-permute-start.3) | collective-permute-done | bytes 69664 | tf_op jit(solution)/shard_map/ppermute | solution.py:617
  11.0 0.3 %shard_map.85.so_far_ref = f32[784,128]{1,0:T(8,128)S(1)} custom-call(f32[128,128]{1,0:T(8,128)S(1)} %shard_map.83.table_ref, f32[784,128]{1,0:T(8,128)S(1)} %shard_map.84.so_far_ref, bf16[272,128]{1,0:T(8,128)(2,1)S(1)} %collective-permute-done.3.block), custom_call_target="tpu_custom_call" | custom-call | flops 51380224 | bytes 262144 | tf_op jit(solution)/shard_map/pallas_call | solution.py:211
  11.3 0.3 %shard_map.86 = (f32[392,128]{1,0:T(8,128)S(1)}, bf16[400,128]{1,0:T(8,128)(2,1)S(1)}) custom-call(f32[128,128]{1,0:T(8,128)S(1)} %shard_map.83.table_ref, f32[784,128]{1,0:T(8,128)S(1)} %shard_map.85.so_far_ref, bf16[272,128]{1,0:T(8,128)(2,1)S(1)} %collective-permute-done.4.block), custom_call_target="tpu_custom_call" | custom-call | flops 51380224 | bytes 262144 | tf_op jit(solution)/shard_map/pallas_call | solution.py:211
  11.7 1.3 %collective-permute-done.5.got_ref = bf16[400,128]{1,0:T(8,128)(2,1)S(1)} collective-permute-done((bf16[400,128]{1,0:T(8,128)(2,1)S(1)}, bf16[400,128]{1,0:T(8,128)(2,1)S(1)}, u32[]{:S(2)}, u32[]{:S(2)}) %collective-permute-start.5) | collective-permute-done | bytes 102432 | tf_op jit(solution)/shard_map/ppermute | solution.py:617
  13.1 1.8 %collective-permute-start.6 = (bf16[272,128]{1,0:T(8,128)(2,1)S(1)}, bf16[272,128]{1,0:T(8,128)(2,1)S(1)}, u32[]{:S(2)}, u32[]{:S(2)}) collective-permute-start(bf16[272,128]{1,0:T(8,128)(2,1)S(1)} %get-tuple-element.19), channel_id=1, source_target_pairs={{0,2},{1,3},{2,0},{3,1},{4,6},{5,7},{6,4},{7,5},{8,10},{9,11},{10,... | collective-permute-start | bytes 208904 | tf_op jit(solution)/shard_map/ppermute | solution.py:617
  14.9 2.6 %collective-permute-done.6.got_ref = bf16[272,128]{1,0:T(8,128)(2,1)S(1)} collective-permute-done((bf16[272,128]{1,0:T(8,128)(2,1)S(1)}, bf16[272,128]{1,0:T(8,128)(2,1)S(1)}, u32[]{:S(2)}, u32[]{:S(2)}) %collective-permute-start.6) | collective-permute-done | bytes 69664 | tf_op jit(solution)/shard_map/ppermute | solution.py:617
  17.5 1.6 %shard_map.88.own = bf16[272,128]{1,0:T(8,128)(2,1)S(1)} custom-call(f32[392,128]{1,0:T(8,128)S(1)} %get-tuple-element.18.sum_ref, bf16[272,128]{1,0:T(8,128)(2,1)S(1)} %collective-permute-done.6.got_ref), custom_call_target="tpu_custom_call" | custom-call | flops 339738624 | bytes 262144 | tf_op jit(solution)/shard_map/pallas_call | solution.py:211
  19.1 0.5 %collective-permute-start.8 = (bf16[272,128]{1,0:T(8,128)(2,1)S(1)}, bf16[272,128]{1,0:T(8,128)(2,1)S(1)}, u32[]{:S(2)}, u32[]{:S(2)}) collective-permute-start(bf16[272,128]{1,0:T(8,128)(2,1)S(1)} %shard_map.88.own), channel_id=1, source_target_pairs={{4,0},{0,1},{6,2},{2,3},{8,4},{1,5},{10,6},{3,7},{12,8},{5,9},{14,... | collective-permute-start | bytes 208904 | tf_op jit(solution)/shard_map/ppermute | solution.py:617
  19.6 1.5 %collective-permute-start.7 = (bf16[272,128]{1,0:T(8,128)(2,1)S(1)}, bf16[272,128]{1,0:T(8,128)(2,1)S(1)}, u32[]{:S(2)}, u32[]{:S(2)}) collective-permute-start(bf16[272,128]{1,0:T(8,128)(2,1)S(1)} %shard_map.88.own), channel_id=1, source_target_pairs={{0,4},{1,0},{2,6},{3,2},{4,8},{5,1},{6,10},{7,3},{8,12},{9,5},{10,... | collective-permute-start | bytes 208904 | tf_op jit(solution)/shard_map/ppermute | solution.py:617
  21.2 0.7 %shard_map.89 = (f32[8,2,128,128]{3,2,1,0:T(8,128)S(1)}, bf16[8,2,128,128]{3,2,1,0:T(8,128)(2,1)S(1)}) custom-call(bf16[2,64,16,128]{3,2,1,0:T(8,128)(2,1)S(1)} %copy-done, bf16[272,128]{1,0:T(8,128)(2,1)S(1)} %shard_map.88.own, bf16[272,128]{1,0:T(8,128)(2,1)S(1)} %collective-permute-done.9.pair), custom_call_target="tpu_custom_call" | custom-call | flops 134217728 | bytes 262144 | tf_op jit(solution)/shard_map/pallas_call | solution.py:211
  21.9 1.5 %collective-permute-done.8.descend = bf16[272,128]{1,0:T(8,128)(2,1)S(1)} collective-permute-done((bf16[272,128]{1,0:T(8,128)(2,1)S(1)}, bf16[272,128]{1,0:T(8,128)(2,1)S(1)}, u32[]{:S(2)}, u32[]{:S(2)}) %collective-permute-start.8) | collective-permute-done | bytes 69664 | tf_op jit(solution)/shard_map/ppermute | solution.py:617
  23.5 0.9 %collective-permute-start.10 = (bf16[272,128]{1,0:T(8,128)(2,1)S(1)}, bf16[272,128]{1,0:T(8,128)(2,1)S(1)}, u32[]{:S(2)}, u32[]{:S(2)}) collective-permute-start(bf16[272,128]{1,0:T(8,128)(2,1)S(1)} %collective-permute-done.7.climb), channel_id=1, source_target_pairs={{0,1},{1,0},{2,3},{3,2},{4,5},{5,4},{6,7},{7,6},{8,9},{9,8},{10,11... | collective-permute-start | bytes 208904 | tf_op jit(solution)/shard_map/ppermute | solution.py:617
  24.3 0.6 %shard_map.90 = (bf16[2,24,16,128]{3,2,1,0:T(8,128)(2,1)S(1)}, bf16[2,128,128]{2,1,0:T(8,128)(2,1)S(1)}) custom-call(f32[8,2,128,128]{3,2,1,0:T(8,128)S(1)} %get-tuple-element.21.part_ref, bf16[8,2,128,128]{3,2,1,0:T(8,128)(2,1)S(1)} %get-tuple-element.22.pert_ref, bf16[272,128]{1,0:T(8,128)(2,1)S(1)} %shard_map.88.own, ...), custom_call_target="tpu_custom_call" | custom-call | flops 50331648 | bytes 262144 | tf_op jit(solution)/shard_map/pallas_call | solution.py:211
  25.0 0.3 %collective-permute-done.10.pair_climb = bf16[272,128]{1,0:T(8,128)(2,1)S(1)} collective-permute-done((bf16[272,128]{1,0:T(8,128)(2,1)S(1)}, bf16[272,128]{1,0:T(8,128)(2,1)S(1)}, u32[]{:S(2)}, u32[]{:S(2)}) %collective-permute-start.10) | collective-permute-done | bytes 69664 | tf_op jit(solution)/shard_map/ppermute | solution.py:617
  25.2 0.4 %collective-permute-done.11.pair_descend = bf16[272,128]{1,0:T(8,128)(2,1)S(1)} collective-permute-done((bf16[272,128]{1,0:T(8,128)(2,1)S(1)}, bf16[272,128]{1,0:T(8,128)(2,1)S(1)}, u32[]{:S(2)}, u32[]{:S(2)}) %collective-permute-start.11) | collective-permute-done | bytes 69664 | tf_op jit(solution)/shard_map/ppermute | solution.py:617
  25.6 1.3 %shard_map.91 = bf16[2,64,16,128]{3,2,1,0:T(8,128)(2,1)} custom-call(f32[8,2,128,128]{3,2,1,0:T(8,128)S(1)} %get-tuple-element.21.part_ref, bf16[8,2,128,128]{3,2,1,0:T(8,128)(2,1)S(1)} %get-tuple-element.22.pert_ref, bf16[272,128]{1,0:T(8,128)(2,1)S(1)} %collective-permute-done.9.pair, bf16[272,128]{1,0:T(8,128)(2,1)S(1)} %collective-permute-done.10.pair_climb, ...), custom_call_target="tpu_custom_call" | custom-call | flops 83886080 | bytes 262144 | tf_op jit(solution)/shard_map/pallas_call | solution.py:211
  (20 shorter events, 0.2 us)
Async XLA Ops:
  0.0 8.5 %copy-start.1 = (s32[4,1,256]{2,1,0:T(1,128)S(1)}, s32[4,1,256]{2,1,0:T(1,128)}, u32[]{:S(2)}) copy-start(s32[4,1,256]{2,1,0:T(1,128)} %owner_ref.1) | copy-start | bytes 12292
  0.0 8.5 %copy-start.2 = (s32[4,1,256]{2,1,0:T(1,128)S(1)}, s32[4,1,256]{2,1,0:T(1,128)}, u32[]{:S(2)}) copy-start(s32[4,1,256]{2,1,0:T(1,128)} %slot_ref.1) | copy-start | bytes 12292
  0.0 8.5 %copy-start.3 = (f32[4,1,256]{2,1,0:T(1,128)S(1)}, f32[4,1,256]{2,1,0:T(1,128)}, u32[]{:S(2)}) copy-start(f32[4,1,256]{2,1,0:T(1,128)} %local_ref.1) | copy-start | bytes 12292
  0.0 8.5 %copy-start.4 = (s32[4,1]{0,1:T(1,128)S(1)}, s32[4,1]{0,1:T(1,128)}, u32[]{:S(2)}) copy-start(s32[4,1]{0,1:T(1,128)} %param.14) | copy-start | bytes 52
  1.0 5.4 %collective-permute-start = (bf16[272,128]{1,0:T(8,128)(2,1)S(1)}, bf16[272,128]{1,0:T(8,128)(2,1)S(1)}, u32[]{:S(2)}, u32[]{:S(2)}) collective-permute-start(bf16[272,128]{1,0:T(8,128)(2,1)S(1)} %shard_map.82.b0), channel_id=1, source_target_pairs={{0,16},{1,17},{2,18},{3,19},{4,20},{5,21},{6,22},{7,23},{8,24},{9,... | collective-permute-start | bytes 208904 | tf_op jit(solution)/shard_map/ppermute | solution.py:617
  4.1 4.9 %collective-permute-start.2 = (bf16[272,128]{1,0:T(8,128)(2,1)S(1)}, bf16[272,128]{1,0:T(8,128)(2,1)S(1)}, u32[]{:S(2)}, u32[]{:S(2)}) collective-permute-start(bf16[272,128]{1,0:T(8,128)(2,1)S(1)} %shard_map.82.b0), channel_id=1, source_target_pairs={{4,0},{0,1},{6,2},{2,3},{8,4},{1,5},{10,6},{3,7},{12,8},{5,9},{14,... | collective-permute-start | bytes 208904 | tf_op jit(solution)/shard_map/ppermute | solution.py:617
  4.1 4.9 %collective-permute-start.1 = (bf16[272,128]{1,0:T(8,128)(2,1)S(1)}, bf16[272,128]{1,0:T(8,128)(2,1)S(1)}, u32[]{:S(2)}, u32[]{:S(2)}) collective-permute-start(bf16[272,128]{1,0:T(8,128)(2,1)S(1)} %shard_map.82.b0), channel_id=1, source_target_pairs={{0,4},{1,0},{2,6},{3,2},{4,8},{5,1},{6,10},{7,3},{8,12},{9,5},{10,... | collective-permute-start | bytes 208904 | tf_op jit(solution)/shard_map/ppermute | solution.py:617
  6.4 4.6 %collective-permute-start.3 = (bf16[272,128]{1,0:T(8,128)(2,1)S(1)}, bf16[272,128]{1,0:T(8,128)(2,1)S(1)}, u32[]{:S(2)}, u32[]{:S(2)}) collective-permute-start(bf16[272,128]{1,0:T(8,128)(2,1)S(1)} %collective-permute-done.other_ref.b3), channel_id=1, source_target_pairs={{4,0},{0,1},{6,2},{2,3},{8,4},{1,5},{10,6},{3,7},{12,8},{5,9},{14,... | collective-permute-start | bytes 208904 | tf_op jit(solution)/shard_map/ppermute | solution.py:617
  6.4 4.9 %collective-permute-start.4 = (bf16[272,128]{1,0:T(8,128)(2,1)S(1)}, bf16[272,128]{1,0:T(8,128)(2,1)S(1)}, u32[]{:S(2)}, u32[]{:S(2)}) collective-permute-start(bf16[272,128]{1,0:T(8,128)(2,1)S(1)} %collective-permute-done.other_ref.b3), channel_id=1, source_target_pairs={{0,4},{1,0},{2,6},{3,2},{4,8},{5,1},{6,10},{7,3},{8,12},{9,5},{10,... | collective-permute-start | bytes 208904 | tf_op jit(solution)/shard_map/ppermute | solution.py:617
  11.6 1.4 %collective-permute-start.5 = (bf16[400,128]{1,0:T(8,128)(2,1)S(1)}, bf16[400,128]{1,0:T(8,128)(2,1)S(1)}, u32[]{:S(2)}, u32[]{:S(2)}) collective-permute-start(bf16[400,128]{1,0:T(8,128)(2,1)S(1)} %get-tuple-element.17), channel_id=1, source_target_pairs={{0,1},{1,0},{2,3},{3,2},{4,5},{5,4},{6,7},{7,6},{8,9},{9,8},{10,11... | collective-permute-start | bytes 307208 | tf_op jit(solution)/shard_map/ppermute | solution.py:617
  13.1 4.4 %collective-permute-start.6 = (bf16[272,128]{1,0:T(8,128)(2,1)S(1)}, bf16[272,128]{1,0:T(8,128)(2,1)S(1)}, u32[]{:S(2)}, u32[]{:S(2)}) collective-permute-start(bf16[272,128]{1,0:T(8,128)(2,1)S(1)} %get-tuple-element.19), channel_id=1, source_target_pairs={{0,2},{1,3},{2,0},{3,1},{4,6},{5,7},{6,4},{7,5},{8,10},{9,11},{10,... | collective-permute-start | bytes 208904 | tf_op jit(solution)/shard_map/ppermute | solution.py:617
  17.5 3.7 %copy-start = (bf16[2,64,16,128]{3,2,1,0:T(8,128)(2,1)S(1)}, bf16[2,64,16,128]{3,2,1,0:T(8,128)(2,1)}, u32[]{:S(2)}) copy-start(bf16[2,64,16,128]{3,2,1,0:T(8,128)(2,1)} %members_ref.1) | copy-start | bytes 1572868
  19.1 2.1 %collective-permute-start.9 = (bf16[272,128]{1,0:T(8,128)(2,1)S(1)}, bf16[272,128]{1,0:T(8,128)(2,1)S(1)}, u32[]{:S(2)}, u32[]{:S(2)}) collective-permute-start(bf16[272,128]{1,0:T(8,128)(2,1)S(1)} %shard_map.88.own), channel_id=1, source_target_pairs={{0,1},{1,0},{2,3},{3,2},{4,5},{5,4},{6,7},{7,6},{8,9},{9,8},{10,11... | collective-permute-start | bytes 208904 | tf_op jit(solution)/shard_map/ppermute | solution.py:617
  19.1 4.3 %collective-permute-start.8 = (bf16[272,128]{1,0:T(8,128)(2,1)S(1)}, bf16[272,128]{1,0:T(8,128)(2,1)S(1)}, u32[]{:S(2)}, u32[]{:S(2)}) collective-permute-start(bf16[272,128]{1,0:T(8,128)(2,1)S(1)} %shard_map.88.own), channel_id=1, source_target_pairs={{4,0},{0,1},{6,2},{2,3},{8,4},{1,5},{10,6},{3,7},{12,8},{5,9},{14,... | collective-permute-start | bytes 208904 | tf_op jit(solution)/shard_map/ppermute | solution.py:617
  19.6 3.8 %collective-permute-start.7 = (bf16[272,128]{1,0:T(8,128)(2,1)S(1)}, bf16[272,128]{1,0:T(8,128)(2,1)S(1)}, u32[]{:S(2)}, u32[]{:S(2)}) collective-permute-start(bf16[272,128]{1,0:T(8,128)(2,1)S(1)} %shard_map.88.own), channel_id=1, source_target_pairs={{0,4},{1,0},{2,6},{3,2},{4,8},{5,1},{6,10},{7,3},{8,12},{9,5},{10,... | collective-permute-start | bytes 208904 | tf_op jit(solution)/shard_map/ppermute | solution.py:617
  23.5 1.8 %collective-permute-start.10 = (bf16[272,128]{1,0:T(8,128)(2,1)S(1)}, bf16[272,128]{1,0:T(8,128)(2,1)S(1)}, u32[]{:S(2)}, u32[]{:S(2)}) collective-permute-start(bf16[272,128]{1,0:T(8,128)(2,1)S(1)} %collective-permute-done.7.climb), channel_id=1, source_target_pairs={{0,1},{1,0},{2,3},{3,2},{4,5},{5,4},{6,7},{7,6},{8,9},{9,8},{10,11... | collective-permute-start | bytes 208904 | tf_op jit(solution)/shard_map/ppermute | solution.py:617
  24.3 1.3 %collective-permute-start.11 = (bf16[272,128]{1,0:T(8,128)(2,1)S(1)}, bf16[272,128]{1,0:T(8,128)(2,1)S(1)}, u32[]{:S(2)}, u32[]{:S(2)}) collective-permute-start(bf16[272,128]{1,0:T(8,128)(2,1)S(1)} %collective-permute-done.8.descend), channel_id=1, source_target_pairs={{0,1},{1,0},{2,3},{3,2},{4,5},{5,4},{6,7},{7,6},{8,9},{9,8},{10,11... | collective-permute-start | bytes 208904 | tf_op jit(solution)/shard_map/ppermute | solution.py:617

commit v10 on v9

--- a/solution.py
+++ b/solution.py
@@ -337,39 +337,51 @@
     out_ref[...] = gram_blocks(rows, cols, 0, [b0, b1, b2, b3], table_ref, turned, plain, scaled)
 
 
-def gram_block(rows, cols, first, block, table_ref, so_far_ref):
+def block_sums(rows, first, block, table_ref, positions):
     per = rows // 128
     tail = block[rows : rows + 16, :].astype(jnp.float32)
-    weights = [table_ref[8 * hi : 8 * hi + 8, :] * tail[hi - first * per : hi - first * per + 1, :] for hi in range(first * per, (first + 1) * per)]
+    weights = [table_ref[8 * hi : 8 * hi + 8, :] * tail[k : k + 1, :] for k, hi in enumerate(range(first * per, (first + 1) * per))]
     products = [w * tail[per + k : per + k + 1, :] for k, w in enumerate(weights)]
     plain = block[0:rows, :]
     turned = plain.astype(jnp.float32).T
-    weight = jnp.concatenate(weights, axis=1)
-    pieces = []
-    for position in range(cols):
-        scaled = (turned * weight[position : position + 1, :]).astype(jnp.bfloat16)
-        pieces.append(so_far_ref[128 * position : 128 * (position + 1), :] + dot(scaled, plain))
-    both = above(*[p.astype(jnp.float32) for p in split2(jnp.concatenate(products, axis=1))]).astype(jnp.bfloat16)
-    pieces.append(so_far_ref[128 * cols : 128 * cols + 16, :] + dot(both, plain))
-    return pieces
-
-
-def gram_next_kernel(rows, cols, first, table_ref, so_far_ref, block, out_ref):
-    for k, piece in enumerate(gram_block(rows, cols, first, block, table_ref, so_far_ref)):
-        out_ref[128 * k : 128 * k + piece.shape[0], :] = piece
-
-
-def gram_last_kernel(rows, cols, first, table_ref, so_far_ref, block, mine_ref, rest_ref):
+    weight = beside(*weights)
+    both = above(*[p.astype(jnp.float32) for p in split2(beside(*products))]).astype(jnp.bfloat16)
+    return [dot((turned * weight[p : p + 1, :]).astype(jnp.bfloat16), plain) for p in positions] + [dot(both, plain)]
+
+
+def earlier_sums(cols, so_far_ref, positions):
+    return [so_far_ref[128 * p : 128 * (p + 1), :] for p in positions] + [so_far_ref[128 * cols : 128 * cols + 16, :]]
+
+
+def rest_next_kernel(rows, cols, first, table_ref, so_far_ref, block, out_ref):
+    positions = range(cols // 2, cols)
+    pieces = zip(earlier_sums(cols, so_far_ref, positions), block_sums(rows, first, block, table_ref, positions))
+    for k, (x, y) in enumerate(pieces):
+        out_ref[128 * k : 128 * k + x.shape[0], :] = x + y
+
+
+def rest_last_kernel(rows, cols, first, table_ref, so_far_ref, block, out_ref):
     half = cols // 2
-    pieces = gram_block(rows, cols, first, block, table_ref, so_far_ref)
+    edge = 128 * half
+    news = block_sums(rows, first, block, table_ref, range(half, cols))
     for k in range(half):
-        mine_ref[128 * k : 128 * (k + 1), :] = pieces[k]
-        rest_ref[128 * k : 128 * (k + 1), :] = pieces[half + k].astype(jnp.bfloat16)
-    projected = pieces[cols][0:8] + pieces[cols][8:16]
-    edge = 128 * half
-    mine_ref[edge : edge + 8, :] = projected
+        part = slice(128 * k, 128 * (k + 1))
+        out_ref[part, :] = (so_far_ref[part, :] + news[k]).astype(jnp.bfloat16)
+    both = so_far_ref[edge : edge + 16, :] + news[half]
+    projected = both[0:8] + both[8:16]
     high, low = split2(above(projected[half : 2 * half], jnp.zeros((8 - half, 128), jnp.float32)))
-    rest_ref[edge : edge + 16, :] = above(high.astype(jnp.float32), low.astype(jnp.float32)).astype(jnp.bfloat16)
+    out_ref[edge : edge + 16, :] = above(high.astype(jnp.float32), low.astype(jnp.float32)).astype(jnp.bfloat16)
+
+
+def mine_kernel(rows, cols, first, table_ref, so_far_ref, b4, b5, out_ref):
+    half = cols // 2
+    positions = range(half)
+    groups = [earlier_sums(cols, so_far_ref, positions)]
+    groups += [block_sums(rows, first + k, block, table_ref, positions) for k, block in enumerate((b4, b5))]
+    sums = [x + y + z for x, y, z in zip(*groups)]
+    for k in range(half):
+        out_ref[128 * k : 128 * (k + 1), :] = sums[k]
+    out_ref[128 * half : 128 * half + 8, :] = sums[half][0:8] + sums[half][8:16]
 
 
 def lanes_from(lane, values, others=0.0):
@@ -660,16 +672,22 @@
         ],
         flops=2 * tall * size * 4 * rows,
     )
-    near = device_call(
-        functools.partial(gram_next_kernel, rows, cols, 5),
+    rest = device_call(
+        functools.partial(rest_next_kernel, rows, cols, 5),
         (table, near, across_descend),
-        shape((tall, size), f32),
-        flops=2 * tall * size * rows,
-    )
-    mine, rest = device_call(
-        functools.partial(gram_last_kernel, rows, cols, 4),
-        (table, near, across_climb),
-        [shape((size * half + 8, size), f32), shape((size * half + 16, size), bf16)],
+        shape((size * half + 16, size), f32),
+        flops=tall * size * rows,
+    )
+    rest = device_call(
+        functools.partial(rest_last_kernel, rows, cols, 4),
+        (table, rest, across_climb),
+        shape((size * half + 16, size), bf16),
+        flops=tall * size * rows,
+    )
+    mine = device_call(
+        functools.partial(mine_kernel, rows, cols, 4),
+        (table, near, across_climb, across_descend),
+        shape((size * half + 8, size), f32),
         flops=2 * tall * size * rows,
     )
     total, half_sum = device_call(

time: 27.1 us -> 27 us (level)
  waiting for transfers between devices: 7.68 us -> 7.35 us
    ppermute x12, waiting for transfers between devices: 7.68 us -> 7.35 us  [send(): return lax.ppermute(value, axes, ways[way])]
    pallas_call x10 -> x11, Pallas kernels: 7.15 us -> 7.4 us  [device_call(): pl.pallas_call(kernel, out_shape=out_shape, in_specs=[hbm if in_hbm else...]
  transfers between devices with their start and end apart: 12 -> 12, of which waited for: 8 -> 8; matrix products, arithmetic and copies ran while one was open for 0% -> 0% of each run, Pallas kernels for 10% -> 11%
where the time goes in v10:
time: 27 us; the launch traced here: 26.9 us
  starting transfers between devices  12 us (44%)
  Pallas kernels  7.4 us (27%)
  waiting for transfers between devices  7.35 us (27%)
    ppermute x12, starting transfers between devices, send(): return lax.ppermute(value, axes, ways[way])  12 us
    pallas_call x11, Pallas kernels, device_call(): pl.pallas_call(kernel, out_shape=out_shape, in_specs=[hbm if in_hbm else...  7.4 us
    ppermute x12, waiting for transfers between devices, send(): return lax.ppermute(value, axes, ways[way])  7.35 us
  transfers between devices with their start and end apart: 12, of which 8 were waited for; matrix products, arithmetic and copies ran while one was open for 0% of the time, Pallas kernels for 11%

profile of v10, /device:TPU:0, one launch (start us, length us, event | category | flops | bytes accessed | tf_op | source)
XLA Modules:
  0.0 26.9 jit_solution(17097023714935649741)
XLA Ops:
  0.0 1.0 %shard_map.82.b0 = bf16[272,128]{1,0:T(8,128)(2,1)S(1)} custom-call(bf16[256,128]{1,0:T(8,128)(2,1)} %pert.1, bf16[2,128]{1,0:T(2,128)(2,1)} %bitcast.5, bf16[2,128]{1,0:T(2,128)(2,1)} %bitcast.6, s32[4,1,256]{2,1,0:T(1,128)} %owner_ref.1, s32[4,1,256]{2,1,0:T(1,128)} %slot_ref.1, s32[1,4]{1,0:T(1,128)} %bitcast.3, f32[4,1,256]{2,1,0:T(1,128)} %local_ref.1), custom_call_target="tpu_custom_call" | custom-call | bytes 262144 | tf_op jit(solution)/shard_map/pallas_call | solution.py:211
  1.0 3.1 %collective-permute-start = (bf16[272,128]{1,0:T(8,128)(2,1)S(1)}, bf16[272,128]{1,0:T(8,128)(2,1)S(1)}, u32[]{:S(2)}, u32[]{:S(2)}) collective-permute-start(bf16[272,128]{1,0:T(8,128)(2,1)S(1)} %shard_map.82.b0), channel_id=1, source_target_pairs={{0,16},{1,17},{2,18},{3,19},{4,20},{5,21},{6,22},{7,23},{8,24},{9,... | collective-permute-start | bytes 208904 | tf_op jit(solution)/shard_map/ppermute | solution.py:629
  4.1 2.0 %collective-permute-start.1 = (bf16[272,128]{1,0:T(8,128)(2,1)S(1)}, bf16[272,128]{1,0:T(8,128)(2,1)S(1)}, u32[]{:S(2)}, u32[]{:S(2)}) collective-permute-start(bf16[272,128]{1,0:T(8,128)(2,1)S(1)} %shard_map.82.b0), channel_id=1, source_target_pairs={{0,4},{1,0},{2,6},{3,2},{4,8},{5,1},{6,10},{7,3},{8,12},{9,5},{10,... | collective-permute-start | bytes 208904 | tf_op jit(solution)/shard_map/ppermute | solution.py:629
  6.1 0.3 collective-permute-done.other_ref.b3
  6.4 2.1 %collective-permute-start.3 = (bf16[272,128]{1,0:T(8,128)(2,1)S(1)}, bf16[272,128]{1,0:T(8,128)(2,1)S(1)}, u32[]{:S(2)}, u32[]{:S(2)}) collective-permute-start(bf16[272,128]{1,0:T(8,128)(2,1)S(1)} %collective-permute-done.other_ref.b3), channel_id=1, source_target_pairs={{0,4},{1,0},{2,6},{3,2},{4,8},{5,1},{6,10},{7,3},{8,12},{9,5},{10,... | collective-permute-start | bytes 208904 | tf_op jit(solution)/shard_map/ppermute | solution.py:629
  8.5 0.5 %shard_map.83.table_ref = f32[128,128]{1,0:T(8,128)S(1)} custom-call(s32[4,1,256]{2,1,0:T(1,128)S(1)} %copy-done.1, s32[4,1,256]{2,1,0:T(1,128)S(1)} %copy-done.2, s32[1,4]{1,0:T(1,128)S(1)} %bitcast.4, f32[4,1,256]{2,1,0:T(1,128)S(1)} %copy-done.3, bf16[272,128]{1,0:T(8,128)(2,1)S(1)} %collective-permute-done.other_ref.b3), custom_call_target="tpu_custom_call" | custom-call | flops 18874368 | bytes 262144 | tf_op jit(solution)/shard_map/pallas_call | solution.py:211
  9.1 0.6 %shard_map.84.so_far_ref = f32[784,128]{1,0:T(8,128)S(1)} custom-call(f32[128,128]{1,0:T(8,128)S(1)} %shard_map.83.table_ref, bf16[272,128]{1,0:T(8,128)(2,1)S(1)} %shard_map.82.b0, bf16[272,128]{1,0:T(8,128)(2,1)S(1)} %collective-permute-done.1.b1, bf16[272,128]{1,0:T(8,128)(2,1)S(1)} %collective-permute-done.2.b2, ...), custom_call_target="tpu_custom_call" | custom-call | flops 205520896 | bytes 262144 | tf_op jit(solution)/shard_map/pallas_call | solution.py:211
  9.7 1.3 %collective-permute-done.4.b5.block = bf16[272,128]{1,0:T(8,128)(2,1)S(1)} collective-permute-done((bf16[272,128]{1,0:T(8,128)(2,1)S(1)}, bf16[272,128]{1,0:T(8,128)(2,1)S(1)}, u32[]{:S(2)}, u32[]{:S(2)}) %collective-permute-start.4) | collective-permute-done | bytes 69664 | tf_op jit(solution)/shard_map/ppermute | solution.py:629
  11.0 0.3 %shard_map.86.so_far_ref = f32[400,128]{1,0:T(8,128)S(1)} custom-call(f32[128,128]{1,0:T(8,128)S(1)} %shard_map.83.table_ref, f32[784,128]{1,0:T(8,128)S(1)} %shard_map.84.so_far_ref, bf16[272,128]{1,0:T(8,128)(2,1)S(1)} %collective-permute-done.4.b5.block), custom_call_target="tpu_custom_call" | custom-call | flops 25690112 | bytes 262144 | tf_op jit(solution)/shard_map/pallas_call | solution.py:211
  11.3 0.3 %shard_map.87 = bf16[400,128]{1,0:T(8,128)(2,1)S(1)} custom-call(f32[128,128]{1,0:T(8,128)S(1)} %shard_map.83.table_ref, f32[400,128]{1,0:T(8,128)S(1)} %shard_map.86.so_far_ref, bf16[272,128]{1,0:T(8,128)(2,1)S(1)} %collective-permute-done.3.b4.block), custom_call_target="tpu_custom_call" | custom-call | flops 25690112 | bytes 262144 | tf_op jit(solution)/shard_map/pallas_call | solution.py:211
  11.6 0.3 %shard_map.85.mine_ref = f32[392,128]{1,0:T(8,128)S(1)} custom-call(f32[128,128]{1,0:T(8,128)S(1)} %shard_map.83.table_ref, f32[784,128]{1,0:T(8,128)S(1)} %shard_map.84.so_far_ref, bf16[272,128]{1,0:T(8,128)(2,1)S(1)} %collective-permute-done.3.b4.block, bf16[272,128]{1,0:T(8,128)(2,1)S(1)} %collective-permute-done.4.b5.block), custom_call_target="tpu_custom_call" | custom-call | flops 51380224 | bytes 262144 | tf_op jit(solution)/shard_map/pallas_call | solution.py:211
  12.0 1.0 %collective-permute-done.5.got_ref = bf16[400,128]{1,0:T(8,128)(2,1)S(1)} collective-permute-done((bf16[400,128]{1,0:T(8,128)(2,1)S(1)}, bf16[400,128]{1,0:T(8,128)(2,1)S(1)}, u32[]{:S(2)}, u32[]{:S(2)}) %collective-permute-start.5) | collective-permute-done | bytes 102432 | tf_op jit(solution)/shard_map/ppermute | solution.py:629
  13.0 1.8 %collective-permute-start.6 = (bf16[272,128]{1,0:T(8,128)(2,1)S(1)}, bf16[272,128]{1,0:T(8,128)(2,1)S(1)}, u32[]{:S(2)}, u32[]{:S(2)}) collective-permute-start(bf16[272,128]{1,0:T(8,128)(2,1)S(1)} %get-tuple-element.15), channel_id=1, source_target_pairs={{0,2},{1,3},{2,0},{3,1},{4,6},{5,7},{6,4},{7,5},{8,10},{9,11},{10,... | collective-permute-start | bytes 208904 | tf_op jit(solution)/shard_map/ppermute | solution.py:629
  14.8 2.6 %collective-permute-done.6.got_ref = bf16[272,128]{1,0:T(8,128)(2,1)S(1)} collective-permute-done((bf16[272,128]{1,0:T(8,128)(2,1)S(1)}, bf16[272,128]{1,0:T(8,128)(2,1)S(1)}, u32[]{:S(2)}, u32[]{:S(2)}) %collective-permute-start.6) | collective-permute-done | bytes 69664 | tf_op jit(solution)/shard_map/ppermute | solution.py:629
  17.4 1.6 %shard_map.89.own = bf16[272,128]{1,0:T(8,128)(2,1)S(1)} custom-call(f32[392,128]{1,0:T(8,128)S(1)} %get-tuple-element.14.sum_ref, bf16[272,128]{1,0:T(8,128)(2,1)S(1)} %collective-permute-done.6.got_ref), custom_call_target="tpu_custom_call" | custom-call | flops 339738624 | bytes 262144 | tf_op jit(solution)/shard_map/pallas_call | solution.py:211
  19.1 0.5 %collective-permute-start.8 = (bf16[272,128]{1,0:T(8,128)(2,1)S(1)}, bf16[272,128]{1,0:T(8,128)(2,1)S(1)}, u32[]{:S(2)}, u32[]{:S(2)}) collective-permute-start(bf16[272,128]{1,0:T(8,128)(2,1)S(1)} %shard_map.89.own), channel_id=1, source_target_pairs={{4,0},{0,1},{6,2},{2,3},{8,4},{1,5},{10,6},{3,7},{12,8},{5,9},{14,... | collective-permute-start | bytes 208904 | tf_op jit(solution)/shard_map/ppermute | solution.py:629
  19.6 1.5 %collective-permute-start.7 = (bf16[272,128]{1,0:T(8,128)(2,1)S(1)}, bf16[272,128]{1,0:T(8,128)(2,1)S(1)}, u32[]{:S(2)}, u32[]{:S(2)}) collective-permute-start(bf16[272,128]{1,0:T(8,128)(2,1)S(1)} %shard_map.89.own), channel_id=1, source_target_pairs={{0,4},{1,0},{2,6},{3,2},{4,8},{5,1},{6,10},{7,3},{8,12},{9,5},{10,... | collective-permute-start | bytes 208904 | tf_op jit(solution)/shard_map/ppermute | solution.py:629
  21.1 0.7 %shard_map.90 = (f32[8,2,128,128]{3,2,1,0:T(8,128)S(1)}, bf16[8,2,128,128]{3,2,1,0:T(8,128)(2,1)S(1)}) custom-call(bf16[2,64,16,128]{3,2,1,0:T(8,128)(2,1)S(1)} %copy-done, bf16[272,128]{1,0:T(8,128)(2,1)S(1)} %shard_map.89.own, bf16[272,128]{1,0:T(8,128)(2,1)S(1)} %collective-permute-done.9.pair), custom_call_target="tpu_custom_call" | custom-call | flops 134217728 | bytes 262144 | tf_op jit(solution)/shard_map/pallas_call | solution.py:211
  21.9 1.5 %collective-permute-done.8.descend = bf16[272,128]{1,0:T(8,128)(2,1)S(1)} collective-permute-done((bf16[272,128]{1,0:T(8,128)(2,1)S(1)}, bf16[272,128]{1,0:T(8,128)(2,1)S(1)}, u32[]{:S(2)}, u32[]{:S(2)}) %collective-permute-start.8) | collective-permute-done | bytes 69664 | tf_op jit(solution)/shard_map/ppermute | solution.py:629
  23.4 0.9 %collective-permute-start.10 = (bf16[272,128]{1,0:T(8,128)(2,1)S(1)}, bf16[272,128]{1,0:T(8,128)(2,1)S(1)}, u32[]{:S(2)}, u32[]{:S(2)}) collective-permute-start(bf16[272,128]{1,0:T(8,128)(2,1)S(1)} %collective-permute-done.7.climb), channel_id=1, source_target_pairs={{0,1},{1,0},{2,3},{3,2},{4,5},{5,4},{6,7},{7,6},{8,9},{9,8},{10,11... | collective-permute-start | bytes 208904 | tf_op jit(solution)/shard_map/ppermute | solution.py:629
  24.3 0.6 %shard_map.91 = (bf16[2,24,16,128]{3,2,1,0:T(8,128)(2,1)S(1)}, bf16[2,128,128]{2,1,0:T(8,128)(2,1)S(1)}) custom-call(f32[8,2,128,128]{3,2,1,0:T(8,128)S(1)} %get-tuple-element.17.part_ref, bf16[8,2,128,128]{3,2,1,0:T(8,128)(2,1)S(1)} %get-tuple-element.18.pert_ref, bf16[272,128]{1,0:T(8,128)(2,1)S(1)} %shard_map.89.own, ...), custom_call_target="tpu_custom_call" | custom-call | flops 50331648 | bytes 262144 | tf_op jit(solution)/shard_map/pallas_call | solution.py:211
  24.9 0.3 %collective-permute-done.10.pair_climb = bf16[272,128]{1,0:T(8,128)(2,1)S(1)} collective-permute-done((bf16[272,128]{1,0:T(8,128)(2,1)S(1)}, bf16[272,128]{1,0:T(8,128)(2,1)S(1)}, u32[]{:S(2)}, u32[]{:S(2)}) %collective-permute-start.10) | collective-permute-done | bytes 69664 | tf_op jit(solution)/shard_map/ppermute | solution.py:629
  25.2 0.4 %collective-permute-done.11.pair_descend = bf16[272,128]{1,0:T(8,128)(2,1)S(1)} collective-permute-done((bf16[272,128]{1,0:T(8,128)(2,1)S(1)}, bf16[272,128]{1,0:T(8,128)(2,1)S(1)}, u32[]{:S(2)}, u32[]{:S(2)}) %collective-permute-start.11) | collective-permute-done | bytes 69664 | tf_op jit(solution)/shard_map/ppermute | solution.py:629
  25.5 1.3 %shard_map.92 = bf16[2,64,16,128]{3,2,1,0:T(8,128)(2,1)} custom-call(f32[8,2,128,128]{3,2,1,0:T(8,128)S(1)} %get-tuple-element.17.part_ref, bf16[8,2,128,128]{3,2,1,0:T(8,128)(2,1)S(1)} %get-tuple-element.18.pert_ref, bf16[272,128]{1,0:T(8,128)(2,1)S(1)} %collective-permute-done.9.pair, bf16[272,128]{1,0:T(8,128)(2,1)S(1)} %collective-permute-done.10.pair_climb, ...), custom_call_target="tpu_custom_call" | custom-call | flops 83886080 | bytes 262144 | tf_op jit(solution)/shard_map/pallas_call | solution.py:211
  (21 shorter events, 0.3 us)
Async XLA Ops:
  0.0 8.5 %copy-start.1 = (s32[4,1,256]{2,1,0:T(1,128)S(1)}, s32[4,1,256]{2,1,0:T(1,128)}, u32[]{:S(2)}) copy-start(s32[4,1,256]{2,1,0:T(1,128)} %owner_ref.1) | copy-start | bytes 12292
  0.0 8.5 %copy-start.2 = (s32[4,1,256]{2,1,0:T(1,128)S(1)}, s32[4,1,256]{2,1,0:T(1,128)}, u32[]{:S(2)}) copy-start(s32[4,1,256]{2,1,0:T(1,128)} %slot_ref.1) | copy-start | bytes 12292
  0.0 8.5 %copy-start.3 = (f32[4,1,256]{2,1,0:T(1,128)S(1)}, f32[4,1,256]{2,1,0:T(1,128)}, u32[]{:S(2)}) copy-start(f32[4,1,256]{2,1,0:T(1,128)} %local_ref.1) | copy-start | bytes 12292
  0.0 8.5 %copy-start.4 = (s32[4,1]{0,1:T(1,128)S(1)}, s32[4,1]{0,1:T(1,128)}, u32[]{:S(2)}) copy-start(s32[4,1]{0,1:T(1,128)} %param.14) | copy-start | bytes 52
  1.0 5.4 %collective-permute-start = (bf16[272,128]{1,0:T(8,128)(2,1)S(1)}, bf16[272,128]{1,0:T(8,128)(2,1)S(1)}, u32[]{:S(2)}, u32[]{:S(2)}) collective-permute-start(bf16[272,128]{1,0:T(8,128)(2,1)S(1)} %shard_map.82.b0), channel_id=1, source_target_pairs={{0,16},{1,17},{2,18},{3,19},{4,20},{5,21},{6,22},{7,23},{8,24},{9,... | collective-permute-start | bytes 208904 | tf_op jit(solution)/shard_map/ppermute | solution.py:629
  4.1 4.9 %collective-permute-start.2 = (bf16[272,128]{1,0:T(8,128)(2,1)S(1)}, bf16[272,128]{1,0:T(8,128)(2,1)S(1)}, u32[]{:S(2)}, u32[]{:S(2)}) collective-permute-start(bf16[272,128]{1,0:T(8,128)(2,1)S(1)} %shard_map.82.b0), channel_id=1, source_target_pairs={{4,0},{0,1},{6,2},{2,3},{8,4},{1,5},{10,6},{3,7},{12,8},{5,9},{14,... | collective-permute-start | bytes 208904 | tf_op jit(solution)/shard_map/ppermute | solution.py:629
  4.1 4.9 %collective-permute-start.1 = (bf16[272,128]{1,0:T(8,128)(2,1)S(1)}, bf16[272,128]{1,0:T(8,128)(2,1)S(1)}, u32[]{:S(2)}, u32[]{:S(2)}) collective-permute-start(bf16[272,128]{1,0:T(8,128)(2,1)S(1)} %shard_map.82.b0), channel_id=1, source_target_pairs={{0,4},{1,0},{2,6},{3,2},{4,8},{5,1},{6,10},{7,3},{8,12},{9,5},{10,... | collective-permute-start | bytes 208904 | tf_op jit(solution)/shard_map/ppermute | solution.py:629
  6.4 4.6 %collective-permute-start.4 = (bf16[272,128]{1,0:T(8,128)(2,1)S(1)}, bf16[272,128]{1,0:T(8,128)(2,1)S(1)}, u32[]{:S(2)}, u32[]{:S(2)}) collective-permute-start(bf16[272,128]{1,0:T(8,128)(2,1)S(1)} %collective-permute-done.other_ref.b3), channel_id=1, source_target_pairs={{4,0},{0,1},{6,2},{2,3},{8,4},{1,5},{10,6},{3,7},{12,8},{5,9},{14,... | collective-permute-start | bytes 208904 | tf_op jit(solution)/shard_map/ppermute | solution.py:629
  6.4 4.8 %collective-permute-start.3 = (bf16[272,128]{1,0:T(8,128)(2,1)S(1)}, bf16[272,128]{1,0:T(8,128)(2,1)S(1)}, u32[]{:S(2)}, u32[]{:S(2)}) collective-permute-start(bf16[272,128]{1,0:T(8,128)(2,1)S(1)} %collective-permute-done.other_ref.b3), channel_id=1, source_target_pairs={{0,4},{1,0},{2,6},{3,2},{4,8},{5,1},{6,10},{7,3},{8,12},{9,5},{10,... | collective-permute-start | bytes 208904 | tf_op jit(solution)/shard_map/ppermute | solution.py:629
  11.5 1.4 %collective-permute-start.5 = (bf16[400,128]{1,0:T(8,128)(2,1)S(1)}, bf16[400,128]{1,0:T(8,128)(2,1)S(1)}, u32[]{:S(2)}, u32[]{:S(2)}) collective-permute-start(bf16[400,128]{1,0:T(8,128)(2,1)S(1)} %shard_map.87), channel_id=1, source_target_pairs={{0,1},{1,0},{2,3},{3,2},{4,5},{5,4},{6,7},{7,6},{8,9},{9,8},{10,11... | collective-permute-start | bytes 307208 | tf_op jit(solution)/shard_map/ppermute | solution.py:629
  13.0 4.4 %collective-permute-start.6 = (bf16[272,128]{1,0:T(8,128)(2,1)S(1)}, bf16[272,128]{1,0:T(8,128)(2,1)S(1)}, u32[]{:S(2)}, u32[]{:S(2)}) collective-permute-start(bf16[272,128]{1,0:T(8,128)(2,1)S(1)} %get-tuple-element.15), channel_id=1, source_target_pairs={{0,2},{1,3},{2,0},{3,1},{4,6},{5,7},{6,4},{7,5},{8,10},{9,11},{10,... | collective-permute-start | bytes 208904 | tf_op jit(solution)/shard_map/ppermute | solution.py:629
  17.4 3.7 %copy-start = (bf16[2,64,16,128]{3,2,1,0:T(8,128)(2,1)S(1)}, bf16[2,64,16,128]{3,2,1,0:T(8,128)(2,1)}, u32[]{:S(2)}) copy-start(bf16[2,64,16,128]{3,2,1,0:T(8,128)(2,1)} %members_ref.1) | copy-start | bytes 1572868
  19.0 2.1 %collective-permute-start.9 = (bf16[272,128]{1,0:T(8,128)(2,1)S(1)}, bf16[272,128]{1,0:T(8,128)(2,1)S(1)}, u32[]{:S(2)}, u32[]{:S(2)}) collective-permute-start(bf16[272,128]{1,0:T(8,128)(2,1)S(1)} %shard_map.89.own), channel_id=1, source_target_pairs={{0,1},{1,0},{2,3},{3,2},{4,5},{5,4},{6,7},{7,6},{8,9},{9,8},{10,11... | collective-permute-start | bytes 208904 | tf_op jit(solution)/shard_map/ppermute | solution.py:629
  19.1 4.3 %collective-permute-start.8 = (bf16[272,128]{1,0:T(8,128)(2,1)S(1)}, bf16[272,128]{1,0:T(8,128)(2,1)S(1)}, u32[]{:S(2)}, u32[]{:S(2)}) collective-permute-start(bf16[272,128]{1,0:T(8,128)(2,1)S(1)} %shard_map.89.own), channel_id=1, source_target_pairs={{4,0},{0,1},{6,2},{2,3},{8,4},{1,5},{10,6},{3,7},{12,8},{5,9},{14,... | collective-permute-start | bytes 208904 | tf_op jit(solution)/shard_map/ppermute | solution.py:629
  19.6 3.8 %collective-permute-start.7 = (bf16[272,128]{1,0:T(8,128)(2,1)S(1)}, bf16[272,128]{1,0:T(8,128)(2,1)S(1)}, u32[]{:S(2)}, u32[]{:S(2)}) collective-permute-start(bf16[272,128]{1,0:T(8,128)(2,1)S(1)} %shard_map.89.own), channel_id=1, source_target_pairs={{0,4},{1,0},{2,6},{3,2},{4,8},{5,1},{6,10},{7,3},{8,12},{9,5},{10,... | collective-permute-start | bytes 208904 | tf_op jit(solution)/shard_map/ppermute | solution.py:629
  23.4 1.8 %collective-permute-start.10 = (bf16[272,128]{1,0:T(8,128)(2,1)S(1)}, bf16[272,128]{1,0:T(8,128)(2,1)S(1)}, u32[]{:S(2)}, u32[]{:S(2)}) collective-permute-start(bf16[272,128]{1,0:T(8,128)(2,1)S(1)} %collective-permute-done.7.climb), channel_id=1, source_target_pairs={{0,1},{1,0},{2,3},{3,2},{4,5},{5,4},{6,7},{7,6},{8,9},{9,8},{10,11... | collective-permute-start | bytes 208904 | tf_op jit(solution)/shard_map/ppermute | solution.py:629
  24.2 1.3 %collective-permute-start.11 = (bf16[272,128]{1,0:T(8,128)(2,1)S(1)}, bf16[272,128]{1,0:T(8,128)(2,1)S(1)}, u32[]{:S(2)}, u32[]{:S(2)}) collective-permute-start(bf16[272,128]{1,0:T(8,128)(2,1)S(1)} %collective-permute-done.8.descend), channel_id=1, source_target_pairs={{0,1},{1,0},{2,3},{3,2},{4,5},{5,4},{6,7},{7,6},{8,9},{9,8},{10,11... | collective-permute-start | bytes 208904 | tf_op jit(solution)/shard_map/ppermute | solution.py:629

commit v11 on v10

--- a/solution.py
+++ b/solution.py
@@ -11,6 +11,7 @@
 SPACING = 16
 NS_STEPS = 4
 VMEM_LIMIT = 12 << 20
+LANES = 128
 
 
 def padded(array, sides, width):
@@ -353,32 +354,26 @@
     return [so_far_ref[128 * p : 128 * (p + 1), :] for p in positions] + [so_far_ref[128 * cols : 128 * cols + 16, :]]
 
 
-def rest_next_kernel(rows, cols, first, table_ref, so_far_ref, block, out_ref):
-    positions = range(cols // 2, cols)
-    pieces = zip(earlier_sums(cols, so_far_ref, positions), block_sums(rows, first, block, table_ref, positions))
-    for k, (x, y) in enumerate(pieces):
-        out_ref[128 * k : 128 * k + x.shape[0], :] = x + y
-
-
-def rest_last_kernel(rows, cols, first, table_ref, so_far_ref, block, out_ref):
+def two_block_sums(rows, cols, first, table_ref, so_far_ref, b4, b5, positions):
+    groups = [earlier_sums(cols, so_far_ref, positions)]
+    groups += [block_sums(rows, first + k, block, table_ref, positions) for k, block in enumerate((b4, b5))]
+    return [x + y + z for x, y, z in zip(*groups)]
+
+
+def rest_kernel(rows, cols, first, table_ref, so_far_ref, b4, b5, out_ref):
     half = cols // 2
     edge = 128 * half
-    news = block_sums(rows, first, block, table_ref, range(half, cols))
+    sums = two_block_sums(rows, cols, first, table_ref, so_far_ref, b4, b5, range(half, cols))
     for k in range(half):
-        part = slice(128 * k, 128 * (k + 1))
-        out_ref[part, :] = (so_far_ref[part, :] + news[k]).astype(jnp.bfloat16)
-    both = so_far_ref[edge : edge + 16, :] + news[half]
-    projected = both[0:8] + both[8:16]
+        out_ref[128 * k : 128 * (k + 1), :] = sums[k].astype(jnp.bfloat16)
+    projected = sums[half][0:8] + sums[half][8:16]
     high, low = split2(above(projected[half : 2 * half], jnp.zeros((8 - half, 128), jnp.float32)))
     out_ref[edge : edge + 16, :] = above(high.astype(jnp.float32), low.astype(jnp.float32)).astype(jnp.bfloat16)
 
 
 def mine_kernel(rows, cols, first, table_ref, so_far_ref, b4, b5, out_ref):
     half = cols // 2
-    positions = range(half)
-    groups = [earlier_sums(cols, so_far_ref, positions)]
-    groups += [block_sums(rows, first + k, block, table_ref, positions) for k, block in enumerate((b4, b5))]
-    sums = [x + y + z for x, y, z in zip(*groups)]
+    sums = two_block_sums(rows, cols, first, table_ref, so_far_ref, b4, b5, range(half))
     for k in range(half):
         out_ref[128 * k : 128 * (k + 1), :] = sums[k]
     out_ref[128 * half : 128 * half + 8, :] = sums[half][0:8] + sums[half][8:16]
@@ -657,7 +652,7 @@
     table = device_call(
         functools.partial(table_kernel, rows, cols),
         (*lists, across),
-        shape((128, 128), f32),
+        shape((136, 128), f32),
         flops=6 * 2 * 48 * 256 * 128,
     )
     tall = size * cols + 16
@@ -673,16 +668,10 @@
         flops=2 * tall * size * 4 * rows,
     )
     rest = device_call(
-        functools.partial(rest_next_kernel, rows, cols, 5),
-        (table, near, across_descend),
-        shape((size * half + 16, size), f32),
-        flops=tall * size * rows,
-    )
-    rest = device_call(
-        functools.partial(rest_last_kernel, rows, cols, 4),
-        (table, rest, across_climb),
+        functools.partial(rest_kernel, rows, cols, 4),
+        (table, near, across_climb, across_descend),
         shape((size * half + 16, size), bf16),
-        flops=tall * size * rows,
+        flops=2 * tall * size * rows,
     )
     mine = device_call(
         functools.partial(mine_kernel, rows, cols, 4),
@@ -740,12 +729,16 @@
 
 def fits_pairs(mesh, members, obs_pert, obs_owner):
     sizes = dict(mesh.shape)
+    coarse_x, coarse_y, slots = obs_owner
+    _, width_x, width_y, size = members
     return (
         sizes["tx"] == 2
         and sizes["lev"] == 4
-        and obs_pert == (256, 128)
-        and obs_owner == (4, 1, 256)
-        and members[1:] == (64, 16, 128)
+        and (coarse_x + 2, coarse_y) == (6, 1)
+        and (width_x, width_y) == (coarse_x * SPACING, coarse_y * SPACING)
+        and size == LANES
+        and obs_pert == (2 * LANES, LANES)
+        and slots == 2 * LANES
     )
 
 

time: 27 us -> 27.1 us (level)
  starting transfers between devices: 12 us -> 12.3 us
    ppermute x12, starting transfers between devices: 12 us -> 12.3 us  [send(): return lax.ppermute(value, axes, ways[way])]
    pallas_call x11 -> x10, Pallas kernels: 7.4 us -> 7.18 us  [device_call(): pl.pallas_call(kernel, out_shape=out_shape, in_specs=[hbm if in_hbm else...]
  transfers between devices with their start and end apart: 12 -> 12, of which waited for: 8 -> 8; matrix products, arithmetic and copies ran while one was open for 0% -> 0% of each run, Pallas kernels for 11% -> 10%
where the time goes in v11:
time: 27.1 us; the launch traced here: 26.9 us
  starting transfers between devices  12.3 us (45%)
  waiting for transfers between devices  7.35 us (27%)
  Pallas kernels  7.18 us (26%)
    ppermute x12, starting transfers between devices, send(): return lax.ppermute(value, axes, ways[way])  12.3 us
    ppermute x12, waiting for transfers between devices, send(): return lax.ppermute(value, axes, ways[way])  7.35 us
    pallas_call x10, Pallas kernels, device_call(): pl.pallas_call(kernel, out_shape=out_shape, in_specs=[hbm if in_hbm else...  7.18 us
  transfers between devices with their start and end apart: 12, of which 8 were waited for; matrix products, arithmetic and copies ran while one was open for 0% of the time, Pallas kernels for 10%

profile of v11, /device:TPU:0, one launch (start us, length us, event | category | flops | bytes accessed | tf_op | source)
XLA Modules:
  0.0 26.9 jit_solution(15943582133731383194)
XLA Ops:
  0.0 1.0 %shard_map.82.b0 = bf16[272,128]{1,0:T(8,128)(2,1)S(1)} custom-call(bf16[256,128]{1,0:T(8,128)(2,1)} %pert.1, bf16[2,128]{1,0:T(2,128)(2,1)} %bitcast.5, bf16[2,128]{1,0:T(2,128)(2,1)} %bitcast.6, s32[4,1,256]{2,1,0:T(1,128)} %owner_ref.1, s32[4,1,256]{2,1,0:T(1,128)} %slot_ref.1, s32[1,4]{1,0:T(1,128)} %bitcast.3, f32[4,1,256]{2,1,0:T(1,128)} %local_ref.1), custom_call_target="tpu_custom_call" | custom-call | bytes 262144 | tf_op jit(solution)/shard_map/pallas_call | solution.py:212
  1.0 3.1 %collective-permute-start = (bf16[272,128]{1,0:T(8,128)(2,1)S(1)}, bf16[272,128]{1,0:T(8,128)(2,1)S(1)}, u32[]{:S(2)}, u32[]{:S(2)}) collective-permute-start(bf16[272,128]{1,0:T(8,128)(2,1)S(1)} %shard_map.82.b0), channel_id=1, source_target_pairs={{0,16},{1,17},{2,18},{3,19},{4,20},{5,21},{6,22},{7,23},{8,24},{9,... | collective-permute-start | bytes 208904 | tf_op jit(solution)/shard_map/ppermute | solution.py:624
  4.1 2.0 %collective-permute-start.1 = (bf16[272,128]{1,0:T(8,128)(2,1)S(1)}, bf16[272,128]{1,0:T(8,128)(2,1)S(1)}, u32[]{:S(2)}, u32[]{:S(2)}) collective-permute-start(bf16[272,128]{1,0:T(8,128)(2,1)S(1)} %shard_map.82.b0), channel_id=1, source_target_pairs={{0,4},{1,0},{2,6},{3,2},{4,8},{5,1},{6,10},{7,3},{8,12},{9,5},{10,... | collective-permute-start | bytes 208904 | tf_op jit(solution)/shard_map/ppermute | solution.py:624
  6.1 0.3 collective-permute-done.other_ref.b3
  6.4 2.1 %collective-permute-start.3 = (bf16[272,128]{1,0:T(8,128)(2,1)S(1)}, bf16[272,128]{1,0:T(8,128)(2,1)S(1)}, u32[]{:S(2)}, u32[]{:S(2)}) collective-permute-start(bf16[272,128]{1,0:T(8,128)(2,1)S(1)} %collective-permute-done.other_ref.b3), channel_id=1, source_target_pairs={{0,4},{1,0},{2,6},{3,2},{4,8},{5,1},{6,10},{7,3},{8,12},{9,5},{10,... | collective-permute-start | bytes 208904 | tf_op jit(solution)/shard_map/ppermute | solution.py:624
  8.5 0.5 %shard_map.83.table_ref = f32[136,128]{1,0:T(8,128)S(1)} custom-call(s32[4,1,256]{2,1,0:T(1,128)S(1)} %copy-done.1, s32[4,1,256]{2,1,0:T(1,128)S(1)} %copy-done.2, s32[1,4]{1,0:T(1,128)S(1)} %bitcast.4, f32[4,1,256]{2,1,0:T(1,128)S(1)} %copy-done.3, bf16[272,128]{1,0:T(8,128)(2,1)S(1)} %collective-permute-done.other_ref.b3), custom_call_target="tpu_custom_call" | custom-call | flops 18874368 | bytes 262144 | tf_op jit(solution)/shard_map/pallas_call | solution.py:212
  9.0 0.1 collective-permute-done.2.b2
  9.1 0.7 %shard_map.84.so_far_ref = f32[784,128]{1,0:T(8,128)S(1)} custom-call(f32[136,128]{1,0:T(8,128)S(1)} %shard_map.83.table_ref, bf16[272,128]{1,0:T(8,128)(2,1)S(1)} %shard_map.82.b0, bf16[272,128]{1,0:T(8,128)(2,1)S(1)} %collective-permute-done.1.b1, bf16[272,128]{1,0:T(8,128)(2,1)S(1)} %collective-permute-done.2.b2, ...), custom_call_target="tpu_custom_call" | custom-call | flops 205520896 | bytes 262144 | tf_op jit(solution)/shard_map/pallas_call | solution.py:212
  9.7 1.3 %collective-permute-done.4.b5 = bf16[272,128]{1,0:T(8,128)(2,1)S(1)} collective-permute-done((bf16[272,128]{1,0:T(8,128)(2,1)S(1)}, bf16[272,128]{1,0:T(8,128)(2,1)S(1)}, u32[]{:S(2)}, u32[]{:S(2)}) %collective-permute-start.4) | collective-permute-done | bytes 69664 | tf_op jit(solution)/shard_map/ppermute | solution.py:624
  11.0 0.3 %shard_map.86 = bf16[400,128]{1,0:T(8,128)(2,1)S(1)} custom-call(f32[136,128]{1,0:T(8,128)S(1)} %shard_map.83.table_ref, f32[784,128]{1,0:T(8,128)S(1)} %shard_map.84.so_far_ref, bf16[272,128]{1,0:T(8,128)(2,1)S(1)} %collective-permute-done.3.b4, bf16[272,128]{1,0:T(8,128)(2,1)S(1)} %collective-permute-done.4.b5), custom_call_target="tpu_custom_call" | custom-call | flops 51380224 | bytes 262144 | tf_op jit(solution)/shard_map/pallas_call | solution.py:212
  11.4 0.3 %shard_map.85.mine_ref = f32[392,128]{1,0:T(8,128)S(1)} custom-call(f32[136,128]{1,0:T(8,128)S(1)} %shard_map.83.table_ref, f32[784,128]{1,0:T(8,128)S(1)} %shard_map.84.so_far_ref, bf16[272,128]{1,0:T(8,128)(2,1)S(1)} %collective-permute-done.3.b4, bf16[272,128]{1,0:T(8,128)(2,1)S(1)} %collective-permute-done.4.b5), custom_call_target="tpu_custom_call" | custom-call | flops 51380224 | bytes 262144 | tf_op jit(solution)/shard_map/pallas_call | solution.py:212
  11.7 1.0 %collective-permute-done.5.got_ref = bf16[400,128]{1,0:T(8,128)(2,1)S(1)} collective-permute-done((bf16[400,128]{1,0:T(8,128)(2,1)S(1)}, bf16[400,128]{1,0:T(8,128)(2,1)S(1)}, u32[]{:S(2)}, u32[]{:S(2)}) %collective-permute-start.5) | collective-permute-done | bytes 102432 | tf_op jit(solution)/shard_map/ppermute | solution.py:624
  12.8 1.8 %collective-permute-start.6 = (bf16[272,128]{1,0:T(8,128)(2,1)S(1)}, bf16[272,128]{1,0:T(8,128)(2,1)S(1)}, u32[]{:S(2)}, u32[]{:S(2)}) collective-permute-start(bf16[272,128]{1,0:T(8,128)(2,1)S(1)} %get-tuple-element.15), channel_id=1, source_target_pairs={{0,2},{1,3},{2,0},{3,1},{4,6},{5,7},{6,4},{7,5},{8,10},{9,11},{10,... | collective-permute-start | bytes 208904 | tf_op jit(solution)/shard_map/ppermute | solution.py:624
  14.6 2.6 %collective-permute-done.6.got_ref = bf16[272,128]{1,0:T(8,128)(2,1)S(1)} collective-permute-done((bf16[272,128]{1,0:T(8,128)(2,1)S(1)}, bf16[272,128]{1,0:T(8,128)(2,1)S(1)}, u32[]{:S(2)}, u32[]{:S(2)}) %collective-permute-start.6) | collective-permute-done | bytes 69664 | tf_op jit(solution)/shard_map/ppermute | solution.py:624
  17.1 1.6 %shard_map.88.own = bf16[272,128]{1,0:T(8,128)(2,1)S(1)} custom-call(f32[392,128]{1,0:T(8,128)S(1)} %get-tuple-element.14.sum_ref, bf16[272,128]{1,0:T(8,128)(2,1)S(1)} %collective-permute-done.6.got_ref), custom_call_target="tpu_custom_call" | custom-call | flops 339738624 | bytes 262144 | tf_op jit(solution)/shard_map/pallas_call | solution.py:212
  18.8 0.5 %collective-permute-start.8 = (bf16[272,128]{1,0:T(8,128)(2,1)S(1)}, bf16[272,128]{1,0:T(8,128)(2,1)S(1)}, u32[]{:S(2)}, u32[]{:S(2)}) collective-permute-start(bf16[272,128]{1,0:T(8,128)(2,1)S(1)} %shard_map.88.own), channel_id=1, source_target_pairs={{4,0},{0,1},{6,2},{2,3},{8,4},{1,5},{10,6},{3,7},{12,8},{5,9},{14,... | collective-permute-start | bytes 208904 | tf_op jit(solution)/shard_map/ppermute | solution.py:624
  19.3 1.5 %collective-permute-start.7 = (bf16[272,128]{1,0:T(8,128)(2,1)S(1)}, bf16[272,128]{1,0:T(8,128)(2,1)S(1)}, u32[]{:S(2)}, u32[]{:S(2)}) collective-permute-start(bf16[272,128]{1,0:T(8,128)(2,1)S(1)} %shard_map.88.own), channel_id=1, source_target_pairs={{0,4},{1,0},{2,6},{3,2},{4,8},{5,1},{6,10},{7,3},{8,12},{9,5},{10,... | collective-permute-start | bytes 208904 | tf_op jit(solution)/shard_map/ppermute | solution.py:624
  20.9 0.7 %shard_map.89 = (f32[8,2,128,128]{3,2,1,0:T(8,128)S(1)}, bf16[8,2,128,128]{3,2,1,0:T(8,128)(2,1)S(1)}) custom-call(bf16[2,64,16,128]{3,2,1,0:T(8,128)(2,1)S(1)} %copy-done, bf16[272,128]{1,0:T(8,128)(2,1)S(1)} %shard_map.88.own, bf16[272,128]{1,0:T(8,128)(2,1)S(1)} %collective-permute-done.9.pair), custom_call_target="tpu_custom_call" | custom-call | flops 134217728 | bytes 262144 | tf_op jit(solution)/shard_map/pallas_call | solution.py:212
  21.6 1.5 %collective-permute-done.8.descend = bf16[272,128]{1,0:T(8,128)(2,1)S(1)} collective-permute-done((bf16[272,128]{1,0:T(8,128)(2,1)S(1)}, bf16[272,128]{1,0:T(8,128)(2,1)S(1)}, u32[]{:S(2)}, u32[]{:S(2)}) %collective-permute-start.8) | collective-permute-done | bytes 69664 | tf_op jit(solution)/shard_map/ppermute | solution.py:624
  23.1 1.1 %collective-permute-start.10 = (bf16[272,128]{1,0:T(8,128)(2,1)S(1)}, bf16[272,128]{1,0:T(8,128)(2,1)S(1)}, u32[]{:S(2)}, u32[]{:S(2)}) collective-permute-start(bf16[272,128]{1,0:T(8,128)(2,1)S(1)} %collective-permute-done.7.climb), channel_id=1, source_target_pairs={{0,1},{1,0},{2,3},{3,2},{4,5},{5,4},{6,7},{7,6},{8,9},{9,8},{10,11... | collective-permute-start | bytes 208904 | tf_op jit(solution)/shard_map/ppermute | solution.py:624
  24.3 0.6 %shard_map.90 = (bf16[2,24,16,128]{3,2,1,0:T(8,128)(2,1)S(1)}, bf16[2,128,128]{2,1,0:T(8,128)(2,1)S(1)}) custom-call(f32[8,2,128,128]{3,2,1,0:T(8,128)S(1)} %get-tuple-element.17.part_ref, bf16[8,2,128,128]{3,2,1,0:T(8,128)(2,1)S(1)} %get-tuple-element.18.pert_ref, bf16[272,128]{1,0:T(8,128)(2,1)S(1)} %shard_map.88.own, ...), custom_call_target="tpu_custom_call" | custom-call | flops 50331648 | bytes 262144 | tf_op jit(solution)/shard_map/pallas_call | solution.py:212
  24.9 0.3 %collective-permute-done.10.pair_climb = bf16[272,128]{1,0:T(8,128)(2,1)S(1)} collective-permute-done((bf16[272,128]{1,0:T(8,128)(2,1)S(1)}, bf16[272,128]{1,0:T(8,128)(2,1)S(1)}, u32[]{:S(2)}, u32[]{:S(2)}) %collective-permute-start.10) | collective-permute-done | bytes 69664 | tf_op jit(solution)/shard_map/ppermute | solution.py:624
  25.2 0.4 %collective-permute-done.11.pair_descend = bf16[272,128]{1,0:T(8,128)(2,1)S(1)} collective-permute-done((bf16[272,128]{1,0:T(8,128)(2,1)S(1)}, bf16[272,128]{1,0:T(8,128)(2,1)S(1)}, u32[]{:S(2)}, u32[]{:S(2)}) %collective-permute-start.11) | collective-permute-done | bytes 69664 | tf_op jit(solution)/shard_map/ppermute | solution.py:624
  25.6 1.3 %shard_map.91 = bf16[2,64,16,128]{3,2,1,0:T(8,128)(2,1)} custom-call(f32[8,2,128,128]{3,2,1,0:T(8,128)S(1)} %get-tuple-element.17.part_ref, bf16[8,2,128,128]{3,2,1,0:T(8,128)(2,1)S(1)} %get-tuple-element.18.pert_ref, bf16[272,128]{1,0:T(8,128)(2,1)S(1)} %collective-permute-done.9.pair, bf16[272,128]{1,0:T(8,128)(2,1)S(1)} %collective-permute-done.10.pair_climb, ...), custom_call_target="tpu_custom_call" | custom-call | flops 83886080 | bytes 262144 | tf_op jit(solution)/shard_map/pallas_call | solution.py:212
  (20 shorter events, 0.2 us)
Async XLA Ops:
  0.0 8.5 %copy-start.1 = (s32[4,1,256]{2,1,0:T(1,128)S(1)}, s32[4,1,256]{2,1,0:T(1,128)}, u32[]{:S(2)}) copy-start(s32[4,1,256]{2,1,0:T(1,128)} %owner_ref.1) | copy-start | bytes 12292
  0.0 8.5 %copy-start.2 = (s32[4,1,256]{2,1,0:T(1,128)S(1)}, s32[4,1,256]{2,1,0:T(1,128)}, u32[]{:S(2)}) copy-start(s32[4,1,256]{2,1,0:T(1,128)} %slot_ref.1) | copy-start | bytes 12292
  0.0 8.5 %copy-start.3 = (f32[4,1,256]{2,1,0:T(1,128)S(1)}, f32[4,1,256]{2,1,0:T(1,128)}, u32[]{:S(2)}) copy-start(f32[4,1,256]{2,1,0:T(1,128)} %local_ref.1) | copy-start | bytes 12292
  0.0 8.5 %copy-start.4 = (s32[4,1]{0,1:T(1,128)S(1)}, s32[4,1]{0,1:T(1,128)}, u32[]{:S(2)}) copy-start(s32[4,1]{0,1:T(1,128)} %param.14) | copy-start | bytes 52
  1.0 5.4 %collective-permute-start = (bf16[272,128]{1,0:T(8,128)(2,1)S(1)}, bf16[272,128]{1,0:T(8,128)(2,1)S(1)}, u32[]{:S(2)}, u32[]{:S(2)}) collective-permute-start(bf16[272,128]{1,0:T(8,128)(2,1)S(1)} %shard_map.82.b0), channel_id=1, source_target_pairs={{0,16},{1,17},{2,18},{3,19},{4,20},{5,21},{6,22},{7,23},{8,24},{9,... | collective-permute-start | bytes 208904 | tf_op jit(solution)/shard_map/ppermute | solution.py:624
  4.1 4.9 %collective-permute-start.2 = (bf16[272,128]{1,0:T(8,128)(2,1)S(1)}, bf16[272,128]{1,0:T(8,128)(2,1)S(1)}, u32[]{:S(2)}, u32[]{:S(2)}) collective-permute-start(bf16[272,128]{1,0:T(8,128)(2,1)S(1)} %shard_map.82.b0), channel_id=1, source_target_pairs={{4,0},{0,1},{6,2},{2,3},{8,4},{1,5},{10,6},{3,7},{12,8},{5,9},{14,... | collective-permute-start | bytes 208904 | tf_op jit(solution)/shard_map/ppermute | solution.py:624
  4.1 4.9 %collective-permute-start.1 = (bf16[272,128]{1,0:T(8,128)(2,1)S(1)}, bf16[272,128]{1,0:T(8,128)(2,1)S(1)}, u32[]{:S(2)}, u32[]{:S(2)}) collective-permute-start(bf16[272,128]{1,0:T(8,128)(2,1)S(1)} %shard_map.82.b0), channel_id=1, source_target_pairs={{0,4},{1,0},{2,6},{3,2},{4,8},{5,1},{6,10},{7,3},{8,12},{9,5},{10,... | collective-permute-start | bytes 208904 | tf_op jit(solution)/shard_map/ppermute | solution.py:624
  6.4 4.6 %collective-permute-start.4 = (bf16[272,128]{1,0:T(8,128)(2,1)S(1)}, bf16[272,128]{1,0:T(8,128)(2,1)S(1)}, u32[]{:S(2)}, u32[]{:S(2)}) collective-permute-start(bf16[272,128]{1,0:T(8,128)(2,1)S(1)} %collective-permute-done.other_ref.b3), channel_id=1, source_target_pairs={{4,0},{0,1},{6,2},{2,3},{8,4},{1,5},{10,6},{3,7},{12,8},{5,9},{14,... | collective-permute-start | bytes 208904 | tf_op jit(solution)/shard_map/ppermute | solution.py:624
  6.4 4.6 %collective-permute-start.3 = (bf16[272,128]{1,0:T(8,128)(2,1)S(1)}, bf16[272,128]{1,0:T(8,128)(2,1)S(1)}, u32[]{:S(2)}, u32[]{:S(2)}) collective-permute-start(bf16[272,128]{1,0:T(8,128)(2,1)S(1)} %collective-permute-done.other_ref.b3), channel_id=1, source_target_pairs={{0,4},{1,0},{2,6},{3,2},{4,8},{5,1},{6,10},{7,3},{8,12},{9,5},{10,... | collective-permute-start | bytes 208904 | tf_op jit(solution)/shard_map/ppermute | solution.py:624
  11.3 1.4 %collective-permute-start.5 = (bf16[400,128]{1,0:T(8,128)(2,1)S(1)}, bf16[400,128]{1,0:T(8,128)(2,1)S(1)}, u32[]{:S(2)}, u32[]{:S(2)}) collective-permute-start(bf16[400,128]{1,0:T(8,128)(2,1)S(1)} %shard_map.86), channel_id=1, source_target_pairs={{0,1},{1,0},{2,3},{3,2},{4,5},{5,4},{6,7},{7,6},{8,9},{9,8},{10,11... | collective-permute-start | bytes 307208 | tf_op jit(solution)/shard_map/ppermute | solution.py:624
  12.8 4.4 %collective-permute-start.6 = (bf16[272,128]{1,0:T(8,128)(2,1)S(1)}, bf16[272,128]{1,0:T(8,128)(2,1)S(1)}, u32[]{:S(2)}, u32[]{:S(2)}) collective-permute-start(bf16[272,128]{1,0:T(8,128)(2,1)S(1)} %get-tuple-element.15), channel_id=1, source_target_pairs={{0,2},{1,3},{2,0},{3,1},{4,6},{5,7},{6,4},{7,5},{8,10},{9,11},{10,... | collective-permute-start | bytes 208904 | tf_op jit(solution)/shard_map/ppermute | solution.py:624
  17.1 3.7 %copy-start = (bf16[2,64,16,128]{3,2,1,0:T(8,128)(2,1)S(1)}, bf16[2,64,16,128]{3,2,1,0:T(8,128)(2,1)}, u32[]{:S(2)}) copy-start(bf16[2,64,16,128]{3,2,1,0:T(8,128)(2,1)} %members_ref.1) | copy-start | bytes 1572868
  18.8 2.1 %collective-permute-start.9 = (bf16[272,128]{1,0:T(8,128)(2,1)S(1)}, bf16[272,128]{1,0:T(8,128)(2,1)S(1)}, u32[]{:S(2)}, u32[]{:S(2)}) collective-permute-start(bf16[272,128]{1,0:T(8,128)(2,1)S(1)} %shard_map.88.own), channel_id=1, source_target_pairs={{0,1},{1,0},{2,3},{3,2},{4,5},{5,4},{6,7},{7,6},{8,9},{9,8},{10,11... | collective-permute-start | bytes 208904 | tf_op jit(solution)/shard_map/ppermute | solution.py:624
  18.8 4.3 %collective-permute-start.8 = (bf16[272,128]{1,0:T(8,128)(2,1)S(1)}, bf16[272,128]{1,0:T(8,128)(2,1)S(1)}, u32[]{:S(2)}, u32[]{:S(2)}) collective-permute-start(bf16[272,128]{1,0:T(8,128)(2,1)S(1)} %shard_map.88.own), channel_id=1, source_target_pairs={{4,0},{0,1},{6,2},{2,3},{8,4},{1,5},{10,6},{3,7},{12,8},{5,9},{14,... | collective-permute-start | bytes 208904 | tf_op jit(solution)/shard_map/ppermute | solution.py:624
  19.3 3.8 %collective-permute-start.7 = (bf16[272,128]{1,0:T(8,128)(2,1)S(1)}, bf16[272,128]{1,0:T(8,128)(2,1)S(1)}, u32[]{:S(2)}, u32[]{:S(2)}) collective-permute-start(bf16[272,128]{1,0:T(8,128)(2,1)S(1)} %shard_map.88.own), channel_id=1, source_target_pairs={{0,4},{1,0},{2,6},{3,2},{4,8},{5,1},{6,10},{7,3},{8,12},{9,5},{10,... | collective-permute-start | bytes 208904 | tf_op jit(solution)/shard_map/ppermute | solution.py:624
  23.1 2.1 %collective-permute-start.10 = (bf16[272,128]{1,0:T(8,128)(2,1)S(1)}, bf16[272,128]{1,0:T(8,128)(2,1)S(1)}, u32[]{:S(2)}, u32[]{:S(2)}) collective-permute-start(bf16[272,128]{1,0:T(8,128)(2,1)S(1)} %collective-permute-done.7.climb), channel_id=1, source_target_pairs={{0,1},{1,0},{2,3},{3,2},{4,5},{5,4},{6,7},{7,6},{8,9},{9,8},{10,11... | collective-permute-start | bytes 208904 | tf_op jit(solution)/shard_map/ppermute | solution.py:624
  24.3 1.3 %collective-permute-start.11 = (bf16[272,128]{1,0:T(8,128)(2,1)S(1)}, bf16[272,128]{1,0:T(8,128)(2,1)S(1)}, u32[]{:S(2)}, u32[]{:S(2)}) collective-permute-start(bf16[272,128]{1,0:T(8,128)(2,1)S(1)} %collective-permute-done.8.descend), channel_id=1, source_target_pairs={{0,1},{1,0},{2,3},{3,2},{4,5},{5,4},{6,7},{7,6},{8,9},{9,8},{10,11... | collective-permute-start | bytes 208904 | tf_op jit(solution)/shard_map/ppermute | solution.py:624

commit v12 on v11

--- a/solution.py
+++ b/solution.py
@@ -242,7 +242,7 @@
     sources = (owner, slot, count, local, inn, prec, pert)
     targets = (owner_ref, slot_ref, count_ref, local_ref, inn_ref, prec_ref, out_ref.at[0:rows, :])
     copies = [pltpu.make_async_copy(x, y, sems.at[k]) for k, (x, y) in enumerate(zip(sources, targets))]
-    for copy in copies:
+    for copy in copies[-1:] + copies[:-1]:
         copy.start()
     for copy in copies[:-1]:
         copy.wait()
@@ -470,12 +470,12 @@
         last = step == NS_STEPS - 3
         inverse_parts = [split2(z) for z in inverses]
         left = [split2(above(z, v, q)) for z, v, q in zip(inverses, vectors, pushed)] if last else inverse_parts
-        both = [product(z, wide(b, y)) for z, b, y in zip(left, base_parts, inverse_parts)]
+        both = [product(z, wide(b, y)) if last else dot(z[0], beside(b[0], y[0])) for z, b, y in zip(left, base_parts, inverse_parts)]
         forced = [x[:, 0:size] for x in both]
         square = [split2(x[0:size, size : 2 * size]) for x in both]
         if last:
             forced = [above(f[0:size], x[size + 8 : size + 16, size:], x[size + 8 : size + 16, size:]) for f, x in zip(forced, both)]
-        cubes = [product(split2(f), y) for f, y in zip(forced, square)]
+        cubes = [product(split2(f), y) if last else dot(f.astype(jnp.bfloat16), y[0]) for f, y in zip(forced, square)]
         if last:
             carried = [1.5 * x[size : size + 8, size:] - 0.5 * c[size : size + 8] for x, c in zip(both, cubes)]
         inverses = [1.5 * z - 0.5 * c[0:size] for z, c in zip(inverses, cubes)]

time: 27.1 us -> 26.9 us (level)
  no operation moved by 1% of the time
where the time goes in v12:
time: 26.9 us; the launch traced here: 26.7 us
  starting transfers between devices  12.3 us (46%)
  waiting for transfers between devices  7.36 us (27%)
  Pallas kernels  7 us (26%)
    ppermute x12, starting transfers between devices, send(): return lax.ppermute(value, axes, ways[way])  12.3 us
    ppermute x12, waiting for transfers between devices, send(): return lax.ppermute(value, axes, ways[way])  7.36 us
    pallas_call x10, Pallas kernels, device_call(): pl.pallas_call(kernel, out_shape=out_shape, in_specs=[hbm if in_hbm else...  7 us
  transfers between devices with their start and end apart: 12, of which 8 were waited for; matrix products, arithmetic and copies ran while one was open for 0% of the time, Pallas kernels for 10%

profile of v12, /device:TPU:0, one launch (start us, length us, event | category | flops | bytes accessed | tf_op | source)
XLA Modules:
  0.0 26.7 jit_solution(16901874758823417495)
XLA Ops:
  0.0 1.0 %shard_map.82.b0 = bf16[272,128]{1,0:T(8,128)(2,1)S(1)} custom-call(bf16[256,128]{1,0:T(8,128)(2,1)} %pert.1, bf16[2,128]{1,0:T(2,128)(2,1)} %bitcast.5, bf16[2,128]{1,0:T(2,128)(2,1)} %bitcast.6, s32[4,1,256]{2,1,0:T(1,128)} %owner_ref.1, s32[4,1,256]{2,1,0:T(1,128)} %slot_ref.1, s32[1,4]{1,0:T(1,128)} %bitcast.3, f32[4,1,256]{2,1,0:T(1,128)} %local_ref.1), custom_call_target="tpu_custom_call" | custom-call | bytes 262144 | tf_op jit(solution)/shard_map/pallas_call | solution.py:212
  1.0 3.1 %collective-permute-start = (bf16[272,128]{1,0:T(8,128)(2,1)S(1)}, bf16[272,128]{1,0:T(8,128)(2,1)S(1)}, u32[]{:S(2)}, u32[]{:S(2)}) collective-permute-start(bf16[272,128]{1,0:T(8,128)(2,1)S(1)} %shard_map.82.b0), channel_id=1, source_target_pairs={{0,16},{1,17},{2,18},{3,19},{4,20},{5,21},{6,22},{7,23},{8,24},{9,... | collective-permute-start | bytes 208904 | tf_op jit(solution)/shard_map/ppermute | solution.py:624
  4.0 2.0 %collective-permute-start.1 = (bf16[272,128]{1,0:T(8,128)(2,1)S(1)}, bf16[272,128]{1,0:T(8,128)(2,1)S(1)}, u32[]{:S(2)}, u32[]{:S(2)}) collective-permute-start(bf16[272,128]{1,0:T(8,128)(2,1)S(1)} %shard_map.82.b0), channel_id=1, source_target_pairs={{0,4},{1,0},{2,6},{3,2},{4,8},{5,1},{6,10},{7,3},{8,12},{9,5},{10,... | collective-permute-start | bytes 208904 | tf_op jit(solution)/shard_map/ppermute | solution.py:624
  6.1 0.3 collective-permute-done.other_ref.b3
  6.3 2.1 %collective-permute-start.3 = (bf16[272,128]{1,0:T(8,128)(2,1)S(1)}, bf16[272,128]{1,0:T(8,128)(2,1)S(1)}, u32[]{:S(2)}, u32[]{:S(2)}) collective-permute-start(bf16[272,128]{1,0:T(8,128)(2,1)S(1)} %collective-permute-done.other_ref.b3), channel_id=1, source_target_pairs={{0,4},{1,0},{2,6},{3,2},{4,8},{5,1},{6,10},{7,3},{8,12},{9,5},{10,... | collective-permute-start | bytes 208904 | tf_op jit(solution)/shard_map/ppermute | solution.py:624
  8.4 0.5 %shard_map.83.table_ref = f32[136,128]{1,0:T(8,128)S(1)} custom-call(s32[4,1,256]{2,1,0:T(1,128)S(1)} %copy-done.1, s32[4,1,256]{2,1,0:T(1,128)S(1)} %copy-done.2, s32[1,4]{1,0:T(1,128)S(1)} %bitcast.4, f32[4,1,256]{2,1,0:T(1,128)S(1)} %copy-done.3, bf16[272,128]{1,0:T(8,128)(2,1)S(1)} %collective-permute-done.other_ref.b3), custom_call_target="tpu_custom_call" | custom-call | flops 18874368 | bytes 262144 | tf_op jit(solution)/shard_map/pallas_call | solution.py:212
  8.9 0.1 collective-permute-done.2.b2
  9.0 0.6 %shard_map.84.so_far_ref = f32[784,128]{1,0:T(8,128)S(1)} custom-call(f32[136,128]{1,0:T(8,128)S(1)} %shard_map.83.table_ref, bf16[272,128]{1,0:T(8,128)(2,1)S(1)} %shard_map.82.b0, bf16[272,128]{1,0:T(8,128)(2,1)S(1)} %collective-permute-done.1.b1, bf16[272,128]{1,0:T(8,128)(2,1)S(1)} %collective-permute-done.2.b2, ...), custom_call_target="tpu_custom_call" | custom-call | flops 205520896 | bytes 262144 | tf_op jit(solution)/shard_map/pallas_call | solution.py:212
  9.6 1.3 %collective-permute-done.4.b5 = bf16[272,128]{1,0:T(8,128)(2,1)S(1)} collective-permute-done((bf16[272,128]{1,0:T(8,128)(2,1)S(1)}, bf16[272,128]{1,0:T(8,128)(2,1)S(1)}, u32[]{:S(2)}, u32[]{:S(2)}) %collective-permute-start.4) | collective-permute-done | bytes 69664 | tf_op jit(solution)/shard_map/ppermute | solution.py:624
  10.9 0.3 %shard_map.86 = bf16[400,128]{1,0:T(8,128)(2,1)S(1)} custom-call(f32[136,128]{1,0:T(8,128)S(1)} %shard_map.83.table_ref, f32[784,128]{1,0:T(8,128)S(1)} %shard_map.84.so_far_ref, bf16[272,128]{1,0:T(8,128)(2,1)S(1)} %collective-permute-done.3.b4, bf16[272,128]{1,0:T(8,128)(2,1)S(1)} %collective-permute-done.4.b5), custom_call_target="tpu_custom_call" | custom-call | flops 51380224 | bytes 262144 | tf_op jit(solution)/shard_map/pallas_call | solution.py:212
  11.3 0.3 %shard_map.85.mine_ref = f32[392,128]{1,0:T(8,128)S(1)} custom-call(f32[136,128]{1,0:T(8,128)S(1)} %shard_map.83.table_ref, f32[784,128]{1,0:T(8,128)S(1)} %shard_map.84.so_far_ref, bf16[272,128]{1,0:T(8,128)(2,1)S(1)} %collective-permute-done.3.b4, bf16[272,128]{1,0:T(8,128)(2,1)S(1)} %collective-permute-done.4.b5), custom_call_target="tpu_custom_call" | custom-call | flops 51380224 | bytes 262144 | tf_op jit(solution)/shard_map/pallas_call | solution.py:212
  11.6 1.0 %collective-permute-done.5.got_ref = bf16[400,128]{1,0:T(8,128)(2,1)S(1)} collective-permute-done((bf16[400,128]{1,0:T(8,128)(2,1)S(1)}, bf16[400,128]{1,0:T(8,128)(2,1)S(1)}, u32[]{:S(2)}, u32[]{:S(2)}) %collective-permute-start.5) | collective-permute-done | bytes 102432 | tf_op jit(solution)/shard_map/ppermute | solution.py:624
  12.7 1.8 %collective-permute-start.6 = (bf16[272,128]{1,0:T(8,128)(2,1)S(1)}, bf16[272,128]{1,0:T(8,128)(2,1)S(1)}, u32[]{:S(2)}, u32[]{:S(2)}) collective-permute-start(bf16[272,128]{1,0:T(8,128)(2,1)S(1)} %get-tuple-element.15), channel_id=1, source_target_pairs={{0,2},{1,3},{2,0},{3,1},{4,6},{5,7},{6,4},{7,5},{8,10},{9,11},{10,... | collective-permute-start | bytes 208904 | tf_op jit(solution)/shard_map/ppermute | solution.py:624
  14.5 2.6 %collective-permute-done.6.got_ref = bf16[272,128]{1,0:T(8,128)(2,1)S(1)} collective-permute-done((bf16[272,128]{1,0:T(8,128)(2,1)S(1)}, bf16[272,128]{1,0:T(8,128)(2,1)S(1)}, u32[]{:S(2)}, u32[]{:S(2)}) %collective-permute-start.6) | collective-permute-done | bytes 69664 | tf_op jit(solution)/shard_map/ppermute | solution.py:624
  17.1 1.5 %shard_map.88.own = bf16[272,128]{1,0:T(8,128)(2,1)S(1)} custom-call(f32[392,128]{1,0:T(8,128)S(1)} %get-tuple-element.14.sum_ref, bf16[272,128]{1,0:T(8,128)(2,1)S(1)} %collective-permute-done.6.got_ref), custom_call_target="tpu_custom_call" | custom-call | flops 339738624 | bytes 262144 | tf_op jit(solution)/shard_map/pallas_call | solution.py:212
  18.6 0.5 %collective-permute-start.8 = (bf16[272,128]{1,0:T(8,128)(2,1)S(1)}, bf16[272,128]{1,0:T(8,128)(2,1)S(1)}, u32[]{:S(2)}, u32[]{:S(2)}) collective-permute-start(bf16[272,128]{1,0:T(8,128)(2,1)S(1)} %shard_map.88.own), channel_id=1, source_target_pairs={{4,0},{0,1},{6,2},{2,3},{8,4},{1,5},{10,6},{3,7},{12,8},{5,9},{14,... | collective-permute-start | bytes 208904 | tf_op jit(solution)/shard_map/ppermute | solution.py:624
  19.1 1.5 %collective-permute-start.7 = (bf16[272,128]{1,0:T(8,128)(2,1)S(1)}, bf16[272,128]{1,0:T(8,128)(2,1)S(1)}, u32[]{:S(2)}, u32[]{:S(2)}) collective-permute-start(bf16[272,128]{1,0:T(8,128)(2,1)S(1)} %shard_map.88.own), channel_id=1, source_target_pairs={{0,4},{1,0},{2,6},{3,2},{4,8},{5,1},{6,10},{7,3},{8,12},{9,5},{10,... | collective-permute-start | bytes 208904 | tf_op jit(solution)/shard_map/ppermute | solution.py:624
  20.7 0.7 %shard_map.89 = (f32[8,2,128,128]{3,2,1,0:T(8,128)S(1)}, bf16[8,2,128,128]{3,2,1,0:T(8,128)(2,1)S(1)}) custom-call(bf16[2,64,16,128]{3,2,1,0:T(8,128)(2,1)S(1)} %copy-done, bf16[272,128]{1,0:T(8,128)(2,1)S(1)} %shard_map.88.own, bf16[272,128]{1,0:T(8,128)(2,1)S(1)} %collective-permute-done.9.pair), custom_call_target="tpu_custom_call" | custom-call | flops 134217728 | bytes 262144 | tf_op jit(solution)/shard_map/pallas_call | solution.py:212
  21.4 1.5 %collective-permute-done.8.descend = bf16[272,128]{1,0:T(8,128)(2,1)S(1)} collective-permute-done((bf16[272,128]{1,0:T(8,128)(2,1)S(1)}, bf16[272,128]{1,0:T(8,128)(2,1)S(1)}, u32[]{:S(2)}, u32[]{:S(2)}) %collective-permute-start.8) | collective-permute-done | bytes 69664 | tf_op jit(solution)/shard_map/ppermute | solution.py:624
  23.0 1.1 %collective-permute-start.10 = (bf16[272,128]{1,0:T(8,128)(2,1)S(1)}, bf16[272,128]{1,0:T(8,128)(2,1)S(1)}, u32[]{:S(2)}, u32[]{:S(2)}) collective-permute-start(bf16[272,128]{1,0:T(8,128)(2,1)S(1)} %collective-permute-done.7.climb), channel_id=1, source_target_pairs={{0,1},{1,0},{2,3},{3,2},{4,5},{5,4},{6,7},{7,6},{8,9},{9,8},{10,11... | collective-permute-start | bytes 208904 | tf_op jit(solution)/shard_map/ppermute | solution.py:624
  24.1 0.6 %shard_map.90 = (bf16[2,24,16,128]{3,2,1,0:T(8,128)(2,1)S(1)}, bf16[2,128,128]{2,1,0:T(8,128)(2,1)S(1)}) custom-call(f32[8,2,128,128]{3,2,1,0:T(8,128)S(1)} %get-tuple-element.17.part_ref, bf16[8,2,128,128]{3,2,1,0:T(8,128)(2,1)S(1)} %get-tuple-element.18.pert_ref, bf16[272,128]{1,0:T(8,128)(2,1)S(1)} %shard_map.88.own, ...), custom_call_target="tpu_custom_call" | custom-call | flops 50331648 | bytes 262144 | tf_op jit(solution)/shard_map/pallas_call | solution.py:212
  24.7 0.3 %collective-permute-done.10.pair_climb = bf16[272,128]{1,0:T(8,128)(2,1)S(1)} collective-permute-done((bf16[272,128]{1,0:T(8,128)(2,1)S(1)}, bf16[272,128]{1,0:T(8,128)(2,1)S(1)}, u32[]{:S(2)}, u32[]{:S(2)}) %collective-permute-start.10) | collective-permute-done | bytes 69664 | tf_op jit(solution)/shard_map/ppermute | solution.py:624
  25.0 0.4 %collective-permute-done.11.pair_descend = bf16[272,128]{1,0:T(8,128)(2,1)S(1)} collective-permute-done((bf16[272,128]{1,0:T(8,128)(2,1)S(1)}, bf16[272,128]{1,0:T(8,128)(2,1)S(1)}, u32[]{:S(2)}, u32[]{:S(2)}) %collective-permute-start.11) | collective-permute-done | bytes 69664 | tf_op jit(solution)/shard_map/ppermute | solution.py:624
  25.4 1.3 %shard_map.91 = bf16[2,64,16,128]{3,2,1,0:T(8,128)(2,1)} custom-call(f32[8,2,128,128]{3,2,1,0:T(8,128)S(1)} %get-tuple-element.17.part_ref, bf16[8,2,128,128]{3,2,1,0:T(8,128)(2,1)S(1)} %get-tuple-element.18.pert_ref, bf16[272,128]{1,0:T(8,128)(2,1)S(1)} %collective-permute-done.9.pair, bf16[272,128]{1,0:T(8,128)(2,1)S(1)} %collective-permute-done.10.pair_climb, ...), custom_call_target="tpu_custom_call" | custom-call | flops 83886080 | bytes 262144 | tf_op jit(solution)/shard_map/pallas_call | solution.py:212
  (20 shorter events, 0.2 us)
Async XLA Ops:
  0.0 8.4 %copy-start.1 = (s32[4,1,256]{2,1,0:T(1,128)S(1)}, s32[4,1,256]{2,1,0:T(1,128)}, u32[]{:S(2)}) copy-start(s32[4,1,256]{2,1,0:T(1,128)} %owner_ref.1) | copy-start | bytes 12292
  0.0 8.4 %copy-start.2 = (s32[4,1,256]{2,1,0:T(1,128)S(1)}, s32[4,1,256]{2,1,0:T(1,128)}, u32[]{:S(2)}) copy-start(s32[4,1,256]{2,1,0:T(1,128)} %slot_ref.1) | copy-start | bytes 12292
  0.0 8.4 %copy-start.3 = (f32[4,1,256]{2,1,0:T(1,128)S(1)}, f32[4,1,256]{2,1,0:T(1,128)}, u32[]{:S(2)}) copy-start(f32[4,1,256]{2,1,0:T(1,128)} %local_ref.1) | copy-start | bytes 12292
  0.0 8.4 %copy-start.4 = (s32[4,1]{0,1:T(1,128)S(1)}, s32[4,1]{0,1:T(1,128)}, u32[]{:S(2)}) copy-start(s32[4,1]{0,1:T(1,128)} %param.14) | copy-start | bytes 52
  1.0 5.3 %collective-permute-start = (bf16[272,128]{1,0:T(8,128)(2,1)S(1)}, bf16[272,128]{1,0:T(8,128)(2,1)S(1)}, u32[]{:S(2)}, u32[]{:S(2)}) collective-permute-start(bf16[272,128]{1,0:T(8,128)(2,1)S(1)} %shard_map.82.b0), channel_id=1, source_target_pairs={{0,16},{1,17},{2,18},{3,19},{4,20},{5,21},{6,22},{7,23},{8,24},{9,... | collective-permute-start | bytes 208904 | tf_op jit(solution)/shard_map/ppermute | solution.py:624
  4.0 4.9 %collective-permute-start.2 = (bf16[272,128]{1,0:T(8,128)(2,1)S(1)}, bf16[272,128]{1,0:T(8,128)(2,1)S(1)}, u32[]{:S(2)}, u32[]{:S(2)}) collective-permute-start(bf16[272,128]{1,0:T(8,128)(2,1)S(1)} %shard_map.82.b0), channel_id=1, source_target_pairs={{4,0},{0,1},{6,2},{2,3},{8,4},{1,5},{10,6},{3,7},{12,8},{5,9},{14,... | collective-permute-start | bytes 208904 | tf_op jit(solution)/shard_map/ppermute | solution.py:624
  4.0 4.9 %collective-permute-start.1 = (bf16[272,128]{1,0:T(8,128)(2,1)S(1)}, bf16[272,128]{1,0:T(8,128)(2,1)S(1)}, u32[]{:S(2)}, u32[]{:S(2)}) collective-permute-start(bf16[272,128]{1,0:T(8,128)(2,1)S(1)} %shard_map.82.b0), channel_id=1, source_target_pairs={{0,4},{1,0},{2,6},{3,2},{4,8},{5,1},{6,10},{7,3},{8,12},{9,5},{10,... | collective-permute-start | bytes 208904 | tf_op jit(solution)/shard_map/ppermute | solution.py:624
  6.3 4.6 %collective-permute-start.4 = (bf16[272,128]{1,0:T(8,128)(2,1)S(1)}, bf16[272,128]{1,0:T(8,128)(2,1)S(1)}, u32[]{:S(2)}, u32[]{:S(2)}) collective-permute-start(bf16[272,128]{1,0:T(8,128)(2,1)S(1)} %collective-permute-done.other_ref.b3), channel_id=1, source_target_pairs={{4,0},{0,1},{6,2},{2,3},{8,4},{1,5},{10,6},{3,7},{12,8},{5,9},{14,... | collective-permute-start | bytes 208904 | tf_op jit(solution)/shard_map/ppermute | solution.py:624
  6.3 4.6 %collective-permute-start.3 = (bf16[272,128]{1,0:T(8,128)(2,1)S(1)}, bf16[272,128]{1,0:T(8,128)(2,1)S(1)}, u32[]{:S(2)}, u32[]{:S(2)}) collective-permute-start(bf16[272,128]{1,0:T(8,128)(2,1)S(1)} %collective-permute-done.other_ref.b3), channel_id=1, source_target_pairs={{0,4},{1,0},{2,6},{3,2},{4,8},{5,1},{6,10},{7,3},{8,12},{9,5},{10,... | collective-permute-start | bytes 208904 | tf_op jit(solution)/shard_map/ppermute | solution.py:624
  11.2 1.4 %collective-permute-start.5 = (bf16[400,128]{1,0:T(8,128)(2,1)S(1)}, bf16[400,128]{1,0:T(8,128)(2,1)S(1)}, u32[]{:S(2)}, u32[]{:S(2)}) collective-permute-start(bf16[400,128]{1,0:T(8,128)(2,1)S(1)} %shard_map.86), channel_id=1, source_target_pairs={{0,1},{1,0},{2,3},{3,2},{4,5},{5,4},{6,7},{7,6},{8,9},{9,8},{10,11... | collective-permute-start | bytes 307208 | tf_op jit(solution)/shard_map/ppermute | solution.py:624
  12.7 4.4 %collective-permute-start.6 = (bf16[272,128]{1,0:T(8,128)(2,1)S(1)}, bf16[272,128]{1,0:T(8,128)(2,1)S(1)}, u32[]{:S(2)}, u32[]{:S(2)}) collective-permute-start(bf16[272,128]{1,0:T(8,128)(2,1)S(1)} %get-tuple-element.15), channel_id=1, source_target_pairs={{0,2},{1,3},{2,0},{3,1},{4,6},{5,7},{6,4},{7,5},{8,10},{9,11},{10,... | collective-permute-start | bytes 208904 | tf_op jit(solution)/shard_map/ppermute | solution.py:624
  17.1 3.6 %copy-start = (bf16[2,64,16,128]{3,2,1,0:T(8,128)(2,1)S(1)}, bf16[2,64,16,128]{3,2,1,0:T(8,128)(2,1)}, u32[]{:S(2)}) copy-start(bf16[2,64,16,128]{3,2,1,0:T(8,128)(2,1)} %members_ref.1) | copy-start | bytes 1572868
  18.6 2.1 %collective-permute-start.9 = (bf16[272,128]{1,0:T(8,128)(2,1)S(1)}, bf16[272,128]{1,0:T(8,128)(2,1)S(1)}, u32[]{:S(2)}, u32[]{:S(2)}) collective-permute-start(bf16[272,128]{1,0:T(8,128)(2,1)S(1)} %shard_map.88.own), channel_id=1, source_target_pairs={{0,1},{1,0},{2,3},{3,2},{4,5},{5,4},{6,7},{7,6},{8,9},{9,8},{10,11... | collective-permute-start | bytes 208904 | tf_op jit(solution)/shard_map/ppermute | solution.py:624
  18.6 4.3 %collective-permute-start.8 = (bf16[272,128]{1,0:T(8,128)(2,1)S(1)}, bf16[272,128]{1,0:T(8,128)(2,1)S(1)}, u32[]{:S(2)}, u32[]{:S(2)}) collective-permute-start(bf16[272,128]{1,0:T(8,128)(2,1)S(1)} %shard_map.88.own), channel_id=1, source_target_pairs={{4,0},{0,1},{6,2},{2,3},{8,4},{1,5},{10,6},{3,7},{12,8},{5,9},{14,... | collective-permute-start | bytes 208904 | tf_op jit(solution)/shard_map/ppermute | solution.py:624
  19.1 3.8 %collective-permute-start.7 = (bf16[272,128]{1,0:T(8,128)(2,1)S(1)}, bf16[272,128]{1,0:T(8,128)(2,1)S(1)}, u32[]{:S(2)}, u32[]{:S(2)}) collective-permute-start(bf16[272,128]{1,0:T(8,128)(2,1)S(1)} %shard_map.88.own), channel_id=1, source_target_pairs={{0,4},{1,0},{2,6},{3,2},{4,8},{5,1},{6,10},{7,3},{8,12},{9,5},{10,... | collective-permute-start | bytes 208904 | tf_op jit(solution)/shard_map/ppermute | solution.py:624
  23.0 2.0 %collective-permute-start.10 = (bf16[272,128]{1,0:T(8,128)(2,1)S(1)}, bf16[272,128]{1,0:T(8,128)(2,1)S(1)}, u32[]{:S(2)}, u32[]{:S(2)}) collective-permute-start(bf16[272,128]{1,0:T(8,128)(2,1)S(1)} %collective-permute-done.7.climb), channel_id=1, source_target_pairs={{0,1},{1,0},{2,3},{3,2},{4,5},{5,4},{6,7},{7,6},{8,9},{9,8},{10,11... | collective-permute-start | bytes 208904 | tf_op jit(solution)/shard_map/ppermute | solution.py:624
  24.1 1.3 %collective-permute-start.11 = (bf16[272,128]{1,0:T(8,128)(2,1)S(1)}, bf16[272,128]{1,0:T(8,128)(2,1)S(1)}, u32[]{:S(2)}, u32[]{:S(2)}) collective-permute-start(bf16[272,128]{1,0:T(8,128)(2,1)S(1)} %collective-permute-done.8.descend), channel_id=1, source_target_pairs={{0,1},{1,0},{2,3},{3,2},{4,5},{5,4},{6,7},{7,6},{8,9},{9,8},{10,11... | collective-permute-start | bytes 208904 | tf_op jit(solution)/shard_map/ppermute | solution.py:624
